TPU v7x, 32 devices: a whole 2x2x4 slice. The times are simulated.
32 devices in a mesh: shard: 4 (over z), ctx: 4 (over y, x), tensor: 2 (over core).
Axes of the slice: x: 2, y: 2, z: 4, core: 2. Of those that a mesh axis runs over, the one named last changes fastest.
Arguments:
- inputs: bfloat16 [2, 1280, 1472], P(None, ('shard', 'ctx')), may hold values from -6 to 6
- cotangent: bfloat16 [2, 1280, 1472], P(None, ('shard', 'ctx')), may hold values from -6 to 6
- norm1_gain: bfloat16 [1472], P('shard'), may hold values from 0.099609375 to 1.8984375
- w_query: bfloat16 [1472, 384], P('shard', 'tensor'), may hold values from -0.0390625 to 0.0390625
- w_key: bfloat16 [1472, 384], P('shard', 'tensor'), may hold values from -0.15625 to 0.15625
- w_value: bfloat16 [1472, 384], P('shard', 'tensor'), may hold values from -0.15625 to 0.15625
- w_out: bfloat16 [384, 1472], P('tensor', 'shard'), may hold values from -1.25 to 1.25
- norm2_gain: bfloat16 [1472], P('shard'), may hold values from 0.099609375 to 1.8984375
- w_gate: bfloat16 [1472, 3584], P('shard', 'tensor'), may hold values from -0.15625 to 0.15625
- w_up: bfloat16 [1472, 3584], P('shard', 'tensor'), may hold values from -0.15625 to 0.15625
- w_down: bfloat16 [3584, 1472], P('tensor', 'shard'), may hold values from -0.1875 to 0.1875
- bias_table: float32 [32, 6], replicated, may hold values from -4 to 4
Outputs:
- output: bfloat16 [2, 1280, 1472], P(None, ('shard', 'ctx'))
- input_grad: bfloat16 [2, 1280, 1472], P(None, ('shard', 'ctx'))
- norm1_gain_grad: float32 [1472], P('shard')
- w_query_grad: float32 [1472, 384], P('shard', 'tensor')
- w_key_grad: float32 [1472, 384], P('shard', 'tensor')
- w_value_grad: float32 [1472, 384], P('shard', 'tensor')
- w_out_grad: float32 [384, 1472], P('tensor', 'shard')
- norm2_gain_grad: float32 [1472], P('shard')
- w_gate_grad: float32 [1472, 3584], P('shard', 'tensor')
- w_up_grad: float32 [1472, 3584], P('shard', 'tensor')
- w_down_grad: float32 [3584, 1472], P('tensor', 'shard')
All inputs are finite; a program needn't handle non-finite values.
Results may differ from a plain program's by a relative error of at most 0.024.
Values may be sent and summed in bfloat16 or wider, within the bound.
No kernel may reach another device: no remote copies, remote signals or barrier semaphores. Data moves between devices by JAX's collectives and lax.ppermute only.
A program may use at most 128 MiB of HBM per device.

v0:
```python
import jax
import jax.numpy as jnp
from jax import lax
from jax.sharding import PartitionSpec as P

DK = 64


norm_eps = 1e-06
distance_marks = (8, 12, 16, 23, 32, 46, 64, 91)
masked_score = -1e30


def for_sending(x):
    return jax.tree.map(lambda a: a.astype(jnp.bfloat16) if a.dtype == jnp.float32 else a, x)


def path_info(token, seg_len):
    segment = jnp.where(
        token < 8 * seg_len,
        0,
        jnp.where(
            token < 12 * seg_len,
            (token - 8 * seg_len) // seg_len + 1,
            (token - 12 * seg_len) // seg_len + 5,
        ),
    )
    parent = jnp.where(segment == 0, -1, jnp.where(segment <= 4, 0, (segment - 5) // 2 + 1))
    place = token - jnp.where(
        segment == 0, 0, jnp.where(segment <= 4, (segment - 1) * seg_len, (segment - 2) * seg_len)
    )
    return (segment, parent, place)


def bucket_of(relative):
    magnitude = jnp.abs(relative)
    marked = sum(((magnitude >= mark).astype(jnp.int32) for mark in distance_marks))
    return jnp.where(relative > 0, 16, 0) + jnp.where(magnitude < 8, magnitude, 7 + marked)


def score_bias(query_token, key_token, table, seg_len):
    query_seg, query_parent, query_place = path_info(query_token, seg_len)
    key_seg, key_parent, key_place = path_info(key_token, seg_len)
    allowed = (
        (key_seg[None, :] == 0)
        | (key_seg[None, :] == query_seg[:, None])
        | (key_seg[None, :] == query_parent[:, None])
    )
    bucket = bucket_of(key_place[None, :] - query_place[:, None])
    looked = jnp.stack([jnp.take(table[:, head], bucket, axis=0) for head in range(table.shape[1])])
    return jnp.where(allowed[None], looked, masked_score)


def left_dot(left, right):
    return lax.dot_general(
        left, right, (((0,), (0,)), ((), ())), preferred_element_type=jnp.float32
    )


def right_dot(left, right):
    return lax.dot_general(
        left, right, (((1,), (1,)), ((), ())), preferred_element_type=jnp.float32
    )


def norm_back(values_in, scale, gain, normed_grad):
    weighted = normed_grad * gain
    value_grad = scale * weighted - values_in * scale**3 * jnp.mean(
        weighted * values_in, axis=-1, keepdims=True
    )
    gain_grad = jnp.sum(normed_grad * values_in * scale, axis=0)
    return (value_grad, gain_grad)


def gelu_tanh(value_in):
    return jax.nn.gelu(value_in, approximate=True)


def one_layer(weights, tokens_in, grad_in, bias_local, row_count, key_count):
    gain_one, w_query, w_key, w_value, w_out, gain_two, w_gate, w_up, w_down = weights
    inner = w_query.shape[1]
    heads_local = inner // DK
    gain_first = gain_one.astype(jnp.float32)
    gain_second = gain_two.astype(jnp.float32)
    start_in = tokens_in.astype(jnp.float32)
    scale_one = lax.rsqrt(jnp.mean(start_in * start_in, axis=-1, keepdims=True) + norm_eps)
    normed_one = (start_in * scale_one * gain_first).astype(jnp.bfloat16)
    queries = jnp.dot(normed_one, w_query, preferred_element_type=jnp.float32).astype(jnp.bfloat16)
    keys = jnp.dot(normed_one, w_key, preferred_element_type=jnp.float32).astype(jnp.bfloat16)
    values = jnp.dot(normed_one, w_value, preferred_element_type=jnp.float32).astype(jnp.bfloat16)
    key_path, value_path = (
        lax.all_gather(keys, "ctx", axis=0, tiled=True),
        lax.all_gather(values, "ctx", axis=0, tiled=True),
    )
    query_heads = queries.reshape(row_count, heads_local, DK)
    key_heads = key_path.reshape(key_count, heads_local, DK)
    value_heads = value_path.reshape(key_count, heads_local, DK)

    def score_block():
        raw = jnp.einsum("qhd,khd->hqk", query_heads, key_heads, preferred_element_type=jnp.float32)
        return raw + bias_local

    scores = score_block()
    row_max = jnp.max(scores, axis=-1, keepdims=True)
    raised = jnp.exp(scores - row_max)
    totals = jnp.sum(raised, axis=-1, keepdims=True)
    log_total = row_max + jnp.log(totals)
    attention = (raised / totals).astype(jnp.bfloat16)
    mixed = jnp.einsum("hqk,khd->qhd", attention, value_heads, preferred_element_type=jnp.float32)
    mixed = mixed.reshape(row_count, inner).astype(jnp.bfloat16)
    attended = lax.psum(
        jnp.dot(mixed, w_out, preferred_element_type=jnp.float32).astype(jnp.bfloat16), "tensor"
    ).astype(jnp.float32)
    middle = start_in + attended
    scale_two = lax.rsqrt(jnp.mean(middle * middle, axis=-1, keepdims=True) + norm_eps)
    normed_two = (middle * scale_two * gain_second).astype(jnp.bfloat16)
    gate_pre = jnp.dot(normed_two, w_gate, preferred_element_type=jnp.float32)
    up_pre = jnp.dot(normed_two, w_up, preferred_element_type=jnp.float32)
    activated = gelu_tanh(gate_pre)
    hidden = (activated * up_pre).astype(jnp.bfloat16)
    feed = lax.psum(
        jnp.dot(hidden, w_down, preferred_element_type=jnp.float32).astype(jnp.bfloat16), "tensor"
    ).astype(jnp.float32)
    produced = (middle + feed).astype(jnp.bfloat16)
    grad_out = grad_in.astype(jnp.float32)
    down_in = grad_out.astype(jnp.bfloat16)
    down_grad = left_dot(hidden, down_in)
    hidden_grad = right_dot(down_in, w_down)
    unused, gelu_pull = jax.vjp(gelu_tanh, gate_pre)
    gate_grad = gelu_pull(hidden_grad * up_pre)[0].astype(jnp.bfloat16)
    up_grad = (hidden_grad * activated).astype(jnp.bfloat16)
    gate_wgrad = left_dot(normed_two, gate_grad)
    up_wgrad = left_dot(normed_two, up_grad)
    normed_two_grad = lax.psum(
        (right_dot(gate_grad, w_gate) + right_dot(up_grad, w_up)).astype(jnp.bfloat16), "tensor"
    ).astype(jnp.float32)
    middle_part, gain_two_grad = norm_back(middle, scale_two, gain_second, normed_two_grad)
    middle_grad = grad_out + middle_part
    out_in = middle_grad.astype(jnp.bfloat16)
    out_wgrad = left_dot(mixed, out_in)
    mixed_grad = right_dot(out_in, w_out).astype(jnp.bfloat16)
    mixed_heads = mixed_grad.reshape(row_count, heads_local, DK)
    soft = jnp.exp(score_block() - log_total)
    soft_low = soft.astype(jnp.bfloat16)
    values_full = jnp.einsum(
        "hqk,qhd->khd", soft_low, mixed_heads, preferred_element_type=jnp.float32
    )
    weight_grad = jnp.einsum(
        "qhd,khd->hqk", mixed_heads, value_heads, preferred_element_type=jnp.float32
    )
    scores_grad = soft * (weight_grad - jnp.sum(weight_grad * soft, axis=-1, keepdims=True))
    scores_grad = scores_grad.astype(jnp.bfloat16)
    queries_grad = jnp.einsum(
        "hqk,khd->qhd", scores_grad, key_heads, preferred_element_type=jnp.float32
    )
    queries_grad = queries_grad.reshape(row_count, inner).astype(jnp.bfloat16)
    keys_full = jnp.einsum(
        "hqk,qhd->khd", scores_grad, query_heads, preferred_element_type=jnp.float32
    )
    keys_own, values_own = (
        lax.psum_scatter(
            keys_full.reshape(key_count, inner).astype(jnp.bfloat16),
            "ctx",
            scatter_dimension=0,
            tiled=True,
        ).astype(jnp.float32),
        lax.psum_scatter(
            values_full.reshape(key_count, inner).astype(jnp.bfloat16),
            "ctx",
            scatter_dimension=0,
            tiled=True,
        ).astype(jnp.float32),
    )
    keys_grad = keys_own.astype(jnp.bfloat16)
    values_grad = values_own.astype(jnp.bfloat16)
    query_wgrad = left_dot(normed_one, queries_grad)
    key_wgrad = left_dot(normed_one, keys_grad)
    value_wgrad = left_dot(normed_one, values_grad)
    local_first = (
        right_dot(queries_grad, w_query)
        + right_dot(keys_grad, w_key)
        + right_dot(values_grad, w_value)
    )
    normed_one_grad = lax.psum(local_first.astype(jnp.bfloat16), "tensor").astype(jnp.float32)
    input_part, gain_one_grad = norm_back(start_in, scale_one, gain_first, normed_one_grad)
    input_grad = (middle_grad + input_part).astype(jnp.bfloat16)
    grads = (
        gain_one_grad,
        query_wgrad,
        key_wgrad,
        value_wgrad,
        out_wgrad,
        gain_two_grad,
        gate_wgrad,
        up_wgrad,
        down_grad,
    )
    return (produced, input_grad, grads)


def on_device(
    inputs,
    cotangent,
    norm1_gain,
    w_query,
    w_key,
    w_value,
    w_out,
    norm2_gain,
    w_gate,
    w_up,
    w_down,
    bias_table,
):
    micro_count = inputs.shape[0]
    row_count = inputs.shape[1]
    key_count = row_count * lax.axis_size("ctx")
    heads_local = w_query.shape[1] // DK
    query_token = lax.axis_index("ctx") * row_count + jnp.arange(row_count, dtype=jnp.int32)
    key_token = jnp.arange(key_count, dtype=jnp.int32)
    table_local = lax.dynamic_slice_in_dim(
        bias_table, lax.axis_index("tensor") * heads_local, heads_local, 1
    )
    bias_local = score_bias(query_token, key_token, table_local, row_count // 5)
    outputs_list = []
    input_grads = []
    running = None
    for micro_step in range(micro_count):
        weights = (
            lax.all_gather(norm1_gain, "shard", axis=0, tiled=True),
            lax.all_gather(w_query, "shard", axis=0, tiled=True),
            lax.all_gather(w_key, "shard", axis=0, tiled=True),
            lax.all_gather(w_value, "shard", axis=0, tiled=True),
            lax.all_gather(w_out, "shard", axis=1, tiled=True),
            lax.all_gather(norm2_gain, "shard", axis=0, tiled=True),
            lax.all_gather(w_gate, "shard", axis=0, tiled=True),
            lax.all_gather(w_up, "shard", axis=0, tiled=True),
            lax.all_gather(w_down, "shard", axis=1, tiled=True),
        )
        produced, input_grad, grads = one_layer(
            weights, inputs[micro_step], cotangent[micro_step], bias_local, row_count, key_count
        )
        outputs_list.append(produced)
        input_grads.append(input_grad)
        running = grads if running is None else jax.tree.map(jnp.add, running, grads)
    owned = (
        lax.psum_scatter(
            running[0].astype(jnp.bfloat16), "shard", scatter_dimension=0, tiled=True
        ).astype(jnp.float32),
        lax.psum_scatter(
            running[1].astype(jnp.bfloat16), "shard", scatter_dimension=0, tiled=True
        ).astype(jnp.float32),
        lax.psum_scatter(
            running[2].astype(jnp.bfloat16), "shard", scatter_dimension=0, tiled=True
        ).astype(jnp.float32),
        lax.psum_scatter(
            running[3].astype(jnp.bfloat16), "shard", scatter_dimension=0, tiled=True
        ).astype(jnp.float32),
        lax.psum_scatter(
            running[4].astype(jnp.bfloat16), "shard", scatter_dimension=1, tiled=True
        ).astype(jnp.float32),
        lax.psum_scatter(
            running[5].astype(jnp.bfloat16), "shard", scatter_dimension=0, tiled=True
        ).astype(jnp.float32),
        lax.psum_scatter(
            running[6].astype(jnp.bfloat16), "shard", scatter_dimension=0, tiled=True
        ).astype(jnp.float32),
        lax.psum_scatter(
            running[7].astype(jnp.bfloat16), "shard", scatter_dimension=0, tiled=True
        ).astype(jnp.float32),
        lax.psum_scatter(
            running[8].astype(jnp.bfloat16), "shard", scatter_dimension=1, tiled=True
        ).astype(jnp.float32),
    )
    final_grads = jax.tree.map(
        lambda part: part.astype(jnp.float32), lax.psum(for_sending(owned), "ctx")
    )
    return (jnp.stack(outputs_list), jnp.stack(input_grads)) + tuple(final_grads)


def solution(mesh):
    placed = (
        P(None, ("shard", "ctx"), None),
        P(None, ("shard", "ctx"), None),
        P("shard"),
        P("shard", "tensor"),
        P("shard", "tensor"),
        P("shard", "tensor"),
        P("tensor", "shard"),
        P("shard"),
        P("shard", "tensor"),
        P("shard", "tensor"),
        P("tensor", "shard"),
        P(),
    )
    return jax.shard_map(
        on_device,
        mesh=mesh,
        in_specs=placed,
        out_specs=(
            P(None, ("shard", "ctx"), None),
            P(None, ("shard", "ctx"), None),
            P("shard"),
            P("shard", "tensor"),
            P("shard", "tensor"),
            P("shard", "tensor"),
            P("tensor", "shard"),
            P("shard"),
            P("shard", "tensor"),
            P("shard", "tensor"),
            P("tensor", "shard"),
        ),
        check_vma=False,
    )
```

profile of v0, /device:TPU:0, one launch (start us, length us, event | category | flops | bytes accessed | tf_op | source)
XLA Modules:
  0.0 1594.6 jit_solution(13874918093051243575)
XLA Ops:
  9.8 18.5 %all-gather = bf16[4,368,192]{1,2,0:T(8,128)(2,1)S(1)} all-gather(bf16[1,368,192]{1,2,0:T(8,128)(2,1)} %bitcast.319), channel_id=1, replica_groups=mesh['shard'=4,'ctx'=4,'tensor'=2] {'shard'}, dimensions={0}, use_global_device_ids=true | all-gather | bytes 706560 | tf_op jit(solution)/shard_map/all_gather | solution.py:233
  34.4 12.9 all-reduce.7
  47.4 15.8 all-gather.1
  67.4 14.9 all-gather.2
  83.9 8.6 all_gather.59
  93.0 151.6 %gather_fusion = f32[25600]{0:T(1024)S(1)} fusion(f32[32]{0:T(128)S(1)} %get-tuple-element.66, s32[25600]{0:T(1024)S(1)} %broadcast_clamp_fusion), kind=kCustom, calls=%fused_computation.clone | custom fusion | bytes 307200 | tf_op jit(solution)/shard_map/jit(_take)/gather | solution.py:50
  244.7 151.6 %gather_fusion.1 = f32[25600]{0:T(1024)S(1)} fusion(f32[32]{0:T(128)S(1)} %get-tuple-element.68, s32[25600]{0:T(1024)S(1)} %broadcast_clamp_fusion), kind=kCustom, calls=%fused_computation.1.clone | custom fusion | bytes 307200 | tf_op jit(solution)/shard_map/jit(_take)/gather | solution.py:50
  396.5 151.6 %gather_fusion.2 = f32[25600]{0:T(1024)S(1)} fusion(f32[32]{0:T(128)S(1)} %get-tuple-element.67, s32[25600]{0:T(1024)S(1)} %broadcast_clamp_fusion), kind=kCustom, calls=%fused_computation.2.clone | custom fusion | bytes 307200 | tf_op jit(solution)/shard_map/jit(_take)/gather | solution.py:50
  548.3 8.6 all_gather.60
  557.1 15.0 all-gather.3
  573.0 7.6 all_gather.50
  580.9 8.6 all_gather.53
  595.8 14.7 all-reduce.22.cloned.1.call-done
  614.3 77.9 %all-gather.8.cloned.1.call-done = bf16[1472,1792]{1,0:T(8,128)(2,1)} async-done(((bf16[368,1792]{1,0:T(8,128)(2,1)}), bf16[1472,1792]{1,0:T(8,128)(2,1)}) %all-gather.8.cloned.1.call-update) | async-done | bytes 5275664 | tf_op jit(solution)/shard_map/all_gather | solution.py:236
  692.2 4.3 fusion.158
  696.5 94.0 %all-gather.10.cloned.1.call-done = bf16[1472,1792]{1,0:T(8,128)(2,1)} async-done(((bf16[368,1792]{1,0:T(8,128)(2,1)}), bf16[1472,1792]{1,0:T(8,128)(2,1)}) %all-gather.10.cloned.1.call-update) | async-done | bytes 5275664 | tf_op jit(solution)/shard_map/all_gather | solution.py:237
  790.5 4.4 fusion.159
  798.5 90.3 %all-gather.12.cloned.1.call-done = bf16[1792,1472]{0,1:T(8,128)(2,1)} async-done(((bf16[1792,368]{0,1:T(8,128)(2,1)}), bf16[1792,1472]{0,1:T(8,128)(2,1)}) %all-gather.12.cloned.1.call-update) | async-done | bytes 5275664 | tf_op jit(solution)/shard_map/all_gather | solution.py:238
  888.8 4.7 multiply_convert_fusion
  893.6 4.4 fusion.162
  902.8 2.4 fusion.6
  905.1 2.4 fusion.4
  907.6 17.1 %all-reduce.20.cloned.1.call-done = (bf16[80,1472]{1,0:T(8,128)(2,1)}, bf16[80,1472]{1,0:T(8,128)(2,1)}) async-done(((bf16[80,1472]{1,0:T(8,128)(2,1)}, bf16[80,1472]{1,0:T(8,128)(2,1)}), (bf16[80,1472]{1,0:T(8,128)(2,1)}, bf16[80,1472]{1,0:T(8,128)(2,1)})) %all-reduce.20.cloned.1.call-update) | async-done | bytes 471056 | tf_op jit(solution)/shard_map/psum | solution.py:134
  924.8 2.1 fusion.53
  949.9 2.2 copy.77
  957.5 2.2 copy.71
  962.6 25.4 %reduce-scatter.38.cloned.1.call-done = bf16[80,192]{1,0:T(8,128)(2,1)} async-done(((bf16[320,192]{1,0:T(8,128)(2,1)}), bf16[80,192]{1,0:T(8,128)(2,1)}) %reduce-scatter.38.cloned.1.call-update) | async-done | bytes 30736
  990.0 2.2 copy.73
  992.3 22.3 %reduce-scatter.36.cloned.1.call-done = bf16[80,192]{1,0:T(8,128)(2,1)} async-done(((bf16[320,192]{1,0:T(8,128)(2,1)}), bf16[80,192]{1,0:T(8,128)(2,1)}) %reduce-scatter.36.cloned.1.call-update) | async-done | bytes 30736
  1015.8 25.4 %reduce-scatter.40.cloned.1.call-done = bf16[80,192]{1,0:T(8,128)(2,1)} async-done(((bf16[320,192]{1,0:T(8,128)(2,1)}), bf16[80,192]{1,0:T(8,128)(2,1)}) %reduce-scatter.40.cloned.1.call-update) | async-done | bytes 30736
  1043.2 2.2 copy.75
  1045.5 2.6 fusion.164
  1048.1 4.0 add_convert_fusion.2
  1054.6 3.9 add_convert_fusion.1
  1061.1 3.9 add_convert_fusion
  1065.4 4.9 convolution_convert_fusion
  1070.3 5.0 convolution_convert_fusion.2
  1080.0 11.6 reduce-scatter.42.cloned.1.call-done
  1093.2 23.3 %reduce-scatter.44.cloned.1.call-done = bf16[368,192]{1,0:T(8,128)(2,1)} async-done(((bf16[1472,192]{1,0:T(8,128)(2,1)}), bf16[368,192]{1,0:T(8,128)(2,1)}) %reduce-scatter.44.cloned.1.call-update) | async-done | bytes 141328
  1118.3 23.1 %reduce-scatter.46.cloned.1.call-done = bf16[368,192]{1,0:T(8,128)(2,1)} async-done(((bf16[1472,192]{1,0:T(8,128)(2,1)}), bf16[368,192]{1,0:T(8,128)(2,1)}) %reduce-scatter.46.cloned.1.call-update) | async-done | bytes 141328
  1143.1 94.0 %reduce-scatter.28.cloned.1.call-done = bf16[368,1792]{1,0:T(8,128)(2,1)} async-done(((bf16[1472,1792]{1,0:T(8,128)(2,1)}), bf16[368,1792]{1,0:T(8,128)(2,1)}) %reduce-scatter.28.cloned.1.call-update) | async-done | bytes 1318928 | tf_op jit(solution)/shard_map/reduce_scatter | solution.py:265
  1237.2 97.0 %reduce-scatter.30.cloned.1.call-done = bf16[368,1792]{1,0:T(8,128)(2,1)} async-done(((bf16[1472,1792]{1,0:T(8,128)(2,1)}), bf16[368,1792]{1,0:T(8,128)(2,1)}) %reduce-scatter.30.cloned.1.call-update) | async-done | bytes 1318928 | tf_op jit(solution)/shard_map/reduce_scatter | solution.py:268
  1334.2 97.1 %reduce-scatter.32.cloned.1.call-done = bf16[1792,368]{0,1:T(8,128)(2,1)} async-done(((bf16[1792,1472]{0,1:T(8,128)(2,1)}), bf16[1792,368]{0,1:T(8,128)(2,1)}) %reduce-scatter.32.cloned.1.call-update) | async-done | bytes 1318928 | tf_op jit(solution)/shard_map/reduce_scatter | solution.py:271
  1432.0 22.5 %all-reduce.18.cloned.1.call-done = (bf16[80,1472]{1,0:T(8,128)(2,1)}, bf16[80,1472]{1,0:T(8,128)(2,1)}, bf16[80,1472]{1,0:T(8,128)(2,1)}, bf16[80,1472]{1,0:T(8,128)(2,1)}) async-done(((bf16[80,1472]{1,0:T(8,128)(2,1)}, bf16[80,1472]{1,0:T(8,128)(2,1)}, bf16[80,1472]{1,0:T(8,128)(2,1)}, bf16[80,1472]{1,0:T(8,128)(2,1)}), (bf16[80,1472]{1,0:T(8,128)(2,1)}, bf16[80,1472]{1,0:T(8,128)(2,1)}, ...) | async-done | bytes 942096 | tf_op jit(solution)/shard_map/psum | solution.py:121
  1455.9 12.2 all-reduce.6
  1468.3 10.1 all-reduce.4
  1483.2 90.6 %all-reduce.16.cloned.1.call-done = (bf16[368,192]{0,1:T(8,128)(2,1)}, bf16[368,192]{0,1:T(8,128)(2,1)}, bf16[368,192]{0,1:T(8,128)(2,1)}, bf16[192,368]{1,0:T(8...) async-done(((bf16[368,192]{0,1:T(8,128)(2,1)}, bf16[368,192]{0,1:T(8,128)(2,1)}, bf16[368,192]{0,1:T(8,128)(2,1)}, ...) | async-done | bytes 4522000 | tf_op jit(solution)/shard_map/psum | solution.py:276
  1580.5 3.0 convert_element_type.467
  (313 shorter events, 101.3 us)
Async XLA Ops:
  8.0 84.6 %copy-start = (f32[32,6]{0,1:T(8,128)S(1)}, f32[32,6]{0,1:T(8,128)}, u32[]{:S(2)}) copy-start(f32[32,6]{0,1:T(8,128)} %param.25) | copy-start | bytes 2308
  8.0 56.7 %copy-start.5 = (bf16[2,80,1472]{2,1,0:T(8,128)(2,1)S(1)}, bf16[2,80,1472]{2,1,0:T(8,128)(2,1)}, u32[]{:S(2)}) copy-start(bf16[2,80,1472]{2,1,0:T(8,128)(2,1)} %param.14) | copy-start | bytes 1413124
  8.0 602.5 %all-reduce.22.cloned.1.call-start = ((), (), s32[]{:S(2)}) async-start(), calls=%async_computation.28 | async-start | bytes 983040 | tf_op jit(solution)/shard_map/psum | solution.py:111
  8.7 83.9 %copy-start.65 = (s32[80]{0:T(128)}, s32[80]{0:T(128)S(1)}, u32[]{:S(2)}) copy-start(s32[80]{0:T(128)S(1)} %fusion.138) | copy-start | bytes 964
  9.8 57.6 %copy-start.50 = (bf16[368,192]{0,1:T(8,128)(2,1)S(1)}, bf16[368,192]{0,1:T(8,128)(2,1)}, u32[]{:S(2)}) copy-start(bf16[368,192]{0,1:T(8,128)(2,1)} %param.18) | copy-start | bytes 423940
  29.2 54.0 %copy-start.17 = (bf16[1472,192]{0,1:T(8,128)(2,1)}, bf16[1472,192]{0,1:T(8,128)(2,1)S(1)}, u32[]{:S(2)}) copy-start(bf16[1472,192]{0,1:T(8,128)(2,1)S(1)} %reshape.446) | copy-start | bytes 1695748
  64.7 179.9 %copy-start.57 = (f32[80]{0:T(128)}, f32[80]{0:T(128)S(1)}, u32[]{:S(2)}) copy-start(f32[80]{0:T(128)S(1)} %get-tuple-element.74) | copy-start | bytes 964
  64.7 179.9 %copy-start.59 = (f32[80]{0:T(128)}, f32[80]{0:T(128)S(1)}, u32[]{:S(2)}) copy-start(f32[80]{0:T(128)S(1)} %get-tuple-element.87) | copy-start | bytes 964
  92.6 498.0 %copy-start.37 = (bf16[320,192]{0,1:T(8,128)(2,1)}, bf16[320,192]{0,1:T(8,128)(2,1)S(1)}, u32[]{:S(2)}) copy-start(bf16[320,192]{0,1:T(8,128)(2,1)S(1)} %copy.58) | copy-start | bytes 368644
  396.4 160.6 %copy-start.51 = (bf16[192,368]{1,0:T(8,128)(2,1)S(1)}, bf16[192,368]{1,0:T(8,128)(2,1)}, u32[]{:S(2)}) copy-start(bf16[192,368]{1,0:T(8,128)(2,1)} %param.20) | copy-start | bytes 423940
  396.4 176.5 %copy-start.54 = (bf16[80,192]{1,0:T(8,128)(2,1)S(1)}, bf16[80,192]{1,0:T(8,128)(2,1)}, u32[]{:S(2)}) copy-start(bf16[80,192]{1,0:T(8,128)(2,1)} %convolution_convert_fusion.19) | copy-start | bytes 92164
  396.4 184.3 %copy-start.53 = (bf16[80,192]{1,0:T(8,128)(2,1)S(1)}, bf16[80,192]{1,0:T(8,128)(2,1)}, u32[]{:S(2)}) copy-start(bf16[80,192]{1,0:T(8,128)(2,1)} %convolution_convert_fusion.18) | copy-start | bytes 92164
  396.5 193.1 %copy-start.66 = (s32[80]{0:T(128)S(1)}, s32[80]{0:T(128)}, u32[]{:S(2)}) copy-start(s32[80]{0:T(128)} %copy-done.65) | copy-start | bytes 964
  548.1 41.8 %copy-start.61 = (s32[320]{0:T(512)S(1)}, s32[320]{0:T(512)}, u32[]{:S(2)}) copy-start(s32[320]{0:T(512)} %fusion.131) | copy-start | bytes 3844
  548.1 41.8 %copy-start.69 = (s32[80]{0:T(128)S(1)}, s32[80]{0:T(128)}, u32[]{:S(2)}) copy-start(s32[80]{0:T(128)} %get-tuple-element.89) | copy-start | bytes 964
  548.1 41.8 %copy-start.70 = (s32[80]{0:T(128)S(1)}, s32[80]{0:T(128)}, u32[]{:S(2)}) copy-start(s32[80]{0:T(128)} %get-tuple-element.90) | copy-start | bytes 964
  548.1 41.8 %copy-start.71 = (pred[320]{0:T(512)(128)(4,1)S(1)}, pred[320]{0:T(512)(128)(4,1)}, u32[]{:S(2)}) copy-start(pred[320]{0:T(512)(128)(4,1)} %broadcast_compare_fusion) | copy-start | bytes 964
  548.3 43.6 %copy-start.42 = (bf16[80,192]{0,1:T(8,128)(2,1)}, bf16[80,192]{0,1:T(8,128)(2,1)S(1)}, u32[]{:S(2)}) copy-start(bf16[80,192]{0,1:T(8,128)(2,1)S(1)} %copy.59) | copy-start | bytes 92164
  557.0 34.8 %copy-start.32 = (bf16[320,192]{0,1:T(8,128)(2,1)}, bf16[320,192]{0,1:T(8,128)(2,1)S(1)}, u32[]{:S(2)}) copy-start(bf16[320,192]{0,1:T(8,128)(2,1)S(1)} %copy.60) | copy-start | bytes 368644
  593.8 98.4 %all-gather.8.cloned.1.call-start = ((), (), s32[]{:S(2)}) async-start(), calls=%async_computation.11 | async-start | bytes 6594560 | tf_op jit(solution)/shard_map/all_gather | solution.py:236
  594.4 196.1 %all-gather.10.cloned.1.call-start = ((), (), s32[]{:S(2)}) async-start(), calls=%async_computation.12 | async-start | bytes 6594560 | tf_op jit(solution)/shard_map/all_gather | solution.py:237
  595.0 293.8 %all-gather.12.cloned.1.call-start = ((), (), s32[]{:S(2)}) async-start(), calls=%async_computation.13 | async-start | bytes 6594560 | tf_op jit(solution)/shard_map/all_gather | solution.py:238
  595.6 329.2 %all-reduce.20.cloned.1.call-start = ((), (), s32[]{:S(2)}) async-start(), calls=%async_computation.27 | async-start | bytes 983040 | tf_op jit(solution)/shard_map/psum | solution.py:134
  595.8 328.9 %copy-start.52 = (f32[1472]{0:T(1024)}, f32[1472]{0:T(1024)S(1)}, u32[]{:S(2)}) copy-start(f32[1472]{0:T(1024)S(1)} %convert_element_type.383) | copy-start | bytes 17668
  612.4 312.3 %copy-start.62 = (f32[80]{0:T(128)}, f32[80]{0:T(128)S(1)}, u32[]{:S(2)}) copy-start(f32[80]{0:T(128)S(1)} %get-tuple-element.76) | copy-start | bytes 964
  613.0 311.7 %copy-start.63 = (f32[80]{0:T(128)}, f32[80]{0:T(128)S(1)}, u32[]{:S(2)}) copy-start(f32[80]{0:T(128)S(1)} %get-tuple-element.78) | copy-start | bytes 964
  614.3 180.6 %copy-start.7 = (bf16[80,1472]{1,0:T(8,128)(2,1)}, bf16[80,1472]{1,0:T(8,128)(2,1)S(1)}, u32[]{:S(2)}) copy-start(bf16[80,1472]{1,0:T(8,128)(2,1)S(1)} %get-tuple-element.60) | copy-start | bytes 706564
  794.9 93.9 %copy-start.6 = (bf16[2,80,1472]{2,1,0:T(8,128)(2,1)S(1)}, bf16[2,80,1472]{2,1,0:T(8,128)(2,1)}, u32[]{:S(2)}) copy-start(bf16[2,80,1472]{2,1,0:T(8,128)(2,1)} %param.15) | copy-start | bytes 1413124
  907.5 53.9 %reduce-scatter.34.cloned.1.call-start = ((), (), s32[]{:S(2)}) async-start(), calls=%async_computation.17 | async-start | bytes 204800
  936.2 51.9 %reduce-scatter.38.cloned.1.call-start = ((), (), s32[]{:S(2)}) async-start(), calls=%async_computation.19 | async-start | bytes 204800
  941.1 73.5 %reduce-scatter.36.cloned.1.call-start = ((), (), s32[]{:S(2)}) async-start(), calls=%async_computation.18 | async-start | bytes 204800
  946.5 94.7 %reduce-scatter.40.cloned.1.call-start = ((), (), s32[]{:S(2)}) async-start(), calls=%async_computation.20 | async-start | bytes 204800
  947.7 130.5 %reduce-scatter.48.cloned.1.call-start = ((), (), s32[]{:S(2)}) async-start(), calls=%async_computation.24 | async-start | bytes 942080
  949.9 38.2 %copy-start.58 = (f32[80]{0:T(128)S(1)}, f32[80]{0:T(128)}, u32[]{:S(2)}) copy-start(f32[80]{0:T(128)} %copy-done.57) | copy-start | bytes 964
  952.1 139.4 %reduce-scatter.42.cloned.1.call-start = ((), (), s32[]{:S(2)}) async-start(), calls=%async_computation.21 | async-start | bytes 942080
  959.7 156.9 %reduce-scatter.44.cloned.1.call-start = ((), (), s32[]{:S(2)}) async-start(), calls=%async_computation.22 | async-start | bytes 942080
  992.2 149.2 %reduce-scatter.46.cloned.1.call-start = ((), (), s32[]{:S(2)}) async-start(), calls=%async_computation.23 | async-start | bytes 942080
  1045.5 191.7 %reduce-scatter.28.cloned.1.call-start = ((), (), s32[]{:S(2)}) async-start(), calls=%async_computation.14 | async-start | bytes 6594560 | tf_op jit(solution)/shard_map/reduce_scatter | solution.py:265
  1052.2 282.0 %reduce-scatter.30.cloned.1.call-start = ((), (), s32[]{:S(2)}) async-start(), calls=%async_computation.15 | async-start | bytes 6594560 | tf_op jit(solution)/shard_map/reduce_scatter | solution.py:268
  1058.5 372.8 %reduce-scatter.32.cloned.1.call-start = ((), (), s32[]{:S(2)}) async-start(), calls=%async_computation.16 | async-start | bytes 6594560 | tf_op jit(solution)/shard_map/reduce_scatter | solution.py:271
  1065.0 389.4 %all-reduce.18.cloned.1.call-start = ((), (), s32[]{:S(2)}) async-start(), calls=%async_computation.26 | async-start | bytes 1966080 | tf_op jit(solution)/shard_map/psum | solution.py:121
  1076.9 355.0 %copy-start.55 = (f32[1472]{0:T(1024)S(1)}, f32[1472]{0:T(1024)}, u32[]{:S(2)}) copy-start(f32[1472]{0:T(1024)} %get-tuple-element.14) | copy-start | bytes 17668
  1076.9 355.0 %copy-start.56 = (f32[1472]{0:T(1024)S(1)}, f32[1472]{0:T(1024)}, u32[]{:S(2)}) copy-start(f32[1472]{0:T(1024)} %get-tuple-element.23) | copy-start | bytes 17668
  1076.9 402.6 %copy-start.10 = (bf16[80,1472]{1,0:T(8,128)(2,1)S(1)}, bf16[80,1472]{1,0:T(8,128)(2,1)}, u32[]{:S(2)}) copy-start(bf16[80,1472]{1,0:T(8,128)(2,1)} %get-tuple-element.47) | copy-start | bytes 706564
  1077.0 402.6 %copy-start.12 = (bf16[80,1472]{1,0:T(8,128)(2,1)S(1)}, bf16[80,1472]{1,0:T(8,128)(2,1)}, u32[]{:S(2)}) copy-start(bf16[80,1472]{1,0:T(8,128)(2,1)} %get-tuple-element.48) | copy-start | bytes 706564
  1077.0 402.5 %copy-start.67 = (f32[80]{0:T(128)S(1)}, f32[80]{0:T(128)}, u32[]{:S(2)}) copy-start(f32[80]{0:T(128)} %get-tuple-element.73) | copy-start | bytes 964
  1077.0 402.5 %copy-start.68 = (f32[80]{0:T(128)S(1)}, f32[80]{0:T(128)}, u32[]{:S(2)}) copy-start(f32[80]{0:T(128)} %get-tuple-element.88) | copy-start | bytes 964
  1078.2 495.6 %all-reduce.16.cloned.1.call-start = ((), (), s32[]{:S(2)}) async-start(), calls=%async_computation.25 | async-start | bytes 9093120 | tf_op jit(solution)/shard_map/psum | solution.py:276
  (46 other events, 358.2 us)
Sparse Core Ops, SparseCore 0:
  593.9 16.6 all-reduce.21
  907.7 17.0 all-reduce.19
  936.3 25.1 reduce-scatter.33
  964.1 23.9 reduce-scatter.37
  990.6 23.9 reduce-scatter.35
  1017.2 23.9 reduce-scatter.39
  1043.5 22.9 reduce-scatter.47
  1069.4 22.0 reduce-scatter.41
  1094.4 22.1 reduce-scatter.43
  1119.3 22.0 reduce-scatter.45
  1143.7 93.3 reduce-scatter.27
  1239.3 94.7 reduce-scatter.29
  1336.5 94.7 reduce-scatter.31
  1434.3 20.1 all-reduce.17
  1460.2 113.4 all-reduce.15
Sparse Core Ops, SparseCore 1:
  595.8 96.3 all-gather.7
  693.6 96.8 all-gather.9
  791.9 96.8 all-gather.11
where the time goes:
time: 1600 us; the launch traced here: 1590 us
  waiting for transfers between devices  830 us (52%)
  local copies, waits for them, and re-layouts  489 us (31%)
  blocking collectives  133 us (8%)
  matrix products  91 us (6%)
  other arithmetic  32.1 us (2%)
  between operations  18.6 us (1%)
    gather x6, local copies, waits for them, and re-layouts, score_bias(): jnp.take(table[:, head], bucket, axis=0)  455 us
    unnamed x26, waiting for transfers between devices  135 us
    reduce_scatter x1, waiting for transfers between devices, on_device(): lax.psum_scatter(running[8].astype(jnp.bfloat16), 'shard', scatter_dimens...  97.1 us
    reduce_scatter x1, waiting for transfers between devices, on_device(): lax.psum_scatter(running[7].astype(jnp.bfloat16), 'shard', scatter_dimens...  97 us
    reduce_scatter x1, waiting for transfers between devices, on_device(): lax.psum_scatter(running[6].astype(jnp.bfloat16), 'shard', scatter_dimens...  94 us
    all_gather x1, waiting for transfers between devices, on_device(): lax.all_gather(w_up, 'shard', axis=0, tiled=True)  94 us
    psum x1, waiting for transfers between devices, on_device(): lax.psum(for_sending(owned), 'ctx')  90.6 us
    all_gather x1, waiting for transfers between devices, on_device(): lax.all_gather(w_down, 'shard', axis=1, tiled=True)  90.3 us
  transfers between devices with their start and end apart: 18, of which 17 were waited for; matrix products, arithmetic and copies ran while one was open for 6% of the time, Pallas kernels for 0%

commit v1 on v0

v1 whole, which is shorter than its diff:
```python
import jax
import jax.numpy as jnp
from jax import lax
from jax.sharding import PartitionSpec as P

DK = 64
norm_eps = 1e-06
distance_marks = (8, 12, 16, 23, 32, 46, 64, 91)
masked_score = -1e30
low = jnp.bfloat16
wide = jnp.float32


def path_info(token, seg_len):
    segment = jnp.where(
        token < 8 * seg_len,
        0,
        jnp.where(
            token < 12 * seg_len,
            (token - 8 * seg_len) // seg_len + 1,
            (token - 12 * seg_len) // seg_len + 5,
        ),
    )
    parent = jnp.where(segment == 0, -1, jnp.where(segment <= 4, 0, (segment - 5) // 2 + 1))
    place = token - jnp.where(
        segment == 0, 0, jnp.where(segment <= 4, (segment - 1) * seg_len, (segment - 2) * seg_len)
    )
    return (segment, parent, place)


def score_bias(token, table, seg_len):
    seg, parent, place = path_info(token, seg_len)
    allowed = (
        (seg[None, :] == 0) | (seg[None, :] == seg[:, None]) | (seg[None, :] == parent[:, None])
    )
    relative = place[None, :] - place[:, None]
    magnitude = jnp.abs(relative)
    marked = sum(((magnitude >= mark).astype(jnp.int32) for mark in distance_marks))
    bucket = jnp.where(relative > 0, 16, 0) + jnp.where(magnitude < 8, magnitude, 7 + marked)
    heads = []
    for head in range(table.shape[1]):
        looked = jnp.full(bucket.shape, table[0, head])
        for place_in in range(1, table.shape[0]):
            looked = jnp.where(bucket == place_in, table[place_in, head], looked)
        heads.append(jnp.where(allowed, looked, masked_score))
    return jnp.stack(heads)


def dot(left, right, left_dim, right_dim):
    return lax.dot_general(
        left, right, (((left_dim,), (right_dim,)), ((), ())), preferred_element_type=wide
    )


def step(x, axis):
    n = lax.axis_size(axis)
    return lax.ppermute(x, axis, [(i, (i + 1) % n) for i in range(n)])


def swap(x, axis, k):
    n = lax.axis_size(axis)
    return lax.ppermute(x, axis, [(i, i ^ k) for i in range(n)])


def pick(stack, index):
    return lax.dynamic_index_in_dim(stack, index, 0, keepdims=False)


def put(stack, part, index):
    return lax.dynamic_update_slice_in_dim(stack, part[None], index, 0)


def ring_gather(x, axis):
    n, me = lax.axis_size(axis), lax.axis_index(axis)
    out = put(jnp.zeros((n,) + x.shape, x.dtype), x, me)
    for k in range(1, n):
        x = step(x, axis)
        out = put(out, x, lax.rem(me - k + n, n))
    return out


def ring_scatter(parts, axis):
    n, me = lax.axis_size(axis), lax.axis_index(axis)
    acc = pick(parts, lax.rem(me + n - 1, n))
    for k in range(2, n + 1):
        got = step(acc.astype(low), axis)
        acc = got.astype(wide) + pick(parts, lax.rem(me + 2 * n - k, n)).astype(wide)
    return acc


def xor_gather(x, axis):
    n = lax.axis_size(axis)
    return [x] + [swap(x, axis, k) for k in range(1, n)]


def xor_scatter(parts, axis):
    n = lax.axis_size(axis)
    acc = parts[0].astype(wide)
    for k in range(1, n):
        acc = acc + swap(parts[k].astype(low), axis, k).astype(wide)
    return acc


def absolute(blocks, axis):
    n, me = lax.axis_size(axis), lax.axis_index(axis)
    out = jnp.zeros((n,) + blocks[0].shape, blocks[0].dtype)
    for k in range(n):
        out = put(out, blocks[k], me ^ k)
    return out


def norm_back(values_in, scale, gain, normed_grad):
    weighted = normed_grad * gain
    value_grad = scale * weighted - values_in * scale**3 * jnp.mean(
        weighted * values_in, axis=-1, keepdims=True
    )
    gain_grad = jnp.sum(normed_grad * values_in * scale, axis=(0, 1))
    return (value_grad, gain_grad)


def gelu_tanh(value_in):
    return jax.nn.gelu(value_in, approximate=True)


def tree_rows(x, half):
    mine, other = pick(x, half), pick(x, 1 - half)
    mine_all = xor_gather(mine, "ctx")
    other_rest = swap(jnp.stack(mine_all[1:]), "tensor", 1)
    return jnp.stack([jnp.stack(mine_all), jnp.concatenate([other[None], other_rest])])


def tree_sum(partial, half):
    both = swap(partial[1].astype(low), "tensor", 1).astype(wide) + partial[0].astype(wide)
    return xor_scatter([both[k] for k in range(both.shape[0])], "ctx")


def on_device(
    inputs,
    cotangent,
    norm1_gain,
    w_query,
    w_key,
    w_value,
    w_out,
    norm2_gain,
    w_gate,
    w_up,
    w_down,
    bias_table,
):
    micro, rows, width = inputs.shape
    shards, ctx = lax.axis_size("shard"), lax.axis_size("ctx")
    own_width = w_query.shape[0]
    inner = w_query.shape[1]
    heads = inner // DK
    me_ctx, half = lax.axis_index("ctx"), lax.axis_index("tensor")
    columns = w_gate.shape[1] // ctx

    tree_in = tree_rows(inputs, half)
    tree_cot = tree_rows(cotangent, half)
    gains = ring_gather(jnp.stack([norm1_gain, norm2_gain]), "shard")
    gains = gains.transpose(1, 0, 2).reshape(2, width).astype(wide)

    four = jnp.stack([w_query, w_key, w_value, w_out.T])
    one = ring_gather(pick(four, me_ctx), "shard")
    four_all = absolute(xor_gather(one, "ctx"), "ctx").reshape(4, width, inner)
    q_w, k_w, v_w, o_w = (four_all[i] for i in range(4))

    start = me_ctx * columns
    three = jnp.stack(
        [
            lax.dynamic_slice_in_dim(w_gate, start, columns, 1),
            lax.dynamic_slice_in_dim(w_up, start, columns, 1),
            lax.dynamic_slice_in_dim(w_down, start, columns, 0).T,
        ]
    )
    three_all = [ring_gather(three[i], "shard").reshape(width, columns) for i in range(3)]
    g_w, u_w, d_w = three_all

    token = (
        (me_ctx ^ jnp.arange(ctx, dtype=jnp.int32))[:, None] * rows
        + jnp.arange(rows, dtype=jnp.int32)[None]
    ).reshape(-1)
    table = lax.dynamic_slice_in_dim(bias_table, half * heads, heads, 1)
    bias = score_bias(token, table, rows // 5)

    length = ctx * rows
    start_in = tree_in.astype(wide).reshape(micro, length, width)
    scale_one = lax.rsqrt(jnp.mean(start_in * start_in, axis=-1, keepdims=True) + norm_eps)
    normed_one = (start_in * scale_one * gains[0]).astype(low).reshape(micro * length, width)
    queries = dot(normed_one, q_w, 1, 0).astype(low)
    keys = dot(normed_one, k_w, 1, 0).astype(low)
    values = dot(normed_one, v_w, 1, 0).astype(low)
    query_heads = queries.reshape(micro, length, heads, DK)
    key_heads = keys.reshape(micro, length, heads, DK)
    value_heads = values.reshape(micro, length, heads, DK)
    scores = (
        jnp.einsum("mqhd,mkhd->mhqk", query_heads, key_heads, preferred_element_type=wide) + bias
    )
    row_max = jnp.max(scores, axis=-1, keepdims=True)
    raised = jnp.exp(scores - row_max)
    soft_all = raised / jnp.sum(raised, axis=-1, keepdims=True)
    mixed_all = jnp.einsum(
        "mhqk,mkhd->mqhd", soft_all.astype(low), value_heads, preferred_element_type=wide
    ).astype(low)
    mixed_all = mixed_all.reshape(micro * length, inner)
    attended = dot(mixed_all, o_w, 1, 1).astype(low).reshape(micro, length, width)
    theirs = swap(attended[::-1], "tensor", 1)
    middle_all = start_in + (attended.astype(wide) + theirs.astype(wide))
    scale_two_all = lax.rsqrt(jnp.mean(middle_all * middle_all, axis=-1, keepdims=True) + norm_eps)
    normed_two = (middle_all * scale_two_all * gains[1]).astype(low).reshape(micro * length, width)

    gate_pre = dot(normed_two, g_w, 1, 0)
    up_pre = dot(normed_two, u_w, 1, 0)
    activated, gelu_pull = jax.vjp(gelu_tanh, gate_pre)
    hidden = (activated * up_pre).astype(low)
    down_in = tree_cot.reshape(micro * length, width)
    hidden_grad = dot(down_in, d_w, 1, 1 - 1)
    gate_grad = gelu_pull(hidden_grad * up_pre)[0].astype(low)
    up_grad = (hidden_grad * activated).astype(low)
    two_partial = dot(gate_grad, g_w, 1, 1) + dot(up_grad, u_w, 1, 1)
    two_mine = tree_sum(two_partial.reshape(micro, ctx, rows, width).astype(low), half).astype(low)
    two_grad = jnp.stack([two_mine, swap(two_mine, "tensor", 1)]).astype(wide)

    feed = dot(hidden, d_w, 1, 1).astype(low).reshape(micro, ctx, rows, width)
    feed_mine = tree_sum(feed, half)

    def own(x):
        return x.reshape((micro, ctx, rows) + x.shape[2:])[:, 0]

    middle = own(middle_all)
    produced_mine = (middle[0] + feed_mine).astype(low)
    produced_other = swap(produced_mine, "tensor", 1)

    wgrads = jnp.stack(
        [
            dot(normed_two, gate_grad, 0, 0).astype(low),
            dot(normed_two, up_grad, 0, 0).astype(low),
            dot(down_in, hidden, 0, 0).astype(low),
        ]
    ).reshape(3, shards, own_width, columns)
    wide_grads = []
    for i in range(3):
        own_columns = ring_scatter(wgrads[i], "shard").astype(low)
        every = absolute(xor_gather(own_columns, "ctx"), "ctx")
        if i < 2:
            every = every.transpose(1, 0, 2).reshape(own_width, ctx * columns)
        else:
            every = every.transpose(0, 2, 1).reshape(ctx * columns, own_width)
        wide_grads.append(every.astype(wide))

    grad_out = own(tree_cot.reshape(micro, length, width)).astype(wide)
    middle_part, gain_two_grad = norm_back(middle, own(scale_two_all), gains[1], two_grad)
    middle_grad = grad_out + middle_part
    out_in = middle_grad.astype(low).reshape(micro * rows, width)
    mixed = own(mixed_all.reshape(micro, length, inner)).reshape(micro * rows, inner)
    out_wgrad = dot(out_in, mixed, 0, 0)
    mixed_grad = dot(out_in, o_w, 1, 0).astype(low).reshape(micro, rows, heads, DK)
    soft = soft_all.reshape(micro, heads, ctx, rows, length)[:, :, 0]
    values_full = jnp.einsum(
        "mhqk,mqhd->mkhd", soft.astype(low), mixed_grad, preferred_element_type=wide
    )
    weight_grad = jnp.einsum("mqhd,mkhd->mhqk", mixed_grad, value_heads, preferred_element_type=wide)
    scores_grad = soft * (weight_grad - jnp.sum(weight_grad * soft, axis=-1, keepdims=True))
    scores_grad = scores_grad.astype(low)
    queries_grad = jnp.einsum("mhqk,mkhd->mqhd", scores_grad, key_heads, preferred_element_type=wide)
    queries_grad = queries_grad.reshape(micro * rows, inner).astype(low)
    own_queries = own(query_heads.reshape(micro, length, inner)).reshape(micro, rows, heads, DK)
    keys_full = jnp.einsum("mhqk,mqhd->mkhd", scores_grad, own_queries, preferred_element_type=wide)
    both_full = jnp.concatenate(
        [keys_full.reshape(micro, length, inner), values_full.reshape(micro, length, inner)], -1
    ).astype(low)
    both_full = both_full.reshape(micro, ctx, rows, 2 * inner)
    both_own = xor_scatter([both_full[:, k] for k in range(ctx)], "ctx").astype(low)
    keys_grad = both_own[..., :inner].reshape(micro * rows, inner)
    values_grad = both_own[..., inner:].reshape(micro * rows, inner)
    normed_own = own(normed_one.reshape(micro, length, width)).reshape(micro * rows, width)
    first = dot(queries_grad, q_w, 1, 1) + dot(keys_grad, k_w, 1, 1) + dot(values_grad, v_w, 1, 1)
    first = first.astype(low).reshape(micro, rows, width)
    normed_one_grad = first.astype(wide) + swap(first[::-1], "tensor", 1).astype(wide)
    x_own = own(start_in)
    input_part, gain_one_grad = norm_back(x_own, own(scale_one), gains[0], normed_one_grad)
    input_grad = (middle_grad + input_part).astype(low)

    four_grads = jnp.stack(
        [
            dot(normed_own, queries_grad, 0, 0).astype(low),
            dot(normed_own, keys_grad, 0, 0).astype(low),
            dot(normed_own, values_grad, 0, 0).astype(low),
            out_wgrad.astype(low),
        ]
    )
    mine = xor_scatter([pick(four_grads, me_ctx ^ k) for k in range(ctx)], "ctx").astype(low)
    mine = ring_scatter(mine.reshape(shards, own_width, inner), "shard").astype(low)
    four_own = absolute(xor_gather(mine, "ctx"), "ctx").astype(wide)
    gain_sum = xor_scatter([jnp.stack([gain_one_grad, gain_two_grad]).astype(low)] * ctx, "ctx")
    gain_parts = gain_sum.reshape(2, shards, own_width).transpose(1, 0, 2)
    gain_own = ring_scatter(gain_parts, "shard")

    def ordered(mine_part, other_part):
        return jnp.where(half == 0, jnp.stack([mine_part, other_part]), jnp.stack([other_part, mine_part]))

    return (
        ordered(produced_mine, produced_other),
        ordered(input_grad[0], input_grad[1]),
        gain_own[0],
        four_own[0],
        four_own[1],
        four_own[2],
        four_own[3].T,
        gain_own[1],
        wide_grads[0],
        wide_grads[1],
        wide_grads[2],
    )


def solution(mesh):
    placed = (
        P(None, ("shard", "ctx"), None),
        P(None, ("shard", "ctx"), None),
        P("shard"),
        P("shard", "tensor"),
        P("shard", "tensor"),
        P("shard", "tensor"),
        P("tensor", "shard"),
        P("shard"),
        P("shard", "tensor"),
        P("shard", "tensor"),
        P("tensor", "shard"),
        P(),
    )
    return jax.shard_map(
        on_device,
        mesh=mesh,
        in_specs=placed,
        out_specs=placed[:2]
        + (
            P("shard"),
            P("shard", "tensor"),
            P("shard", "tensor"),
            P("shard", "tensor"),
            P("tensor", "shard"),
            P("shard"),
            P("shard", "tensor"),
            P("shard", "tensor"),
            P("tensor", "shard"),
        ),
        check_vma=False,
    )
```

time: 1600 us -> 577 us (0.36)
  waiting for transfers between devices: 830 us -> 167 us
  local copies, waits for them, and re-layouts: 489 us -> 162 us
  blocking collectives: 133 us -> 0 us
  other arithmetic: 32.1 us -> 123 us
  starting transfers between devices: 1.38 us -> 70.4 us
  matrix products: 91 us -> 42.4 us
  between operations: 18.6 us -> 2.23 us
    gather x6 -> x0, local copies, waits for them, and re-layouts: 455 us -> none  [score_bias(): jnp.take(table[:, head], bucket, axis=0)]
    reduce_scatter x3 -> x0, waiting for transfers between devices: 288 us -> none  [the longest x1 97.1 us: on_device(): lax.psum_scatter(running[8].astype(jnp.bfloat16), 'shard', scatter_dimens...]
    all_gather x3 -> x0, waiting for transfers between devices: 262 us -> none  [the longest x1 94 us: on_device(): lax.all_gather(w_up, 'shard', axis=0, tiled=True)]
    ppermute x0 -> x74, waiting for transfers between devices: none -> 167 us  [the longest x30 90.8 us: step(): return lax.ppermute(x, axis, [(i, (i + 1) % n) for i in range(n)])]
    psum x4 -> x0, waiting for transfers between devices: 145 us -> none  [the longest x1 90.6 us: on_device(): lax.psum(for_sending(owned), 'ctx')]
    unnamed x26 -> x0, waiting for transfers between devices: 135 us -> none
    all_gather x8 -> x0, blocking collectives: 97.5 us -> none  [the longest x1 18.5 us: on_device(): lax.all_gather(w_value, 'shard', axis=0, tiled=True)]
    ppermute x0 -> x74, starting transfers between devices: none -> 70.4 us  [the longest x44 42.6 us: swap(): return lax.ppermute(x, axis, [(i, i ^ k) for i in range(n)])]
  transfers between devices with their start and end apart: 18 -> 74, of which waited for: 17 -> 28; matrix products, arithmetic and copies ran while one was open for 6% -> 51% of each run, Pallas kernels for 0% -> 0%
where the time goes in v1:
time: 577 us; the launch traced here: 567 us
  waiting for transfers between devices  167 us (29%)
  local copies, waits for them, and re-layouts  162 us (28%)
  other arithmetic  123 us (21%)
  starting transfers between devices  70.4 us (12%)
  matrix products  42.4 us (7%)
    ppermute x30, waiting for transfers between devices, step(): return lax.ppermute(x, axis, [(i, (i + 1) % n) for i in range(n)])  90.8 us
    ppermute x44, waiting for transfers between devices, swap(): return lax.ppermute(x, axis, [(i, i ^ k) for i in range(n)])  76 us
    select_n x3, other arithmetic, score_bias(): heads.append(jnp.where(allowed, looked, masked_score))  65.1 us
    dynamic_update_slice x36, local copies, waits for them, and re-layouts, put(): return lax.dynamic_update_slice_in_dim(stack, part[None], index, 0)  45.9 us
    ppermute x44, starting transfers between devices, swap(): return lax.ppermute(x, axis, [(i, i ^ k) for i in range(n)])  42.6 us
    dot_general x21, matrix products, dot(): lax.dot_general(left, right, (((left_dim,), (right_dim,)), ((), ())), pre...  35.1 us
    ppermute x30, starting transfers between devices, step(): return lax.ppermute(x, axis, [(i, (i + 1) % n) for i in range(n)])  27.8 us
    reshape x3, local copies, waits for them, and re-layouts, on_device(): ring_gather(three[i], 'shard').reshape(width, columns)  20.7 us
  transfers between devices with their start and end apart: 74, of which 28 were waited for; matrix products, arithmetic and copies ran while one was open for 51% of the time, Pallas kernels for 0%

profile of v1, /device:TPU:0, one launch (start us, length us, event | category | flops | bytes accessed | tf_op | source)
XLA Modules:
  0.0 567.2 jit_solution(7315792207820433093)
XLA Ops:
  2.9 3.9 collective-permute-start.30
  29.8 21.9 %select_select_fusion = f32[1,320,320]{2,1,0:T(8,128)S(1)} fusion(f32[]{:T(128)} %bitcast.120, f32[]{:T(128)} %bitcast.119, f32[]{:T(128)} %bitcast.118, f32[]{:T(128)} %bitcast.117, f32[]{:T(128)} %bitcast.116, f32[]{:T(128)} %bitcast.115, f32[]{:T(128)} %bitcast.114, f32[]{:T(128)} %bitcast.113, f32[]{:T(128)} %bitcast.112, f32[]{:T(128)} %bitcast.111, ...), kind=kLoop, calls=%fused_computation.166 | loop fusion | flops 10035200 | bytes 413888 | tf_op jit(solution)/shard_map/jit(_where)/select_n | solution.py:45
  51.7 21.6 %select_select_fusion.1 = f32[1,320,320]{2,1,0:T(8,128)S(1)} fusion(f32[]{:T(128)} %bitcast.88, f32[]{:T(128)} %bitcast.87, f32[]{:T(128)} %bitcast.86, f32[]{:T(128)} %bitcast.85, f32[]{:T(128)} %bitcast.84, f32[]{:T(128)} %bitcast.83, f32[]{:T(128)} %bitcast.82, f32[]{:T(128)} %bitcast.81, f32[]{:T(128)} %bitcast.80, f32[]{:T(128)} %bitcast.79, ...), kind=kLoop, calls=%fused_computation.167 | loop fusion | flops 10035200 | bytes 413888 | tf_op jit(solution)/shard_map/jit(_where)/select_n | solution.py:45
  73.4 21.5 %select_select_fusion.2 = f32[1,320,320]{2,1,0:T(8,128)S(1)} fusion(f32[]{:T(128)} %bitcast.56, f32[]{:T(128)} %bitcast.55, f32[]{:T(128)} %bitcast.54, f32[]{:T(128)} %bitcast.53, f32[]{:T(128)} %bitcast.52, f32[]{:T(128)} %bitcast.51, f32[]{:T(128)} %bitcast.50, f32[]{:T(128)} %bitcast.49, f32[]{:T(128)} %bitcast.48, f32[]{:T(128)} %bitcast.47, ...), kind=kLoop, calls=%fused_computation.168 | loop fusion | flops 10035200 | bytes 413888 | tf_op jit(solution)/shard_map/jit(_where)/select_n | solution.py:45
  99.5 3.8 collective-permute-done.5
  103.3 5.4 collective-permute-done.6
  108.8 6.8 %collective-permute-done.7 = bf16[368,192]{0,1:T(8,128)(2,1)} collective-permute-done((bf16[368,192]{0,1:T(8,128)(2,1)S(1)}, bf16[368,192]{0,1:T(8,128)(2,1)}, u32[]{:S(2)}, u32[]{:S(2)}) %collective-permute-start.7) | collective-permute-done | bytes 141344 | tf_op jit(solution)/shard_map/ppermute | solution.py:57
  127.6 15.8 %collective-permute-done.8 = bf16[368,192]{0,1:T(8,128)(2,1)} collective-permute-done((bf16[368,192]{0,1:T(8,128)(2,1)}, bf16[368,192]{0,1:T(8,128)(2,1)}, u32[]{:S(2)}, u32[]{:S(2)}) %collective-permute-start.8) | collective-permute-done | bytes 141344 | tf_op jit(solution)/shard_map/ppermute | solution.py:57
  153.6 2.7 collective-permute-start.15
  161.4 7.8 %collective-permute-done.21 = bf16[368,448]{1,0:T(8,128)(2,1)} collective-permute-done((bf16[368,448]{1,0:T(8,128)(2,1)}, bf16[368,448]{1,0:T(8,128)(2,1)}, u32[]{:S(2)}, u32[]{:S(2)}) %collective-permute-start.21) | collective-permute-done | bytes 329760 | tf_op jit(solution)/shard_map/ppermute | solution.py:57
  188.7 12.9 %collective-permute-done.11 = bf16[4,368,192]{1,2,0:T(8,128)(2,1)} collective-permute-done((bf16[4,368,192]{1,2,0:T(8,128)(2,1)}, bf16[4,368,192]{1,2,0:T(8,128)(2,1)}, u32[]{:S(2)}, u32[]{:S(2)}) %collective-permute-start.11) | collective-permute-done | bytes 565280 | tf_op jit(solution)/shard_map/ppermute | solution.py:62
  206.3 3.2 fusion.123
  232.2 2.7 copy.263
  245.2 3.5 copy.272
  248.7 3.7 reshape.1633
  254.5 3.5 copy.267
  257.9 13.2 %reshape.1632 = bf16[1472,448]{0,1:T(8,128)(2,1)} reshape(bf16[4,368,448]{1,0,2:T(4,128)(2,1)} %copy.267) | data formatting | bytes 2637824 | tf_op jit(solution)/shard_map/reshape | solution.py:177
  271.2 3.5 copy.265
  274.7 3.7 reshape.1631
  278.4 4.3 fusion.136
  286.9 5.0 multiply_reduce_fusion
  312.5 3.6 squeeze.559
  316.1 3.9 constant_dynamic-slice_fusion.9
  320.8 3.4 squeeze.561
  324.2 4.0 constant_dynamic-slice_fusion.5
  330.2 3.8 squeeze.563
  334.0 2.8 constant_dynamic-slice_fusion.1
  336.9 3.7 collective-permute-start.68
  344.0 5.8 %collective-permute-done.68 = bf16[368,448]{0,1:T(8,128)(2,1)S(1)} collective-permute-done((bf16[368,448]{0,1:T(8,128)(2,1)S(1)}, bf16[368,448]{0,1:T(8,128)(2,1)S(1)}, u32[]{:S(2)}, u32[]{:S(2)}) %collective-permute-start.68) | collective-permute-done | bytes 329760 | tf_op jit(solution)/shard_map/ppermute | solution.py:57
  351.7 5.4 collective-permute-done.57
  359.1 5.4 collective-permute-done.63
  366.5 5.4 collective-permute-done.69
  380.9 5.7 %collective-permute-done.64 = bf16[368,448]{0,1:T(8,128)(2,1)S(1)} collective-permute-done((bf16[368,448]{0,1:T(8,128)(2,1)S(1)}, bf16[368,448]{0,1:T(8,128)(2,1)S(1)}, u32[]{:S(2)}, u32[]{:S(2)}) %collective-permute-start.64) | collective-permute-done | bytes 329760 | tf_op jit(solution)/shard_map/ppermute | solution.py:57
  388.4 4.9 collective-permute-done.70
  406.3 6.7 %collective-permute-done.59 = bf16[368,448]{0,1:T(8,128)(2,1)S(1)} collective-permute-done((bf16[368,448]{0,1:T(8,128)(2,1)S(1)}, bf16[368,448]{0,1:T(8,128)(2,1)S(1)}, u32[]{:S(2)}, u32[]{:S(2)}) %collective-permute-start.59) | collective-permute-done | bytes 329760 | tf_op jit(solution)/shard_map/ppermute | solution.py:62
  415.2 5.2 collective-permute-done.61
  422.0 5.9 %collective-permute-done.65 = bf16[368,448]{0,1:T(8,128)(2,1)S(1)} collective-permute-done((bf16[368,448]{0,1:T(8,128)(2,1)S(1)}, bf16[368,448]{0,1:T(8,128)(2,1)S(1)}, u32[]{:S(2)}, u32[]{:S(2)}) %collective-permute-start.65) | collective-permute-done | bytes 329760 | tf_op jit(solution)/shard_map/ppermute | solution.py:62
  428.5 6.7 %collective-permute-done.67 = bf16[368,448]{0,1:T(8,128)(2,1)S(1)} collective-permute-done((bf16[368,448]{0,1:T(8,128)(2,1)S(1)}, bf16[368,448]{0,1:T(8,128)(2,1)S(1)}, u32[]{:S(2)}, u32[]{:S(2)}) %collective-permute-start.67) | collective-permute-done | bytes 329760 | tf_op jit(solution)/shard_map/ppermute | solution.py:62
  435.3 7.4 %collective-permute-done.71 = bf16[368,448]{0,1:T(8,128)(2,1)S(1)} collective-permute-done((bf16[368,448]{0,1:T(8,128)(2,1)S(1)}, bf16[368,448]{0,1:T(8,128)(2,1)S(1)}, u32[]{:S(2)}, u32[]{:S(2)}) %collective-permute-start.71) | collective-permute-done | bytes 329760 | tf_op jit(solution)/shard_map/ppermute | solution.py:62
  445.1 3.3 copy.312
  450.1 3.3 copy.313
  456.9 3.1 convert_element_type.820
  459.9 3.4 copy.314
  506.9 21.6 %collective-permute-done.43 = bf16[2,1472]{1,0:T(2,128)(2,1)S(1)} collective-permute-done((bf16[2,1472]{1,0:T(2,128)(2,1)S(1)}, bf16[2,1472]{1,0:T(2,128)(2,1)S(1)}, u32[]{:S(2)}, u32[]{:S(2)}) %collective-permute-start.43) | collective-permute-done | bytes 5920 | tf_op jit(solution)/shard_map/ppermute | solution.py:62
  538.6 4.3 collective-permute-done.50
  544.0 6.0 %collective-permute-done.51 = bf16[368,192]{0,1:T(8,128)(2,1)S(1)} collective-permute-done((bf16[368,192]{0,1:T(8,128)(2,1)S(1)}, bf16[368,192]{0,1:T(8,128)(2,1)S(1)}, u32[]{:S(2)}, u32[]{:S(2)}) %collective-permute-start.51) | collective-permute-done | bytes 141344 | tf_op jit(solution)/shard_map/ppermute | solution.py:57
  550.5 6.5 %collective-permute-done.52 = bf16[368,192]{0,1:T(8,128)(2,1)S(1)} collective-permute-done((bf16[368,192]{0,1:T(8,128)(2,1)S(1)}, bf16[368,192]{0,1:T(8,128)(2,1)S(1)}, u32[]{:S(2)}, u32[]{:S(2)}) %collective-permute-start.52) | collective-permute-done | bytes 141344 | tf_op jit(solution)/shard_map/ppermute | solution.py:57
  562.3 2.9 collective-permute-done.54
  (444 shorter events, 250.5 us)
Async XLA Ops:
  2.9 114.9 %collective-permute-start.30 = (bf16[80,1472]{1,0:T(8,128)(2,1)S(1)}, bf16[80,1472]{1,0:T(8,128)(2,1)S(1)}, u32[]{:S(2)}, u32[]{:S(2)}) collective-permute-start(bf16[80,1472]{1,0:T(8,128)(2,1)S(1)} %bitcast.596), channel_id=1, source_target_pairs={{0,6},{2,4},{4,2},{6,0},{1,7},{3,5},{5,3},{7,1},{8,14},{10,12},{12... | collective-permute-start | bytes 706568 | tf_op jit(solution)/shard_map/ppermute | solution.py:62
  6.8 111.5 %collective-permute-start.29 = (bf16[80,1472]{1,0:T(8,128)(2,1)S(1)}, bf16[80,1472]{1,0:T(8,128)(2,1)S(1)}, u32[]{:S(2)}, u32[]{:S(2)}) collective-permute-start(bf16[80,1472]{1,0:T(8,128)(2,1)S(1)} %bitcast.597), channel_id=1, source_target_pairs={{0,4},{2,6},{4,0},{6,2},{1,5},{3,7},{5,1},{7,3},{8,12},{10,14},{12... | collective-permute-start | bytes 706568 | tf_op jit(solution)/shard_map/ppermute | solution.py:62
  7.3 111.0 %collective-permute-start.28 = (bf16[80,1472]{1,0:T(8,128)(2,1)S(1)}, bf16[80,1472]{1,0:T(8,128)(2,1)S(1)}, u32[]{:S(2)}, u32[]{:S(2)}) collective-permute-start(bf16[80,1472]{1,0:T(8,128)(2,1)S(1)} %bitcast.598), channel_id=1, source_target_pairs={{0,2},{2,0},{4,6},{6,4},{1,3},{3,1},{5,7},{7,5},{8,10},{10,8},{12,... | collective-permute-start | bytes 706568 | tf_op jit(solution)/shard_map/ppermute | solution.py:62
  7.4 90.5 %collective-permute-start.4 = (bf16[2,368]{1,0:T(2,128)(2,1)S(1)}, bf16[2,368]{1,0:T(2,128)(2,1)S(1)}, u32[]{:S(2)}, u32[]{:S(2)}) collective-permute-start(bf16[2,368]{1,0:T(2,128)(2,1)S(1)} %get-tuple-element.78), channel_id=1, source_target_pairs={{0,8},{8,16},{16,24},{24,0},{1,9},{9,17},{17,25},{25,1},{2,10},{10... | collective-permute-start | bytes 4424 | tf_op jit(solution)/shard_map/ppermute | solution.py:57
  9.5 109.9 %collective-permute-start.2 = (bf16[80,1472]{1,0:T(8,128)(2,1)S(1)}, bf16[80,1472]{1,0:T(8,128)(2,1)}, u32[]{:S(2)}, u32[]{:S(2)}) collective-permute-start(bf16[80,1472]{1,0:T(8,128)(2,1)S(1)} %bitcast.593), channel_id=1, source_target_pairs={{0,6},{2,4},{4,2},{6,0},{1,7},{3,5},{5,3},{7,1},{8,14},{10,12},{12... | collective-permute-start | bytes 706568 | tf_op jit(solution)/shard_map/ppermute | solution.py:62
  118.2 26.7 %collective-permute-start.17 = (bf16[368,448]{0,1:T(8,128)(2,1)}, bf16[368,448]{0,1:T(8,128)(2,1)}, u32[]{:S(2)}, u32[]{:S(2)}) collective-permute-start(bf16[368,448]{0,1:T(8,128)(2,1)} %copy.328), channel_id=1, source_target_pairs={{0,8},{8,16},{16,24},{24,0},{1,9},{9,17},{17,25},{25,1},{2,10},{10... | collective-permute-start | bytes 989192 | tf_op jit(solution)/shard_map/ppermute | solution.py:57
  118.2 28.5 %collective-permute-start.14 = (bf16[368,448]{0,1:T(8,128)(2,1)}, bf16[368,448]{0,1:T(8,128)(2,1)S(1)}, u32[]{:S(2)}, u32[]{:S(2)}) collective-permute-start(bf16[368,448]{0,1:T(8,128)(2,1)} %copy.329), channel_id=1, source_target_pairs={{0,8},{8,16},{16,24},{24,0},{1,9},{9,17},{17,25},{25,1},{2,10},{10... | collective-permute-start | bytes 989192 | tf_op jit(solution)/shard_map/ppermute | solution.py:57
  119.4 27.3 %collective-permute-start.20 = (bf16[368,448]{1,0:T(8,128)(2,1)S(1)}, bf16[368,448]{1,0:T(8,128)(2,1)}, u32[]{:S(2)}, u32[]{:S(2)}) collective-permute-start(bf16[368,448]{1,0:T(8,128)(2,1)S(1)} %copy-done.44), channel_id=1, source_target_pairs={{0,8},{8,16},{16,24},{24,0},{1,9},{9,17},{17,25},{25,1},{2,10},{10... | collective-permute-start | bytes 989192 | tf_op jit(solution)/shard_map/ppermute | solution.py:57
  121.9 21.5 %collective-permute-start.8 = (bf16[368,192]{0,1:T(8,128)(2,1)}, bf16[368,192]{0,1:T(8,128)(2,1)}, u32[]{:S(2)}, u32[]{:S(2)}) collective-permute-start(bf16[368,192]{0,1:T(8,128)(2,1)} %collective-permute-done.7), channel_id=1, source_target_pairs={{0,8},{8,16},{16,24},{24,0},{1,9},{9,17},{17,25},{25,1},{2,10},{10... | collective-permute-start | bytes 423944 | tf_op jit(solution)/shard_map/ppermute | solution.py:57
  127.6 108.7 %collective-permute-start.31 = (bf16[3,80,1472]{2,1,0:T(8,128)(2,1)}, bf16[3,80,1472]{2,1,0:T(8,128)(2,1)}, u32[]{:S(2)}, u32[]{:S(2)}) collective-permute-start(bf16[3,80,1472]{2,1,0:T(8,128)(2,1)} %pad_maximum_fusion.7), channel_id=1, source_target_pairs={{0,1},{1,0},{2,3},{3,2},{4,5},{5,4},{6,7},{7,6},{8,9},{9,8},{10,11... | collective-permute-start | bytes 2119688 | tf_op jit(solution)/shard_map/ppermute | solution.py:62
  143.3 37.0 %collective-permute-start.3 = (bf16[3,80,1472]{2,1,0:T(8,128)(2,1)}, bf16[3,80,1472]{2,1,0:T(8,128)(2,1)}, u32[]{:S(2)}, u32[]{:S(2)}) collective-permute-start(bf16[3,80,1472]{2,1,0:T(8,128)(2,1)} %pad_maximum_fusion.6), channel_id=1, source_target_pairs={{0,1},{1,0},{2,3},{3,2},{4,5},{5,4},{6,7},{7,6},{8,9},{9,8},{10,11... | collective-permute-start | bytes 2119688 | tf_op jit(solution)/shard_map/ppermute | solution.py:62
  146.7 27.6 %collective-permute-start.18 = (bf16[368,448]{0,1:T(8,128)(2,1)}, bf16[368,448]{0,1:T(8,128)(2,1)}, u32[]{:S(2)}, u32[]{:S(2)}) collective-permute-start(bf16[368,448]{0,1:T(8,128)(2,1)} %collective-permute-done.17), channel_id=1, source_target_pairs={{0,8},{8,16},{16,24},{24,0},{1,9},{9,17},{17,25},{25,1},{2,10},{10... | collective-permute-start | bytes 989192 | tf_op jit(solution)/shard_map/ppermute | solution.py:57
  146.8 22.4 %collective-permute-start.21 = (bf16[368,448]{1,0:T(8,128)(2,1)}, bf16[368,448]{1,0:T(8,128)(2,1)}, u32[]{:S(2)}, u32[]{:S(2)}) collective-permute-start(bf16[368,448]{1,0:T(8,128)(2,1)} %collective-permute-done.20), channel_id=1, source_target_pairs={{0,8},{8,16},{16,24},{24,0},{1,9},{9,17},{17,25},{25,1},{2,10},{10... | collective-permute-start | bytes 989192 | tf_op jit(solution)/shard_map/ppermute | solution.py:57
  153.6 24.1 %collective-permute-start.15 = (bf16[368,448]{0,1:T(8,128)(2,1)}, bf16[368,448]{0,1:T(8,128)(2,1)}, u32[]{:S(2)}, u32[]{:S(2)}) collective-permute-start(bf16[368,448]{0,1:T(8,128)(2,1)} %copy-done.45), channel_id=1, source_target_pairs={{0,8},{8,16},{16,24},{24,0},{1,9},{9,17},{17,25},{25,1},{2,10},{10... | collective-permute-start | bytes 989192 | tf_op jit(solution)/shard_map/ppermute | solution.py:57
  169.1 17.1 %collective-permute-start.10 = (bf16[4,368,192]{1,2,0:T(8,128)(2,1)}, bf16[4,368,192]{1,2,0:T(8,128)(2,1)}, u32[]{:S(2)}, u32[]{:S(2)}) collective-permute-start(bf16[4,368,192]{1,2,0:T(8,128)(2,1)} %bitcast_dynamic-update-slice_fusion.24), channel_id=1, source_target_pairs={{0,2},{2,0},{4,6},{6,4},{1,3},{3,1},{5,7},{7,5},{8,10},{10,8},{12,... | collective-permute-start | bytes 1695752 | tf_op jit(solution)/shard_map/ppermute | solution.py:62
  174.4 27.3 %collective-permute-start.11 = (bf16[4,368,192]{1,2,0:T(8,128)(2,1)}, bf16[4,368,192]{1,2,0:T(8,128)(2,1)}, u32[]{:S(2)}, u32[]{:S(2)}) collective-permute-start(bf16[4,368,192]{1,2,0:T(8,128)(2,1)} %bitcast_dynamic-update-slice_fusion.24), channel_id=1, source_target_pairs={{0,4},{2,6},{4,0},{6,2},{1,5},{3,7},{5,1},{7,3},{8,12},{10,14},{12... | collective-permute-start | bytes 1695752 | tf_op jit(solution)/shard_map/ppermute | solution.py:62
  177.7 26.3 %collective-permute-start.12 = (bf16[4,368,192]{1,2,0:T(8,128)(2,1)}, bf16[4,368,192]{1,2,0:T(8,128)(2,1)}, u32[]{:S(2)}, u32[]{:S(2)}) collective-permute-start(bf16[4,368,192]{1,2,0:T(8,128)(2,1)} %bitcast_dynamic-update-slice_fusion.24), channel_id=1, source_target_pairs={{0,6},{2,4},{4,2},{6,0},{1,7},{3,5},{5,3},{7,1},{8,14},{10,12},{12... | collective-permute-start | bytes 1695752 | tf_op jit(solution)/shard_map/ppermute | solution.py:62
  180.4 61.2 %collective-permute-start.22 = (bf16[368,448]{1,0:T(8,128)(2,1)}, bf16[368,448]{1,0:T(8,128)(2,1)}, u32[]{:S(2)}, u32[]{:S(2)}) collective-permute-start(bf16[368,448]{1,0:T(8,128)(2,1)} %collective-permute-done.21), channel_id=1, source_target_pairs={{0,8},{8,16},{16,24},{24,0},{1,9},{9,17},{17,25},{25,1},{2,10},{10... | collective-permute-start | bytes 989192 | tf_op jit(solution)/shard_map/ppermute | solution.py:57
  186.3 66.2 %collective-permute-start.19 = (bf16[368,448]{0,1:T(8,128)(2,1)}, bf16[368,448]{0,1:T(8,128)(2,1)}, u32[]{:S(2)}, u32[]{:S(2)}) collective-permute-start(bf16[368,448]{0,1:T(8,128)(2,1)} %collective-permute-done.18), channel_id=1, source_target_pairs={{0,8},{8,16},{16,24},{24,0},{1,9},{9,17},{17,25},{25,1},{2,10},{10... | collective-permute-start | bytes 989192 | tf_op jit(solution)/shard_map/ppermute | solution.py:57
  201.6 50.8 %collective-permute-start.16 = (bf16[368,448]{0,1:T(8,128)(2,1)}, bf16[368,448]{0,1:T(8,128)(2,1)}, u32[]{:S(2)}, u32[]{:S(2)}) collective-permute-start(bf16[368,448]{0,1:T(8,128)(2,1)} %collective-permute-done.15), channel_id=1, source_target_pairs={{0,8},{8,16},{16,24},{24,0},{1,9},{9,17},{17,25},{25,1},{2,10},{10... | collective-permute-start | bytes 989192 | tf_op jit(solution)/shard_map/ppermute | solution.py:57
  236.2 50.6 %collective-permute-start.13 = (bf16[2,320,1472]{2,1,0:T(8,128)(2,1)}, bf16[2,320,1472]{2,1,0:T(8,128)(2,1)}, u32[]{:S(2)}, u32[]{:S(2)}) collective-permute-start(bf16[2,320,1472]{2,1,0:T(8,128)(2,1)} %rev.6), channel_id=1, source_target_pairs={{0,1},{1,0},{2,3},{3,2},{4,5},{5,4},{6,7},{7,6},{8,9},{9,8},{10,11... | collective-permute-start | bytes 5652488 | tf_op jit(solution)/shard_map/ppermute | solution.py:62
  307.1 66.8 %collective-permute-start.23 = (bf16[4,80,1472]{2,1,0:T(8,128)(2,1)}, bf16[4,80,1472]{2,1,0:T(8,128)(2,1)}, u32[]{:S(2)}, u32[]{:S(2)}) collective-permute-start(bf16[4,80,1472]{2,1,0:T(8,128)(2,1)} %bitcast.139), channel_id=1, source_target_pairs={{0,1},{1,0},{2,3},{3,2},{4,5},{5,4},{6,7},{7,6},{8,9},{9,8},{10,11... | collective-permute-start | bytes 2826248 | tf_op jit(solution)/shard_map/ppermute | solution.py:62
  312.5 64.5 %collective-permute-start.32 = (bf16[4,80,1472]{2,1,0:T(8,128)(2,1)}, bf16[4,80,1472]{2,1,0:T(8,128)(2,1)}, u32[]{:S(2)}, u32[]{:S(2)}) collective-permute-start(bf16[4,80,1472]{2,1,0:T(8,128)(2,1)} %bitcast.156), channel_id=1, source_target_pairs={{0,1},{1,0},{2,3},{3,2},{4,5},{5,4},{6,7},{7,6},{8,9},{9,8},{10,11... | collective-permute-start | bytes 2826248 | tf_op jit(solution)/shard_map/ppermute | solution.py:62
  320.8 19.8 %collective-permute-start.56 = (bf16[368,448]{0,1:T(8,128)(2,1)}, bf16[368,448]{0,1:T(8,128)(2,1)}, u32[]{:S(2)}, u32[]{:S(2)}) collective-permute-start(bf16[368,448]{0,1:T(8,128)(2,1)} %bitcast.544), channel_id=1, source_target_pairs={{0,8},{8,16},{16,24},{24,0},{1,9},{9,17},{17,25},{25,1},{2,10},{10... | collective-permute-start | bytes 989192 | tf_op jit(solution)/shard_map/ppermute | solution.py:57
  341.7 15.4 %collective-permute-start.57 = (bf16[368,448]{0,1:T(8,128)(2,1)S(1)}, bf16[368,448]{0,1:T(8,128)(2,1)S(1)}, u32[]{:S(2)}, u32[]{:S(2)}) collective-permute-start(bf16[368,448]{0,1:T(8,128)(2,1)S(1)} %fusion.68), channel_id=1, source_target_pairs={{0,8},{8,16},{16,24},{24,0},{1,9},{9,17},{17,25},{25,1},{2,10},{10... | collective-permute-start | bytes 989192 | tf_op jit(solution)/shard_map/ppermute | solution.py:57
  343.8 20.7 %collective-permute-start.63 = (bf16[368,448]{0,1:T(8,128)(2,1)S(1)}, bf16[368,448]{0,1:T(8,128)(2,1)S(1)}, u32[]{:S(2)}, u32[]{:S(2)}) collective-permute-start(bf16[368,448]{0,1:T(8,128)(2,1)S(1)} %fusion.65), channel_id=1, source_target_pairs={{0,8},{8,16},{16,24},{24,0},{1,9},{9,17},{17,25},{25,1},{2,10},{10... | collective-permute-start | bytes 989192 | tf_op jit(solution)/shard_map/ppermute | solution.py:57
  349.9 22.0 %collective-permute-start.69 = (bf16[368,448]{0,1:T(8,128)(2,1)S(1)}, bf16[368,448]{0,1:T(8,128)(2,1)S(1)}, u32[]{:S(2)}, u32[]{:S(2)}) collective-permute-start(bf16[368,448]{0,1:T(8,128)(2,1)S(1)} %fusion.62), channel_id=1, source_target_pairs={{0,8},{8,16},{16,24},{24,0},{1,9},{9,17},{17,25},{25,1},{2,10},{10... | collective-permute-start | bytes 989192 | tf_op jit(solution)/shard_map/ppermute | solution.py:57
  357.2 22.0 %collective-permute-start.58 = (bf16[368,448]{0,1:T(8,128)(2,1)S(1)}, bf16[368,448]{0,1:T(8,128)(2,1)S(1)}, u32[]{:S(2)}, u32[]{:S(2)}) collective-permute-start(bf16[368,448]{0,1:T(8,128)(2,1)S(1)} %fusion.67), channel_id=1, source_target_pairs={{0,8},{8,16},{16,24},{24,0},{1,9},{9,17},{17,25},{25,1},{2,10},{10... | collective-permute-start | bytes 989192 | tf_op jit(solution)/shard_map/ppermute | solution.py:57
  364.6 22.0 %collective-permute-start.64 = (bf16[368,448]{0,1:T(8,128)(2,1)S(1)}, bf16[368,448]{0,1:T(8,128)(2,1)S(1)}, u32[]{:S(2)}, u32[]{:S(2)}) collective-permute-start(bf16[368,448]{0,1:T(8,128)(2,1)S(1)} %fusion.64), channel_id=1, source_target_pairs={{0,8},{8,16},{16,24},{24,0},{1,9},{9,17},{17,25},{25,1},{2,10},{10... | collective-permute-start | bytes 989192 | tf_op jit(solution)/shard_map/ppermute | solution.py:57
  372.0 21.3 %collective-permute-start.70 = (bf16[368,448]{0,1:T(8,128)(2,1)S(1)}, bf16[368,448]{0,1:T(8,128)(2,1)S(1)}, u32[]{:S(2)}, u32[]{:S(2)}) collective-permute-start(bf16[368,448]{0,1:T(8,128)(2,1)S(1)} %fusion.61), channel_id=1, source_target_pairs={{0,8},{8,16},{16,24},{24,0},{1,9},{9,17},{17,25},{25,1},{2,10},{10... | collective-permute-start | bytes 989192 | tf_op jit(solution)/shard_map/ppermute | solution.py:57
  375.4 21.4 %collective-permute-start.26 = (bf16[80,1472]{1,0:T(8,128)(2,1)S(1)}, bf16[80,1472]{1,0:T(8,128)(2,1)S(1)}, u32[]{:S(2)}, u32[]{:S(2)}) collective-permute-start(bf16[80,1472]{1,0:T(8,128)(2,1)S(1)} %get-tuple-element.123), channel_id=1, source_target_pairs={{0,6},{2,4},{4,2},{6,0},{1,7},{3,5},{5,3},{7,1},{8,14},{10,12},{12... | collective-permute-start | bytes 706568 | tf_op jit(solution)/shard_map/ppermute | solution.py:62
  377.0 20.4 %collective-permute-start.25 = (bf16[80,1472]{1,0:T(8,128)(2,1)S(1)}, bf16[80,1472]{1,0:T(8,128)(2,1)S(1)}, u32[]{:S(2)}, u32[]{:S(2)}) collective-permute-start(bf16[80,1472]{1,0:T(8,128)(2,1)S(1)} %get-tuple-element.124), channel_id=1, source_target_pairs={{0,4},{2,6},{4,0},{6,2},{1,5},{3,7},{5,1},{7,3},{8,12},{10,14},{12... | collective-permute-start | bytes 706568 | tf_op jit(solution)/shard_map/ppermute | solution.py:62
  379.3 19.6 %collective-permute-start.24 = (bf16[80,1472]{1,0:T(8,128)(2,1)S(1)}, bf16[80,1472]{1,0:T(8,128)(2,1)S(1)}, u32[]{:S(2)}, u32[]{:S(2)}) collective-permute-start(bf16[80,1472]{1,0:T(8,128)(2,1)S(1)} %get-tuple-element.122), channel_id=1, source_target_pairs={{0,2},{2,0},{4,6},{6,4},{1,3},{3,1},{5,7},{7,5},{8,10},{10,8},{12,... | collective-permute-start | bytes 706568 | tf_op jit(solution)/shard_map/ppermute | solution.py:62
  397.4 15.7 %collective-permute-start.59 = (bf16[368,448]{0,1:T(8,128)(2,1)S(1)}, bf16[368,448]{0,1:T(8,128)(2,1)S(1)}, u32[]{:S(2)}, u32[]{:S(2)}) collective-permute-start(bf16[368,448]{0,1:T(8,128)(2,1)S(1)} %get-tuple-element.68), channel_id=1, source_target_pairs={{0,2},{2,0},{4,6},{6,4},{1,3},{3,1},{5,7},{7,5},{8,10},{10,8},{12,... | collective-permute-start | bytes 989192 | tf_op jit(solution)/shard_map/ppermute | solution.py:62
  401.2 19.2 %collective-permute-start.61 = (bf16[368,448]{0,1:T(8,128)(2,1)S(1)}, bf16[368,448]{0,1:T(8,128)(2,1)S(1)}, u32[]{:S(2)}, u32[]{:S(2)}) collective-permute-start(bf16[368,448]{0,1:T(8,128)(2,1)S(1)} %get-tuple-element.68), channel_id=1, source_target_pairs={{0,6},{2,4},{4,2},{6,0},{1,7},{3,5},{5,3},{7,1},{8,14},{10,12},{12... | collective-permute-start | bytes 989192 | tf_op jit(solution)/shard_map/ppermute | solution.py:62
  402.7 25.2 %collective-permute-start.65 = (bf16[368,448]{0,1:T(8,128)(2,1)S(1)}, bf16[368,448]{0,1:T(8,128)(2,1)S(1)}, u32[]{:S(2)}, u32[]{:S(2)}) collective-permute-start(bf16[368,448]{0,1:T(8,128)(2,1)S(1)} %get-tuple-element.66), channel_id=1, source_target_pairs={{0,2},{2,0},{4,6},{6,4},{1,3},{3,1},{5,7},{7,5},{8,10},{10,8},{12,... | collective-permute-start | bytes 989192 | tf_op jit(solution)/shard_map/ppermute | solution.py:62
  405.7 22.7 %collective-permute-start.66 = (bf16[368,448]{0,1:T(8,128)(2,1)S(1)}, bf16[368,448]{0,1:T(8,128)(2,1)S(1)}, u32[]{:S(2)}, u32[]{:S(2)}) collective-permute-start(bf16[368,448]{0,1:T(8,128)(2,1)S(1)} %get-tuple-element.66), channel_id=1, source_target_pairs={{0,4},{2,6},{4,0},{6,2},{1,5},{3,7},{5,1},{7,3},{8,12},{10,14},{12... | collective-permute-start | bytes 989192 | tf_op jit(solution)/shard_map/ppermute | solution.py:62
  413.1 22.2 %collective-permute-start.67 = (bf16[368,448]{0,1:T(8,128)(2,1)S(1)}, bf16[368,448]{0,1:T(8,128)(2,1)S(1)}, u32[]{:S(2)}, u32[]{:S(2)}) collective-permute-start(bf16[368,448]{0,1:T(8,128)(2,1)S(1)} %get-tuple-element.66), channel_id=1, source_target_pairs={{0,6},{2,4},{4,2},{6,0},{1,7},{3,5},{5,3},{7,1},{8,14},{10,12},{12... | collective-permute-start | bytes 989192 | tf_op jit(solution)/shard_map/ppermute | solution.py:62
  413.6 29.1 %collective-permute-start.71 = (bf16[368,448]{0,1:T(8,128)(2,1)S(1)}, bf16[368,448]{0,1:T(8,128)(2,1)S(1)}, u32[]{:S(2)}, u32[]{:S(2)}) collective-permute-start(bf16[368,448]{0,1:T(8,128)(2,1)S(1)} %get-tuple-element.64), channel_id=1, source_target_pairs={{0,2},{2,0},{4,6},{6,4},{1,3},{3,1},{5,7},{7,5},{8,10},{10,8},{12,... | collective-permute-start | bytes 989192 | tf_op jit(solution)/shard_map/ppermute | solution.py:62
  420.4 33.0 %collective-permute-start.72 = (bf16[368,448]{0,1:T(8,128)(2,1)S(1)}, bf16[368,448]{0,1:T(8,128)(2,1)}, u32[]{:S(2)}, u32[]{:S(2)}) collective-permute-start(bf16[368,448]{0,1:T(8,128)(2,1)S(1)} %get-tuple-element.64), channel_id=1, source_target_pairs={{0,4},{2,6},{4,0},{6,2},{1,5},{3,7},{5,1},{7,3},{8,12},{10,14},{12... | collective-permute-start | bytes 989192 | tf_op jit(solution)/shard_map/ppermute | solution.py:62
  427.9 27.3 %collective-permute-start.73 = (bf16[368,448]{0,1:T(8,128)(2,1)S(1)}, bf16[368,448]{0,1:T(8,128)(2,1)}, u32[]{:S(2)}, u32[]{:S(2)}) collective-permute-start(bf16[368,448]{0,1:T(8,128)(2,1)S(1)} %get-tuple-element.64), channel_id=1, source_target_pairs={{0,6},{2,4},{4,2},{6,0},{1,7},{3,5},{5,3},{7,1},{8,14},{10,12},{12... | collective-permute-start | bytes 989192 | tf_op jit(solution)/shard_map/ppermute | solution.py:62
  428.4 54.5 %collective-permute-start.27 = (bf16[80,1472]{1,0:T(8,128)(2,1)}, bf16[80,1472]{1,0:T(8,128)(2,1)}, u32[]{:S(2)}, u32[]{:S(2)}) collective-permute-start(bf16[80,1472]{1,0:T(8,128)(2,1)} %fusion.80), channel_id=1, source_target_pairs={{0,1},{1,0},{2,3},{3,2},{4,5},{5,4},{6,7},{7,6},{8,9},{9,8},{10,11... | collective-permute-start | bytes 706568 | tf_op jit(solution)/shard_map/ppermute | solution.py:62
  435.2 28.1 %collective-permute-start.36 = (bf16[80,1472]{1,0:T(8,128)(2,1)S(1)}, bf16[80,1472]{1,0:T(8,128)(2,1)S(1)}, u32[]{:S(2)}, u32[]{:S(2)}) collective-permute-start(bf16[80,1472]{1,0:T(8,128)(2,1)S(1)} %fusion.75), channel_id=1, source_target_pairs={{0,1},{1,0},{2,3},{3,2},{4,5},{5,4},{6,7},{7,6},{8,9},{9,8},{10,11... | collective-permute-start | bytes 706568 | tf_op jit(solution)/shard_map/ppermute | solution.py:62
  498.9 33.4 %collective-permute-start.49 = (bf16[1472,192]{0,1:T(8,128)(2,1)}, bf16[1472,192]{0,1:T(8,128)(2,1)S(1)}, u32[]{:S(2)}, u32[]{:S(2)}) collective-permute-start(bf16[1472,192]{0,1:T(8,128)(2,1)} %get-tuple-element.80), channel_id=1, source_target_pairs={{0,6},{2,4},{4,2},{6,0},{1,7},{3,5},{5,3},{7,1},{8,14},{10,12},{12... | collective-permute-start | bytes 1695752 | tf_op jit(solution)/shard_map/ppermute | solution.py:62
  499.5 32.8 %collective-permute-start.48 = (bf16[1472,192]{0,1:T(8,128)(2,1)}, bf16[1472,192]{0,1:T(8,128)(2,1)}, u32[]{:S(2)}, u32[]{:S(2)}) collective-permute-start(bf16[1472,192]{0,1:T(8,128)(2,1)} %get-tuple-element.81), channel_id=1, source_target_pairs={{0,4},{2,6},{4,0},{6,2},{1,5},{3,7},{5,1},{7,3},{8,12},{10,14},{12... | collective-permute-start | bytes 1695752 | tf_op jit(solution)/shard_map/ppermute | solution.py:62
  501.0 31.3 %collective-permute-start.47 = (bf16[1472,192]{0,1:T(8,128)(2,1)}, bf16[1472,192]{0,1:T(8,128)(2,1)}, u32[]{:S(2)}, u32[]{:S(2)}) collective-permute-start(bf16[1472,192]{0,1:T(8,128)(2,1)} %get-tuple-element.79), channel_id=1, source_target_pairs={{0,2},{2,0},{4,6},{6,4},{1,3},{3,1},{5,7},{7,5},{8,10},{10,8},{12,... | collective-permute-start | bytes 1695752 | tf_op jit(solution)/shard_map/ppermute | solution.py:62
  502.8 25.8 %collective-permute-start.43 = (bf16[2,1472]{1,0:T(2,128)(2,1)S(1)}, bf16[2,1472]{1,0:T(2,128)(2,1)S(1)}, u32[]{:S(2)}, u32[]{:S(2)}) collective-permute-start(bf16[2,1472]{1,0:T(2,128)(2,1)S(1)} %pad_maximum_fusion.9), channel_id=1, source_target_pairs={{0,6},{2,4},{4,2},{6,0},{1,7},{3,5},{5,3},{7,1},{8,14},{10,12},{12... | collective-permute-start | bytes 17672 | tf_op jit(solution)/shard_map/ppermute | solution.py:62
  503.4 26.7 %collective-permute-start.42 = (bf16[2,1472]{1,0:T(2,128)(2,1)S(1)}, bf16[2,1472]{1,0:T(2,128)(2,1)S(1)}, u32[]{:S(2)}, u32[]{:S(2)}) collective-permute-start(bf16[2,1472]{1,0:T(2,128)(2,1)S(1)} %pad_maximum_fusion.9), channel_id=1, source_target_pairs={{0,4},{2,6},{4,0},{6,2},{1,5},{3,7},{5,1},{7,3},{8,12},{10,14},{12... | collective-permute-start | bytes 17672 | tf_op jit(solution)/shard_map/ppermute | solution.py:62
  (80 other events, 592.6 us)

commit v2 on v1

v2 whole, which is shorter than its diff:
```python
import functools

import jax
import jax.numpy as jnp
from jax import lax
from jax.experimental import pallas as pl
from jax.experimental.pallas import tpu as pltpu
from jax.sharding import PartitionSpec as P

DK = 64
norm_eps = 1e-06
distance_marks = (8, 12, 16, 23, 32, 46, 64, 91)
masked_score = -1e30
low = jnp.bfloat16
wide = jnp.float32
LANES = 128


def dot_nn(left, right):
    return lax.dot_general(left, right, (((1,), (0,)), ((), ())), preferred_element_type=wide)


def dot_nt(left, right):
    return lax.dot_general(left, right, (((1,), (1,)), ((), ())), preferred_element_type=wide)


def dot_tn(left, right):
    return lax.dot_general(left, right, (((0,), (0,)), ((), ())), preferred_element_type=wide)


def wrap(value, n):
    return lax.rem(value + 2 * n, n)


def run(body, name, outs, operands, scratch=(), scalars=1, flops=0):
    moved = sum(a.size * a.dtype.itemsize for a in operands)
    moved += sum(functools.reduce(lambda a, b: a * b, s, 1) * jnp.dtype(d).itemsize for s, d in outs)
    return pl.pallas_call(
        body,
        name=name,
        out_shape=[jax.ShapeDtypeStruct(s, d) for s, d in outs],
        in_specs=[pl.BlockSpec(memory_space=pltpu.SMEM)] * scalars
        + [pl.BlockSpec(memory_space=pltpu.VMEM)] * (len(operands) - scalars),
        out_specs=[pl.BlockSpec(memory_space=pltpu.VMEM)] * len(outs),
        scratch_shapes=list(scratch),
        compiler_params=pltpu.CompilerParams(vmem_limit_bytes=40 * 2**20),
        cost_estimate=pl.CostEstimate(flops=flops, bytes_accessed=moved, transcendentals=0),
    )(*operands)


def step(x, axis, k=1):
    n = lax.axis_size(axis)
    return lax.ppermute(x, axis, [(i, (i + k) % n) for i in range(n)])


def swap(x, axis, k=1):
    n = lax.axis_size(axis)
    return lax.ppermute(x, axis, [(i, i ^ k) for i in range(n)])


def ring_gather(x, axis):
    out = [x]
    for _ in range(1, lax.axis_size(axis)):
        out.append(step(out[-1], axis))
    return out


def ring_scatter(parts, axis):
    acc = parts[0]
    for part in parts[1:]:
        acc = (step(acc, axis).astype(wide) + part.astype(wide)).astype(low)
    return acc


def xor_gather(x, axis):
    return [x] + [swap(x, axis, k) for k in range(1, lax.axis_size(axis))]


def pack_attention(n_ctx, idx, w_q, w_k, w_v, w_o, g1, g2, own_t, buf):
    c = idx[1]
    inner, r = w_o.shape
    for i, ref in enumerate((w_q, w_k, w_v)):
        own_t[i * inner : (i + 1) * inner, :] = ref[...].T
    for v in range(n_ctx):

        @pl.when(c == v)
        def _(v=v):
            if v < 3:
                buf[0:inner, 0:r] = own_t[v * inner : (v + 1) * inner, :]
            else:
                buf[0:inner, 0:r] = w_o[...]

    buf[inner : inner + 1, 0:r] = g1[...]
    buf[inner + 1 : inner + 2, 0:r] = g2[...]


def pack_wide(n_ctx, widths, rp, idx, w_g, w_u, w_d, *refs):
    bufs, stage = refs[:-1], refs[-1]
    r = w_g.shape[0]
    columns = sum(widths)
    for v in range(n_ctx):

        @pl.when(idx[1] == v)
        def _(v=v):
            at = v * columns
            for n, buf in zip(widths, bufs, strict=True):
                stage[:, 0:n] = w_g[:, at : at + n]
                stage[:, n : 2 * n] = w_u[:, at : at + n]
                for q in range(2 * n // LANES):
                    buf[rp * q : rp * q + r, :] = stage[:, LANES * q : LANES * (q + 1)]
                base = rp * (2 * n // LANES)
                for q in range(pl.cdiv(r, LANES)):
                    wide_q = min(LANES, r - LANES * q)
                    buf[base + n * q : base + n * (q + 1), 0:wide_q] = w_d[
                        at : at + n, LANES * q : LANES * q + wide_q
                    ]
                at += n


def bias_body(rows, seg_len, marks, idx, table, out):
    c = idx[1]
    heads, length, _ = out.shape

    def info(position):
        block = sum(((position >= rows * b).astype(jnp.int32) for b in range(1, length // rows)))
        token = (block ^ c) * rows + position - block * rows
        seg = sum(((token >= q * seg_len).astype(jnp.int32) for q in range(8, 20)))
        parent = jnp.where(seg == 0, -1, jnp.where(seg <= 4, 0, (seg - 3) >> 1))
        shift = jnp.where(seg == 0, 0, jnp.where(seg <= 4, seg - 1, seg - 2))
        return seg, parent, token - shift * seg_len

    key_seg, _, key_place = info(lax.broadcasted_iota(jnp.int32, (16, length), 1))

    def rows_of(i, _):
        at = pl.multiple_of(i * 16, 16)
        seg, parent, place = info(lax.broadcasted_iota(jnp.int32, (16, length), 0) + at)
        allowed = (key_seg == 0) | (key_seg == seg) | (key_seg == parent)
        relative = key_place - place
        magnitude = jnp.abs(relative)
        marked = sum(((magnitude >= mark).astype(jnp.int32) for mark in marks))
        bucket = jnp.where(relative > 0, 16, 0) + jnp.where(magnitude < 8, magnitude, 7 + marked)
        looked = [jnp.full(bucket.shape, table[0, h], wide) for h in range(heads)]
        for b in range(1, table.shape[0]):
            hit = bucket == b
            looked = [jnp.where(hit, table[b, h], looked[h]) for h in range(heads)]
        for h in range(heads):
            out[h, pl.ds(at, 16), :] = jnp.where(allowed, looked[h], masked_score)
        return 0

    lax.fori_loop(0, length // 16, rows_of, 0)


def norm_one(n_ctx, n_shard, idx, x_in, *refs):
    s, half = idx[0], idx[2]
    mine, rest = refs[: n_ctx - 1], refs[n_ctx - 1]
    g1, g2 = refs[n_ctx], refs[n_ctx + 1]
    bufs = refs[n_ctx + 2 : n_ctx + 1 + n_shard]
    normed, x_mine, x_own, gains = refs[n_ctx + 1 + n_shard :]
    r = normed.shape[2]
    inner = bufs[0].shape[0] - 16
    _, rows, width = x_in.shape
    gains[s, 0:1, :] = g1[...].astype(wide)
    gains[s, 1:2, :] = g2[...].astype(wide)
    for k, buf in enumerate(bufs):
        both = buf[inner : inner + 2, 0:r].astype(wide)
        gains[wrap(s - 1 - k, n_shard), 0:2, :] = both
    for m in range(2):
        for k in range(n_ctx):
            if k == 0:
                x = x_in[half if m == 0 else 1 - half]
            else:
                x = mine[k - 1][...] if m == 0 else rest[k - 1]
            x = x.astype(wide)
            y = x * lax.rsqrt(jnp.mean(x * x, axis=-1, keepdims=True) + norm_eps)
            at = (m * n_ctx + k) * rows
            for j in range(n_shard):
                piece = slice(r * j, r * (j + 1))
                normed[j, at : at + rows, :] = (y[:, piece] * gains[j, 0:1, :]).astype(low)
                if m == 0:
                    x_mine[j, at : at + rows, :] = x[:, piece].astype(low)
                    if k == 0:
                        x_own[j] = x[:, piece]


def chunk_cot(n_ctx, n_shard, idx, x_in, *refs):
    half = idx[2]
    mine, rest = refs[: n_ctx - 1], refs[n_ctx - 1]
    out, own = refs[n_ctx:]
    r = out.shape[2]
    _, rows, _ = x_in.shape
    for m in range(2):
        for k in range(n_ctx):
            if k == 0:
                x = x_in[half if m == 0 else 1 - half]
            else:
                x = mine[k - 1][...] if m == 0 else rest[k - 1]
            at = (m * n_ctx + k) * rows
            for j in range(n_shard):
                out[j, at : at + rows, :] = x[:, r * j : r * (j + 1)]
                if m == 0 and k == 0:
                    own[j] = x[:, r * j : r * (j + 1)]


def attend(n_ctx, n_shard, rows, heads, idx, normed, own_t, w_o, bias, *refs):
    s, c = idx[0], idx[1]
    first, later = refs[:n_ctx], refs[n_ctx : 2 * n_ctx]
    att_mine, att_other, soft, qkv, mixed_own, every, mixed = refs[2 * n_ctx :]
    inner, r = w_o.shape
    length = n_ctx * rows
    every[s, 0 : 3 * inner, :] = own_t[...]
    every[s, 3 * inner : 4 * inner, :] = w_o[...]
    for v in range(n_ctx):

        @pl.when(c == v)
        def _(v=v):
            for k in range(n_ctx):
                at = slice((v ^ k) * inner, ((v ^ k) + 1) * inner)
                every[wrap(s - 1, n_shard), at, :] = first[k][0:inner, 0:r]
                for z in range(2, n_shard):
                    every[wrap(s - z, n_shard), at, :] = later[k][z - 2, 0:inner, 0:r]

    for m in range(2):
        low_row = m * length
        acc = dot_nt(normed[0, low_row : low_row + length, :], every[0, 0 : 3 * inner, :])
        for j in range(1, n_shard):
            acc += dot_nt(normed[j, low_row : low_row + length, :], every[j, 0 : 3 * inner, :])
        qkv[low_row : low_row + length, :] = acc.astype(low)
        for h in range(heads):
            at = DK * h
            keys = qkv[low_row : low_row + length, inner + at : inner + at + DK]
            values = qkv[low_row : low_row + length, 2 * inner + at : 2 * inner + at + DK]
            for b in range(n_ctx):
                top = low_row + b * rows
                scores = dot_nt(qkv[top : top + rows, at : at + DK], keys)
                scores += bias[h, b * rows : (b + 1) * rows, :]
                raised = jnp.exp(scores - jnp.max(scores, axis=-1, keepdims=True))
                share = raised / jnp.sum(raised, axis=-1, keepdims=True)
                if b == 0:
                    soft[m, h] = share
                got = dot_nn(share.astype(low), values).astype(low)
                mixed[top : top + rows, at : at + DK] = got
                if b == 0:
                    mixed_own[m * rows : (m + 1) * rows, at : at + DK] = got
        out = att_mine if m == 0 else att_other
        for j in range(n_shard):
            out[j] = dot_nn(
                mixed[low_row : low_row + length, :], every[j, 3 * inner : 4 * inner, :]
            ).astype(low)


def middle_norm(n_ctx, n_shard, width, x_mine, att, got, gains, normed, middle_own):
    length = x_mine.shape[1]
    rows = length // n_ctx
    for b in range(n_ctx):
        at = slice(b * rows, (b + 1) * rows)
        mids, total = [], 0.0
        for j in range(n_shard):
            mid = x_mine[j, at, :].astype(wide) + (
                att[j, at, :].astype(wide) + got[j, at, :].astype(wide)
            )
            total += jnp.sum(mid * mid, axis=-1, keepdims=True)
            mids.append(mid)
        scale = lax.rsqrt(total / width + norm_eps)
        for j in range(n_shard):
            normed[j, at, :] = (mids[j] * scale * gains[j, 1:2, :]).astype(low)
            if b == 0:
                middle_own[j] = mids[j]


def feed_forward(n_ctx, n_shard, n, rp, first, idx, nt_mine, nt_other, cot, *refs):
    s = idx[0]
    bufs, refs = refs[:n_shard], refs[n_shard:]
    before = None
    if not first:
        before, refs = refs[:4], refs[4:]
    grads, refs = refs[:n_shard], refs[n_shard:]
    feed, two, refs = refs[0:2], refs[2:4], refs[4:]
    w_in, w_down, hidden, pair = refs
    _, length, r = nt_mine.shape
    rows = length // n_ctx
    tiles, base = 2 * n // LANES, rp * (2 * n // LANES)
    down_tiles = [(q, min(LANES, r - LANES * q)) for q in range(pl.cdiv(r, LANES))]
    for k in range(n_shard):
        for q in range(tiles):
            w_in[k, :, LANES * q : LANES * (q + 1)] = bufs[k][rp * q : rp * q + r, :]
        for q, size in down_tiles:
            w_down[k, :, LANES * q : LANES * q + size] = bufs[k][
                base + n * q : base + n * (q + 1), 0:size
            ]
    c0, c1 = 0.7978845608028654, 0.044715
    span = 2 * rows
    for m, nt in ((0, nt_mine), (1, nt_other)):

        def block(b, _, m=m, nt=nt):
            at = pl.ds(pl.multiple_of(b * span, span), span)
            all_at = pl.ds(pl.multiple_of(m * length + b * span, span), span)
            both, back = 0.0, 0.0
            for k in range(n_shard):
                j = wrap(s - k, n_shard)
                both += dot_nn(nt[j, at, :], w_in[k])
                back += dot_nt(cot[j, all_at, :], w_down[k])
            gate, up = both[:, :n], both[:, n:]
            square = gate * gate
            bent = jnp.tanh(c0 * (gate + c1 * gate * square))
            half_one = 0.5 * (1.0 + bent)
            active = gate * half_one
            slope = half_one + 0.5 * gate * (1.0 - bent * bent) * (c0 * (1.0 + 3.0 * c1 * square))
            hid = (active * up).astype(low)
            hidden[all_at, :] = hid
            pair[all_at, 0:n] = (back * up * slope).astype(low)
            pair[all_at, n : 2 * n] = (back * active).astype(low)
            both_grad = pair[all_at, :]
            for k in range(n_shard):
                j = wrap(s - k, n_shard)
                made = dot_nn(hid, w_down[k])
                back_in = dot_nt(both_grad, w_in[k])
                for i in range(2):
                    piece = slice(i * rows, (i + 1) * rows)
                    out, out_two = made[piece], back_in[piece]
                    if before is not None:
                        out = out + before[m][2 * b + i, j].astype(wide)
                        out_two = out_two + before[2 + m][2 * b + i, j].astype(wide)
                    feed[m][2 * b + i, j] = out.astype(low)
                    two[m][2 * b + i, j] = out_two.astype(low)
            return 0

        lax.fori_loop(0, n_ctx // 2, block, 0)
    for p in range(n_shard):
        j = wrap(s - 1 - p, n_shard)
        got = dot_tn(nt_mine[j], pair[0:length, :]) + dot_tn(nt_other[j], pair[length:, :])
        for q in range(tiles):
            grads[p][rp * q : rp * q + r, :] = got[:, LANES * q : LANES * (q + 1)].astype(low)
        got = dot_tn(hidden[...], cot[j])
        for q, size in down_tiles:
            grads[p][base + n * q : base + n * (q + 1), 0:size] = got[
                :, LANES * q : LANES * q + size
            ].astype(low)


def norm_two_back(n_shard, width, n_parts, *refs):
    parts, refs = refs[:n_parts], refs[n_parts:]
    middle, cot, gains, out_in, grad, gain_grad = refs
    mids = [middle[j] for j in range(n_shard)]
    twos = [sum((p[j].astype(wide) for p in parts)) for j in range(n_shard)]
    mean = sum((jnp.sum(a * a, axis=-1, keepdims=True) for a in mids)) / width
    scale = lax.rsqrt(mean + norm_eps)
    us = [twos[j] * gains[j, 1:2, :] for j in range(n_shard)]
    inner = sum((jnp.sum(a * b, axis=-1, keepdims=True) for a, b in zip(us, mids, strict=True)))
    inner = inner / width * (scale * scale * scale)
    for j in range(n_shard):
        back = cot[j].astype(wide) + scale * us[j] - mids[j] * inner
        grad[j] = back
        out_in[j] = back.astype(low)
        gain_grad[j] = jnp.sum(twos[j] * mids[j] * scale, axis=0, keepdims=True)


def attend_back(n_ctx, n_shard, heads, idx, o_mine, o_other, soft, qkv, mixed, every, normed, *refs):
    s, c = idx[0], idx[1]
    kv, (q_grad, stack, kv_all, mixed_grad) = refs[:n_ctx], refs[n_ctx:]
    _, rows, r = o_mine.shape
    length = n_ctx * rows
    inner = heads * DK
    for m, o_in in ((0, o_mine), (1, o_other)):
        top, own = m * length, m * rows
        acc = 0.0
        for j in range(n_shard):
            acc += dot_nt(o_in[j], every[j, 3 * inner : 4 * inner, :])
        mixed_grad[own : own + rows, :] = acc.astype(low)
        for h in range(heads):
            at = DK * h
            share = soft[m, h]
            grad = mixed_grad[own : own + rows, at : at + DK]
            keys = qkv[top : top + length, inner + at : inner + at + DK]
            values = qkv[top : top + length, 2 * inner + at : 2 * inner + at + DK]
            queries = qkv[top : top + rows, at : at + DK]
            weight = dot_nt(grad, values)
            ds = share * (weight - jnp.sum(weight * share, axis=-1, keepdims=True))
            ds = ds.astype(low)
            q_grad[own : own + rows, at : at + DK] = dot_nn(ds, keys).astype(low)
            kv_all[top : top + length, at : at + DK] = dot_tn(ds, queries).astype(low)
            kv_all[top : top + length, inner + at : inner + at + DK] = dot_tn(
                share.astype(low), grad
            ).astype(low)
        for k in range(n_ctx):
            kv[k][own : own + rows, :] = kv_all[top + k * rows : top + (k + 1) * rows, :]
    for p in range(n_shard):
        j = wrap(s - 1 - p, n_shard)
        for_q = dot_tn(q_grad[0:rows, :], normed[j, 0:rows, :])
        for_q += dot_tn(q_grad[rows:, :], normed[j, length : length + rows, :])
        for_kv = dot_tn(kv_all[...], normed[j])
        for_o = dot_tn(mixed[0:rows, :], o_mine[j]) + dot_tn(mixed[rows:, :], o_other[j])
        stack[c, p] = for_q.astype(low)
        stack[c ^ 1, p] = for_kv[0:inner].astype(low)
        stack[c ^ 2, p] = for_kv[inner:].astype(low)
        stack[c ^ 3, p] = for_o.astype(low)


def first_grad(n_shard, n_parts, *refs):
    parts, (q_grad, every, out_mine, out_other, three) = refs[:n_parts], refs[n_parts:]
    rows2, inner = q_grad.shape
    rows = rows2 // 2
    three[:, 0:inner] = q_grad[...]
    three[:, inner:] = sum((p[...].astype(wide) for p in parts)).astype(low)
    for j in range(n_shard):
        got = dot_nn(three[...], every[j, 0 : 3 * inner, :]).astype(low)
        out_mine[j] = got[0:rows]
        out_other[j] = got[rows:]


def norm_one_back(n_shard, width, mine, got, x_own, grad, gains, out, gain_grad):
    r = x_own.shape[2]
    xs = [x_own[j] for j in range(n_shard)]
    ones = [mine[j].astype(wide) + got[j].astype(wide) for j in range(n_shard)]
    mean = sum((jnp.sum(a * a, axis=-1, keepdims=True) for a in xs)) / width
    scale = lax.rsqrt(mean + norm_eps)
    us = [ones[j] * gains[j, 0:1, :] for j in range(n_shard)]
    inner = sum((jnp.sum(a * b, axis=-1, keepdims=True) for a, b in zip(us, xs, strict=True)))
    inner = inner / width * (scale * scale * scale)
    for j in range(n_shard):
        back = grad[j] + scale * us[j] - xs[j] * inner
        out[:, r * j : r * (j + 1)] = back.astype(low)
        gain_grad[j] = jnp.sum(ones[j] * xs[j] * scale, axis=0, keepdims=True)


def produce(n_shard, n_parts, *refs):
    parts, (middle, out) = refs[:n_parts], refs[n_parts:]
    r = middle.shape[2]
    for j in range(n_shard):
        fed = sum((p[j].astype(wide) for p in parts))
        out[:, r * j : r * (j + 1)] = (middle[j] + fed).astype(low)


def finish_wide(n_ctx, widths, rp, idx, *refs):
    pieces, (out_g, out_u, out_d, stage) = refs[: len(widths) * n_ctx], refs[len(widths) * n_ctx :]
    r = out_g.shape[0]
    columns = sum(widths)
    for i, n in enumerate(widths):
        base = rp * (2 * n // LANES)
        for k in range(n_ctx):
            piece = pieces[i * n_ctx + k]
            for q in range(2 * n // LANES):
                stage[:, LANES * q : LANES * (q + 1)] = piece[rp * q : rp * q + r, :].astype(wide)
            for v in range(n_ctx):

                @pl.when(idx[1] == v)
                def _(v=v, n=n, i=i, k=k, piece=piece, base=base):
                    at = (v ^ k) * columns + sum(widths[:i])
                    out_g[:, at : at + n] = stage[:, 0:n]
                    out_u[:, at : at + n] = stage[:, n : 2 * n]
                    for q in range(pl.cdiv(r, LANES)):
                        size = min(LANES, r - LANES * q)
                        out_d[at : at + n, LANES * q : LANES * q + size] = piece[
                            base + n * q : base + n * (q + 1), 0:size
                        ].astype(wide)


def finish_attention(n_ctx, idx, *refs):
    pieces, outs = refs[:n_ctx], refs[n_ctx:]
    for v in range(n_ctx):

        @pl.when(idx[1] == v)
        def _(v=v):
            for k in range(n_ctx):
                got = pieces[k][...].astype(wide)
                outs[v ^ k][...] = got if (v ^ k) == 3 else got.T


def on_device(
    inputs,
    cotangent,
    norm1_gain,
    w_query,
    w_key,
    w_value,
    w_out,
    norm2_gain,
    w_gate,
    w_up,
    w_down,
    bias_table,
):
    _, rows, width = inputs.shape
    shards, ctx = lax.axis_size("shard"), lax.axis_size("ctx")
    r, inner = w_query.shape
    heads = inner // DK
    length = ctx * rows
    columns = w_gate.shape[1] // ctx
    first_width = pl.cdiv(columns, 2 * LANES) * LANES
    widths = (first_width, columns - first_width)
    rp = pl.cdiv(r, 16) * 16
    lanes_r = pl.cdiv(r, LANES) * LANES
    s, c, half = lax.axis_index("shard"), lax.axis_index("ctx"), lax.axis_index("tensor")
    idx = jnp.stack([s, c, half]).astype(jnp.int32)
    token_flops = 2 * 2 * length * width

    own_x = lax.dynamic_index_in_dim(inputs, half, 0, keepdims=False)
    mine_x = xor_gather(own_x, "ctx")[1:]
    own_t, own_buf = run(
        functools.partial(pack_attention, ctx),
        "pack_attention",
        [((3 * inner, r), low), ((inner + 16, lanes_r), low)],
        [idx, w_query, w_key, w_value, w_out, norm1_gain[None], norm2_gain[None]],
    )
    ring = ring_gather(own_buf, "shard")
    gathered_first = xor_gather(ring[1], "ctx")
    gathered_later = xor_gather(jnp.stack(ring[2:]), "ctx")
    rest_x = swap(jnp.stack(mine_x), "tensor")
    packed = run(
        functools.partial(pack_wide, ctx, widths, rp),
        "pack_wide",
        [((rp * (2 * n // LANES) + n * (lanes_r // LANES), LANES), low) for n in widths],
        [idx, w_gate, w_up, w_down],
        scratch=[pltpu.VMEM((r, 2 * max(widths)), low)],
    )
    wide_rings = [ring_gather(buf, "shard") for buf in packed]

    table = lax.dynamic_slice_in_dim(bias_table, half * heads, heads, 1)
    (bias,) = run(
        functools.partial(bias_body, rows, rows // 5, distance_marks),
        "bias",
        [((heads, length, length), wide)],
        [idx, table],
        scalars=2,
    )
    normed_one, x_mine, x_own, gains = run(
        functools.partial(norm_one, ctx, shards),
        "norm_one",
        [
            ((shards, 2 * length, r), low),
            ((shards, length, r), low),
            ((shards, rows, r), wide),
            ((shards, 2, r), wide),
        ],
        [idx, inputs, *mine_x, rest_x, norm1_gain[None], norm2_gain[None], *ring[1:]],
    )
    own_cot = lax.dynamic_index_in_dim(cotangent, half, 0, keepdims=False)
    mine_cot = xor_gather(own_cot, "ctx")[1:]
    rest_cot = swap(jnp.stack(mine_cot), "tensor")
    cot, cot_own = run(
        functools.partial(chunk_cot, ctx, shards),
        "chunk_cot",
        [((shards, 2 * length, r), low), ((shards, rows, r), low)],
        [idx, cotangent, *mine_cot, rest_cot],
    )
    att_mine, att_other, soft, qkv, mixed_own, every = run(
        functools.partial(attend, ctx, shards, rows, heads),
        "attend",
        [
            ((shards, length, r), low),
            ((shards, length, r), low),
            ((2, heads, rows, length), wide),
            ((2 * length, 3 * inner), low),
            ((2 * rows, inner), low),
            ((shards, 4 * inner, r), low),
        ],
        [idx, normed_one, own_t, w_out, bias, *gathered_first, *gathered_later],
        scratch=[pltpu.VMEM((2 * length, inner), low)],
        flops=token_flops * 4 * inner,
    )
    att_got = swap(att_other, "tensor")
    nt_mine, middle_own = run(
        functools.partial(middle_norm, ctx, shards, width),
        "middle_norm",
        [((shards, length, r), low), ((shards, rows, r), wide)],
        [x_mine, att_mine, att_got, gains],
        scalars=0,
    )
    nt_other = swap(nt_mine, "tensor")

    before = []
    wide_grads = []
    for i, n in enumerate(widths):
        tokens_out = ((ctx, shards, rows, r), low)
        got = run(
            functools.partial(feed_forward, ctx, shards, n, rp, i == 0),
            "feed_forward",
            [(packed[i].shape, low)] * shards + [tokens_out] * 4,
            [idx, nt_mine, nt_other, cot, *wide_rings[i], *before],
            scratch=[
                pltpu.VMEM((shards, r, 2 * n), low),
                pltpu.VMEM((shards, n, r), low),
                pltpu.VMEM((2 * length, n), low),
                pltpu.VMEM((2 * length, 2 * n), low),
            ],
            flops=token_flops * 9 * n,
        )
        wide_grads.append(got[:shards])
        before = list(got[shards:])
    feed_mine, feed_other, two_mine, two_other = before

    def tree_sum(mine, other):
        theirs = swap(other, "tensor")
        both = [(mine[k].astype(wide) + theirs[k].astype(wide)).astype(low) for k in range(ctx)]
        return [both[0]] + [swap(both[k], "ctx", k) for k in range(1, ctx)]

    two_parts = tree_sum(two_mine, two_other)
    out_in, middle_grad, gain_two = run(
        functools.partial(norm_two_back, shards, width, ctx),
        "norm_two_back",
        [((shards, rows, r), low), ((shards, rows, r), wide), ((shards, 1, r), wide)],
        [*two_parts, middle_own, cot_own, gains],
        scalars=0,
    )
    out_in_other = swap(out_in, "tensor")
    got = run(
        functools.partial(attend_back, ctx, shards, heads),
        "attend_back",
        [((2 * rows, 2 * inner), low)] * ctx
        + [((2 * rows, inner), low), ((4, shards, inner, r), low)],
        [idx, out_in, out_in_other, soft, qkv, mixed_own, every, normed_one],
        scratch=[pltpu.VMEM((2 * length, 2 * inner), low), pltpu.VMEM((2 * rows, inner), low)],
        flops=token_flops * 3 * inner,
    )
    kv_parts, q_grad, stack = got[:ctx], got[ctx], got[ctx + 1]
    kv_parts = [kv_parts[0]] + [swap(kv_parts[k], "ctx", k) for k in range(1, ctx)]
    first_mine, first_other = run(
        functools.partial(first_grad, shards, ctx),
        "first_grad",
        [((shards, rows, r), low)] * 2,
        [*kv_parts, q_grad, every],
        scalars=0,
        scratch=[pltpu.VMEM((2 * rows, 3 * inner), low)],
    )
    first_got = swap(first_other, "tensor")
    input_mine, gain_one = run(
        functools.partial(norm_one_back, shards, width),
        "norm_one_back",
        [((rows, width), low), ((shards, 1, r), wide)],
        [first_mine, first_got, x_own, middle_grad, gains],
        scalars=0,
    )
    input_other = swap(input_mine, "tensor")

    feed_parts = tree_sum(feed_mine, feed_other)
    (produced_mine,) = run(
        functools.partial(produce, shards, ctx),
        "produce",
        [((rows, width), low)],
        [*feed_parts, middle_own],
        scalars=0,
    )
    produced_other = swap(produced_mine, "tensor")

    pieces = []
    for grads in wide_grads:
        pieces += xor_gather(ring_scatter(grads, "shard"), "ctx")
    out_g, out_u, out_d = run(
        functools.partial(finish_wide, ctx, widths, rp),
        "finish_wide",
        [(w_gate.shape, wide), (w_up.shape, wide), (w_down.shape, wide)],
        [idx, *pieces],
        scratch=[pltpu.VMEM((r, 2 * max(widths)), wide)],
    )
    four = stack[0].astype(wide)
    for k in range(1, ctx):
        four = four + swap(stack[k], "ctx", k).astype(wide)
    four = four.astype(low)
    four = xor_gather(ring_scatter([four[p] for p in range(shards)], "shard"), "ctx")
    out_q, out_k, out_v, out_o = run(
        functools.partial(finish_attention, ctx),
        "finish_attention",
        [((r, inner), wide)] * 3 + [((inner, r), wide)],
        [idx, *four],
    )
    gain = jnp.concatenate([gain_one, gain_two], 1)
    gain = gain + swap(gain, "tensor")
    gain = sum(xor_gather(gain, "ctx"))
    own_gain = lax.dynamic_index_in_dim(gain, s, 0, keepdims=False)
    for k in range(1, shards):
        part = lax.dynamic_index_in_dim(gain, wrap(s + k, shards), 0, keepdims=False)
        own_gain = own_gain + step(part, "shard", k)

    def ordered(mine, other):
        return jnp.where(half == 0, jnp.stack([mine, other]), jnp.stack([other, mine]))

    return (
        ordered(produced_mine, produced_other),
        ordered(input_mine, input_other),
        own_gain[0],
        out_q,
        out_k,
        out_v,
        out_o,
        own_gain[1],
        out_g,
        out_u,
        out_d,
    )


def solution(mesh):
    placed = (
        P(None, ("shard", "ctx"), None),
        P(None, ("shard", "ctx"), None),
        P("shard"),
        P("shard", "tensor"),
        P("shard", "tensor"),
        P("shard", "tensor"),
        P("tensor", "shard"),
        P("shard"),
        P("shard", "tensor"),
        P("shard", "tensor"),
        P("tensor", "shard"),
        P(),
    )
    return jax.shard_map(
        on_device, mesh=mesh, in_specs=placed, out_specs=placed[:2] + placed[2:11], check_vma=False
    )
```

time: 577 us -> 369 us (0.64)
  local copies, waits for them, and re-layouts: 162 us -> 32 us
  other arithmetic: 123 us -> 6.07 us
  Pallas kernels: 0 us -> 62.2 us
  matrix products: 42.4 us -> 0 us
  waiting for transfers between devices: 167 us -> 197 us
    select_n x6 -> x2, other arithmetic: 68.1 us -> 1.7 us  [ordered(): jnp.where(half == 0, jnp.stack([mine, other]), jnp.stack([other, mine]))]
    pallas_call x0 -> x16, Pallas kernels: none -> 62.2 us  [run(): pl.pallas_call(body, name=name, out_shape=[jax.ShapeDtypeStruct(s, d) for...]
    dynamic_update_slice x36 -> x0, local copies, waits for them, and re-layouts: 45.9 us -> none  [put(): return lax.dynamic_update_slice_in_dim(stack, part[None], index, 0)]
    dot_general x27 -> x0, matrix products: 42.4 us -> none  [the longest x21 35.1 us: dot(): lax.dot_general(left, right, (((left_dim,), (right_dim,)), ((), ())), pre...]
    ppermute x30 -> x21, waiting for transfers between devices: 90.8 us -> 116 us  [step(): return lax.ppermute(x, axis, [(i, (i + k) % n) for i in range(n)])]
    convert_element_type x26 -> x12, other arithmetic: 26.8 us -> 4.01 us  [the longest x9 3.2 us: ring_scatter(): acc = (step(acc, axis).astype(wide) + part.astype(wide)).astype(low)]
    reshape x11 -> x0, local copies, waits for them, and re-layouts: 22.6 us -> none  [the longest x3 20.7 us: on_device(): ring_gather(three[i], 'shard').reshape(width, columns)]
    dynamic_slice x7 -> x0, local copies, waits for them, and re-layouts: 15.5 us -> none  [the longest x5 14.1 us: pick(): return lax.dynamic_index_in_dim(stack, index, 0, keepdims=False)]
  transfers between devices with their start and end apart: 74 -> 68, of which waited for: 28 -> 28; matrix products, arithmetic and copies ran while one was open for 51% -> 4% of each run, Pallas kernels for 0% -> 10%
where the time goes in v2:
time: 369 us; the launch traced here: 364 us
  waiting for transfers between devices  197 us (53%)
  starting transfers between devices  65.2 us (18%)
  Pallas kernels  62.2 us (17%)
  local copies, waits for them, and re-layouts  32 us (9%)
  other arithmetic  6.07 us (2%)
    ppermute x21, waiting for transfers between devices, step(): return lax.ppermute(x, axis, [(i, (i + k) % n) for i in range(n)])  116 us
    ppermute x47, waiting for transfers between devices, swap(): return lax.ppermute(x, axis, [(i, i ^ k) for i in range(n)])  81.5 us
    pallas_call x16, Pallas kernels, run(): pl.pallas_call(body, name=name, out_shape=[jax.ShapeDtypeStruct(s, d) for...  62.2 us
    ppermute x47, starting transfers between devices, swap(): return lax.ppermute(x, axis, [(i, i ^ k) for i in range(n)])  46.7 us
    unnamed x95, local copies, waits for them, and re-layouts  28.7 us
    ppermute x21, starting transfers between devices, step(): return lax.ppermute(x, axis, [(i, (i + k) % n) for i in range(n)])  18.5 us
  transfers between devices with their start and end apart: 68, of which 28 were waited for; matrix products, arithmetic and copies ran while one was open for 4% of the time, Pallas kernels for 10%

profile of v2, /device:TPU:0, one launch (start us, length us, event | category | flops | bytes accessed | tf_op | source)
XLA Modules:
  0.0 364.2 jit_solution(14949281003478933933)
XLA Ops:
  1.7 3.0 collective-permute-start
  4.7 1.5 collective-permute-start.1
  10.7 2.1 collective-permute-start.4
  12.8 4.6 %collective-permute-done.1.refs_1_ = bf16[80,1472]{1,0:T(8,128)(2,1)S(1)} collective-permute-done((bf16[80,1472]{1,0:T(8,128)(2,1)S(1)}, bf16[80,1472]{1,0:T(8,128)(2,1)S(1)}, u32[]{:S(2)}, u32[]{:S(2)}) %collective-permute-start.1) | collective-permute-done | bytes 235552 | tf_op jit(solution)/shard_map/ppermute | solution.py:58
  19.2 6.7 %collective-permute-done.5.refs_7_ = bf16[208,384]{1,0:T(8,128)(2,1)S(1)} collective-permute-done((bf16[208,384]{1,0:T(8,128)(2,1)S(1)}, bf16[208,384]{1,0:T(8,128)(2,1)S(1)}, u32[]{:S(2)}, u32[]{:S(2)}) %collective-permute-start.5) | collective-permute-done | bytes 159776 | tf_op jit(solution)/shard_map/ppermute | solution.py:53
  27.2 5.8 %collective-permute-done.6.refs_8_ = bf16[208,384]{1,0:T(8,128)(2,1)S(1)} collective-permute-done((bf16[208,384]{1,0:T(8,128)(2,1)S(1)}, bf16[208,384]{1,0:T(8,128)(2,1)S(1)}, u32[]{:S(2)}, u32[]{:S(2)}) %collective-permute-start.6) | collective-permute-done | bytes 159776 | tf_op jit(solution)/shard_map/ppermute | solution.py:53
  37.3 1.5 collective-permute-start.8
  40.1 5.3 %bias.1 = f32[3,320,320]{2,1,0:T(8,128)S(1)} custom-call(s32[3]{0:T(128)S(1)} %pad_add_fusion.idx, f32[32,3]{1,0:T(8,128)S(1)} %copy.32.table), custom_call_target="tpu_custom_call" | custom-call | bytes 1229196 | tf_op jit(solution)/shard_map/bias/pallas_call | solution.py:38
  45.4 3.3 norm_one.1
  50.4 4.4 %collective-permute-done.8.refs_2_ = bf16[208,384]{1,0:T(8,128)(2,1)} collective-permute-done((bf16[208,384]{1,0:T(8,128)(2,1)S(1)}, bf16[208,384]{1,0:T(8,128)(2,1)}, u32[]{:S(2)}, u32[]{:S(2)}) %collective-permute-start.8) | collective-permute-done | bytes 159776 | tf_op jit(solution)/shard_map/ppermute | solution.py:58
  54.9 13.9 %attend.1 = (bf16[4,320,368]{2,1,0:T(8,128)(2,1)S(1)}, bf16[4,320,368]{2,1,0:T(8,128)(2,1)}, f32[2,3,80,320]{3,2,1,0:T(8,128)S(1)}, bf16[640,576]{1,0:T(8,128)(2...) custom-call(s32[3]{0:T(128)S(1)} %pad_add_fusion.idx, ...), custom_call_target="tpu_custom_call" | custom-call | flops 1447034880 | bytes 11153420 | tf_op jit(solution)/shard_map/attend/pallas_call | solution.py:38
  71.5 2.5 copy.27.w_d
  79.2 1.6 collective-permute-start.15
  82.8 13.6 %collective-permute-done.22.refs_1_ = bf16[2240,128]{1,0:T(8,128)(2,1)S(1)} collective-permute-done((bf16[2240,128]{1,0:T(8,128)(2,1)S(1)}, bf16[2240,128]{1,0:T(8,128)(2,1)S(1)}, u32[]{:S(2)}, u32[]{:S(2)}) %collective-permute-start.22) | collective-permute-done | bytes 573472 | tf_op jit(solution)/shard_map/ppermute | solution.py:53
  100.0 14.1 %collective-permute-done.23.refs_2_ = bf16[2240,128]{1,0:T(8,128)(2,1)S(1)} collective-permute-done((bf16[2240,128]{1,0:T(8,128)(2,1)S(1)}, bf16[2240,128]{1,0:T(8,128)(2,1)S(1)}, u32[]{:S(2)}, u32[]{:S(2)}) %collective-permute-start.23) | collective-permute-done | bytes 573472 | tf_op jit(solution)/shard_map/ppermute | solution.py:53
  114.0 9.2 %collective-permute-done.19.refs_1_ = bf16[1680,128]{1,0:T(8,128)(2,1)S(1)} collective-permute-done((bf16[1680,128]{1,0:T(8,128)(2,1)S(1)}, bf16[1680,128]{1,0:T(8,128)(2,1)S(1)}, u32[]{:S(2)}, u32[]{:S(2)}) %collective-permute-start.19) | collective-permute-done | bytes 430112 | tf_op jit(solution)/shard_map/ppermute | solution.py:53
  123.2 20.2 %collective-permute-done.20.refs_2_ = bf16[1680,128]{1,0:T(8,128)(2,1)S(1)} collective-permute-done((bf16[1680,128]{1,0:T(8,128)(2,1)S(1)}, bf16[1680,128]{1,0:T(8,128)(2,1)S(1)}, u32[]{:S(2)}, u32[]{:S(2)}) %collective-permute-start.20) | collective-permute-done | bytes 430112 | tf_op jit(solution)/shard_map/ppermute | solution.py:53
  145.4 11.2 %feed_forward.2 = (bf16[2240,128]{1,0:T(8,128)(2,1)}, bf16[2240,128]{1,0:T(8,128)(2,1)S(1)}, bf16[2240,128]{1,0:T(8,128)(2,1)S(1)}, bf16[2240,128]{1,0:T(8,128)(...) custom-call(s32[3]{0:T(128)S(1)} %pad_add_fusion.idx, ...), custom_call_target="tpu_custom_call" | custom-call | flops 4341104640 | bytes 12124172 | tf_op jit(solution)/shard_map/feed_forward/pallas_call | solution.py:38
  158.3 10.1 %feed_forward.3 = (bf16[1680,128]{1,0:T(8,128)(2,1)}, bf16[1680,128]{1,0:T(8,128)(2,1)S(1)}, bf16[1680,128]{1,0:T(8,128)(2,1)S(1)}, bf16[1680,128]{1,0:T(8,128)(...) custom-call(s32[3]{0:T(128)S(1)} %pad_add_fusion.idx, ...), custom_call_target="tpu_custom_call" | custom-call | flops 3255828480 | bytes 14745612 | tf_op jit(solution)/shard_map/feed_forward/pallas_call | solution.py:38
  174.8 13.8 %collective-permute-done.62 = bf16[1680,128]{1,0:T(8,128)(2,1)} collective-permute-done((bf16[1680,128]{1,0:T(8,128)(2,1)}, bf16[1680,128]{1,0:T(8,128)(2,1)}, u32[]{:S(2)}, u32[]{:S(2)}) %collective-permute-start.62) | collective-permute-done | bytes 430112 | tf_op jit(solution)/shard_map/ppermute | solution.py:53
  189.9 11.0 %collective-permute-done.56 = bf16[2240,128]{1,0:T(8,128)(2,1)} collective-permute-done((bf16[2240,128]{1,0:T(8,128)(2,1)}, bf16[2240,128]{1,0:T(8,128)(2,1)}, u32[]{:S(2)}, u32[]{:S(2)}) %collective-permute-start.56) | collective-permute-done | bytes 573472 | tf_op jit(solution)/shard_map/ppermute | solution.py:53
  202.3 7.7 %collective-permute-done.63 = bf16[1680,128]{1,0:T(8,128)(2,1)S(1)} collective-permute-done((bf16[1680,128]{1,0:T(8,128)(2,1)S(1)}, bf16[1680,128]{1,0:T(8,128)(2,1)S(1)}, u32[]{:S(2)}, u32[]{:S(2)}) %collective-permute-start.63) | collective-permute-done | bytes 430112 | tf_op jit(solution)/shard_map/ppermute | solution.py:53
  210.1 8.7 %collective-permute-start.64 = (bf16[1680,128]{1,0:T(8,128)(2,1)S(1)}, bf16[1680,128]{1,0:T(8,128)(2,1)S(1)}, u32[]{:S(2)}, u32[]{:S(2)}) collective-permute-start(bf16[1680,128]{1,0:T(8,128)(2,1)S(1)} %add_convert_fusion.4), channel_id=1, source_target_pairs={{0,8},{8,16},{16,24},{24,0},{1,9},{9,17},{17,25},{25,1},{2,10},{10... | collective-permute-start | bytes 1290248 | tf_op jit(solution)/shard_map/ppermute | solution.py:53
  219.1 1.6 collective-permute-start.31
  223.0 5.1 %collective-permute-done.31.refs_1_ = bf16[4,80,368]{2,1,0:T(8,128)(2,1)S(1)} collective-permute-done((bf16[4,80,368]{2,1,0:T(8,128)(2,1)S(1)}, bf16[4,80,368]{2,1,0:T(8,128)(2,1)S(1)}, u32[]{:S(2)}, u32[]{:S(2)}) %collective-permute-start.31) | collective-permute-done | bytes 235552 | tf_op jit(solution)/shard_map/ppermute | solution.py:58
  230.8 3.0 collective-permute-done.33.refs_3_
  233.9 2.0 collective-permute-start.28
  237.5 3.4 collective-permute-done.28.refs_3_
  241.3 6.1 %attend_back.1 = (bf16[160,384]{1,0:T(8,128)(2,1)S(1)}, bf16[160,384]{1,0:T(8,128)(2,1)S(1)}, bf16[160,384]{1,0:T(8,128)(2,1)S(1)}, bf16[160,384]{1,0:T(8,128)(2...) custom-call(s32[3]{0:T(128)S(1)} %pad_add_fusion.idx, ...), custom_call_target="tpu_custom_call" | custom-call | flops 1085276160 | bytes 8843276 | tf_op jit(solution)/shard_map/attend_back/pallas_call | solution.py:38
  247.4 1.8 collective-permute-start.35
  251.1 2.1 collective-permute-done.35.refs_1_
  253.2 4.1 %collective-permute-done.36.refs_2_ = bf16[160,384]{1,0:T(8,128)(2,1)S(1)} collective-permute-done((bf16[160,384]{1,0:T(8,128)(2,1)S(1)}, bf16[160,384]{1,0:T(8,128)(2,1)S(1)}, u32[]{:S(2)}, u32[]{:S(2)}) %collective-permute-start.36) | collective-permute-done | bytes 122912 | tf_op jit(solution)/shard_map/ppermute | solution.py:58
  260.2 1.7 collective-permute-start.49
  264.1 10.5 %collective-permute-done.47 = bf16[4,192,368]{2,1,0:T(8,128)(2,1)S(1)} collective-permute-done((bf16[4,192,368]{2,1,0:T(8,128)(2,1)S(1)}, bf16[4,192,368]{2,1,0:T(8,128)(2,1)S(1)}, u32[]{:S(2)}, u32[]{:S(2)}) %collective-permute-start.47) | collective-permute-done | bytes 565280 | tf_op jit(solution)/shard_map/ppermute | solution.py:58
  276.3 11.1 %collective-permute-done.49 = bf16[4,192,368]{2,1,0:T(8,128)(2,1)S(1)} collective-permute-done((bf16[4,192,368]{2,1,0:T(8,128)(2,1)S(1)}, bf16[4,192,368]{2,1,0:T(8,128)(2,1)S(1)}, u32[]{:S(2)}, u32[]{:S(2)}) %collective-permute-start.49) | collective-permute-done | bytes 565280 | tf_op jit(solution)/shard_map/ppermute | solution.py:58
  287.4 2.7 collective-permute-start.43
  290.4 6.0 %collective-permute-done.41 = f32[4,2,368]{2,1,0:T(2,128)S(1)} collective-permute-done((f32[4,2,368]{2,1,0:T(2,128)S(1)}, f32[4,2,368]{2,1,0:T(2,128)S(1)}, u32[]{:S(2)}, u32[]{:S(2)}) %collective-permute-start.41) | collective-permute-done | bytes 11808 | tf_op jit(solution)/shard_map/ppermute | solution.py:58
  298.3 2.6 collective-permute-start.44
  300.8 3.3 collective-permute-done.50
  305.5 2.4 collective-permute-start.45
  307.9 3.4 collective-permute-done.51
  312.6 2.3 collective-permute-done.46
  317.7 4.1 %collective-permute-done.52 = bf16[192,368]{1,0:T(8,128)(2,1)S(1)} collective-permute-done((bf16[192,368]{1,0:T(8,128)(2,1)S(1)}, bf16[192,368]{1,0:T(8,128)(2,1)S(1)}, u32[]{:S(2)}, u32[]{:S(2)}) %collective-permute-start.52) | collective-permute-done | bytes 141344 | tf_op jit(solution)/shard_map/ppermute | solution.py:53
  322.4 8.0 %collective-permute-done.67.refs_7_ = bf16[1680,128]{1,0:T(8,128)(2,1)S(1)} collective-permute-done((bf16[1680,128]{1,0:T(8,128)(2,1)S(1)}, bf16[1680,128]{1,0:T(8,128)(2,1)S(1)}, u32[]{:S(2)}, u32[]{:S(2)}) %collective-permute-start.67) | collective-permute-done | bytes 430112 | tf_op jit(solution)/shard_map/ppermute | solution.py:58
  332.2 1.7 collective-permute-start.55
  334.8 17.7 %collective-permute-done.60.refs_2_ = bf16[2240,128]{1,0:T(8,128)(2,1)S(1)} collective-permute-done((bf16[2240,128]{1,0:T(8,128)(2,1)S(1)}, bf16[2240,128]{1,0:T(8,128)(2,1)S(1)}, u32[]{:S(2)}, u32[]{:S(2)}) %collective-permute-start.60) | collective-permute-done | bytes 573472 | tf_op jit(solution)/shard_map/ppermute | solution.py:58
  352.5 5.2 %finish_wide.1 = (f32[368,1792]{1,0:T(8,128)}, f32[368,1792]{1,0:T(8,128)}, f32[1792,368]{1,0:T(8,128)S(1)}) custom-call(s32[3]{0:T(128)S(1)} %pad_add_fusion.idx, bf16[2240,128]{1,0:T(8,128)(2,1)S(1)} %add_convert_fusion.refs_0_, bf16[2240,128]{1,0:T(8,128)(2,1)S(1)} %collective-permute-done.59.refs_1_, ...), custom_call_target="tpu_custom_call" | custom-call | bytes 11927564 | tf_op jit(solution)/shard_map/finish_wide/pallas_call | solution.py:38
  357.8 2.1 copy.31
  (230 shorter events, 72.5 us)
Async XLA Ops:
  1.7 11.1 %collective-permute-start = (bf16[80,1472]{1,0:T(8,128)(2,1)S(1)}, bf16[80,1472]{1,0:T(8,128)(2,1)S(1)}, u32[]{:S(2)}, u32[]{:S(2)}) collective-permute-start(bf16[80,1472]{1,0:T(8,128)(2,1)S(1)} %dynamic-slice_bitcast_fusion.1), channel_id=1, source_target_pairs={{0,2},{2,0},{4,6},{6,4},{1,3},{3,1},{5,7},{7,5},{8,10},{10,8},{12,... | collective-permute-start | bytes 706568 | tf_op jit(solution)/shard_map/ppermute | solution.py:58
  4.7 12.7 %collective-permute-start.1 = (bf16[80,1472]{1,0:T(8,128)(2,1)S(1)}, bf16[80,1472]{1,0:T(8,128)(2,1)S(1)}, u32[]{:S(2)}, u32[]{:S(2)}) collective-permute-start(bf16[80,1472]{1,0:T(8,128)(2,1)S(1)} %dynamic-slice_bitcast_fusion.1), channel_id=1, source_target_pairs={{0,4},{2,6},{4,0},{6,2},{1,5},{3,7},{5,1},{7,3},{8,12},{10,14},{12... | collective-permute-start | bytes 706568 | tf_op jit(solution)/shard_map/ppermute | solution.py:58
  6.2 11.2 %collective-permute-start.2 = (bf16[80,1472]{1,0:T(8,128)(2,1)S(1)}, bf16[80,1472]{1,0:T(8,128)(2,1)S(1)}, u32[]{:S(2)}, u32[]{:S(2)}) collective-permute-start(bf16[80,1472]{1,0:T(8,128)(2,1)S(1)} %dynamic-slice_bitcast_fusion.1), channel_id=1, source_target_pairs={{0,6},{2,4},{4,2},{6,0},{1,7},{3,5},{5,3},{7,1},{8,14},{10,12},{12... | collective-permute-start | bytes 706568 | tf_op jit(solution)/shard_map/ppermute | solution.py:58
  17.5 21.3 %collective-permute-start.3 = (bf16[3,80,1472]{2,1,0:T(8,128)(2,1)S(1)}, bf16[3,80,1472]{2,1,0:T(8,128)(2,1)S(1)}, u32[]{:S(2)}, u32[]{:S(2)}) collective-permute-start(bf16[3,80,1472]{2,1,0:T(8,128)(2,1)S(1)} %pad_maximum_fusion), channel_id=1, source_target_pairs={{0,1},{1,0},{2,3},{3,2},{4,5},{5,4},{6,7},{7,6},{8,9},{9,8},{10,11... | collective-permute-start | bytes 2119688 | tf_op jit(solution)/shard_map/ppermute | solution.py:58
  25.9 10.7 %collective-permute-start.7 = (bf16[208,384]{1,0:T(8,128)(2,1)S(1)}, bf16[208,384]{1,0:T(8,128)(2,1)S(1)}, u32[]{:S(2)}, u32[]{:S(2)}) collective-permute-start(bf16[208,384]{1,0:T(8,128)(2,1)S(1)} %collective-permute-done.4.refs_6_.refs_0_), channel_id=1, source_target_pairs={{0,2},{2,0},{4,6},{6,4},{1,3},{3,1},{5,7},{7,5},{8,10},{10,8},{12,... | collective-permute-start | bytes 479240 | tf_op jit(solution)/shard_map/ppermute | solution.py:58
  33.1 21.8 %collective-permute-start.10 = (bf16[2,208,384]{2,1,0:T(8,128)(2,1)S(1)}, bf16[2,208,384]{2,1,0:T(8,128)(2,1)}, u32[]{:S(2)}, u32[]{:S(2)}) collective-permute-start(bf16[2,208,384]{2,1,0:T(8,128)(2,1)S(1)} %pad_maximum_fusion.2.refs_4_), channel_id=1, source_target_pairs={{0,2},{2,0},{4,6},{6,4},{1,3},{3,1},{5,7},{7,5},{8,10},{10,8},{12,... | collective-permute-start | bytes 958472 | tf_op jit(solution)/shard_map/ppermute | solution.py:58
  34.4 20.5 %collective-permute-start.11 = (bf16[2,208,384]{2,1,0:T(8,128)(2,1)S(1)}, bf16[2,208,384]{2,1,0:T(8,128)(2,1)}, u32[]{:S(2)}, u32[]{:S(2)}) collective-permute-start(bf16[2,208,384]{2,1,0:T(8,128)(2,1)S(1)} %pad_maximum_fusion.2.refs_4_), channel_id=1, source_target_pairs={{0,4},{2,6},{4,0},{6,2},{1,5},{3,7},{5,1},{7,3},{8,12},{10,14},{12... | collective-permute-start | bytes 958472 | tf_op jit(solution)/shard_map/ppermute | solution.py:58
  35.6 19.3 %collective-permute-start.12 = (bf16[2,208,384]{2,1,0:T(8,128)(2,1)S(1)}, bf16[2,208,384]{2,1,0:T(8,128)(2,1)}, u32[]{:S(2)}, u32[]{:S(2)}) collective-permute-start(bf16[2,208,384]{2,1,0:T(8,128)(2,1)S(1)} %pad_maximum_fusion.2.refs_4_), channel_id=1, source_target_pairs={{0,6},{2,4},{4,2},{6,0},{1,7},{3,5},{5,3},{7,1},{8,14},{10,12},{12... | collective-permute-start | bytes 958472 | tf_op jit(solution)/shard_map/ppermute | solution.py:58
  37.3 17.5 %collective-permute-start.8 = (bf16[208,384]{1,0:T(8,128)(2,1)S(1)}, bf16[208,384]{1,0:T(8,128)(2,1)}, u32[]{:S(2)}, u32[]{:S(2)}) collective-permute-start(bf16[208,384]{1,0:T(8,128)(2,1)S(1)} %collective-permute-done.4.refs_6_.refs_0_), channel_id=1, source_target_pairs={{0,4},{2,6},{4,0},{6,2},{1,5},{3,7},{5,1},{7,3},{8,12},{10,14},{12... | collective-permute-start | bytes 479240 | tf_op jit(solution)/shard_map/ppermute | solution.py:58
  38.8 16.0 %collective-permute-start.9 = (bf16[208,384]{1,0:T(8,128)(2,1)S(1)}, bf16[208,384]{1,0:T(8,128)(2,1)}, u32[]{:S(2)}, u32[]{:S(2)}) collective-permute-start(bf16[208,384]{1,0:T(8,128)(2,1)S(1)} %collective-permute-done.4.refs_6_.refs_0_), channel_id=1, source_target_pairs={{0,6},{2,4},{4,2},{6,0},{1,7},{3,5},{5,3},{7,1},{8,14},{10,12},{12... | collective-permute-start | bytes 479240 | tf_op jit(solution)/shard_map/ppermute | solution.py:58
  71.5 24.8 %collective-permute-start.13 = (bf16[4,320,368]{2,1,0:T(8,128)(2,1)}, bf16[4,320,368]{2,1,0:T(8,128)(2,1)S(1)}, u32[]{:S(2)}, u32[]{:S(2)}) collective-permute-start(bf16[4,320,368]{2,1,0:T(8,128)(2,1)} %get-tuple-element.70), channel_id=1, source_target_pairs={{0,1},{1,0},{2,3},{3,2},{4,5},{5,4},{6,7},{7,6},{8,9},{9,8},{10,11... | collective-permute-start | bytes 2826248 | tf_op jit(solution)/shard_map/ppermute | solution.py:58
  79.1 17.2 %collective-permute-start.22 = (bf16[2240,128]{1,0:T(8,128)(2,1)S(1)}, bf16[2240,128]{1,0:T(8,128)(2,1)S(1)}, u32[]{:S(2)}, u32[]{:S(2)}) collective-permute-start(bf16[2240,128]{1,0:T(8,128)(2,1)S(1)} %get-tuple-element.75.refs_0_), channel_id=1, source_target_pairs={{0,8},{8,16},{16,24},{24,0},{1,9},{9,17},{17,25},{25,1},{2,10},{10... | collective-permute-start | bytes 1720328 | tf_op jit(solution)/shard_map/ppermute | solution.py:53
  79.2 20.0 %collective-permute-start.15 = (bf16[80,1472]{1,0:T(8,128)(2,1)S(1)}, bf16[80,1472]{1,0:T(8,128)(2,1)S(1)}, u32[]{:S(2)}, u32[]{:S(2)}) collective-permute-start(bf16[80,1472]{1,0:T(8,128)(2,1)S(1)} %dynamic-slice_bitcast_fusion), channel_id=1, source_target_pairs={{0,2},{2,0},{4,6},{6,4},{1,3},{3,1},{5,7},{7,5},{8,10},{10,8},{12,... | collective-permute-start | bytes 706568 | tf_op jit(solution)/shard_map/ppermute | solution.py:58
  80.8 18.5 %collective-permute-start.16 = (bf16[80,1472]{1,0:T(8,128)(2,1)S(1)}, bf16[80,1472]{1,0:T(8,128)(2,1)S(1)}, u32[]{:S(2)}, u32[]{:S(2)}) collective-permute-start(bf16[80,1472]{1,0:T(8,128)(2,1)S(1)} %dynamic-slice_bitcast_fusion), channel_id=1, source_target_pairs={{0,4},{2,6},{4,0},{6,2},{1,5},{3,7},{5,1},{7,3},{8,12},{10,14},{12... | collective-permute-start | bytes 706568 | tf_op jit(solution)/shard_map/ppermute | solution.py:58
  82.1 17.2 %collective-permute-start.17 = (bf16[80,1472]{1,0:T(8,128)(2,1)S(1)}, bf16[80,1472]{1,0:T(8,128)(2,1)S(1)}, u32[]{:S(2)}, u32[]{:S(2)}) collective-permute-start(bf16[80,1472]{1,0:T(8,128)(2,1)S(1)} %dynamic-slice_bitcast_fusion), channel_id=1, source_target_pairs={{0,6},{2,4},{4,2},{6,0},{1,7},{3,5},{5,3},{7,1},{8,14},{10,12},{12... | collective-permute-start | bytes 706568 | tf_op jit(solution)/shard_map/ppermute | solution.py:58
  96.3 17.7 %collective-permute-start.23 = (bf16[2240,128]{1,0:T(8,128)(2,1)S(1)}, bf16[2240,128]{1,0:T(8,128)(2,1)S(1)}, u32[]{:S(2)}, u32[]{:S(2)}) collective-permute-start(bf16[2240,128]{1,0:T(8,128)(2,1)S(1)} %collective-permute-done.22.refs_1_), channel_id=1, source_target_pairs={{0,8},{8,16},{16,24},{24,0},{1,9},{9,17},{17,25},{25,1},{2,10},{10... | collective-permute-start | bytes 1720328 | tf_op jit(solution)/shard_map/ppermute | solution.py:53
  97.3 25.9 %collective-permute-start.19 = (bf16[1680,128]{1,0:T(8,128)(2,1)S(1)}, bf16[1680,128]{1,0:T(8,128)(2,1)S(1)}, u32[]{:S(2)}, u32[]{:S(2)}) collective-permute-start(bf16[1680,128]{1,0:T(8,128)(2,1)S(1)} %get-tuple-element.74.refs_0_), channel_id=1, source_target_pairs={{0,8},{8,16},{16,24},{24,0},{1,9},{9,17},{17,25},{25,1},{2,10},{10... | collective-permute-start | bytes 1290248 | tf_op jit(solution)/shard_map/ppermute | solution.py:53
  99.2 46.2 %collective-permute-start.14 = (bf16[4,320,368]{2,1,0:T(8,128)(2,1)S(1)}, bf16[4,320,368]{2,1,0:T(8,128)(2,1)S(1)}, u32[]{:S(2)}, u32[]{:S(2)}) collective-permute-start(bf16[4,320,368]{2,1,0:T(8,128)(2,1)S(1)} %get-tuple-element.72.nt_mine), channel_id=1, source_target_pairs={{0,1},{1,0},{2,3},{3,2},{4,5},{5,4},{6,7},{7,6},{8,9},{9,8},{10,11... | collective-permute-start | bytes 2826248 | tf_op jit(solution)/shard_map/ppermute | solution.py:58
  99.4 44.0 %collective-permute-start.18 = (bf16[3,80,1472]{2,1,0:T(8,128)(2,1)S(1)}, bf16[3,80,1472]{2,1,0:T(8,128)(2,1)S(1)}, u32[]{:S(2)}, u32[]{:S(2)}) collective-permute-start(bf16[3,80,1472]{2,1,0:T(8,128)(2,1)S(1)} %pad_maximum_fusion.1), channel_id=1, source_target_pairs={{0,1},{1,0},{2,3},{3,2},{4,5},{5,4},{6,7},{7,6},{8,9},{9,8},{10,11... | collective-permute-start | bytes 2119688 | tf_op jit(solution)/shard_map/ppermute | solution.py:58
  114.0 31.4 %collective-permute-start.24 = (bf16[2240,128]{1,0:T(8,128)(2,1)S(1)}, bf16[2240,128]{1,0:T(8,128)(2,1)S(1)}, u32[]{:S(2)}, u32[]{:S(2)}) collective-permute-start(bf16[2240,128]{1,0:T(8,128)(2,1)S(1)} %collective-permute-done.23.refs_2_), channel_id=1, source_target_pairs={{0,8},{8,16},{16,24},{24,0},{1,9},{9,17},{17,25},{25,1},{2,10},{10... | collective-permute-start | bytes 1720328 | tf_op jit(solution)/shard_map/ppermute | solution.py:53
  123.2 20.2 %collective-permute-start.20 = (bf16[1680,128]{1,0:T(8,128)(2,1)S(1)}, bf16[1680,128]{1,0:T(8,128)(2,1)S(1)}, u32[]{:S(2)}, u32[]{:S(2)}) collective-permute-start(bf16[1680,128]{1,0:T(8,128)(2,1)S(1)} %collective-permute-done.19.refs_1_), channel_id=1, source_target_pairs={{0,8},{8,16},{16,24},{24,0},{1,9},{9,17},{17,25},{25,1},{2,10},{10... | collective-permute-start | bytes 1290248 | tf_op jit(solution)/shard_map/ppermute | solution.py:53
  143.5 14.8 %collective-permute-start.21 = (bf16[1680,128]{1,0:T(8,128)(2,1)S(1)}, bf16[1680,128]{1,0:T(8,128)(2,1)S(1)}, u32[]{:S(2)}, u32[]{:S(2)}) collective-permute-start(bf16[1680,128]{1,0:T(8,128)(2,1)S(1)} %collective-permute-done.20.refs_2_), channel_id=1, source_target_pairs={{0,8},{8,16},{16,24},{24,0},{1,9},{9,17},{17,25},{25,1},{2,10},{10... | collective-permute-start | bytes 1290248 | tf_op jit(solution)/shard_map/ppermute | solution.py:53
  173.6 15.0 %collective-permute-start.62 = (bf16[1680,128]{1,0:T(8,128)(2,1)}, bf16[1680,128]{1,0:T(8,128)(2,1)}, u32[]{:S(2)}, u32[]{:S(2)}) collective-permute-start(bf16[1680,128]{1,0:T(8,128)(2,1)} %get-tuple-element.112), channel_id=1, source_target_pairs={{0,8},{8,16},{16,24},{24,0},{1,9},{9,17},{17,25},{25,1},{2,10},{10... | collective-permute-start | bytes 1290248 | tf_op jit(solution)/shard_map/ppermute | solution.py:53
  174.0 26.9 %collective-permute-start.56 = (bf16[2240,128]{1,0:T(8,128)(2,1)}, bf16[2240,128]{1,0:T(8,128)(2,1)}, u32[]{:S(2)}, u32[]{:S(2)}) collective-permute-start(bf16[2240,128]{1,0:T(8,128)(2,1)} %get-tuple-element.108), channel_id=1, source_target_pairs={{0,8},{8,16},{16,24},{24,0},{1,9},{9,17},{17,25},{25,1},{2,10},{10... | collective-permute-start | bytes 1720328 | tf_op jit(solution)/shard_map/ppermute | solution.py:53
  174.3 44.6 %collective-permute-start.30 = (bf16[4,4,80,368]{3,2,1,0:T(8,128)(2,1)}, bf16[4,4,80,368]{3,2,1,0:T(8,128)(2,1)S(1)}, u32[]{:S(2)}, u32[]{:S(2)}) collective-permute-start(bf16[4,4,80,368]{3,2,1,0:T(8,128)(2,1)} %copy-done.41), channel_id=1, source_target_pairs={{0,1},{1,0},{2,3},{3,2},{4,5},{5,4},{6,7},{7,6},{8,9},{9,8},{10,11... | collective-permute-start | bytes 2826248 | tf_op jit(solution)/shard_map/ppermute | solution.py:58
  174.3 47.8 %collective-permute-start.25 = (bf16[4,4,80,368]{3,2,1,0:T(8,128)(2,1)}, bf16[4,4,80,368]{3,2,1,0:T(8,128)(2,1)S(1)}, u32[]{:S(2)}, u32[]{:S(2)}) collective-permute-start(bf16[4,4,80,368]{3,2,1,0:T(8,128)(2,1)} %copy-done.40), channel_id=1, source_target_pairs={{0,1},{1,0},{2,3},{3,2},{4,5},{5,4},{6,7},{7,6},{8,9},{9,8},{10,11... | collective-permute-start | bytes 2826248 | tf_op jit(solution)/shard_map/ppermute | solution.py:58
  189.9 20.1 %collective-permute-start.63 = (bf16[1680,128]{1,0:T(8,128)(2,1)S(1)}, bf16[1680,128]{1,0:T(8,128)(2,1)S(1)}, u32[]{:S(2)}, u32[]{:S(2)}) collective-permute-start(bf16[1680,128]{1,0:T(8,128)(2,1)S(1)} %add_convert_fusion.5), channel_id=1, source_target_pairs={{0,8},{8,16},{16,24},{24,0},{1,9},{9,17},{17,25},{25,1},{2,10},{10... | collective-permute-start | bytes 1290248 | tf_op jit(solution)/shard_map/ppermute | solution.py:53
  202.2 34.0 %collective-permute-start.57 = (bf16[2240,128]{1,0:T(8,128)(2,1)S(1)}, bf16[2240,128]{1,0:T(8,128)(2,1)S(1)}, u32[]{:S(2)}, u32[]{:S(2)}) collective-permute-start(bf16[2240,128]{1,0:T(8,128)(2,1)S(1)} %add_convert_fusion.2), channel_id=1, source_target_pairs={{0,8},{8,16},{16,24},{24,0},{1,9},{9,17},{17,25},{25,1},{2,10},{10... | collective-permute-start | bytes 1720328 | tf_op jit(solution)/shard_map/ppermute | solution.py:53
  210.1 39.9 %collective-permute-start.64 = (bf16[1680,128]{1,0:T(8,128)(2,1)S(1)}, bf16[1680,128]{1,0:T(8,128)(2,1)S(1)}, u32[]{:S(2)}, u32[]{:S(2)}) collective-permute-start(bf16[1680,128]{1,0:T(8,128)(2,1)S(1)} %add_convert_fusion.4), channel_id=1, source_target_pairs={{0,8},{8,16},{16,24},{24,0},{1,9},{9,17},{17,25},{25,1},{2,10},{10... | collective-permute-start | bytes 1290248 | tf_op jit(solution)/shard_map/ppermute | solution.py:53
  222.1 11.8 %collective-permute-start.33 = (bf16[4,80,368]{2,1,0:T(8,128)(2,1)S(1)}, bf16[4,80,368]{2,1,0:T(8,128)(2,1)S(1)}, u32[]{:S(2)}, u32[]{:S(2)}) collective-permute-start(bf16[4,80,368]{2,1,0:T(8,128)(2,1)S(1)} %get-tuple-element.135), channel_id=1, source_target_pairs={{0,6},{2,4},{4,2},{6,0},{1,7},{3,5},{5,3},{7,1},{8,14},{10,12},{12... | collective-permute-start | bytes 706568 | tf_op jit(solution)/shard_map/ppermute | solution.py:58
  236.5 67.8 %collective-permute-start.58 = (bf16[2240,128]{1,0:T(8,128)(2,1)S(1)}, bf16[2240,128]{1,0:T(8,128)(2,1)S(1)}, u32[]{:S(2)}, u32[]{:S(2)}) collective-permute-start(bf16[2240,128]{1,0:T(8,128)(2,1)S(1)} %add_convert_fusion.1), channel_id=1, source_target_pairs={{0,8},{8,16},{16,24},{24,0},{1,9},{9,17},{17,25},{25,1},{2,10},{10... | collective-permute-start | bytes 1720328 | tf_op jit(solution)/shard_map/ppermute | solution.py:53
  241.1 21.2 %collective-permute-start.29 = (bf16[80,1472]{1,0:T(8,128)(2,1)S(1)}, bf16[80,1472]{1,0:T(8,128)(2,1)S(1)}, u32[]{:S(2)}, u32[]{:S(2)}) collective-permute-start(bf16[80,1472]{1,0:T(8,128)(2,1)S(1)} %produce.1), channel_id=1, source_target_pairs={{0,1},{1,0},{2,3},{3,2},{4,5},{5,4},{6,7},{7,6},{8,9},{9,8},{10,11... | collective-permute-start | bytes 706568 | tf_op jit(solution)/shard_map/ppermute | solution.py:58
  258.4 16.2 %collective-permute-start.47 = (bf16[4,192,368]{2,1,0:T(8,128)(2,1)S(1)}, bf16[4,192,368]{2,1,0:T(8,128)(2,1)S(1)}, u32[]{:S(2)}, u32[]{:S(2)}) collective-permute-start(bf16[4,192,368]{2,1,0:T(8,128)(2,1)S(1)} %get-tuple-element.132), channel_id=1, source_target_pairs={{0,2},{2,0},{4,6},{6,4},{1,3},{3,1},{5,7},{7,5},{8,10},{10,8},{12,... | collective-permute-start | bytes 1695752 | tf_op jit(solution)/shard_map/ppermute | solution.py:58
  258.9 16.1 %collective-permute-start.48 = (bf16[4,192,368]{2,1,0:T(8,128)(2,1)S(1)}, bf16[4,192,368]{2,1,0:T(8,128)(2,1)S(1)}, u32[]{:S(2)}, u32[]{:S(2)}) collective-permute-start(bf16[4,192,368]{2,1,0:T(8,128)(2,1)S(1)} %get-tuple-element.134), channel_id=1, source_target_pairs={{0,4},{2,6},{4,0},{6,2},{1,5},{3,7},{5,1},{7,3},{8,12},{10,14},{12... | collective-permute-start | bytes 1695752 | tf_op jit(solution)/shard_map/ppermute | solution.py:58
  260.2 27.2 %collective-permute-start.49 = (bf16[4,192,368]{2,1,0:T(8,128)(2,1)S(1)}, bf16[4,192,368]{2,1,0:T(8,128)(2,1)S(1)}, u32[]{:S(2)}, u32[]{:S(2)}) collective-permute-start(bf16[4,192,368]{2,1,0:T(8,128)(2,1)S(1)} %get-tuple-element.133), channel_id=1, source_target_pairs={{0,6},{2,4},{4,2},{6,0},{1,7},{3,5},{5,3},{7,1},{8,14},{10,12},{12... | collective-permute-start | bytes 1695752 | tf_op jit(solution)/shard_map/ppermute | solution.py:58
  263.6 51.3 %collective-permute-start.65 = (bf16[1680,128]{1,0:T(8,128)(2,1)S(1)}, bf16[1680,128]{1,0:T(8,128)(2,1)S(1)}, u32[]{:S(2)}, u32[]{:S(2)}) collective-permute-start(bf16[1680,128]{1,0:T(8,128)(2,1)S(1)} %add_convert_fusion.3.refs_4_), channel_id=1, source_target_pairs={{0,2},{2,0},{4,6},{6,4},{1,3},{3,1},{5,7},{7,5},{8,10},{10,8},{12,... | collective-permute-start | bytes 1290248 | tf_op jit(solution)/shard_map/ppermute | solution.py:58
  274.5 21.9 %collective-permute-start.41 = (f32[4,2,368]{2,1,0:T(2,128)S(1)}, f32[4,2,368]{2,1,0:T(2,128)S(1)}, u32[]{:S(2)}, u32[]{:S(2)}) collective-permute-start(f32[4,2,368]{2,1,0:T(2,128)S(1)} %fusion.16), channel_id=1, source_target_pairs={{0,2},{2,0},{4,6},{6,4},{1,3},{3,1},{5,7},{7,5},{8,10},{10,8},{12,... | collective-permute-start | bytes 35336 | tf_op jit(solution)/shard_map/ppermute | solution.py:58
  275.0 22.2 %collective-permute-start.42 = (f32[4,2,368]{2,1,0:T(2,128)S(1)}, f32[4,2,368]{2,1,0:T(2,128)S(1)}, u32[]{:S(2)}, u32[]{:S(2)}) collective-permute-start(f32[4,2,368]{2,1,0:T(2,128)S(1)} %fusion.16), channel_id=1, source_target_pairs={{0,4},{2,6},{4,0},{6,2},{1,5},{3,7},{5,1},{7,3},{8,12},{10,14},{12... | collective-permute-start | bytes 35336 | tf_op jit(solution)/shard_map/ppermute | solution.py:58
  287.4 10.8 %collective-permute-start.43 = (f32[4,2,368]{2,1,0:T(2,128)S(1)}, f32[4,2,368]{2,1,0:T(2,128)S(1)}, u32[]{:S(2)}, u32[]{:S(2)}) collective-permute-start(f32[4,2,368]{2,1,0:T(2,128)S(1)} %fusion.16), channel_id=1, source_target_pairs={{0,6},{2,4},{4,2},{6,0},{1,7},{3,5},{5,3},{7,1},{8,14},{10,12},{12... | collective-permute-start | bytes 35336 | tf_op jit(solution)/shard_map/ppermute | solution.py:58
  296.4 19.8 %collective-permute-start.66 = (bf16[1680,128]{1,0:T(8,128)(2,1)S(1)}, bf16[1680,128]{1,0:T(8,128)(2,1)S(1)}, u32[]{:S(2)}, u32[]{:S(2)}) collective-permute-start(bf16[1680,128]{1,0:T(8,128)(2,1)S(1)} %add_convert_fusion.3.refs_4_), channel_id=1, source_target_pairs={{0,4},{2,6},{4,0},{6,2},{1,5},{3,7},{5,1},{7,3},{8,12},{10,14},{12... | collective-permute-start | bytes 1290248 | tf_op jit(solution)/shard_map/ppermute | solution.py:58
  304.4 27.8 %collective-permute-start.59 = (bf16[2240,128]{1,0:T(8,128)(2,1)S(1)}, bf16[2240,128]{1,0:T(8,128)(2,1)S(1)}, u32[]{:S(2)}, u32[]{:S(2)}) collective-permute-start(bf16[2240,128]{1,0:T(8,128)(2,1)S(1)} %add_convert_fusion.refs_0_), channel_id=1, source_target_pairs={{0,2},{2,0},{4,6},{6,4},{1,3},{3,1},{5,7},{7,5},{8,10},{10,8},{12,... | collective-permute-start | bytes 1720328 | tf_op jit(solution)/shard_map/ppermute | solution.py:58
  311.3 19.1 %collective-permute-start.67 = (bf16[1680,128]{1,0:T(8,128)(2,1)S(1)}, bf16[1680,128]{1,0:T(8,128)(2,1)S(1)}, u32[]{:S(2)}, u32[]{:S(2)}) collective-permute-start(bf16[1680,128]{1,0:T(8,128)(2,1)S(1)} %add_convert_fusion.3.refs_4_), channel_id=1, source_target_pairs={{0,6},{2,4},{4,2},{6,0},{1,7},{3,5},{5,3},{7,1},{8,14},{10,12},{12... | collective-permute-start | bytes 1290248 | tf_op jit(solution)/shard_map/ppermute | solution.py:58
  314.9 37.7 %collective-permute-start.60 = (bf16[2240,128]{1,0:T(8,128)(2,1)S(1)}, bf16[2240,128]{1,0:T(8,128)(2,1)S(1)}, u32[]{:S(2)}, u32[]{:S(2)}) collective-permute-start(bf16[2240,128]{1,0:T(8,128)(2,1)S(1)} %add_convert_fusion.refs_0_), channel_id=1, source_target_pairs={{0,4},{2,6},{4,0},{6,2},{1,5},{3,7},{5,1},{7,3},{8,12},{10,14},{12... | collective-permute-start | bytes 1720328 | tf_op jit(solution)/shard_map/ppermute | solution.py:58
  316.2 36.3 %collective-permute-start.61 = (bf16[2240,128]{1,0:T(8,128)(2,1)S(1)}, bf16[2240,128]{1,0:T(8,128)(2,1)S(1)}, u32[]{:S(2)}, u32[]{:S(2)}) collective-permute-start(bf16[2240,128]{1,0:T(8,128)(2,1)S(1)} %add_convert_fusion.refs_0_), channel_id=1, source_target_pairs={{0,6},{2,4},{4,2},{6,0},{1,7},{3,5},{5,3},{7,1},{8,14},{10,12},{12... | collective-permute-start | bytes 1720328 | tf_op jit(solution)/shard_map/ppermute | solution.py:58
  321.8 9.1 %collective-permute-start.39 = (bf16[80,1472]{1,0:T(8,128)(2,1)S(1)}, bf16[80,1472]{1,0:T(8,128)(2,1)S(1)}, u32[]{:S(2)}, u32[]{:S(2)}) collective-permute-start(bf16[80,1472]{1,0:T(8,128)(2,1)S(1)} %get-tuple-element.100), channel_id=1, source_target_pairs={{0,1},{1,0},{2,3},{3,2},{4,5},{5,4},{6,7},{7,6},{8,9},{9,8},{10,11... | collective-permute-start | bytes 706568 | tf_op jit(solution)/shard_map/ppermute | solution.py:58
  330.5 29.4 %collective-permute-start.53 = (bf16[192,368]{1,0:T(8,128)(2,1)S(1)}, bf16[192,368]{1,0:T(8,128)(2,1)S(1)}, u32[]{:S(2)}, u32[]{:S(2)}) collective-permute-start(bf16[192,368]{1,0:T(8,128)(2,1)S(1)} %fusion.3.refs_0_), channel_id=1, source_target_pairs={{0,2},{2,0},{4,6},{6,4},{1,3},{3,1},{5,7},{7,5},{8,10},{10,8},{12,... | collective-permute-start | bytes 423944 | tf_op jit(solution)/shard_map/ppermute | solution.py:58
  330.9 29.0 %collective-permute-start.54 = (bf16[192,368]{1,0:T(8,128)(2,1)S(1)}, bf16[192,368]{1,0:T(8,128)(2,1)S(1)}, u32[]{:S(2)}, u32[]{:S(2)}) collective-permute-start(bf16[192,368]{1,0:T(8,128)(2,1)S(1)} %fusion.3.refs_0_), channel_id=1, source_target_pairs={{0,4},{2,6},{4,0},{6,2},{1,5},{3,7},{5,1},{7,3},{8,12},{10,14},{12... | collective-permute-start | bytes 423944 | tf_op jit(solution)/shard_map/ppermute | solution.py:58
  332.2 27.7 %collective-permute-start.55 = (bf16[192,368]{1,0:T(8,128)(2,1)S(1)}, bf16[192,368]{1,0:T(8,128)(2,1)S(1)}, u32[]{:S(2)}, u32[]{:S(2)}) collective-permute-start(bf16[192,368]{1,0:T(8,128)(2,1)S(1)} %fusion.3.refs_0_), channel_id=1, source_target_pairs={{0,6},{2,4},{4,2},{6,0},{1,7},{3,5},{5,3},{7,1},{8,14},{10,12},{12... | collective-permute-start | bytes 423944 | tf_op jit(solution)/shard_map/ppermute | solution.py:58
  (63 other events, 445.0 us)

commit v3 on v2

v3 whole, which is shorter than its diff:
```python
import functools

import jax
import jax.numpy as jnp
from jax import lax
from jax.experimental import pallas as pl
from jax.experimental.pallas import tpu as pltpu
from jax.sharding import PartitionSpec as P

DK = 64
norm_eps = 1e-06
distance_marks = (8, 12, 16, 23, 32, 46, 64, 91)
masked_score = -1e30
low = jnp.bfloat16
wide = jnp.float32
LANES = 128
COST = 1e8


def dot_nn(left, right):
    return lax.dot_general(left, right, (((1,), (0,)), ((), ())), preferred_element_type=wide)


def dot_nt(left, right):
    return lax.dot_general(left, right, (((1,), (1,)), ((), ())), preferred_element_type=wide)


def dot_tn(left, right):
    return lax.dot_general(left, right, (((0,), (0,)), ((), ())), preferred_element_type=wide)


def wrap(value, n):
    return lax.rem(value + 2 * n, n)


def run(body, name, outs, operands, scratch=(), scalars=1, cost=1, far=0, vmem=40):
    return pl.pallas_call(
        body,
        name=name,
        out_shape=[jax.ShapeDtypeStruct(s, d) for s, d in outs],
        in_specs=[pl.BlockSpec(memory_space=pltpu.SMEM)] * scalars
        + [pl.BlockSpec(memory_space=pl.ANY)] * far
        + [pl.BlockSpec(memory_space=pltpu.VMEM)] * (len(operands) - scalars - far),
        out_specs=[pl.BlockSpec(memory_space=pltpu.VMEM)] * len(outs),
        scratch_shapes=list(scratch),
        compiler_params=pltpu.CompilerParams(vmem_limit_bytes=vmem * 2**20),
        cost_estimate=pl.CostEstimate(flops=int(cost * COST), bytes_accessed=0, transcendentals=0),
    )(*operands)


def step(x, axis, k=1):
    n = lax.axis_size(axis)
    return lax.ppermute(x, axis, [(i, (i + k) % n) for i in range(n)])


def swap(x, axis, k=1):
    n = lax.axis_size(axis)
    return lax.ppermute(x, axis, [(i, i ^ k) for i in range(n)])


def after(x, *others):
    return lax.optimization_barrier((x, *others))[0]


def gather_ctx(x):
    n = lax.axis_size("ctx")
    if n != 4:
        return [swap(x, "ctx", k) for k in range(1, n)]
    half = x.shape[0] // 2
    one, two = swap(x, "ctx", 1), swap(x, "ctx", 2)
    return [one, two, swap(one[:half], "ctx", 2), swap(two[half:], "ctx", 1)]


def xor_gather(x, axis):
    return [x] + [swap(x, axis, k) for k in range(1, lax.axis_size(axis))]


def pack_attention(n_ctx, idx, w_q, w_k, w_v, w_o, gain, buf, held, sem):
    inner, r = w_o.shape
    for v, ref in enumerate((w_q, w_k, w_v, w_o)):

        @pl.when(idx[1] == v)
        def _(ref=ref):
            copy = pltpu.make_async_copy(ref, held, sem)
            copy.start()
            copy.wait()

    buf[0:inner, 0:r] = held[...]

    buf[inner : inner + 2, 0:r] = gain[...]


def wide_tiles(r, widths):
    rp = pl.cdiv(r, 16) * 16
    row, parts = 0, []
    for n in widths:
        full, left = divmod(3 * n, LANES)
        pieces = [(row + rp * q, r, 0, LANES * q, LANES, 0) for q in range(full)]
        row += rp * full
        if left:
            assert 2 * left == LANES
            pieces.append((row, r // 2, 0, LANES * full, left, 0))
            pieces.append((row, r // 2, r // 2, LANES * full, left, left))
            row += pl.cdiv(r // 2, 8) * 8
        parts.append(pieces)
    return parts, pl.cdiv(row, 32) * 32


def pack_wide(n_ctx, widths, window, idx, w_g, w_u, w_d, buf, stage, held, sems):
    r = w_g.shape[0]
    columns = sum(widths)
    parts, _ = wide_tiles(r, widths)
    for v in range(n_ctx):

        @pl.when(idx[1] == v)
        def _(v=v):
            start = min(v * columns // LANES * LANES, w_g.shape[1] - window)
            copies = [
                pltpu.make_async_copy(ref.at[:, start : start + window], held.at[i], sems.at[i])
                for i, ref in enumerate((w_g, w_u, w_d))
            ]
            for copy in copies:
                copy.start()
            for copy in copies:
                copy.wait()
            at = v * columns - start
            for n, pieces in zip(widths, parts, strict=True):
                for i in range(3):
                    stage[:, i * n : (i + 1) * n] = held[i, :, at : at + n]
                for row, size, top, lane, lanes, to in pieces:
                    buf[row : row + size, to : to + lanes] = stage[
                        top : top + size, lane : lane + lanes
                    ]
                at += n


def bias_body(rows, seg_len, marks, idx, table, out):
    c = idx[1]
    heads, length, _ = out.shape

    def info(position):
        block = sum(((position >= rows * b).astype(jnp.int32) for b in range(1, length // rows)))
        token = (block ^ c) * rows + position - block * rows
        seg = sum(((token >= q * seg_len).astype(jnp.int32) for q in range(8, 20)))
        parent = jnp.where(seg == 0, -1, jnp.where(seg <= 4, 0, (seg - 3) >> 1))
        shift = jnp.where(seg == 0, 0, jnp.where(seg <= 4, seg - 1, seg - 2))
        return seg, parent, token - shift * seg_len

    key_seg, _, key_place = info(lax.broadcasted_iota(jnp.int32, (16, length), 1))

    def rows_of(i, _):
        at = pl.multiple_of(i * 16, 16)
        seg, parent, place = info(lax.broadcasted_iota(jnp.int32, (16, length), 0) + at)
        allowed = (key_seg == 0) | (key_seg == seg) | (key_seg == parent)
        relative = key_place - place
        magnitude = jnp.abs(relative)
        marked = sum(((magnitude >= mark).astype(jnp.int32) for mark in marks))
        bucket = jnp.where(relative > 0, 16, 0) + jnp.where(magnitude < 8, magnitude, 7 + marked)
        looked = [jnp.full(bucket.shape, table[0, h], wide) for h in range(heads)]
        for b in range(1, table.shape[0]):
            hit = bucket == b
            looked = [jnp.where(hit, table[b, h], looked[h]) for h in range(heads)]
        for h in range(heads):
            out[h, pl.ds(at, 16), :] = jnp.where(allowed, looked[h], masked_score)
        return 0

    lax.fori_loop(0, length // 16, rows_of, 0)


def norm_one(n_ctx, n_shard, idx, x_in, *refs):
    s, half = idx[0], idx[2]
    mine, rest = refs[: n_ctx - 1], refs[n_ctx - 1]
    bufs = refs[n_ctx : n_ctx + n_shard]
    normed, x_mine, x_own, gains = refs[n_ctx + n_shard :]
    r = normed.shape[2]
    _, rows, width = x_in.shape
    for k, buf in enumerate(bufs):
        at = buf.shape[0] - 16
        gains[wrap(s - k, n_shard), 0:2, :] = buf[at : at + 2, 0:r].astype(wide)
    for m in range(2):
        for k in range(n_ctx):
            if k == 0:
                x = x_in[half if m == 0 else 1 - half]
            else:
                x = mine[k - 1][...] if m == 0 else rest[k - 1]
            x = x.astype(wide)
            y = x * lax.rsqrt(jnp.mean(x * x, axis=-1, keepdims=True) + norm_eps)
            at = (m * n_ctx + k) * rows
            for j in range(n_shard):
                piece = slice(r * j, r * (j + 1))
                normed[j, at : at + rows, :] = (y[:, piece] * gains[j, 0:1, :]).astype(low)
                if m == 0:
                    x_mine[j, at : at + rows, :] = x[:, piece].astype(low)
                    if k == 0:
                        x_own[j] = x[:, piece]


def chunk_cot(n_ctx, n_shard, idx, x_in, *refs):
    half = idx[2]
    mine, rest = refs[: n_ctx - 1], refs[n_ctx - 1]
    out, own = refs[n_ctx:]
    r = out.shape[2]
    _, rows, _ = x_in.shape
    for m in range(2):
        for k in range(n_ctx):
            if k == 0:
                x = x_in[half if m == 0 else 1 - half]
            else:
                x = mine[k - 1][...] if m == 0 else rest[k - 1]
            at = (m * n_ctx + k) * rows
            for j in range(n_shard):
                out[j, at : at + rows, :] = x[:, r * j : r * (j + 1)]
                if m == 0 and k == 0:
                    own[j] = x[:, r * j : r * (j + 1)]


def attend(n_ctx, n_shard, rows, heads, place, idx, normed, w_q, w_k, w_v, w_o, bias, *refs):
    s, c = idx[0], idx[1]
    groups = 1 + max((g for pieces in place.values() for g, _, _ in pieces))
    got = [refs[g * n_ctx : (g + 1) * n_ctx] for g in range(groups)]
    att_mine, att_other, soft, qkv, mixed_own, every, mixed = refs[groups * n_ctx :]
    inner, r = w_o.shape
    length = n_ctx * rows
    for i, ref in enumerate((w_q, w_k, w_v, w_o)):
        every[s, i * inner : (i + 1) * inner, :] = ref[...]
    for v in range(n_ctx):

        @pl.when(c == v)
        def _(v=v):
            for k in range(n_ctx):
                for z, pieces in place.items():
                    at, last = (v ^ k) * inner, ((v ^ k) + 1) * inner
                    for g, row, size in pieces:
                        size = min(size, last - at)
                        every[wrap(s - z, n_shard), at : at + size, :] = got[g][k][
                            row : row + size, 0:r
                        ]
                        at += size

    for m in range(2):
        low_row = m * length
        acc = dot_nt(normed[0, low_row : low_row + length, :], every[0, 0 : 3 * inner, :])
        for j in range(1, n_shard):
            acc += dot_nt(normed[j, low_row : low_row + length, :], every[j, 0 : 3 * inner, :])
        qkv[low_row : low_row + length, :] = acc.astype(low)
        for h in range(heads):
            at = DK * h
            keys = qkv[low_row : low_row + length, inner + at : inner + at + DK]
            values = qkv[low_row : low_row + length, 2 * inner + at : 2 * inner + at + DK]
            for b in range(n_ctx):
                top = low_row + b * rows
                scores = dot_nt(qkv[top : top + rows, at : at + DK], keys)
                scores += bias[h, b * rows : (b + 1) * rows, :]
                raised = jnp.exp(scores - jnp.max(scores, axis=-1, keepdims=True))
                share = raised / jnp.sum(raised, axis=-1, keepdims=True)
                if b == 0:
                    soft[m, h] = share
                got = dot_nn(share.astype(low), values).astype(low)
                mixed[top : top + rows, at : at + DK] = got
                if b == 0:
                    mixed_own[m * rows : (m + 1) * rows, at : at + DK] = got
        out = att_mine if m == 0 else att_other
        for j in range(n_shard):
            out[j] = dot_nn(
                mixed[low_row : low_row + length, :], every[j, 3 * inner : 4 * inner, :]
            ).astype(low)


def middle_norm(n_ctx, n_shard, width, x_mine, att, got, gains, normed, middle_own):
    length = x_mine.shape[1]
    rows = length // n_ctx
    for b in range(n_ctx):
        at = slice(b * rows, (b + 1) * rows)
        mids, total = [], 0.0
        for j in range(n_shard):
            mid = x_mine[j, at, :].astype(wide) + (
                att[j, at, :].astype(wide) + got[j, at, :].astype(wide)
            )
            total += jnp.sum(mid * mid, axis=-1, keepdims=True)
            mids.append(mid)
        scale = lax.rsqrt(total / width + norm_eps)
        for j in range(n_shard):
            normed[j, at, :] = (mids[j] * scale * gains[j, 1:2, :]).astype(low)
            if b == 0:
                middle_own[j] = mids[j]


def feed_forward(n_ctx, n_shard, widths, idx, nt_mine, nt_other, cot, buf, *refs):
    sent, feed, two = refs[0], refs[1:3], refs[3:5]
    n_parts = len(widths)
    weights, hidden, pair = (refs[5 + i * n_parts : 5 + (i + 1) * n_parts] for i in range(3))
    _, length, r = nt_mine.shape
    rows = length // n_ctx
    parts, _ = wide_tiles(r, widths)
    for j in range(n_shard):
        for e, pieces in enumerate(parts):
            for row, size, top, lane, lanes, at in pieces:
                weights[e][j, top : top + size, lane : lane + lanes] = buf[
                    j, row : row + size, at : at + lanes
                ]
    w_in = [[weights[e].at[j, :, 0 : 2 * n] for j in range(n_shard)] for e, n in enumerate(widths)]
    w_down = [
        [weights[e].at[j, :, 2 * n : 3 * n] for j in range(n_shard)] for e, n in enumerate(widths)
    ]
    c0, c1 = 0.7978845608028654, 0.044715
    span = 2 * rows
    for m, nt in ((0, nt_mine), (1, nt_other)):

        def block(b, _, m=m, nt=nt):
            at = pl.ds(pl.multiple_of(b * span, span), span)
            all_at = pl.ds(pl.multiple_of(m * length + b * span, span), span)
            for e, n in enumerate(widths):
                both, back = 0.0, 0.0
                for j in range(n_shard):
                    both += dot_nn(nt[j, at, :], w_in[e][j][...])
                    back += dot_nn(cot[j, all_at, :], w_down[e][j][...])
                gate, up = both[:, :n], both[:, n:]
                square = gate * gate
                bent = jnp.tanh(c0 * (gate + c1 * gate * square))
                half_one = 0.5 * (1.0 + bent)
                active = gate * half_one
                slope = half_one + 0.5 * gate * (1.0 - bent * bent) * (
                    c0 * (1.0 + 3.0 * c1 * square)
                )
                hidden[e][all_at, :] = (active * up).astype(low)
                pair[e][all_at, 0:n] = (back * up * slope).astype(low)
                pair[e][all_at, n : 2 * n] = (back * active).astype(low)
            for j in range(n_shard):
                made, back_in = 0.0, 0.0
                for e in range(n_parts):
                    made += dot_nt(hidden[e][all_at, :], w_down[e][j][...])
                    back_in += dot_nt(pair[e][all_at, :], w_in[e][j][...])
                for i in range(2):
                    piece = slice(i * rows, (i + 1) * rows)
                    feed[m][2 * b + i, j] = made[piece].astype(low)
                    two[m][2 * b + i, j] = back_in[piece].astype(low)
            return 0

        lax.fori_loop(0, n_ctx // 2, block, 0)
    for j in range(n_shard):
        for e, n in enumerate(widths):
            for_in = dot_tn(nt_mine[j], pair[e][0:length, :])
            for_in += dot_tn(nt_other[j], pair[e][length:, :])
            for_in = for_in.astype(low)
            for_down = dot_tn(cot[j], hidden[e][...]).astype(low)
            for row, size, top, lane, lanes, at in parts[e]:
                inside = max(0, min(lanes, 2 * n - lane))
                if inside:
                    sent[j, row : row + size, at : at + inside] = for_in[
                        top : top + size, lane : lane + inside
                    ]
                if inside < lanes:
                    begin = lane + inside - 2 * n
                    sent[j, row : row + size, at + inside : at + lanes] = for_down[
                        top : top + size, begin : begin + lanes - inside
                    ]


def norm_two_back(n_shard, width, n_parts, *refs):
    parts, refs = refs[:n_parts], refs[n_parts:]
    middle, cot, gains, out_in, grad, gain_grad = refs
    mids = [middle[j] for j in range(n_shard)]
    twos = [sum((p[j].astype(wide) for p in parts)) for j in range(n_shard)]
    mean = sum((jnp.sum(a * a, axis=-1, keepdims=True) for a in mids)) / width
    scale = lax.rsqrt(mean + norm_eps)
    us = [twos[j] * gains[j, 1:2, :] for j in range(n_shard)]
    inner = sum((jnp.sum(a * b, axis=-1, keepdims=True) for a, b in zip(us, mids, strict=True)))
    inner = inner / width * (scale * scale * scale)
    for j in range(n_shard):
        back = cot[j].astype(wide) + scale * us[j] - mids[j] * inner
        grad[j] = back
        out_in[j] = back.astype(low)
        gain_grad[j] = jnp.sum(twos[j] * mids[j] * scale, axis=0, keepdims=True)


def attend_back(n_ctx, n_shard, heads, idx, o_mine, o_other, soft, qkv, mixed, every, normed, *refs):
    s, c = idx[0], idx[1]
    kv, (q_grad, stack, kv_all, mixed_grad) = refs[:n_ctx], refs[n_ctx:]
    _, rows, r = o_mine.shape
    length = n_ctx * rows
    inner = heads * DK
    for m, o_in in ((0, o_mine), (1, o_other)):
        top, own = m * length, m * rows
        acc = 0.0
        for j in range(n_shard):
            acc += dot_nt(o_in[j], every[j, 3 * inner : 4 * inner, :])
        mixed_grad[own : own + rows, :] = acc.astype(low)
        for h in range(heads):
            at = DK * h
            share = soft[m, h]
            grad = mixed_grad[own : own + rows, at : at + DK]
            keys = qkv[top : top + length, inner + at : inner + at + DK]
            values = qkv[top : top + length, 2 * inner + at : 2 * inner + at + DK]
            queries = qkv[top : top + rows, at : at + DK]
            weight = dot_nt(grad, values)
            ds = share * (weight - jnp.sum(weight * share, axis=-1, keepdims=True))
            ds = ds.astype(low)
            q_grad[own : own + rows, at : at + DK] = dot_nn(ds, keys).astype(low)
            kv_all[top : top + length, at : at + DK] = dot_tn(ds, queries).astype(low)
            kv_all[top : top + length, inner + at : inner + at + DK] = dot_tn(
                share.astype(low), grad
            ).astype(low)
        for k in range(n_ctx):
            kv[k][own : own + rows, :] = kv_all[top + k * rows : top + (k + 1) * rows, :]
    for p in range(n_shard):
        j = wrap(s + p, n_shard)
        for_q = dot_tn(q_grad[0:rows, :], normed[j, 0:rows, :])
        for_q += dot_tn(q_grad[rows:, :], normed[j, length : length + rows, :])
        for_kv = dot_tn(kv_all[...], normed[j])
        for_o = dot_tn(mixed[0:rows, :], o_mine[j]) + dot_tn(mixed[rows:, :], o_other[j])
        stack[c, p] = for_q.astype(low)
        stack[c ^ 1, p] = for_kv[0:inner].astype(low)
        stack[c ^ 2, p] = for_kv[inner:].astype(low)
        stack[c ^ 3, p] = for_o.astype(low)


def first_grad(n_shard, n_parts, *refs):
    parts, (q_grad, every, out_mine, out_other, three) = refs[:n_parts], refs[n_parts:]
    rows2, inner = q_grad.shape
    rows = rows2 // 2
    three[:, 0:inner] = q_grad[...]
    three[:, inner:] = sum((p[...].astype(wide) for p in parts)).astype(low)
    for j in range(n_shard):
        got = dot_nn(three[...], every[j, 0 : 3 * inner, :]).astype(low)
        out_mine[j] = got[0:rows]
        out_other[j] = got[rows:]


def norm_one_back(n_shard, width, mine, got, x_own, grad, gains, out, gain_grad):
    r = x_own.shape[2]
    xs = [x_own[j] for j in range(n_shard)]
    ones = [mine[j].astype(wide) + got[j].astype(wide) for j in range(n_shard)]
    mean = sum((jnp.sum(a * a, axis=-1, keepdims=True) for a in xs)) / width
    scale = lax.rsqrt(mean + norm_eps)
    us = [ones[j] * gains[j, 0:1, :] for j in range(n_shard)]
    inner = sum((jnp.sum(a * b, axis=-1, keepdims=True) for a, b in zip(us, xs, strict=True)))
    inner = inner / width * (scale * scale * scale)
    for j in range(n_shard):
        back = grad[j] + scale * us[j] - xs[j] * inner
        out[:, r * j : r * (j + 1)] = back.astype(low)
        gain_grad[j] = jnp.sum(ones[j] * xs[j] * scale, axis=0, keepdims=True)


def produce(n_shard, n_parts, *refs):
    parts, (middle, out) = refs[:n_parts], refs[n_parts:]
    r = middle.shape[2]
    for j in range(n_shard):
        fed = sum((p[j].astype(wide) for p in parts))
        out[:, r * j : r * (j + 1)] = (middle[j] + fed).astype(low)


def finish_wide(n_ctx, widths, idx, own, *refs):
    n_got = len(refs) - 4
    got, (out_g, out_u, out_d, stage) = refs[:n_got], refs[n_got:]
    r = out_g.shape[0]
    columns = sum(widths)
    parts, rows = wide_tiles(r, widths)
    sources = [[own], [got[0]], [got[1]], list(got[2:])] if n_ctx == 4 else [[own]] + [[g] for g in got]
    for k, source in enumerate(sources):
        size_each = rows // len(source)
        for i, n in enumerate(widths):
            for row, size, top, lane, lanes, at in parts[i]:
                done = 0
                while done < size:
                    which, here = divmod(row + done, size_each)
                    count = min(size - done, size_each - here)
                    stage[top + done : top + done + count, lane : lane + lanes] = source[which][
                        here : here + count, at : at + lanes
                    ].astype(wide)
                    done += count
            for v in range(n_ctx):

                @pl.when(idx[1] == v)
                def _(v=v, n=n, i=i, k=k):
                    at = (v ^ k) * columns + sum(widths[:i])
                    for j, out in enumerate((out_g, out_u, out_d)):
                        out[:, at : at + n] = stage[:, j * n : (j + 1) * n]


def finish_attention(n_ctx, idx, *refs):
    pieces, outs = refs[:n_ctx], refs[n_ctx:]
    for v in range(n_ctx):

        @pl.when(idx[1] == v)
        def _(v=v):
            for k in range(n_ctx):
                outs[v ^ k][...] = pieces[k][...].astype(wide)


def on_device(
    inputs,
    cotangent,
    norm1_gain,
    w_query,
    w_key,
    w_value,
    w_out,
    norm2_gain,
    w_gate,
    w_up,
    w_down,
    bias_table,
):
    _, rows, width = inputs.shape
    shards, ctx = lax.axis_size("shard"), lax.axis_size("ctx")
    inner, r = w_out.shape
    heads = inner // DK
    length = ctx * rows
    columns = w_gate.shape[1] // ctx
    first_width = pl.cdiv(columns, 2 * LANES) * LANES
    widths = (first_width, columns - first_width)
    lanes_r = pl.cdiv(r, LANES) * LANES
    s, c, half = lax.axis_index("shard"), lax.axis_index("ctx"), lax.axis_index("tensor")
    idx = jnp.stack([s, c, half]).astype(jnp.int32)
    attention_weights = (w_query.T, w_key.T, w_value.T, w_out)


    wide_rows = wide_tiles(r, widths)[1]
    window = min(pl.cdiv(columns, LANES) * LANES, w_gate.shape[1])
    (packed,) = run(
        functools.partial(pack_wide, ctx, widths, window),
        "pack_wide",
        [((wide_rows, LANES), low)],
        [idx, w_gate, w_up, w_down.T],
        scratch=[
            pltpu.VMEM((r, 3 * max(widths)), low),
            pltpu.VMEM((3, r, window), low),
            pltpu.SemaphoreType.DMA((3,)),
        ],
        cost=2,
        far=3,
    )
    chunks = lax.all_gather(packed, "shard", axis=0, tiled=False)
    own_x = lax.dynamic_index_in_dim(inputs, half, 0, keepdims=False)
    (own_buf,) = run(
        functools.partial(pack_attention, ctx),
        "pack_attention",
        [((inner + 16, lanes_r), low)],
        [after(idx, packed), *attention_weights, jnp.stack([norm1_gain, norm2_gain])],
        scratch=[pltpu.VMEM((inner, r), low), pltpu.SemaphoreType.DMA],
        far=4,
    )
    from_shard = [step(own_buf, "shard", k) for k in range(1, shards)]
    mine_x = [swap(own_x, "ctx", k) for k in range(1, ctx)]
    table = lax.dynamic_slice_in_dim(bias_table, half * heads, heads, 1)
    (bias,) = run(
        functools.partial(bias_body, rows, rows // 5, distance_marks),
        "bias",
        [((heads, length, length), wide)],
        [after(idx, own_buf), table],
        scalars=2,
        cost=5,
    )
    now = after(idx, *from_shard, *mine_x, bias)

    group = jnp.concatenate(from_shard)
    buf_rows = inner + 16
    place = {z: [(0, (z - 1) * buf_rows, inner)] for z in range(1, shards)}
    gathered = [group] + [swap(after(group, now), "ctx", k) for k in range(1, ctx)]
    rest_x = swap(after(jnp.stack(mine_x), now), "tensor")
    normed_one, x_mine, x_own, gains = run(
        functools.partial(norm_one, ctx, shards),
        "norm_one",
        [
            ((shards, 2 * length, r), low),
            ((shards, length, r), low),
            ((shards, rows, r), wide),
            ((shards, 2, r), wide),
        ],
        [now, inputs, *mine_x, rest_x, own_buf, *from_shard],
        cost=3,
    )
    now = after(now, *gathered[1:], normed_one)

    own_cot = lax.dynamic_index_in_dim(cotangent, half, 0, keepdims=False)
    mine_cot = [swap(after(own_cot, now), "ctx", k) for k in range(1, ctx)]
    att_mine, att_other, soft, qkv, mixed_own, every = run(
        functools.partial(attend, ctx, shards, rows, heads, place),
        "attend",
        [
            ((shards, length, r), low),
            ((shards, length, r), low),
            ((2, heads, rows, length), wide),
            ((2 * length, 3 * inner), low),
            ((2 * rows, inner), low),
            ((shards, 4 * inner, r), low),
        ],
        [now, normed_one, *attention_weights, bias, *gathered],
        scratch=[pltpu.VMEM((2 * length, inner), low)],
        cost=14,
    )
    now = after(now, *mine_cot, att_other)

    att_got = swap(after(att_other, now), "tensor")
    rest_cot = swap(after(jnp.stack(mine_cot), now), "tensor")
    nt_mine, middle_own = run(
        functools.partial(middle_norm, ctx, shards, width),
        "middle_norm",
        [((shards, length, r), low), ((shards, rows, r), wide)],
        [x_mine, att_mine, att_got, gains],
        scalars=0,
    )
    nt_other = swap(nt_mine, "tensor")
    cot, cot_own = run(
        functools.partial(chunk_cot, ctx, shards),
        "chunk_cot",
        [((shards, 2 * length, r), low), ((shards, rows, r), low)],
        [now, cotangent, *mine_cot, rest_cot],
        cost=1,
    )
    now = after(now, nt_other, cot)

    def add(a, b):
        return (a.astype(wide) + b.astype(wide)).astype(low)

    tokens_out = ((ctx, shards, rows, r), low)
    wide_grads, feed_mine, feed_other, two_mine, two_other = run(
        functools.partial(feed_forward, ctx, shards, widths),
        "feed_forward",
        [((shards, wide_rows, LANES), low)] + [tokens_out] * 4,
        [now, nt_mine, nt_other, cot, chunks],
        scratch=[pltpu.VMEM((shards, r, 3 * n), low) for n in widths]
        + [pltpu.VMEM((2 * length, n), low) for n in widths]
        + [pltpu.VMEM((2 * length, 2 * n), low) for n in widths],
        cost=20,
        vmem=48,
    )
    wide_own = lax.psum_scatter(wide_grads, "shard", scatter_dimension=0, tiled=False)
    now = after(now, two_other)

    two_got = swap(after(two_other, now), "tensor")
    two_both = [add(two_mine[k], two_got[k]) for k in range(ctx)]
    feed_got = swap(after(feed_other, two_got), "tensor")
    feed_both = [add(feed_mine[k], feed_got[k]) for k in range(ctx)]
    now = after(now, *two_both, *feed_both)

    two_parts = [two_both[0]] + [swap(after(two_both[k], now), "ctx", k) for k in range(1, ctx)]
    out_in, middle_grad, gain_two = run(
        functools.partial(norm_two_back, shards, width, ctx),
        "norm_two_back",
        [((shards, rows, r), low), ((shards, rows, r), wide), ((shards, 1, r), wide)],
        [*two_parts, middle_own, cot_own, gains],
        scalars=0,
    )
    out_in_other = swap(out_in, "tensor")
    now = after(now, out_in_other)

    feed_parts = [feed_both[0]] + [swap(after(feed_both[k], now), "ctx", k) for k in range(1, ctx)]
    got = run(
        functools.partial(attend_back, ctx, shards, heads),
        "attend_back",
        [((2 * rows, 2 * inner), low)] * ctx
        + [((2 * rows, inner), low), ((4, shards, inner, r), low)],
        [now, out_in, out_in_other, soft, qkv, mixed_own, every, normed_one],
        scratch=[pltpu.VMEM((2 * length, 2 * inner), low), pltpu.VMEM((2 * rows, inner), low)],
        cost=6,
    )
    kv_parts, q_grad, stack = got[:ctx], got[ctx], got[ctx + 1]
    now = after(now, *feed_parts[1:], q_grad)

    kv_parts = [kv_parts[0]] + [swap(after(kv_parts[k], now), "ctx", k) for k in range(1, ctx)]
    four_got = [swap(after(stack[k], now), "ctx", k) for k in range(1, 3)]
    (produced_mine,) = run(
        functools.partial(produce, shards, ctx),
        "produce",
        [((rows, width), low)],
        [*feed_parts, middle_own],
        scalars=0,
    )
    produced_other = swap(after(produced_mine, now), "tensor")
    now = after(now, *kv_parts, *four_got, produced_other)

    four_got += [swap(after(stack[k], now), "ctx", k) for k in range(3, ctx)]
    first_mine, first_other = run(
        functools.partial(first_grad, shards, ctx),
        "first_grad",
        [((shards, rows, r), low)] * 2,
        [*kv_parts, q_grad, every],
        scalars=0,
        scratch=[pltpu.VMEM((2 * rows, 3 * inner), low)],
    )
    first_got = swap(after(first_other, now), "tensor")
    input_mine, gain_one = run(
        functools.partial(norm_one_back, shards, width),
        "norm_one_back",
        [((rows, width), low), ((shards, 1, r), wide)],
        [first_mine, first_got, x_own, middle_grad, gains],
        scalars=0,
    )
    input_other = swap(input_mine, "tensor")
    gain = jnp.concatenate([gain_one, gain_two], 1)
    gain = gain + swap(gain, "tensor")
    now = after(now, *four_got, input_other, gain)

    four = stack[0].astype(wide)
    for got in four_got:
        four = four + got.astype(wide)
    four = four.astype(low)
    four_shard = [four[0]] + [step(after(four[d], now), "shard", d) for d in range(1, shards)]
    gain_got = [swap(after(gain, now), "ctx", k) for k in range(1, ctx)]
    now = after(now, *four_shard, *gain_got)

    four_own = sum((part.astype(wide) for part in four_shard)).astype(low)
    four_all = [four_own] + [swap(after(four_own, now), "ctx", k) for k in range(1, ctx)]
    gain = gain + sum(gain_got)
    own_gain = lax.dynamic_index_in_dim(gain, s, 0, keepdims=False)
    for k in range(1, shards):
        part = lax.dynamic_index_in_dim(gain, wrap(s + k, shards), 0, keepdims=False)
        own_gain = own_gain + step(after(part, now), "shard", k)
    out_q, out_k, out_v, out_o = run(
        functools.partial(finish_attention, ctx),
        "finish_attention",
        [((inner, r), wide)] * 4,
        [now, *four_all],
    )
    now = after(now, out_q, own_gain)

    wide_own = after(wide_own, now)
    wide_all = gather_ctx(wide_own)
    out_g, out_u, out_d = run(
        functools.partial(finish_wide, ctx, widths),
        "finish_wide",
        [(w_gate.shape, wide)] * 3,
        [now, wide_own, *wide_all],
        scratch=[pltpu.VMEM((r, 3 * max(widths)), wide)],
        cost=5,
    )

    def ordered(mine, other):
        return jnp.where(half == 0, jnp.stack([mine, other]), jnp.stack([other, mine]))

    return (
        ordered(produced_mine, produced_other),
        ordered(input_mine, input_other),
        own_gain[0],
        out_q.T,
        out_k.T,
        out_v.T,
        out_o,
        own_gain[1],
        out_g,
        out_u,
        out_d.T,
    )


def solution(mesh):
    placed = (
        P(None, ("shard", "ctx"), None),
        P(None, ("shard", "ctx"), None),
        P("shard"),
        P("shard", "tensor"),
        P("shard", "tensor"),
        P("shard", "tensor"),
        P("tensor", "shard"),
        P("shard"),
        P("shard", "tensor"),
        P("shard", "tensor"),
        P("tensor", "shard"),
        P(),
    )
    return jax.shard_map(
        on_device, mesh=mesh, in_specs=placed, out_specs=placed[:2] + placed[2:11], check_vma=False
    )
```

time: 369 us -> 293 us (0.79)
  waiting for transfers between devices: 197 us -> 130 us
  local copies, waits for them, and re-layouts: 32 us -> 16.3 us
  between operations: 1.57 us -> 15.1 us
  starting transfers between devices: 65.2 us -> 55.1 us
    ppermute x21 -> x9, waiting for transfers between devices: 116 us -> 18 us  [step(): return lax.ppermute(x, axis, [(i, (i + k) % n) for i in range(n)])]
    ppermute x47 -> x42, waiting for transfers between devices: 81.5 us -> 104 us  [swap(): return lax.ppermute(x, axis, [(i, i ^ k) for i in range(n)])]
    unnamed x95 -> x81, local copies, waits for them, and re-layouts: 28.7 us -> 14.3 us
    all_gather x0 -> x1, waiting for transfers between devices: none -> 8.74 us  [on_device(): chunks = lax.all_gather(packed, 'shard', axis=0, tiled=False)]
    ppermute x47 -> x42, starting transfers between devices: 46.7 us -> 40.3 us  [swap(): return lax.ppermute(x, axis, [(i, i ^ k) for i in range(n)])]
    ppermute x21 -> x9, starting transfers between devices: 18.5 us -> 14.8 us  [step(): return lax.ppermute(x, axis, [(i, (i + k) % n) for i in range(n)])]
    pallas_call x16 -> x15, Pallas kernels: 62.2 us -> 63.9 us  [run(): pl.pallas_call(body, name=name, out_shape=[jax.ShapeDtypeStruct(s, d) for...]
  transfers between devices with their start and end apart: 68 -> 53, of which waited for: 28 -> 25; matrix products, arithmetic and copies ran while one was open for 4% -> 3% of each run, Pallas kernels for 10% -> 11%
where the time goes in v3:
time: 293 us; the launch traced here: 288 us
  waiting for transfers between devices  130 us (44%)
  Pallas kernels  63.9 us (22%)
  starting transfers between devices  55.1 us (19%)
  local copies, waits for them, and re-layouts  16.3 us (6%)
  between operations  15.1 us (5%)
  other arithmetic  6.82 us (2%)
    ppermute x42, waiting for transfers between devices, swap(): return lax.ppermute(x, axis, [(i, i ^ k) for i in range(n)])  104 us
    pallas_call x15, Pallas kernels, run(): pl.pallas_call(body, name=name, out_shape=[jax.ShapeDtypeStruct(s, d) for...  63.9 us
    ppermute x42, starting transfers between devices, swap(): return lax.ppermute(x, axis, [(i, i ^ k) for i in range(n)])  40.3 us
    ppermute x9, waiting for transfers between devices, step(): return lax.ppermute(x, axis, [(i, (i + k) % n) for i in range(n)])  18 us
    ppermute x9, starting transfers between devices, step(): return lax.ppermute(x, axis, [(i, (i + k) % n) for i in range(n)])  14.8 us
    unnamed x81, local copies, waits for them, and re-layouts  14.3 us
    all_gather x1, waiting for transfers between devices, on_device(): chunks = lax.all_gather(packed, 'shard', axis=0, tiled=False)  8.74 us
  transfers between devices with their start and end apart: 53, of which 25 were waited for; matrix products, arithmetic and copies ran while one was open for 3% of the time, Pallas kernels for 11%

profile of v3, /device:TPU:0, one launch (start us, length us, event | category | flops | bytes accessed | tf_op | source)
XLA Modules:
  0.0 287.6 jit_solution(7509319334511993283)
XLA Ops:
  11.3 1.9 pack_wide.1
  14.2 3.1 %collective-permute-start = (bf16[208,384]{1,0:T(8,128)(2,1)S(1)}, bf16[208,384]{1,0:T(8,128)(2,1)S(1)}, u32[]{:S(2)}, u32[]{:S(2)}) collective-permute-start(bf16[208,384]{1,0:T(8,128)(2,1)S(1)} %pack_attention.1.refs_4_), channel_id=1, source_target_pairs={{0,8},{8,16},{16,24},{24,0},{1,9},{9,17},{17,25},{25,1},{2,10},{10... | collective-permute-start | bytes 479240 | tf_op jit(solution)/shard_map/ppermute | solution.py:53
  17.3 2.0 collective-permute-start.3
  19.3 1.5 collective-permute-start.4
  20.8 2.6 collective-permute-start.1
  23.4 1.7 collective-permute-start.2
  25.2 5.3 %bias.1 = f32[3,320,320]{2,1,0:T(8,128)S(1)} custom-call(s32[3]{0:T(128)S(1)} %pad_add_fusion.idx, f32[32,3]{1,0:T(8,128)S(1)} %copy.24.table), custom_call_target="tpu_custom_call" | custom-call | flops 500000000 | tf_op jit(solution)/shard_map/bias/pallas_call | solution.py:37
  30.5 5.2 %collective-permute-done.1.refs_6_ = bf16[208,384]{1,0:T(8,128)(2,1)S(1)} collective-permute-done((bf16[208,384]{1,0:T(8,128)(2,1)S(1)}, bf16[208,384]{1,0:T(8,128)(2,1)S(1)}, u32[]{:S(2)}, u32[]{:S(2)}) %collective-permute-start.1) | collective-permute-done | bytes 159776 | tf_op jit(solution)/shard_map/ppermute | solution.py:53
  36.9 2.1 collective-permute-start.6
  39.0 1.6 collective-permute-start.7
  40.6 3.3 %norm_one.1 = (bf16[4,640,368]{2,1,0:T(8,128)(2,1)S(1)}, bf16[4,320,368]{2,1,0:T(8,128)(2,1)S(1)}, f32[4,80,368]{2,1,0:T(8,128)S(1)}, f32[4,2,368]{2,1,0:T(2,128)S(1)}) custom-call(s32[3]{0:T(128)S(1)} %pad_add_fusion.idx, bf16[2,80,1472]{2,1,0:T(8,128)(2,1)S(1)} %copy-done.9, bf16[80,1472]{1,0:T(8,128)(2,1)S(1)} %collective-permute-done.3.refs_0_, ...), custom_call_target="tpu_custom_call" | custom-call | flops 300000000 | tf_op jit(solution)/shard_map/norm_one/pallas_call | solution.py:37
  44.7 6.2 %collective-permute-done.6.refs_1_ = bf16[624,384]{1,0:T(8,128)(2,1)S(1)} collective-permute-done((bf16[624,384]{1,0:T(8,128)(2,1)S(1)}, bf16[624,384]{1,0:T(8,128)(2,1)S(1)}, u32[]{:S(2)}, u32[]{:S(2)}) %collective-permute-start.6) | collective-permute-done | bytes 479264 | tf_op jit(solution)/shard_map/ppermute | solution.py:58
  50.8 11.5 %collective-permute-done.7.refs_2_ = bf16[624,384]{1,0:T(8,128)(2,1)S(1)} collective-permute-done((bf16[624,384]{1,0:T(8,128)(2,1)S(1)}, bf16[624,384]{1,0:T(8,128)(2,1)S(1)}, u32[]{:S(2)}, u32[]{:S(2)}) %collective-permute-start.7) | collective-permute-done | bytes 479264 | tf_op jit(solution)/shard_map/ppermute | solution.py:58
  64.3 1.6 collective-permute-start.12
  65.9 12.3 %attend.1 = (bf16[4,320,368]{2,1,0:T(8,128)(2,1)S(1)}, bf16[4,320,368]{2,1,0:T(8,128)(2,1)S(1)}, f32[2,3,80,320]{3,2,1,0:T(8,128)S(1)}, bf16[640,576]{1,0:T(8,12...) custom-call(s32[3]{0:T(128)S(1)} %pad_add_fusion.idx, ...), custom_call_target="tpu_custom_call" | custom-call | flops 1400000000 | tf_op jit(solution)/shard_map/attend/pallas_call | solution.py:37
  78.9 2.6 collective-permute-done.13.got
  82.9 2.9 %collective-permute-done.15.refs_3_ = bf16[3,80,1472]{2,1,0:T(8,128)(2,1)S(1)} collective-permute-done((bf16[3,80,1472]{2,1,0:T(8,128)(2,1)S(1)}, bf16[3,80,1472]{2,1,0:T(8,128)(2,1)S(1)}, u32[]{:S(2)}, u32[]{:S(2)}) %collective-permute-start.15) | collective-permute-done | bytes 706592 | tf_op jit(solution)/shard_map/ppermute | solution.py:58
  89.3 8.7 %all-gather.3.cloned.1.call-done = bf16[15488,128]{1,0:T(8,128)(2,1)} async-done(((bf16[3872,128]{1,0:T(8,128)(2,1)}), bf16[15488,128]{1,0:T(8,128)(2,1)}) %all-gather.3.cloned.1.call-update) | async-done | bytes 3964944 | tf_op jit(solution)/shard_map/all_gather | solution.py:533
  100.5 22.8 %feed_forward.1 = (bf16[4,3872,128]{2,1,0:T(8,128)(2,1)}, bf16[4,4,80,368]{3,2,1,0:T(8,128)(2,1)S(1)}, bf16[4,4,80,368]{3,2,1,0:T(8,128)(2,1)S(1)}, bf16[4,4,80,...) custom-call(s32[3]{0:T(128)S(1)} %pad_add_fusion.idx, bf16[4,320,368]{2,1,0:T(8,128)(2,1)S(1)} %copy-done.15, ...), custom_call_target="tpu_custom_call" | custom-call | flops 2000000000 | tf_op jit(solution)/shard_map/feed_forward/pallas_call | solution.py:37
  127.3 2.7 collective-permute-done.16
  130.2 1.6 fusion.8
  133.1 2.9 %collective-permute-start.20 = (bf16[4,80,368]{2,1,0:T(8,128)(2,1)S(1)}, bf16[4,80,368]{2,1,0:T(8,128)(2,1)S(1)}, u32[]{:S(2)}, u32[]{:S(2)}) collective-permute-start(bf16[4,80,368]{2,1,0:T(8,128)(2,1)S(1)} %get-tuple-element.122), channel_id=1, source_target_pairs={{0,6},{2,4},{4,2},{6,0},{1,7},{3,5},{5,3},{7,1},{8,14},{10,12},{12... | collective-permute-start | bytes 706568 | tf_op jit(solution)/shard_map/ppermute | solution.py:58
  136.7 6.2 %collective-permute-done.20.refs_3_ = bf16[4,80,368]{2,1,0:T(8,128)(2,1)S(1)} collective-permute-done((bf16[4,80,368]{2,1,0:T(8,128)(2,1)S(1)}, bf16[4,80,368]{2,1,0:T(8,128)(2,1)S(1)}, u32[]{:S(2)}, u32[]{:S(2)}) %collective-permute-start.20) | collective-permute-done | bytes 235552 | tf_op jit(solution)/shard_map/ppermute | solution.py:58
  142.9 4.7 %collective-permute-done.19.refs_2_ = bf16[4,80,368]{2,1,0:T(8,128)(2,1)S(1)} collective-permute-done((bf16[4,80,368]{2,1,0:T(8,128)(2,1)S(1)}, bf16[4,80,368]{2,1,0:T(8,128)(2,1)S(1)}, u32[]{:S(2)}, u32[]{:S(2)}) %collective-permute-start.19) | collective-permute-done | bytes 235552 | tf_op jit(solution)/shard_map/ppermute | solution.py:58
  148.1 1.4 collective-permute-done.21.o_other
  149.5 1.8 collective-permute-start.24
  151.3 1.4 collective-permute-start.23
  153.0 6.1 %attend_back.1 = (bf16[160,384]{1,0:T(8,128)(2,1)S(1)}, bf16[160,384]{1,0:T(8,128)(2,1)S(1)}, bf16[160,384]{1,0:T(8,128)(2,1)S(1)}, bf16[160,384]{1,0:T(8,128)(2...) custom-call(s32[3]{0:T(128)S(1)} %pad_add_fusion.idx, ...), custom_call_target="tpu_custom_call" | custom-call | flops 600000000 | tf_op jit(solution)/shard_map/attend_back/pallas_call | solution.py:37
  160.3 3.4 %collective-permute-done.23.refs_2_ = bf16[4,80,368]{2,1,0:T(8,128)(2,1)S(1)} collective-permute-done((bf16[4,80,368]{2,1,0:T(8,128)(2,1)S(1)}, bf16[4,80,368]{2,1,0:T(8,128)(2,1)S(1)}, u32[]{:S(2)}, u32[]{:S(2)}) %collective-permute-start.23) | collective-permute-done | bytes 235552 | tf_op jit(solution)/shard_map/ppermute | solution.py:58
  168.8 14.1 %collective-permute-done.28.refs_3_ = bf16[160,384]{1,0:T(8,128)(2,1)S(1)} collective-permute-done((bf16[160,384]{1,0:T(8,128)(2,1)S(1)}, bf16[160,384]{1,0:T(8,128)(2,1)S(1)}, u32[]{:S(2)}, u32[]{:S(2)}) %collective-permute-start.28) | collective-permute-done | bytes 122912 | tf_op jit(solution)/shard_map/ppermute | solution.py:58
  183.0 1.4 collective-permute-start.26
  184.4 3.5 %collective-permute-done.26.refs_1_ = bf16[160,384]{1,0:T(8,128)(2,1)S(1)} collective-permute-done((bf16[160,384]{1,0:T(8,128)(2,1)S(1)}, bf16[160,384]{1,0:T(8,128)(2,1)S(1)}, u32[]{:S(2)}, u32[]{:S(2)}) %collective-permute-start.26) | collective-permute-done | bytes 122912 | tf_op jit(solution)/shard_map/ppermute | solution.py:58
  188.7 1.7 collective-permute-start.34
  192.6 12.9 %collective-permute-done.34 = bf16[4,192,368]{2,1,0:T(8,128)(2,1)S(1)} collective-permute-done((bf16[4,192,368]{2,1,0:T(8,128)(2,1)}, bf16[4,192,368]{2,1,0:T(8,128)(2,1)S(1)}, u32[]{:S(2)}, u32[]{:S(2)}) %collective-permute-start.34) | collective-permute-done | bytes 565280 | tf_op jit(solution)/shard_map/ppermute | solution.py:58
  209.4 1.8 fusion.2
  211.2 2.3 collective-permute-start.40
  214.6 3.2 %collective-permute-done.40 = bf16[192,368]{1,0:T(8,128)(2,1)S(1)} collective-permute-done((bf16[192,368]{1,0:T(8,128)(2,1)S(1)}, bf16[192,368]{1,0:T(8,128)(2,1)S(1)}, u32[]{:S(2)}, u32[]{:S(2)}) %collective-permute-start.40) | collective-permute-done | bytes 141344 | tf_op jit(solution)/shard_map/ppermute | solution.py:53
  217.8 8.7 %collective-permute-done.39 = bf16[192,368]{1,0:T(8,128)(2,1)S(1)} collective-permute-done((bf16[192,368]{1,0:T(8,128)(2,1)S(1)}, bf16[192,368]{1,0:T(8,128)(2,1)S(1)}, u32[]{:S(2)}, u32[]{:S(2)}) %collective-permute-start.39) | collective-permute-done | bytes 141344 | tf_op jit(solution)/shard_map/ppermute | solution.py:53
  227.7 2.9 %collective-permute-start.43 = (f32[2,368]{1,0:T(2,128)S(1)}, f32[2,368]{1,0:T(2,128)S(1)}, u32[]{:S(2)}, u32[]{:S(2)}) collective-permute-start(f32[2,368]{1,0:T(2,128)S(1)} %get-tuple-element.165), channel_id=1, source_target_pairs={{0,24},{8,0},{16,8},{24,16},{1,25},{9,1},{17,9},{25,17},{2,26},{10... | collective-permute-start | bytes 8840 | tf_op jit(solution)/shard_map/ppermute | solution.py:53
  230.7 1.7 collective-permute-start.44
  234.3 3.1 %collective-permute-done.44.refs_1_ = bf16[192,368]{1,0:T(8,128)(2,1)S(1)} collective-permute-done((bf16[192,368]{1,0:T(8,128)(2,1)S(1)}, bf16[192,368]{1,0:T(8,128)(2,1)S(1)}, u32[]{:S(2)}, u32[]{:S(2)}) %collective-permute-start.44) | collective-permute-done | bytes 141344 | tf_op jit(solution)/shard_map/ppermute | solution.py:58
  237.4 2.0 collective-permute-done.45.refs_2_
  239.4 1.7 finish_attention.1
  242.9 19.1 %collective-permute-done.47.refs_0_ = bf16[3872,128]{1,0:T(8,128)(2,1)S(1)} collective-permute-done((bf16[3872,128]{1,0:T(8,128)(2,1)}, bf16[3872,128]{1,0:T(8,128)(2,1)S(1)}, u32[]{:S(2)}, u32[]{:S(2)}) %collective-permute-start.47) | collective-permute-done | bytes 991264 | tf_op jit(solution)/shard_map/ppermute | solution.py:58
  262.0 2.6 collective-permute-start.49
  266.6 1.9 maximum_select_fusion.1
  269.2 4.8 %collective-permute-done.49.refs_2_ = bf16[1936,128]{1,0:T(8,128)(2,1)S(1)} collective-permute-done((bf16[1936,128]{1,0:T(8,128)(2,1)S(1)}, bf16[1936,128]{1,0:T(8,128)(2,1)S(1)}, u32[]{:S(2)}, u32[]{:S(2)}) %collective-permute-start.49) | collective-permute-done | bytes 495648 | tf_op jit(solution)/shard_map/ppermute | solution.py:58
  274.1 6.1 %finish_wide.1 = (f32[368,1792]{1,0:T(8,128)}, f32[368,1792]{1,0:T(8,128)}, f32[368,1792]{1,0:T(8,128)}) custom-call(s32[3]{0:T(128)S(1)} %pad_add_fusion.idx, bf16[3872,128]{1,0:T(8,128)(2,1)S(1)} %bitcast.77, bf16[3872,128]{1,0:T(8,128)(2,1)S(1)} %collective-permute-done.47.refs_0_, bf16[3872,128]{1,0:T(8,128)(2,1)S(1)} %collective-permute-done.48.refs_1_, ...), custom_call_target="tpu_custom_call" | custom-call | flops 500000000 | tf_op jit(solution)/shard_map/finish_wide/pallas_call | solution.py:37
  (182 shorter events, 45.7 us)
Async XLA Ops:
  7.2 90.9 %all-gather.3.cloned.1.call-start = ((), (), s32[]{:S(2)}) async-start(), calls=%async_computation.2 | async-start | bytes 4956160 | tf_op jit(solution)/shard_map/all_gather | solution.py:533
  13.2 227.8 %reduce-scatter.2.cloned.1.call-start = ((), (), s32[]{:S(2)}) async-start(), calls=%async_computation.1 | async-start | bytes 4956160 | tf_op jit(solution)/shard_map/reduce_scatter | solution.py:628
  14.2 9.2 %collective-permute-start = (bf16[208,384]{1,0:T(8,128)(2,1)S(1)}, bf16[208,384]{1,0:T(8,128)(2,1)S(1)}, u32[]{:S(2)}, u32[]{:S(2)}) collective-permute-start(bf16[208,384]{1,0:T(8,128)(2,1)S(1)} %pack_attention.1.refs_4_), channel_id=1, source_target_pairs={{0,8},{8,16},{16,24},{24,0},{1,9},{9,17},{17,25},{25,1},{2,10},{10... | collective-permute-start | bytes 479240 | tf_op jit(solution)/shard_map/ppermute | solution.py:53
  17.3 19.3 %collective-permute-start.3 = (bf16[80,1472]{1,0:T(8,128)(2,1)S(1)}, bf16[80,1472]{1,0:T(8,128)(2,1)S(1)}, u32[]{:S(2)}, u32[]{:S(2)}) collective-permute-start(bf16[80,1472]{1,0:T(8,128)(2,1)S(1)} %dynamic-slice_bitcast_fusion.1), channel_id=1, source_target_pairs={{0,2},{2,0},{4,6},{6,4},{1,3},{3,1},{5,7},{7,5},{8,10},{10,8},{12,... | collective-permute-start | bytes 706568 | tf_op jit(solution)/shard_map/ppermute | solution.py:58
  19.3 17.4 %collective-permute-start.4 = (bf16[80,1472]{1,0:T(8,128)(2,1)S(1)}, bf16[80,1472]{1,0:T(8,128)(2,1)S(1)}, u32[]{:S(2)}, u32[]{:S(2)}) collective-permute-start(bf16[80,1472]{1,0:T(8,128)(2,1)S(1)} %dynamic-slice_bitcast_fusion.1), channel_id=1, source_target_pairs={{0,4},{2,6},{4,0},{6,2},{1,5},{3,7},{5,1},{7,3},{8,12},{10,14},{12... | collective-permute-start | bytes 706568 | tf_op jit(solution)/shard_map/ppermute | solution.py:58
  20.8 15.8 %collective-permute-start.5 = (bf16[80,1472]{1,0:T(8,128)(2,1)S(1)}, bf16[80,1472]{1,0:T(8,128)(2,1)S(1)}, u32[]{:S(2)}, u32[]{:S(2)}) collective-permute-start(bf16[80,1472]{1,0:T(8,128)(2,1)S(1)} %dynamic-slice_bitcast_fusion.1), channel_id=1, source_target_pairs={{0,6},{2,4},{4,2},{6,0},{1,7},{3,5},{5,3},{7,1},{8,14},{10,12},{12... | collective-permute-start | bytes 706568 | tf_op jit(solution)/shard_map/ppermute | solution.py:58
  20.8 14.9 %collective-permute-start.1 = (bf16[208,384]{1,0:T(8,128)(2,1)S(1)}, bf16[208,384]{1,0:T(8,128)(2,1)S(1)}, u32[]{:S(2)}, u32[]{:S(2)}) collective-permute-start(bf16[208,384]{1,0:T(8,128)(2,1)S(1)} %pack_attention.1.refs_4_), channel_id=1, source_target_pairs={{0,16},{8,24},{16,0},{24,8},{1,17},{9,25},{17,1},{25,9},{2,18},{10... | collective-permute-start | bytes 479240 | tf_op jit(solution)/shard_map/ppermute | solution.py:53
  23.4 13.2 %collective-permute-start.2 = (bf16[208,384]{1,0:T(8,128)(2,1)S(1)}, bf16[208,384]{1,0:T(8,128)(2,1)S(1)}, u32[]{:S(2)}, u32[]{:S(2)}) collective-permute-start(bf16[208,384]{1,0:T(8,128)(2,1)S(1)} %pack_attention.1.refs_4_), channel_id=1, source_target_pairs={{0,24},{8,0},{16,8},{24,16},{1,25},{9,1},{17,9},{25,17},{2,26},{10... | collective-permute-start | bytes 479240 | tf_op jit(solution)/shard_map/ppermute | solution.py:53
  36.7 3.9 %collective-permute-start.9 = (bf16[3,80,1472]{2,1,0:T(8,128)(2,1)S(1)}, bf16[3,80,1472]{2,1,0:T(8,128)(2,1)S(1)}, u32[]{:S(2)}, u32[]{:S(2)}) collective-permute-start(bf16[3,80,1472]{2,1,0:T(8,128)(2,1)S(1)} %pad_maximum_fusion), channel_id=1, source_target_pairs={{0,1},{1,0},{2,3},{3,2},{4,5},{5,4},{6,7},{7,6},{8,9},{9,8},{10,11... | collective-permute-start | bytes 2119688 | tf_op jit(solution)/shard_map/ppermute | solution.py:58
  36.9 13.9 %collective-permute-start.6 = (bf16[624,384]{1,0:T(8,128)(2,1)S(1)}, bf16[624,384]{1,0:T(8,128)(2,1)S(1)}, u32[]{:S(2)}, u32[]{:S(2)}) collective-permute-start(bf16[624,384]{1,0:T(8,128)(2,1)S(1)} %constant_dynamic-update-slice_fusion.refs_0_), channel_id=1, source_target_pairs={{0,2},{2,0},{4,6},{6,4},{1,3},{3,1},{5,7},{7,5},{8,10},{10,8},{12,... | collective-permute-start | bytes 1437704 | tf_op jit(solution)/shard_map/ppermute | solution.py:58
  39.0 23.3 %collective-permute-start.7 = (bf16[624,384]{1,0:T(8,128)(2,1)S(1)}, bf16[624,384]{1,0:T(8,128)(2,1)S(1)}, u32[]{:S(2)}, u32[]{:S(2)}) collective-permute-start(bf16[624,384]{1,0:T(8,128)(2,1)S(1)} %constant_dynamic-update-slice_fusion.refs_0_), channel_id=1, source_target_pairs={{0,4},{2,6},{4,0},{6,2},{1,5},{3,7},{5,1},{7,3},{8,12},{10,14},{12... | collective-permute-start | bytes 1437704 | tf_op jit(solution)/shard_map/ppermute | solution.py:58
  40.6 21.8 %collective-permute-start.8 = (bf16[624,384]{1,0:T(8,128)(2,1)S(1)}, bf16[624,384]{1,0:T(8,128)(2,1)S(1)}, u32[]{:S(2)}, u32[]{:S(2)}) collective-permute-start(bf16[624,384]{1,0:T(8,128)(2,1)S(1)} %constant_dynamic-update-slice_fusion.refs_0_), channel_id=1, source_target_pairs={{0,6},{2,4},{4,2},{6,0},{1,7},{3,5},{5,3},{7,1},{8,14},{10,12},{12... | collective-permute-start | bytes 1437704 | tf_op jit(solution)/shard_map/ppermute | solution.py:58
  62.4 16.5 %collective-permute-start.10 = (bf16[80,1472]{1,0:T(8,128)(2,1)S(1)}, bf16[80,1472]{1,0:T(8,128)(2,1)S(1)}, u32[]{:S(2)}, u32[]{:S(2)}) collective-permute-start(bf16[80,1472]{1,0:T(8,128)(2,1)S(1)} %dynamic-slice_bitcast_fusion), channel_id=1, source_target_pairs={{0,2},{2,0},{4,6},{6,4},{1,3},{3,1},{5,7},{7,5},{8,10},{10,8},{12,... | collective-permute-start | bytes 706568 | tf_op jit(solution)/shard_map/ppermute | solution.py:58
  63.6 15.2 %collective-permute-start.11 = (bf16[80,1472]{1,0:T(8,128)(2,1)S(1)}, bf16[80,1472]{1,0:T(8,128)(2,1)S(1)}, u32[]{:S(2)}, u32[]{:S(2)}) collective-permute-start(bf16[80,1472]{1,0:T(8,128)(2,1)S(1)} %dynamic-slice_bitcast_fusion), channel_id=1, source_target_pairs={{0,4},{2,6},{4,0},{6,2},{1,5},{3,7},{5,1},{7,3},{8,12},{10,14},{12... | collective-permute-start | bytes 706568 | tf_op jit(solution)/shard_map/ppermute | solution.py:58
  64.3 14.6 %collective-permute-start.12 = (bf16[80,1472]{1,0:T(8,128)(2,1)S(1)}, bf16[80,1472]{1,0:T(8,128)(2,1)S(1)}, u32[]{:S(2)}, u32[]{:S(2)}) collective-permute-start(bf16[80,1472]{1,0:T(8,128)(2,1)S(1)} %dynamic-slice_bitcast_fusion), channel_id=1, source_target_pairs={{0,6},{2,4},{4,2},{6,0},{1,7},{3,5},{5,3},{7,1},{8,14},{10,12},{12... | collective-permute-start | bytes 706568 | tf_op jit(solution)/shard_map/ppermute | solution.py:58
  82.2 6.2 %collective-permute-start.14 = (bf16[4,320,368]{2,1,0:T(8,128)(2,1)S(1)}, bf16[4,320,368]{2,1,0:T(8,128)(2,1)S(1)}, u32[]{:S(2)}, u32[]{:S(2)}) collective-permute-start(bf16[4,320,368]{2,1,0:T(8,128)(2,1)S(1)} %get-tuple-element.108.nt_mine), channel_id=1, source_target_pairs={{0,1},{1,0},{2,3},{3,2},{4,5},{5,4},{6,7},{7,6},{8,9},{9,8},{10,11... | collective-permute-start | bytes 2826248 | tf_op jit(solution)/shard_map/ppermute | solution.py:58
  82.5 3.4 %collective-permute-start.15 = (bf16[3,80,1472]{2,1,0:T(8,128)(2,1)S(1)}, bf16[3,80,1472]{2,1,0:T(8,128)(2,1)S(1)}, u32[]{:S(2)}, u32[]{:S(2)}) collective-permute-start(bf16[3,80,1472]{2,1,0:T(8,128)(2,1)S(1)} %pad_maximum_fusion.1), channel_id=1, source_target_pairs={{0,1},{1,0},{2,3},{3,2},{4,5},{5,4},{6,7},{7,6},{8,9},{9,8},{10,11... | collective-permute-start | bytes 2119688 | tf_op jit(solution)/shard_map/ppermute | solution.py:58
  127.2 2.8 collective-permute-start.16
  130.0 2.8 collective-permute-start.17
  133.1 9.8 %collective-permute-start.20 = (bf16[4,80,368]{2,1,0:T(8,128)(2,1)S(1)}, bf16[4,80,368]{2,1,0:T(8,128)(2,1)S(1)}, u32[]{:S(2)}, u32[]{:S(2)}) collective-permute-start(bf16[4,80,368]{2,1,0:T(8,128)(2,1)S(1)} %get-tuple-element.122), channel_id=1, source_target_pairs={{0,6},{2,4},{4,2},{6,0},{1,7},{3,5},{5,3},{7,1},{8,14},{10,12},{12... | collective-permute-start | bytes 706568 | tf_op jit(solution)/shard_map/ppermute | solution.py:58
  136.0 11.5 %collective-permute-start.19 = (bf16[4,80,368]{2,1,0:T(8,128)(2,1)S(1)}, bf16[4,80,368]{2,1,0:T(8,128)(2,1)S(1)}, u32[]{:S(2)}, u32[]{:S(2)}) collective-permute-start(bf16[4,80,368]{2,1,0:T(8,128)(2,1)S(1)} %get-tuple-element.121), channel_id=1, source_target_pairs={{0,4},{2,6},{4,0},{6,2},{1,5},{3,7},{5,1},{7,3},{8,12},{10,14},{12... | collective-permute-start | bytes 706568 | tf_op jit(solution)/shard_map/ppermute | solution.py:58
  136.5 11.0 %collective-permute-start.18 = (bf16[4,80,368]{2,1,0:T(8,128)(2,1)S(1)}, bf16[4,80,368]{2,1,0:T(8,128)(2,1)S(1)}, u32[]{:S(2)}, u32[]{:S(2)}) collective-permute-start(bf16[4,80,368]{2,1,0:T(8,128)(2,1)S(1)} %get-tuple-element.120), channel_id=1, source_target_pairs={{0,2},{2,0},{4,6},{6,4},{1,3},{3,1},{5,7},{7,5},{8,10},{10,8},{12,... | collective-permute-start | bytes 706568 | tf_op jit(solution)/shard_map/ppermute | solution.py:58
  149.5 10.8 %collective-permute-start.24 = (bf16[4,80,368]{2,1,0:T(8,128)(2,1)S(1)}, bf16[4,80,368]{2,1,0:T(8,128)(2,1)S(1)}, u32[]{:S(2)}, u32[]{:S(2)}) collective-permute-start(bf16[4,80,368]{2,1,0:T(8,128)(2,1)S(1)} %get-tuple-element.129), channel_id=1, source_target_pairs={{0,6},{2,4},{4,2},{6,0},{1,7},{3,5},{5,3},{7,1},{8,14},{10,12},{12... | collective-permute-start | bytes 706568 | tf_op jit(solution)/shard_map/ppermute | solution.py:58
  151.3 12.3 %collective-permute-start.23 = (bf16[4,80,368]{2,1,0:T(8,128)(2,1)S(1)}, bf16[4,80,368]{2,1,0:T(8,128)(2,1)S(1)}, u32[]{:S(2)}, u32[]{:S(2)}) collective-permute-start(bf16[4,80,368]{2,1,0:T(8,128)(2,1)S(1)} %get-tuple-element.128), channel_id=1, source_target_pairs={{0,4},{2,6},{4,0},{6,2},{1,5},{3,7},{5,1},{7,3},{8,12},{10,14},{12... | collective-permute-start | bytes 706568 | tf_op jit(solution)/shard_map/ppermute | solution.py:58
  152.8 10.9 %collective-permute-start.22 = (bf16[4,80,368]{2,1,0:T(8,128)(2,1)S(1)}, bf16[4,80,368]{2,1,0:T(8,128)(2,1)S(1)}, u32[]{:S(2)}, u32[]{:S(2)}) collective-permute-start(bf16[4,80,368]{2,1,0:T(8,128)(2,1)S(1)} %get-tuple-element.127), channel_id=1, source_target_pairs={{0,2},{2,0},{4,6},{6,4},{1,3},{3,1},{5,7},{7,5},{8,10},{10,8},{12,... | collective-permute-start | bytes 706568 | tf_op jit(solution)/shard_map/ppermute | solution.py:58
  163.7 24.9 %collective-permute-start.30 = (bf16[4,192,368]{2,1,0:T(8,128)(2,1)S(1)}, bf16[4,192,368]{2,1,0:T(8,128)(2,1)S(1)}, u32[]{:S(2)}, u32[]{:S(2)}) collective-permute-start(bf16[4,192,368]{2,1,0:T(8,128)(2,1)S(1)} %get-tuple-element.148), channel_id=1, source_target_pairs={{0,4},{2,6},{4,0},{6,2},{1,5},{3,7},{5,1},{7,3},{8,12},{10,14},{12... | collective-permute-start | bytes 1695752 | tf_op jit(solution)/shard_map/ppermute | solution.py:58
  165.0 23.6 %collective-permute-start.29 = (bf16[4,192,368]{2,1,0:T(8,128)(2,1)S(1)}, bf16[4,192,368]{2,1,0:T(8,128)(2,1)S(1)}, u32[]{:S(2)}, u32[]{:S(2)}) collective-permute-start(bf16[4,192,368]{2,1,0:T(8,128)(2,1)S(1)} %get-tuple-element.147), channel_id=1, source_target_pairs={{0,2},{2,0},{4,6},{6,4},{1,3},{3,1},{5,7},{7,5},{8,10},{10,8},{12,... | collective-permute-start | bytes 1695752 | tf_op jit(solution)/shard_map/ppermute | solution.py:58
  166.1 16.9 %collective-permute-start.28 = (bf16[160,384]{1,0:T(8,128)(2,1)S(1)}, bf16[160,384]{1,0:T(8,128)(2,1)S(1)}, u32[]{:S(2)}, u32[]{:S(2)}) collective-permute-start(bf16[160,384]{1,0:T(8,128)(2,1)S(1)} %get-tuple-element.143), channel_id=1, source_target_pairs={{0,6},{2,4},{4,2},{6,0},{1,7},{3,5},{5,3},{7,1},{8,14},{10,12},{12... | collective-permute-start | bytes 368648 | tf_op jit(solution)/shard_map/ppermute | solution.py:58
  167.4 21.2 %collective-permute-start.25 = (bf16[80,1472]{1,0:T(8,128)(2,1)S(1)}, bf16[80,1472]{1,0:T(8,128)(2,1)S(1)}, u32[]{:S(2)}, u32[]{:S(2)}) collective-permute-start(bf16[80,1472]{1,0:T(8,128)(2,1)S(1)} %produce.1), channel_id=1, source_target_pairs={{0,1},{1,0},{2,3},{3,2},{4,5},{5,4},{6,7},{7,6},{8,9},{9,8},{10,11... | collective-permute-start | bytes 706568 | tf_op jit(solution)/shard_map/ppermute | solution.py:58
  167.5 16.9 %collective-permute-start.27 = (bf16[160,384]{1,0:T(8,128)(2,1)S(1)}, bf16[160,384]{1,0:T(8,128)(2,1)S(1)}, u32[]{:S(2)}, u32[]{:S(2)}) collective-permute-start(bf16[160,384]{1,0:T(8,128)(2,1)S(1)} %get-tuple-element.141), channel_id=1, source_target_pairs={{0,4},{2,6},{4,0},{6,2},{1,5},{3,7},{5,1},{7,3},{8,12},{10,14},{12... | collective-permute-start | bytes 368648 | tf_op jit(solution)/shard_map/ppermute | solution.py:58
  183.0 4.9 %collective-permute-start.26 = (bf16[160,384]{1,0:T(8,128)(2,1)S(1)}, bf16[160,384]{1,0:T(8,128)(2,1)S(1)}, u32[]{:S(2)}, u32[]{:S(2)}) collective-permute-start(bf16[160,384]{1,0:T(8,128)(2,1)S(1)} %get-tuple-element.139), channel_id=1, source_target_pairs={{0,2},{2,0},{4,6},{6,4},{1,3},{3,1},{5,7},{7,5},{8,10},{10,8},{12,... | collective-permute-start | bytes 368648 | tf_op jit(solution)/shard_map/ppermute | solution.py:58
  188.7 16.9 %collective-permute-start.34 = (bf16[4,192,368]{2,1,0:T(8,128)(2,1)}, bf16[4,192,368]{2,1,0:T(8,128)(2,1)S(1)}, u32[]{:S(2)}, u32[]{:S(2)}) collective-permute-start(bf16[4,192,368]{2,1,0:T(8,128)(2,1)} %get-tuple-element.156), channel_id=1, source_target_pairs={{0,6},{2,4},{4,2},{6,0},{1,7},{3,5},{5,3},{7,1},{8,14},{10,12},{12... | collective-permute-start | bytes 1695752 | tf_op jit(solution)/shard_map/ppermute | solution.py:58
  205.6 9.0 %collective-permute-start.35 = (f32[4,2,368]{2,1,0:T(2,128)S(1)}, f32[4,2,368]{2,1,0:T(2,128)S(1)}, u32[]{:S(2)}, u32[]{:S(2)}) collective-permute-start(f32[4,2,368]{2,1,0:T(2,128)S(1)} %fusion.13), channel_id=1, source_target_pairs={{0,2},{2,0},{4,6},{6,4},{1,3},{3,1},{5,7},{7,5},{8,10},{10,8},{12,... | collective-permute-start | bytes 35336 | tf_op jit(solution)/shard_map/ppermute | solution.py:58
  207.0 7.6 %collective-permute-start.36 = (f32[4,2,368]{2,1,0:T(2,128)S(1)}, f32[4,2,368]{2,1,0:T(2,128)S(1)}, u32[]{:S(2)}, u32[]{:S(2)}) collective-permute-start(f32[4,2,368]{2,1,0:T(2,128)S(1)} %fusion.13), channel_id=1, source_target_pairs={{0,4},{2,6},{4,0},{6,2},{1,5},{3,7},{5,1},{7,3},{8,12},{10,14},{12... | collective-permute-start | bytes 35336 | tf_op jit(solution)/shard_map/ppermute | solution.py:58
  208.0 6.5 %collective-permute-start.37 = (f32[4,2,368]{2,1,0:T(2,128)S(1)}, f32[4,2,368]{2,1,0:T(2,128)S(1)}, u32[]{:S(2)}, u32[]{:S(2)}) collective-permute-start(f32[4,2,368]{2,1,0:T(2,128)S(1)} %fusion.13), channel_id=1, source_target_pairs={{0,6},{2,4},{4,2},{6,0},{1,7},{3,5},{5,3},{7,1},{8,14},{10,12},{12... | collective-permute-start | bytes 35336 | tf_op jit(solution)/shard_map/ppermute | solution.py:58
  211.2 6.6 %collective-permute-start.40 = (bf16[192,368]{1,0:T(8,128)(2,1)S(1)}, bf16[192,368]{1,0:T(8,128)(2,1)S(1)}, u32[]{:S(2)}, u32[]{:S(2)}) collective-permute-start(bf16[192,368]{1,0:T(8,128)(2,1)S(1)} %get-tuple-element.161), channel_id=1, source_target_pairs={{0,24},{8,0},{16,8},{24,16},{1,25},{9,1},{17,9},{25,17},{2,26},{10... | collective-permute-start | bytes 423944 | tf_op jit(solution)/shard_map/ppermute | solution.py:53
  213.5 13.0 %collective-permute-start.39 = (bf16[192,368]{1,0:T(8,128)(2,1)S(1)}, bf16[192,368]{1,0:T(8,128)(2,1)S(1)}, u32[]{:S(2)}, u32[]{:S(2)}) collective-permute-start(bf16[192,368]{1,0:T(8,128)(2,1)S(1)} %get-tuple-element.160), channel_id=1, source_target_pairs={{0,16},{8,24},{16,0},{24,8},{1,17},{9,25},{17,1},{25,9},{2,18},{10... | collective-permute-start | bytes 423944 | tf_op jit(solution)/shard_map/ppermute | solution.py:53
  214.5 12.0 %collective-permute-start.38 = (bf16[192,368]{1,0:T(8,128)(2,1)S(1)}, bf16[192,368]{1,0:T(8,128)(2,1)S(1)}, u32[]{:S(2)}, u32[]{:S(2)}) collective-permute-start(bf16[192,368]{1,0:T(8,128)(2,1)S(1)} %get-tuple-element.159), channel_id=1, source_target_pairs={{0,8},{8,16},{16,24},{24,0},{1,9},{9,17},{17,25},{25,1},{2,10},{10... | collective-permute-start | bytes 423944 | tf_op jit(solution)/shard_map/ppermute | solution.py:53
  226.6 6.4 %collective-permute-start.41 = (f32[2,368]{1,0:T(2,128)S(1)}, f32[2,368]{1,0:T(2,128)S(1)}, u32[]{:S(2)}, u32[]{:S(2)}) collective-permute-start(f32[2,368]{1,0:T(2,128)S(1)} %get-tuple-element.163), channel_id=1, source_target_pairs={{0,8},{8,16},{16,24},{24,0},{1,9},{9,17},{17,25},{25,1},{2,10},{10... | collective-permute-start | bytes 8840 | tf_op jit(solution)/shard_map/ppermute | solution.py:53
  226.6 7.7 %collective-permute-start.42 = (f32[2,368]{1,0:T(2,128)S(1)}, f32[2,368]{1,0:T(2,128)S(1)}, u32[]{:S(2)}, u32[]{:S(2)}) collective-permute-start(f32[2,368]{1,0:T(2,128)S(1)} %get-tuple-element.164), channel_id=1, source_target_pairs={{0,16},{8,24},{16,0},{24,8},{1,17},{9,25},{17,1},{25,9},{2,18},{10... | collective-permute-start | bytes 8840 | tf_op jit(solution)/shard_map/ppermute | solution.py:53
  227.7 6.6 %collective-permute-start.43 = (f32[2,368]{1,0:T(2,128)S(1)}, f32[2,368]{1,0:T(2,128)S(1)}, u32[]{:S(2)}, u32[]{:S(2)}) collective-permute-start(f32[2,368]{1,0:T(2,128)S(1)} %get-tuple-element.165), channel_id=1, source_target_pairs={{0,24},{8,0},{16,8},{24,16},{1,25},{9,1},{17,9},{25,17},{2,26},{10... | collective-permute-start | bytes 8840 | tf_op jit(solution)/shard_map/ppermute | solution.py:53
  230.7 6.7 %collective-permute-start.44 = (bf16[192,368]{1,0:T(8,128)(2,1)S(1)}, bf16[192,368]{1,0:T(8,128)(2,1)S(1)}, u32[]{:S(2)}, u32[]{:S(2)}) collective-permute-start(bf16[192,368]{1,0:T(8,128)(2,1)S(1)} %add_convert_fusion.8.refs_0_), channel_id=1, source_target_pairs={{0,2},{2,0},{4,6},{6,4},{1,3},{3,1},{5,7},{7,5},{8,10},{10,8},{12,... | collective-permute-start | bytes 423944 | tf_op jit(solution)/shard_map/ppermute | solution.py:58
  232.4 7.0 %collective-permute-start.45 = (bf16[192,368]{1,0:T(8,128)(2,1)S(1)}, bf16[192,368]{1,0:T(8,128)(2,1)S(1)}, u32[]{:S(2)}, u32[]{:S(2)}) collective-permute-start(bf16[192,368]{1,0:T(8,128)(2,1)S(1)} %add_convert_fusion.8.refs_0_), channel_id=1, source_target_pairs={{0,4},{2,6},{4,0},{6,2},{1,5},{3,7},{5,1},{7,3},{8,12},{10,14},{12... | collective-permute-start | bytes 423944 | tf_op jit(solution)/shard_map/ppermute | solution.py:58
  233.0 6.4 %collective-permute-start.46 = (bf16[192,368]{1,0:T(8,128)(2,1)S(1)}, bf16[192,368]{1,0:T(8,128)(2,1)S(1)}, u32[]{:S(2)}, u32[]{:S(2)}) collective-permute-start(bf16[192,368]{1,0:T(8,128)(2,1)S(1)} %add_convert_fusion.8.refs_0_), channel_id=1, source_target_pairs={{0,6},{2,4},{4,2},{6,0},{1,7},{3,5},{5,3},{7,1},{8,14},{10,12},{12... | collective-permute-start | bytes 423944 | tf_op jit(solution)/shard_map/ppermute | solution.py:58
  241.0 20.9 %collective-permute-start.47 = (bf16[3872,128]{1,0:T(8,128)(2,1)}, bf16[3872,128]{1,0:T(8,128)(2,1)S(1)}, u32[]{:S(2)}, u32[]{:S(2)}) collective-permute-start(bf16[3872,128]{1,0:T(8,128)(2,1)} %bitcast.75), channel_id=1, source_target_pairs={{0,2},{2,0},{4,6},{6,4},{1,3},{3,1},{5,7},{7,5},{8,10},{10,8},{12,... | collective-permute-start | bytes 2973704 | tf_op jit(solution)/shard_map/ppermute | solution.py:58
  242.1 22.6 %collective-permute-start.48 = (bf16[3872,128]{1,0:T(8,128)(2,1)}, bf16[3872,128]{1,0:T(8,128)(2,1)S(1)}, u32[]{:S(2)}, u32[]{:S(2)}) collective-permute-start(bf16[3872,128]{1,0:T(8,128)(2,1)} %bitcast.76), channel_id=1, source_target_pairs={{0,4},{2,6},{4,0},{6,2},{1,5},{3,7},{5,1},{7,3},{8,12},{10,14},{12... | collective-permute-start | bytes 2973704 | tf_op jit(solution)/shard_map/ppermute | solution.py:58
  262.0 11.9 %collective-permute-start.49 = (bf16[1936,128]{1,0:T(8,128)(2,1)S(1)}, bf16[1936,128]{1,0:T(8,128)(2,1)S(1)}, u32[]{:S(2)}, u32[]{:S(2)}) collective-permute-start(bf16[1936,128]{1,0:T(8,128)(2,1)S(1)} %slice.126), channel_id=1, source_target_pairs={{0,4},{2,6},{4,0},{6,2},{1,5},{3,7},{5,1},{7,3},{8,12},{10,14},{12... | collective-permute-start | bytes 1486856 | tf_op jit(solution)/shard_map/ppermute | solution.py:58
  264.7 9.4 %collective-permute-start.50 = (bf16[1936,128]{1,0:T(8,128)(2,1)S(1)}, bf16[1936,128]{1,0:T(8,128)(2,1)S(1)}, u32[]{:S(2)}, u32[]{:S(2)}) collective-permute-start(bf16[1936,128]{1,0:T(8,128)(2,1)S(1)} %slice.127), channel_id=1, source_target_pairs={{0,2},{2,0},{4,6},{6,4},{1,3},{3,1},{5,7},{7,5},{8,10},{10,8},{12,... | collective-permute-start | bytes 1486856 | tf_op jit(solution)/shard_map/ppermute | solution.py:58
  (44 other events, 331.5 us)
Sparse Core Ops, SparseCore 0:
  13.4 84.6 all-gather.2
  127.3 73.3 reduce-scatter.1

commit v4 on v3

v4 whole, which is shorter than its diff:
```python
import functools

import jax
import jax.numpy as jnp
from jax import lax
from jax.experimental import pallas as pl
from jax.experimental.pallas import tpu as pltpu
from jax.sharding import PartitionSpec as P

DK = 64
norm_eps = 1e-06
distance_marks = (8, 12, 16, 23, 32, 46, 64, 91)
masked_score = -1e30
low = jnp.bfloat16
wide = jnp.float32
LANES = 128
COST = 1e8


def dot_nn(left, right):
    return lax.dot_general(left, right, (((1,), (0,)), ((), ())), preferred_element_type=wide)


def dot_nt(left, right):
    return lax.dot_general(left, right, (((1,), (1,)), ((), ())), preferred_element_type=wide)


def dot_tn(left, right):
    return lax.dot_general(left, right, (((0,), (0,)), ((), ())), preferred_element_type=wide)


def wrap(value, n):
    return lax.rem(value + 2 * n, n)


def run(body, name, outs, operands, scratch=(), scalars=1, cost=1, far=0, far_out=False, into=0, vmem=16):
    return pl.pallas_call(
        body,
        name=name,
        out_shape=[jax.ShapeDtypeStruct(s, d) for s, d in outs],
        in_specs=[pl.BlockSpec(memory_space=pltpu.SMEM)] * scalars
        + [pl.BlockSpec(memory_space=pltpu.HBM)] * far
        + [pl.BlockSpec(memory_space=pltpu.VMEM)] * (len(operands) - scalars - far - into)
        + [pl.BlockSpec(memory_space=pltpu.HBM)] * into,
        out_specs=[pl.BlockSpec(memory_space=pltpu.HBM if far_out else pltpu.VMEM)] * len(outs),
        scratch_shapes=list(scratch),
        input_output_aliases={len(operands) - into + i: i for i in range(into)},
        compiler_params=pltpu.CompilerParams(vmem_limit_bytes=vmem * 2**20),
        cost_estimate=pl.CostEstimate(flops=int(cost * COST), bytes_accessed=0, transcendentals=0),
    )(*operands)


def step(x, axis, k=1):
    n = lax.axis_size(axis)
    return lax.ppermute(x, axis, [(i, (i + k) % n) for i in range(n)])


def swap(x, axis, k=1):
    n = lax.axis_size(axis)
    return lax.ppermute(x, axis, [(i, i ^ k) for i in range(n)])


def after(x, *others):
    return lax.optimization_barrier((x, *others))[0]


def pack_attention(n_ctx, idx, w_q, w_k, w_v, w_o, gain, buf, held, sem):
    inner, r = w_o.shape
    for v, ref in enumerate((w_q, w_k, w_v, w_o)):

        @pl.when(idx[1] == v)
        def _(ref=ref):
            copy = pltpu.make_async_copy(ref, held, sem)
            copy.start()
            copy.wait()

    buf[0:inner, 0:r] = held[...]

    buf[inner : inner + 2, 0:r] = gain[...]


def wide_tiles(r, widths):
    rp = pl.cdiv(r, 16) * 16
    row, parts = 0, []
    for n in widths:
        full, left = divmod(3 * n, LANES)
        pieces = [(row + rp * q, r, 0, LANES * q, LANES, 0) for q in range(full)]
        row += rp * full
        if left:
            assert 2 * left == LANES
            pieces.append((row, r // 2, 0, LANES * full, left, 0))
            pieces.append((row, r // 2, r // 2, LANES * full, left, left))
            row += pl.cdiv(r // 2, 8) * 8
        parts.append(pieces)
    return parts, pl.cdiv(row, 32) * 32


def pack_wide(n_ctx, widths, window, idx, w_g, w_u, w_d, buf, stage, held, sems):
    r = w_g.shape[0]
    columns = sum(widths)
    parts, _ = wide_tiles(r, widths)
    for v in range(n_ctx):

        @pl.when(idx[1] == v)
        def _(v=v):
            start = min(v * columns // LANES * LANES, w_g.shape[1] - window)
            copies = [
                pltpu.make_async_copy(ref.at[:, start : start + window], held.at[i], sems.at[i])
                for i, ref in enumerate((w_g, w_u, w_d))
            ]
            for copy in copies:
                copy.start()
            for copy in copies:
                copy.wait()
            at = v * columns - start
            for n, pieces in zip(widths, parts, strict=True):
                for i in range(3):
                    stage[:, i * n : (i + 1) * n] = held[i, :, at : at + n]
                for row, size, top, lane, lanes, to in pieces:
                    buf[row : row + size, to : to + lanes] = stage[
                        top : top + size, lane : lane + lanes
                    ]
                at += n


def bias_body(rows, seg_len, marks, idx, table, out):
    c = idx[1]
    heads, length, _ = out.shape

    def info(position):
        block = sum(((position >= rows * b).astype(jnp.int32) for b in range(1, length // rows)))
        token = (block ^ c) * rows + position - block * rows
        seg = sum(((token >= q * seg_len).astype(jnp.int32) for q in range(8, 20)))
        parent = jnp.where(seg == 0, -1, jnp.where(seg <= 4, 0, (seg - 3) >> 1))
        shift = jnp.where(seg == 0, 0, jnp.where(seg <= 4, seg - 1, seg - 2))
        return seg, parent, token - shift * seg_len

    key_seg, _, key_place = info(lax.broadcasted_iota(jnp.int32, (16, length), 1))

    def rows_of(i, _):
        at = pl.multiple_of(i * 16, 16)
        seg, parent, place = info(lax.broadcasted_iota(jnp.int32, (16, length), 0) + at)
        allowed = (key_seg == 0) | (key_seg == seg) | (key_seg == parent)
        relative = key_place - place
        magnitude = jnp.abs(relative)
        marked = sum(((magnitude >= mark).astype(jnp.int32) for mark in marks))
        bucket = jnp.where(relative > 0, 16, 0) + jnp.where(magnitude < 8, magnitude, 7 + marked)
        looked = [jnp.full(bucket.shape, table[0, h], wide) for h in range(heads)]
        for b in range(1, table.shape[0]):
            hit = bucket == b
            looked = [jnp.where(hit, table[b, h], looked[h]) for h in range(heads)]
        for h in range(heads):
            out[h, pl.ds(at, 16), :] = jnp.where(allowed, looked[h], masked_score)
        return 0

    lax.fori_loop(0, length // 16, rows_of, 0)


def tree_blocks(n_ctx, half, own, mine, rest):
    for k in range(n_ctx):
        yield 0, k, own[half] if k == 0 else mine[k - 1][...]
    for k in range(n_ctx):
        yield 1, k, own[1 - half] if k == 0 else rest[k - 1]


def norm_one(n_ctx, n_shard, idx, x_in, *refs):
    s, half = idx[0], idx[2]
    mine, rest = refs[: n_ctx - 1], refs[n_ctx - 1]
    bufs = refs[n_ctx : n_ctx + n_shard]
    normed, gains, held = refs[n_ctx + n_shard :]
    r = held.shape[2]
    _, rows, width = x_in.shape
    for k, buf in enumerate(bufs):
        at = buf.shape[0] - 16
        held[wrap(s - k, n_shard), 0:2, :] = buf[at : at + 2, 0:r].astype(wide)
    for j in range(n_shard):
        gains[:, r * j : r * (j + 1)] = held[j, 0:2, :]
    for m, k, x in tree_blocks(n_ctx, half, x_in, mine, rest):
        x = x.astype(wide)
        y = x * lax.rsqrt(jnp.mean(x * x, axis=-1, keepdims=True) + norm_eps)
        at = (m * n_ctx + k) * rows
        normed[at : at + rows, :] = (y * gains[0:1, :]).astype(low)


def attend(n_ctx, n_shard, rows, heads, place, idx, normed, w_q, w_k, w_v, w_o, bias, *refs):
    s, c = idx[0], idx[1]
    groups = 1 + max((g for pieces in place.values() for g, _, _ in pieces))
    got = [refs[g * n_ctx : (g + 1) * n_ctx] for g in range(groups)]
    att_mine, att_other, soft, qkv, mixed, every, held = refs[groups * n_ctx :]
    inner, r = w_o.shape
    length = n_ctx * rows
    for i, ref in enumerate((w_q, w_k, w_v, w_o)):
        held[s, i * inner : (i + 1) * inner, :] = ref[...]
    for v in range(n_ctx):

        @pl.when(c == v)
        def _(v=v):
            for k in range(n_ctx):
                for z, pieces in place.items():
                    at, last = (v ^ k) * inner, ((v ^ k) + 1) * inner
                    for g, row, size in pieces:
                        size = min(size, last - at)
                        held[wrap(s - z, n_shard), at : at + size, :] = got[g][k][
                            row : row + size, 0:r
                        ]
                        at += size

    for j in range(n_shard):
        every[:, r * j : r * (j + 1)] = held[j]
    qkv[...] = dot_nt(normed[...], every[0 : 3 * inner, :]).astype(low)
    for m in (1, 0):
        low_row = m * length
        for h in range(heads):
            at = DK * h
            keys = qkv[low_row : low_row + length, inner + at : inner + at + DK]
            values = qkv[low_row : low_row + length, 2 * inner + at : 2 * inner + at + DK]
            for b in range(n_ctx):
                top = low_row + b * rows
                scores = dot_nt(qkv[top : top + rows, at : at + DK], keys)
                scores += bias[h, b * rows : (b + 1) * rows, :]
                raised = jnp.exp(scores - jnp.max(scores, axis=-1, keepdims=True))
                share = raised / jnp.sum(raised, axis=-1, keepdims=True)
                if b == 0:
                    soft[m, h] = share
                mixed[top : top + rows, at : at + DK] = dot_nn(share.astype(low), values).astype(low)
        out = att_mine if m == 0 else att_other
        out[...] = dot_nn(
            mixed[low_row : low_row + length, :], every[3 * inner : 4 * inner, :]
        ).astype(low)


def middle_norm(n_ctx, idx, x_in, *refs):
    mine, (att, got, gains, normed, middle_own) = refs[: n_ctx - 1], refs[n_ctx - 1 :]
    rows = x_in.shape[1]
    for k in range(n_ctx):
        at = slice(k * rows, (k + 1) * rows)
        x = x_in[idx[2]] if k == 0 else mine[k - 1][...]
        mid = x.astype(wide) + (att[at, :].astype(wide) + got[at, :].astype(wide))
        scale = lax.rsqrt(jnp.mean(mid * mid, axis=-1, keepdims=True) + norm_eps)
        normed[at, :] = (mid * scale * gains[1:2, :]).astype(low)
        if k == 0:
            middle_own[...] = mid


def feed_forward(n_ctx, n_shard, widths, idx, buf_far, nt_mine, nt_other, cot_in, *refs):
    half = idx[2]
    mine, rest, refs = refs[: n_ctx - 1], refs[n_ctx - 1], refs[n_ctx:]
    sent, feed, two = refs[0], refs[1:3], refs[3:5]
    n_parts = len(widths)
    buf, nt, cot, feed_held, two_held, sems, sems_out = refs[5:12]
    weights, hidden, pair = (refs[12 + i * n_parts : 12 + (i + 1) * n_parts] for i in range(3))
    length, _ = nt_mine.shape
    rows = length // n_ctx
    r = weights[0].shape[0] // n_shard

    def blocks(m, first, count=1):
        at = (m * n_ctx + first) * rows
        return slice(at, at + count * rows)

    begun = [pltpu.make_async_copy(buf_far.at[0], buf.at[0], sems.at[0])]
    moves = [
        (nt_mine, nt.at[0:length, :]),
        (nt_other, nt.at[length : 2 * length, :]),
        (cot_in.at[half], cot.at[blocks(0, 0), :]),
        (cot_in.at[1 - half], cot.at[blocks(1, 0), :]),
    ]
    moves += [(buf_far.at[j], buf.at[j]) for j in range(1, n_shard)]
    for k in range(1, n_ctx):
        moves.append((mine[k - 1], cot.at[blocks(0, k), :]))
        moves.append((rest.at[k - 1], cot.at[blocks(1, k), :]))
    begun += [pltpu.make_async_copy(a, b, sems.at[i + 1]) for i, (a, b) in enumerate(moves)]
    for copy in begun:
        copy.start()
    loads = [begun[0]] + begun[5 : 4 + n_shard]
    parts, _ = wide_tiles(r, widths)
    for j in range(n_shard):
        loads[j].wait()
        for e, pieces in enumerate(parts):
            for row, size, top, lane, lanes, at in pieces:
                weights[e][r * j + top : r * j + top + size, lane : lane + lanes] = buf[
                    j, row : row + size, at : at + lanes
                ]
    for copy in begun[1:5] + begun[4 + n_shard :]:
        copy.wait()
    c0, c1 = 0.7978845608028654, 0.044715
    out = []

    def write(source, target):
        copy = pltpu.make_async_copy(source, target, sems_out.at[len(out)])
        copy.start()
        out.append(copy)

    for m in (1, 0):
        at = slice(m * length, (m + 1) * length)
        for e, n in enumerate(widths):
            both = dot_nn(nt[at, :], weights[e][:, 0 : 2 * n])
            back = dot_nn(cot[at, :], weights[e][:, 2 * n : 3 * n])
            gate, up = both[:, :n], both[:, n:]
            square = gate * gate
            bent = jnp.tanh(c0 * (gate + c1 * gate * square))
            half_one = 0.5 * (1.0 + bent)
            active = gate * half_one
            slope = half_one + 0.5 * gate * (1.0 - bent * bent) * (c0 * (1.0 + 3.0 * c1 * square))
            hidden[e][at, :] = (active * up).astype(low)
            pair[e][at, 0:n] = (back * up * slope).astype(low)
            pair[e][at, n : 2 * n] = (back * active).astype(low)
        for held, given, make in (
            (two_held, two, lambda e, n: dot_nt(pair[e][at, :], weights[e][:, 0 : 2 * n])),
            (feed_held, feed, lambda e, n: dot_nt(hidden[e][at, :], weights[e][:, 2 * n : 3 * n])),
        ):
            total = sum((make(e, n) for e, n in enumerate(widths)))
            for i in range(n_ctx):
                held[m, i] = total[i * rows : (i + 1) * rows].astype(low)
            write(held.at[m], given[m])
    for e, n in enumerate(widths):
        for_in = dot_tn(nt[...], pair[e][...]).astype(low)
        for_down = dot_tn(cot[...], hidden[e][...]).astype(low)
        first, last = parts[e][0][0], parts[e][-1][0] + parts[e][-1][1]
        for j in range(n_shard):
            for row, size, top, lane, lanes, at in parts[e]:
                top = r * j + top
                inside = max(0, min(lanes, 2 * n - lane))
                if inside:
                    buf[j, row : row + size, at : at + inside] = for_in[
                        top : top + size, lane : lane + inside
                    ]
                if inside < lanes:
                    begin = lane + inside - 2 * n
                    buf[j, row : row + size, at + inside : at + lanes] = for_down[
                        top : top + size, begin : begin + lanes - inside
                    ]
            here = slice(first, last if e < n_parts - 1 else buf.shape[1])
            write(buf.at[j, here, :], sent.at[j, here, :])
    for copy in out:
        copy.wait()


def norm_two_back(n_shard, n_parts, idx, cot_in, *refs):
    parts, refs = refs[:n_parts], refs[n_parts:]
    middle, gains, out_in, grad, gain_grad = refs
    r = gain_grad.shape[2]
    mid = middle[...]
    two = sum((p[...].astype(wide) for p in parts))
    scale = lax.rsqrt(jnp.mean(mid * mid, axis=-1, keepdims=True) + norm_eps)
    u = two * gains[1:2, :]
    inner = jnp.mean(u * mid, axis=-1, keepdims=True) * (scale * scale * scale)
    back = cot_in[idx[2]].astype(wide) + scale * u - mid * inner
    grad[...] = back
    out_in[...] = back.astype(low)
    total = jnp.sum(two * mid * scale, axis=0, keepdims=True)
    for j in range(n_shard):
        gain_grad[j] = total[:, r * j : r * (j + 1)]


def attend_back(n_ctx, heads, o_mine, o_other, soft, qkv, every, *refs):
    kv, (q_grad, kv_all, mixed_grad) = refs[:n_ctx], refs[n_ctx:]
    rows = o_mine.shape[0]
    length = n_ctx * rows
    inner = heads * DK
    for m, o_in in ((0, o_mine), (1, o_other)):
        top, own = m * length, m * rows
        mixed_grad[own : own + rows, :] = dot_nt(o_in[...], every[3 * inner :, :]).astype(low)
        for h in range(heads):
            at = DK * h
            share = soft[m, h]
            grad = mixed_grad[own : own + rows, at : at + DK]
            keys = qkv[top : top + length, inner + at : inner + at + DK]
            values = qkv[top : top + length, 2 * inner + at : 2 * inner + at + DK]
            queries = qkv[top : top + rows, at : at + DK]
            weight = dot_nt(grad, values)
            ds = share * (weight - jnp.sum(weight * share, axis=-1, keepdims=True))
            ds = ds.astype(low)
            q_grad[own : own + rows, at : at + DK] = dot_nn(ds, keys).astype(low)
            kv_all[top : top + length, at : at + DK] = dot_tn(ds, queries).astype(low)
            kv_all[top : top + length, inner + at : inner + at + DK] = dot_tn(
                share.astype(low), grad
            ).astype(low)
        for k in range(n_ctx):
            kv[k][own : own + rows, :] = kv_all[top + k * rows : top + (k + 1) * rows, :]


def first_grad(n_ctx, idx, *refs):
    parts, (q_grad, every, out_mine, out_other), pieces, three = (
        refs[:n_ctx],
        refs[n_ctx : n_ctx + 4],
        refs[n_ctx + 4 : 2 * n_ctx + 4],
        refs[2 * n_ctx + 4],
    )
    rows2, inner = q_grad.shape
    rows = rows2 // 2
    three[:, 0:inner] = q_grad[...]
    three[:, inner:] = sum((p[...].astype(wide) for p in parts)).astype(low)
    for v in range(n_ctx):

        @pl.when(idx[1] == v)
        def _(v=v):
            for k in range(n_ctx):
                which = min(v ^ k, 2)
                pieces[k][...] = three[:, which * inner : (which + 1) * inner]

    got = dot_nn(three[...], every[0 : 3 * inner, :]).astype(low)
    out_mine[...] = got[0:rows]
    out_other[...] = got[rows:]


def weight_grads(n_ctx, n_shard, idx, normed, mixed, *refs):
    pieces, outs_mine, refs = refs[:n_ctx], refs[n_ctx : 2 * n_ctx], refs[2 * n_ctx :]
    outs_rest, gain_one, gain_two = refs[:2], refs[2], refs[3]
    stack, grads, held, pieces_held, sems = refs[4:]
    s, c = idx[0], idx[1]
    rows = outs_mine[0].shape[0]
    length = n_ctx * rows
    r = stack.shape[2]
    inner = grads.shape[1]
    for j in range(n_shard):
        stack[wrap(j - s, n_shard), inner : inner + 1, :] = gain_one[j].astype(low)
        stack[wrap(j - s, n_shard), inner + 1 : inner + 2, :] = gain_two[j].astype(low)

    def fetch(moves):
        copies = [pltpu.make_async_copy(x, y, sems.at[i]) for i, (x, y) in enumerate(moves)]
        for copy in copies:
            copy.start()
        for copy in copies:
            copy.wait()

    def emit(got):
        for j in range(n_shard):
            stack[wrap(j - s, n_shard), 0:inner, :] = got[:, r * j : r * (j + 1)].astype(low)

    @pl.when(c != 3)
    def _():
        fetch([(normed, held)] + [(pieces[k], pieces_held.at[k]) for k in range(n_ctx)])
        for m in range(2):
            for k in range(n_ctx):
                at = (m * n_ctx + k) * rows
                grads[at : at + rows, :] = pieces_held[k, m * rows : (m + 1) * rows, :]
        emit(dot_tn(grads[...], held[...]))

    @pl.when(c == 3)
    def _():
        moves = [(mixed, grads)]
        for k in range(n_ctx):
            moves.append((outs_mine[k], held.at[k * rows : (k + 1) * rows, :]))
        moves.append((outs_rest[0], held.at[length : length + rows, :]))
        for k in range(1, n_ctx):
            at = length + k * rows
            moves.append((outs_rest[1].at[k - 1], held.at[at : at + rows, :]))
        fetch(moves)
        emit(dot_tn(grads[...], held[...]))


def place_outputs(idx, a_mine, a_other, b_mine, b_other, a, b):
    half = idx[2]
    a[half] = a_mine[...]
    a[1 - half] = a_other[...]
    b[half] = b_mine[...]
    b[1 - half] = b_other[...]


def norm_one_back(n_shard, idx, x_in, mine, got, grad, gains, out, gain_grad):
    r = gain_grad.shape[2]
    x = x_in[idx[2]].astype(wide)
    one = mine[...].astype(wide) + got[...].astype(wide)
    scale = lax.rsqrt(jnp.mean(x * x, axis=-1, keepdims=True) + norm_eps)
    u = one * gains[0:1, :]
    inner = jnp.mean(u * x, axis=-1, keepdims=True) * (scale * scale * scale)
    out[...] = (grad[...] + scale * u - x * inner).astype(low)
    total = jnp.sum(one * x * scale, axis=0, keepdims=True)
    for j in range(n_shard):
        gain_grad[j] = total[:, r * j : r * (j + 1)]


def produce(n_parts, *refs):
    parts, (middle, out) = refs[:n_parts], refs[n_parts:]
    out[...] = (middle[...] + sum((p[...].astype(wide) for p in parts))).astype(low)


def finish_wide(n_ctx, widths, which, idx, *refs):
    count = sum((n for _, n in which))
    sources, refs = refs[:count], refs[count:]
    outs, (stage, held, sems) = refs[-6:-3], refs[-3:]
    r = outs[0].shape[0]
    columns = sum(widths)
    parts, rows = wide_tiles(r, widths)
    span = held.shape[2]
    for v in range(n_ctx):
        start = min(((v ^ k) * columns for k, _ in which))

        @pl.when(idx[1] == v)
        def _(v=v, start=start):
            first = 0
            for k, pieces in which:
                size_each = rows // pieces
                for i, n in enumerate(widths):
                    for row, size, top, lane, lanes, at in parts[i]:
                        done = 0
                        while done < size:
                            part, here = divmod(row + done, size_each)
                            many = min(size - done, size_each - here)
                            stage[top + done : top + done + many, lane : lane + lanes] = sources[
                                first + part
                            ][here : here + many, at : at + lanes].astype(wide)
                            done += many
                    at = (v ^ k) * columns + sum(widths[:i]) - start
                    for j in range(3):
                        held[j, :, at : at + n] = stage[:, j * n : (j + 1) * n]
                first += pieces
            copies = [
                pltpu.make_async_copy(
                    held.at[j], outs[j].at[:, start : start + span], sems.at[j]
                )
                for j in range(3)
            ]
            for copy in copies:
                copy.start()
            for copy in copies:
                copy.wait()


def finish_attention(n_ctx, idx, *refs):
    pieces, (outs, gains) = refs[:n_ctx], (refs[n_ctx:-1], refs[-1])
    inner, r = outs[0].shape
    for v in range(n_ctx):

        @pl.when(idx[1] == v)
        def _(v=v):
            for k in range(n_ctx):
                outs[v ^ k][...] = pieces[k][0:inner, 0:r].astype(wide)

    gains[...] = sum((p[inner : inner + 2, 0:r].astype(wide) for p in pieces))


def on_device(
    inputs,
    cotangent,
    norm1_gain,
    w_query,
    w_key,
    w_value,
    w_out,
    norm2_gain,
    w_gate,
    w_up,
    w_down,
    bias_table,
):
    _, rows, width = inputs.shape
    shards, ctx = lax.axis_size("shard"), lax.axis_size("ctx")
    inner, r = w_out.shape
    heads = inner // DK
    length = ctx * rows
    columns = w_gate.shape[1] // ctx
    first_width = pl.cdiv(columns, 2 * LANES) * LANES
    widths = (first_width, columns - first_width)
    lanes_r = pl.cdiv(r, LANES) * LANES
    s, c, half = lax.axis_index("shard"), lax.axis_index("ctx"), lax.axis_index("tensor")
    idx = jnp.stack([s, c, half]).astype(jnp.int32)
    attention_weights = (w_query.T, w_key.T, w_value.T, w_out)


    wide_rows = wide_tiles(r, widths)[1]
    window = min(pl.cdiv(columns, LANES) * LANES, w_gate.shape[1])
    (packed,) = run(
        functools.partial(pack_wide, ctx, widths, window),
        "pack_wide",
        [((wide_rows, LANES), low)],
        [idx, w_gate, w_up, w_down.T],
        scratch=[
            pltpu.VMEM((r, 3 * max(widths)), low),
            pltpu.VMEM((3, r, window), low),
            pltpu.SemaphoreType.DMA((3,)),
        ],
        cost=2,
        far=3,
        vmem=60,
    )
    chunks = lax.all_gather(packed, "shard", axis=0, tiled=False)
    own_x = lax.dynamic_index_in_dim(inputs, half, 0, keepdims=False)
    (own_buf,) = run(
        functools.partial(pack_attention, ctx),
        "pack_attention",
        [((inner + 16, lanes_r), low)],
        [after(idx, packed), *attention_weights, jnp.stack([norm1_gain, norm2_gain])],
        scratch=[pltpu.VMEM((inner, r), low), pltpu.SemaphoreType.DMA],
        far=4,
        vmem=60,
    )
    from_shard = [step(own_buf, "shard", k) for k in range(1, shards)]
    mine_x = [swap(own_x, "ctx", k) for k in range(1, ctx)]
    table = lax.dynamic_slice_in_dim(bias_table, half * heads, heads, 1)
    (bias,) = run(
        functools.partial(bias_body, rows, rows // 5, distance_marks),
        "bias",
        [((heads, length, length), wide)],
        [after(idx, own_buf), table],
        scalars=2,
        cost=5,
    )
    now = after(idx, *from_shard, *mine_x, bias)

    group = jnp.concatenate(from_shard)
    buf_rows = inner + 16
    place = {z: [(0, (z - 1) * buf_rows, inner)] for z in range(1, shards)}
    gathered = [group] + [swap(after(group, now), "ctx", k) for k in range(1, ctx)]
    rest_x = swap(after(jnp.stack(mine_x), now), "tensor")
    normed_one, gains = run(
        functools.partial(norm_one, ctx, shards),
        "norm_one",
        [((2 * length, width), low), ((2, width), wide)],
        [now, inputs, *mine_x, rest_x, own_buf, *from_shard],
        scratch=[pltpu.VMEM((shards, 8, r), wide)],
        cost=3,
    )
    now = after(now, *gathered[1:], normed_one)

    own_cot = lax.dynamic_index_in_dim(cotangent, half, 0, keepdims=False)
    mine_cot = [swap(after(own_cot, now), "ctx", k) for k in range(1, ctx)]
    att_mine, att_other, soft, qkv, mixed, every = run(
        functools.partial(attend, ctx, shards, rows, heads, place),
        "attend",
        [
            ((length, width), low),
            ((length, width), low),
            ((2, heads, rows, length), wide),
            ((2 * length, 3 * inner), low),
            ((2 * length, inner), low),
            ((4 * inner, width), low),
        ],
        [now, normed_one, *attention_weights, bias, *gathered],
        scratch=[pltpu.VMEM((shards, 4 * inner, r), low)],
        cost=14,
        vmem=24,
    )
    now = after(now, *mine_cot, att_other)

    att_got = swap(after(att_other, now), "tensor")
    rest_cot = swap(after(jnp.stack(mine_cot), now), "tensor")
    nt_mine, middle_own = run(
        functools.partial(middle_norm, ctx),
        "middle_norm",
        [((length, width), low), ((rows, width), wide)],
        [now, inputs, *mine_x, att_mine, att_got, gains],
    )
    nt_other = swap(nt_mine, "tensor")
    now = after(now, nt_other, rest_cot)

    def add(a, b):
        return (a.astype(wide) + b.astype(wide)).astype(low)

    tokens_out = ((ctx, rows, width), low)
    wide_grads, feed_mine, feed_other, two_mine, two_other = run(
        functools.partial(feed_forward, ctx, shards, widths),
        "feed_forward",
        [((shards, wide_rows, LANES), low)] + [tokens_out] * 4,
        [now, chunks, nt_mine, nt_other, cotangent, *mine_cot, rest_cot],
        scratch=[
            pltpu.VMEM((shards, wide_rows, LANES), low),
            pltpu.VMEM((2 * length, width), low),
            pltpu.VMEM((2 * length, width), low),
            pltpu.VMEM((2, ctx, rows, width), low),
            pltpu.VMEM((2, ctx, rows, width), low),
            pltpu.SemaphoreType.DMA((3 + shards + 2 * ctx,)),
            pltpu.SemaphoreType.DMA((4 + shards * len(widths),)),
        ]
        + [pltpu.VMEM((width, 3 * n), low) for n in widths]
        + [pltpu.VMEM((2 * length, n), low) for n in widths]
        + [pltpu.VMEM((2 * length, 2 * n), low) for n in widths],
        far=5 + ctx - 1,
        far_out=True,
        cost=20,
        vmem=60,
    )
    wide_own = lax.psum_scatter(wide_grads, "shard", scatter_dimension=0, tiled=False)
    now = after(now, two_other)

    two_got = swap(after(two_other, now), "tensor")
    two_both = [add(two_mine[k], two_got[k]) for k in range(ctx)]
    two_parts = [two_both[0]] + [swap(two_both[k], "ctx", k) for k in range(1, ctx)]
    out_in, middle_grad, gain_two = run(
        functools.partial(norm_two_back, shards, ctx),
        "norm_two_back",
        [((rows, width), low), ((rows, width), wide), ((shards, 1, r), wide)],
        [now, cotangent, *two_parts, middle_own, gains],
    )
    out_in_other = swap(out_in, "tensor")
    now = after(now, out_in_other)

    feed_got = swap(after(feed_other, now), "tensor")
    got = run(
        functools.partial(attend_back, ctx, heads),
        "attend_back",
        [((2 * rows, 2 * inner), low)] * ctx + [((2 * rows, inner), low)],
        [out_in, out_in_other, soft, qkv, every],
        scalars=0,
        scratch=[pltpu.VMEM((2 * length, 2 * inner), low), pltpu.VMEM((2 * rows, inner), low)],
        cost=4,
        vmem=24,
    )
    kv_parts, q_grad = got[:ctx], got[ctx]
    now = after(now, feed_got, q_grad)

    kv_parts = [kv_parts[0]] + [swap(after(kv_parts[k], now), "ctx", k) for k in range(1, ctx)]
    outs_mine = [out_in] + [
        lax.ppermute(after(out_in, now), "ctx", [((ctx - 1) ^ k, ctx - 1)]) for k in range(1, ctx)
    ]
    feed_both = [add(feed_mine[k], feed_got[k]) for k in range(ctx)]
    got = run(
        functools.partial(first_grad, ctx),
        "first_grad",
        [((rows, width), low)] * 2 + [((2 * rows, inner), low)] * ctx,
        [now, *kv_parts, q_grad, every],
        scratch=[pltpu.VMEM((2 * rows, 3 * inner), low)],
    )
    first_mine, first_other, pieces = got[0], got[1], got[2:]
    now = after(now, first_other, *feed_both)

    pieces = [pieces[0]] + [swap(after(pieces[k], now), "ctx", k) for k in range(1, ctx)]
    first_got = swap(after(first_other, now), "tensor")
    input_mine, gain_one = run(
        functools.partial(norm_one_back, shards),
        "norm_one_back",
        [((rows, width), low), ((shards, 1, r), wide)],
        [now, inputs, first_mine, first_got, middle_grad, gains],
    )
    outs_rest = [out_in_other, swap(jnp.stack(outs_mine[1:]), "tensor")]
    now = after(now, *pieces[1:], input_mine, outs_rest[1])

    feed_parts = [feed_both[0]] + [swap(after(feed_both[k], now), "ctx", k) for k in range(1, ctx)]
    input_other = swap(after(input_mine, now), "tensor")
    (four,) = run(
        functools.partial(weight_grads, ctx, shards),
        "weight_grads",
        [((shards, inner + 16, r), low)],
        [now, normed_one, mixed, *pieces, *outs_mine, *outs_rest, gain_one, gain_two],
        scratch=[
            pltpu.VMEM((2 * length, inner), low),
            pltpu.VMEM((2 * length, width), low),
            pltpu.VMEM((ctx, 2 * rows, inner), low),
            pltpu.SemaphoreType.DMA((2 * ctx + 1,)),
        ],
        far=4 + 2 * ctx,
        cost=2,
        vmem=60,
    )
    (produced_mine,) = run(
        functools.partial(produce, ctx),
        "produce",
        [((rows, width), low)],
        [*feed_parts, middle_own],
        scalars=0,
    )
    now = after(now, produced_mine, four, input_other)

    four_shard = [four[0]] + [step(after(four[d], now), "shard", d) for d in range(1, shards)]
    produced_other = swap(after(produced_mine, now), "tensor")
    out_y, out_x = run(
        place_outputs,
        "place_outputs",
        [(inputs.shape, low)] * 2,
        [now, produced_mine, produced_other, input_mine, input_other],
    )
    now = after(now, wide_own, out_y)

    wide_own = after(wide_own, now)
    half_rows = wide_rows // 2
    pair = ctx == 4
    wide_all = [swap(wide_own, "ctx", k) for k in ((1, 2) if pair else range(1, ctx))]
    four_own = sum((part.astype(wide) for part in four_shard)).astype(low)
    four_all = [four_own] + [swap(after(four_own, now), "ctx", k) for k in range(1, ctx)]
    now = after(now, *wide_all, *four_all[1:])

    far_halves = []
    if pair:
        far_halves = [
            swap(after(wide_all[0], now)[:half_rows], "ctx", 2),
            swap(after(wide_all[1], now)[half_rows:], "ctx", 1),
        ]
    out_q, out_k, out_v, out_o, own_gain = run(
        functools.partial(finish_attention, ctx),
        "finish_attention",
        [((inner, r), wide)] * 4 + [((2, r), wide)],
        [now, *four_all],
    )
    own_gain = own_gain + swap(own_gain, "tensor")

    def finish(now, which, sources, span, before):
        return run(
            functools.partial(finish_wide, ctx, widths, which),
            "finish_wide",
            [(w_gate.shape, wide)] * 3,
            [now, *sources, *before],
            scratch=[
                pltpu.VMEM((r, 3 * max(widths)), wide),
                pltpu.VMEM((3, r, span), wide),
                pltpu.SemaphoreType.DMA((3,)),
            ],
            far_out=True,
            into=len(before),
            cost=3,
            vmem=24,
        )

    if pair and 2 * columns % LANES == 0:
        outs = finish(now, [(0, 1), (1, 1)], [wide_own, wide_all[0]], 2 * columns, [])
        now = after(now, *far_halves, outs[0], own_gain)
        outs = finish(now, [(2, 1), (3, 2)], [wide_all[1], *far_halves], 2 * columns, outs)
    else:
        which = [(k, 1) for k in range(ctx)]
        outs = finish(now, which, [wide_own, *wide_all], ctx * columns, [])
    out_g, out_u, out_d = outs

    return (
        out_y,
        out_x,
        own_gain[0],
        out_q.T,
        out_k.T,
        out_v.T,
        out_o,
        own_gain[1],
        out_g,
        out_u,
        out_d.T,
    )


def solution(mesh):
    placed = (
        P(None, ("shard", "ctx"), None),
        P(None, ("shard", "ctx"), None),
        P("shard"),
        P("shard", "tensor"),
        P("shard", "tensor"),
        P("shard", "tensor"),
        P("tensor", "shard"),
        P("shard"),
        P("shard", "tensor"),
        P("shard", "tensor"),
        P("tensor", "shard"),
        P(),
    )
    return jax.shard_map(
        on_device, mesh=mesh, in_specs=placed, out_specs=placed[:2] + placed[2:11], check_vma=False
    )
```

time: 293 us -> 246 us (0.84); the launches traced: 288 us -> 245 us
  waiting for transfers between devices: 130 us -> 104 us
  local copies, waits for them, and re-layouts: 16.3 us -> 4.81 us
    ppermute x42 -> x40, waiting for transfers between devices: 104 us -> 69 us  [swap(): return lax.ppermute(x, axis, [(i, i ^ k) for i in range(n)])]
    unnamed x81 -> x103, local copies, waits for them, and re-layouts: 14.3 us -> 4.02 us
    ppermute x9 -> x6, waiting for transfers between devices: 18 us -> 25.8 us  [step(): return lax.ppermute(x, axis, [(i, (i + k) % n) for i in range(n)])]
    all_gather x1, waiting for transfers between devices: 8.74 us -> 2.24 us  [on_device(): chunks = lax.all_gather(packed, 'shard', axis=0, tiled=False)]
    ppermute x0 -> x3, starting transfers between devices: none -> 5.11 us  [on_device(): lax.ppermute(after(out_in, now), 'ctx', [(ctx - 1 ^ k, ctx - 1)])]
    ppermute x9 -> x6, starting transfers between devices: 14.8 us -> 10.6 us  [step(): return lax.ppermute(x, axis, [(i, (i + k) % n) for i in range(n)])]
    reduce_scatter x1, waiting for transfers between devices: 0.01 us -> 3.59 us  [on_device(): lax.psum_scatter(wide_grads, 'shard', scatter_dimension=0, tiled=False)]
    ppermute x0 -> x3, waiting for transfers between devices: none -> 3 us  [on_device(): lax.ppermute(after(out_in, now), 'ctx', [(ctx - 1 ^ k, ctx - 1)])]
  transfers between devices with their start and end apart: 53 -> 51, of which waited for: 25 -> 25; matrix products, arithmetic and copies ran while one was open for 3% -> 2% of each run, Pallas kernels for 11% -> 16%
where the time goes in v4:
time: 246 us; the launch traced here: 245 us
  waiting for transfers between devices  104 us (42%)
  Pallas kernels  61.2 us (25%)
  starting transfers between devices  56.6 us (23%)
  between operations  14.8 us (6%)
  local copies, waits for them, and re-layouts  4.81 us (2%)
  other arithmetic  4.17 us (2%)
    ppermute x40, waiting for transfers between devices, swap(): return lax.ppermute(x, axis, [(i, i ^ k) for i in range(n)])  69 us
    pallas_call x17, Pallas kernels, run(): pl.pallas_call(body, name=name, out_shape=[jax.ShapeDtypeStruct(s, d) for...  61.2 us
    ppermute x40, starting transfers between devices, swap(): return lax.ppermute(x, axis, [(i, i ^ k) for i in range(n)])  40.9 us
    ppermute x6, waiting for transfers between devices, step(): return lax.ppermute(x, axis, [(i, (i + k) % n) for i in range(n)])  25.8 us
    ppermute x6, starting transfers between devices, step(): return lax.ppermute(x, axis, [(i, (i + k) % n) for i in range(n)])  10.6 us
    ppermute x3, starting transfers between devices, on_device(): lax.ppermute(after(out_in, now), 'ctx', [(ctx - 1 ^ k, ctx - 1)])  5.11 us
  transfers between devices with their start and end apart: 51, of which 25 were waited for; matrix products, arithmetic and copies ran while one was open for 2% of the time, Pallas kernels for 16%

profile of v4, /device:TPU:0, one launch (start us, length us, event | category | flops | bytes accessed | tf_op | source)
XLA Modules:
  0.0 245.3 jit_solution(6509581385794273382)
XLA Ops:
  7.9 3.3 %pack_wide.1 = bf16[3872,128]{1,0:T(8,128)(2,1)} custom-call(s32[3]{0:T(128)} %pad_add_fusion.idx, bf16[368,1792]{1,0:T(8,128)(2,1)} %w_g.1, bf16[368,1792]{1,0:T(8,128)(2,1)} %w_u.1, bf16[368,1792]{1,0:T(8,128)(2,1)} %bitcast.67), custom_call_target="tpu_custom_call" | custom-call | flops 200000000 | tf_op jit(solution)/shard_map/pack_wide/pallas_call | solution.py:37
  11.9 2.4 pack_attention.1.refs_4_
  14.3 5.1 %collective-permute-start.2 = (bf16[208,384]{1,0:T(8,128)(2,1)}, bf16[208,384]{1,0:T(8,128)(2,1)S(1)}, u32[]{:S(2)}, u32[]{:S(2)}) collective-permute-start(bf16[208,384]{1,0:T(8,128)(2,1)} %pack_attention.1.refs_4_), channel_id=1, source_target_pairs={{0,24},{8,0},{16,8},{24,16},{1,25},{9,1},{17,9},{25,17},{2,26},{10... | collective-permute-start | bytes 479240 | tf_op jit(solution)/shard_map/ppermute | solution.py:55
  19.4 2.9 %collective-permute-start.5 = (bf16[80,1472]{1,0:T(8,128)(2,1)S(1)}, bf16[80,1472]{1,0:T(8,128)(2,1)S(1)}, u32[]{:S(2)}, u32[]{:S(2)}) collective-permute-start(bf16[80,1472]{1,0:T(8,128)(2,1)S(1)} %dynamic-slice_bitcast_fusion.1), channel_id=1, source_target_pairs={{0,6},{2,4},{4,2},{6,0},{1,7},{3,5},{5,3},{7,1},{8,14},{10,12},{12... | collective-permute-start | bytes 706568 | tf_op jit(solution)/shard_map/ppermute | solution.py:60
  24.1 5.3 %bias.1 = f32[3,320,320]{2,1,0:T(8,128)S(1)} custom-call(s32[3]{0:T(128)S(1)} %copy-done.28, f32[32,3]{1,0:T(8,128)S(1)} %copy.27.table), custom_call_target="tpu_custom_call" | custom-call | flops 500000000 | tf_op jit(solution)/shard_map/bias/pallas_call | solution.py:37
  29.4 16.2 %collective-permute-done.1.refs_6_ = bf16[208,384]{1,0:T(8,128)(2,1)S(1)} collective-permute-done((bf16[208,384]{1,0:T(8,128)(2,1)}, bf16[208,384]{1,0:T(8,128)(2,1)S(1)}, u32[]{:S(2)}, u32[]{:S(2)}) %collective-permute-start.1) | collective-permute-done | bytes 159776 | tf_op jit(solution)/shard_map/ppermute | solution.py:55
  46.1 2.9 %collective-permute-start.8 = (bf16[624,384]{1,0:T(8,128)(2,1)S(1)}, bf16[624,384]{1,0:T(8,128)(2,1)S(1)}, u32[]{:S(2)}, u32[]{:S(2)}) collective-permute-start(bf16[624,384]{1,0:T(8,128)(2,1)S(1)} %constant_dynamic-update-slice_fusion.refs_0_), channel_id=1, source_target_pairs={{0,6},{2,4},{4,2},{6,0},{1,7},{3,5},{5,3},{7,1},{8,14},{10,12},{12... | collective-permute-start | bytes 1437704 | tf_op jit(solution)/shard_map/ppermute | solution.py:60
  51.0 9.8 %collective-permute-done.8.refs_3_ = bf16[624,384]{1,0:T(8,128)(2,1)S(1)} collective-permute-done((bf16[624,384]{1,0:T(8,128)(2,1)S(1)}, bf16[624,384]{1,0:T(8,128)(2,1)S(1)}, u32[]{:S(2)}, u32[]{:S(2)}) %collective-permute-start.8) | collective-permute-done | bytes 479264 | tf_op jit(solution)/shard_map/ppermute | solution.py:60
  60.9 10.0 %collective-permute-done.7.refs_2_ = bf16[624,384]{1,0:T(8,128)(2,1)S(1)} collective-permute-done((bf16[624,384]{1,0:T(8,128)(2,1)S(1)}, bf16[624,384]{1,0:T(8,128)(2,1)S(1)}, u32[]{:S(2)}, u32[]{:S(2)}) %collective-permute-start.7) | collective-permute-done | bytes 479264 | tf_op jit(solution)/shard_map/ppermute | solution.py:60
  70.9 1.9 collective-permute-start.12
  74.5 11.7 %attend.1 = (bf16[320,1472]{1,0:T(8,128)(2,1)S(1)}, bf16[320,1472]{1,0:T(8,128)(2,1)S(1)}, f32[2,3,80,320]{3,2,1,0:T(8,128)S(1)}, bf16[640,576]{1,0:T(8,128)(2,1...) custom-call(s32[3]{0:T(128)S(1)} %copy-done.28, bf16[640,1472]{1,0:T(8,128)(2,1)S(1)} %get-tuple-element.102.normed, ...), custom_call_target="tpu_custom_call" | custom-call | flops 1400000000 | tf_op jit(solution)/shard_map/attend/pallas_call | solution.py:37
  86.3 2.6 %collective-permute-done.13.refs_4_ = bf16[320,1472]{1,0:T(8,128)(2,1)S(1)} collective-permute-done((bf16[320,1472]{1,0:T(8,128)(2,1)S(1)}, bf16[320,1472]{1,0:T(8,128)(2,1)S(1)}, u32[]{:S(2)}, u32[]{:S(2)}) %collective-permute-start.13) | collective-permute-done | bytes 942112 | tf_op jit(solution)/shard_map/ppermute | solution.py:60
  92.6 2.9 %collective-permute-done.15.refs_3_ = bf16[3,80,1472]{2,1,0:T(8,128)(2,1)S(1)} collective-permute-done((bf16[3,80,1472]{2,1,0:T(8,128)(2,1)S(1)}, bf16[3,80,1472]{2,1,0:T(8,128)(2,1)S(1)}, u32[]{:S(2)}, u32[]{:S(2)}) %collective-permute-start.15) | collective-permute-done | bytes 706592 | tf_op jit(solution)/shard_map/ppermute | solution.py:60
  96.5 2.2 all-gather.3.cloned.1.call-done
  98.7 15.7 %feed_forward.1 = (bf16[4,3872,128]{2,1,0:T(8,128)(2,1)}, bf16[4,80,1472]{2,1,0:T(8,128)(2,1)}, bf16[4,80,1472]{2,1,0:T(8,128)(2,1)}, bf16[4,80,1472]{2,1,0:T(8,128)(2,1)}, bf16[4,80,1472]{2,1,0:T(8,128)(2,1)}) custom-call(s32[3]{0:T(128)} %pad_add_fusion.idx, bf16[4,3872,128]{2,1,0:T(8,128)(2,1)} %bitcast.65, bf16[320,1472]{1,0:T(8,128)(2,1)} %copy-done.15, ...), custom_call_target="tpu_custom_call" | custom-call | flops 2000000000 | tf_op jit(solution)/shard_map/feed_forward/pallas_call | solution.py:37
  114.6 2.7 %collective-permute-done.16 = bf16[4,80,1472]{2,1,0:T(8,128)(2,1)S(1)} collective-permute-done((bf16[4,80,1472]{2,1,0:T(8,128)(2,1)}, bf16[4,80,1472]{2,1,0:T(8,128)(2,1)S(1)}, u32[]{:S(2)}, u32[]{:S(2)}) %collective-permute-start.16) | collective-permute-done | bytes 942112 | tf_op jit(solution)/shard_map/ppermute | solution.py:60
  117.3 1.5 fusion.6
  118.9 2.9 %collective-permute-start.19 = (bf16[80,1472]{1,0:T(8,128)(2,1)S(1)}, bf16[80,1472]{1,0:T(8,128)(2,1)S(1)}, u32[]{:S(2)}, u32[]{:S(2)}) collective-permute-start(bf16[80,1472]{1,0:T(8,128)(2,1)S(1)} %get-tuple-element.189), channel_id=1, source_target_pairs={{0,6},{2,4},{4,2},{6,0},{1,7},{3,5},{5,3},{7,1},{8,14},{10,12},{12... | collective-permute-start | bytes 706568 | tf_op jit(solution)/shard_map/ppermute | solution.py:60
  122.4 6.2 %collective-permute-done.19.refs_3_ = bf16[80,1472]{1,0:T(8,128)(2,1)S(1)} collective-permute-done((bf16[80,1472]{1,0:T(8,128)(2,1)S(1)}, bf16[80,1472]{1,0:T(8,128)(2,1)S(1)}, u32[]{:S(2)}, u32[]{:S(2)}) %collective-permute-start.19) | collective-permute-done | bytes 235552 | tf_op jit(solution)/shard_map/ppermute | solution.py:60
  128.7 4.6 %collective-permute-done.18.refs_2_ = bf16[80,1472]{1,0:T(8,128)(2,1)S(1)} collective-permute-done((bf16[80,1472]{1,0:T(8,128)(2,1)S(1)}, bf16[80,1472]{1,0:T(8,128)(2,1)S(1)}, u32[]{:S(2)}, u32[]{:S(2)}) %collective-permute-start.18) | collective-permute-done | bytes 235552 | tf_op jit(solution)/shard_map/ppermute | solution.py:60
  135.1 1.4 collective-permute-done.20.o_other.refs_8_
  136.6 3.3 %attend_back.1 = (bf16[160,384]{1,0:T(8,128)(2,1)S(1)}, bf16[160,384]{1,0:T(8,128)(2,1)S(1)}, bf16[160,384]{1,0:T(8,128)(2,1)S(1)}, bf16[160,384]{1,0:T(8,128)(2,1)S(1)}, bf16[160,192]{1,0:T(8,128)(2,1)S(1)}) custom-call(bf16[80,1472]{1,0:T(8,128)(2,1)S(1)} %get-tuple-element.147.o_mine.refs_4_, ...), custom_call_target="tpu_custom_call" | custom-call | flops 400000000 | tf_op jit(solution)/shard_map/attend_back/pallas_call | solution.py:37
  140.0 3.8 %collective-permute-start.31 = (bf16[80,1472]{1,0:T(8,128)(2,1)S(1)}, bf16[80,1472]{1,0:T(8,128)(2,1)S(1)}, u32[]{:S(2)}, u32[]{:S(2)}) collective-permute-start(bf16[80,1472]{1,0:T(8,128)(2,1)S(1)} %get-tuple-element.147.o_mine.refs_4_), channel_id=1, source_target_pairs={{0,6},{1,7},{8,14},{9,15},{16,22},{17,23},{24,30},{25,31}} | collective-permute-start | bytes 706568 | tf_op jit(solution)/shard_map/ppermute | solution.py:704
  147.0 3.0 %collective-permute-done.31.refs_7_ = bf16[80,1472]{1,0:T(8,128)(2,1)S(1)} collective-permute-done((bf16[80,1472]{1,0:T(8,128)(2,1)S(1)}, bf16[80,1472]{1,0:T(8,128)(2,1)S(1)}, u32[]{:S(2)}, u32[]{:S(2)}) %collective-permute-start.31) | collective-permute-done | bytes 235552 | tf_op jit(solution)/shard_map/ppermute | solution.py:704
  150.0 3.4 %collective-permute-start.24 = (bf16[160,384]{1,0:T(8,128)(2,1)S(1)}, bf16[160,384]{1,0:T(8,128)(2,1)S(1)}, u32[]{:S(2)}, u32[]{:S(2)}) collective-permute-start(bf16[160,384]{1,0:T(8,128)(2,1)S(1)} %get-tuple-element.133), channel_id=1, source_target_pairs={{0,6},{2,4},{4,2},{6,0},{1,7},{3,5},{5,3},{7,1},{8,14},{10,12},{12... | collective-permute-start | bytes 368648 | tf_op jit(solution)/shard_map/ppermute | solution.py:60
  157.7 5.3 %collective-permute-start.25 = (bf16[160,192]{1,0:T(8,128)(2,1)S(1)}, bf16[160,192]{1,0:T(8,128)(2,1)S(1)}, u32[]{:S(2)}, u32[]{:S(2)}) collective-permute-start(bf16[160,192]{1,0:T(8,128)(2,1)S(1)} %get-tuple-element.138), channel_id=1, source_target_pairs={{0,2},{2,0},{4,6},{6,4},{1,3},{3,1},{5,7},{7,5},{8,10},{10,8},{12,... | collective-permute-start | bytes 184328 | tf_op jit(solution)/shard_map/ppermute | solution.py:60
  163.0 2.5 %collective-permute-start.26 = (bf16[160,192]{1,0:T(8,128)(2,1)S(1)}, bf16[160,192]{1,0:T(8,128)(2,1)S(1)}, u32[]{:S(2)}, u32[]{:S(2)}) collective-permute-start(bf16[160,192]{1,0:T(8,128)(2,1)S(1)} %get-tuple-element.140), channel_id=1, source_target_pairs={{0,4},{2,6},{4,0},{6,2},{1,5},{3,7},{5,1},{7,3},{8,12},{10,14},{12... | collective-permute-start | bytes 184328 | tf_op jit(solution)/shard_map/ppermute | solution.py:60
  166.5 2.8 %collective-permute-done.26.refs_2_ = bf16[160,192]{1,0:T(8,128)(2,1)S(1)} collective-permute-done((bf16[160,192]{1,0:T(8,128)(2,1)S(1)}, bf16[160,192]{1,0:T(8,128)(2,1)S(1)}, u32[]{:S(2)}, u32[]{:S(2)}) %collective-permute-start.26) | collective-permute-done | bytes 61472 | tf_op jit(solution)/shard_map/ppermute | solution.py:60
  169.2 1.6 collective-permute-done.27.refs_3_
  172.1 2.3 collective-permute-start.35
  174.5 4.0 %weight_grads.1 = bf16[4,208,368]{2,1,0:T(8,128)(2,1)} custom-call(s32[3]{0:T(128)} %pad_add_fusion.idx, bf16[640,1472]{1,0:T(8,128)(2,1)} %copy-done.2, bf16[640,192]{1,0:T(8,128)(2,1)} %copy-done.27, bf16[160,192]{1,0:T(8,128)(2,1)} %copy-done.31, bf16[160,192]{1,0:T(8,128)(2,1)} %copy-done.44, bf16[160,192]{1,0:T(8,128)(2,1)} %copy-done.45, ...), custom_call_target="tpu_custom_call" | custom-call | flops 200000000 | tf_op jit(solution)/shard_map/weight_grads/pallas_call | solution.py:37
  178.5 1.5 collective-permute-done.33.refs_1_
  180.0 4.1 %collective-permute-done.34.refs_2_ = bf16[80,1472]{1,0:T(8,128)(2,1)S(1)} collective-permute-done((bf16[80,1472]{1,0:T(8,128)(2,1)}, bf16[80,1472]{1,0:T(8,128)(2,1)S(1)}, u32[]{:S(2)}, u32[]{:S(2)}) %collective-permute-start.34) | collective-permute-done | bytes 235552 | tf_op jit(solution)/shard_map/ppermute | solution.py:60
  184.3 1.5 collective-permute-done.37.a_other
  185.9 1.5 place_outputs.1
  187.4 3.6 %reduce-scatter.2.cloned.1.call-done = bf16[1,3872,128]{2,1,0:T(8,128)(2,1)} async-done(((bf16[4,3872,128]{2,1,0:T(8,128)(2,1)}), bf16[1,3872,128]{2,1,0:T(8,128)(2,1)}) %reduce-scatter.2.cloned.1.call-update) | async-done | bytes 991248 | tf_op jit(solution)/shard_map/reduce_scatter | solution.py:673
  191.0 1.5 collective-permute-start.39
  192.4 1.5 collective-permute-start.38
  194.0 2.8 %collective-permute-start.41 = (bf16[208,368]{1,0:T(8,128)(2,1)S(1)}, bf16[208,368]{1,0:T(8,128)(2,1)S(1)}, u32[]{:S(2)}, u32[]{:S(2)}) collective-permute-start(bf16[208,368]{1,0:T(8,128)(2,1)S(1)} %get-tuple-element.165), channel_id=1, source_target_pairs={{0,16},{8,24},{16,0},{24,8},{1,17},{9,25},{17,1},{25,9},{2,18},{10... | collective-permute-start | bytes 459272 | tf_op jit(solution)/shard_map/ppermute | solution.py:55
  198.9 9.2 %collective-permute-done.41 = bf16[208,368]{1,0:T(8,128)(2,1)S(1)} collective-permute-done((bf16[208,368]{1,0:T(8,128)(2,1)S(1)}, bf16[208,368]{1,0:T(8,128)(2,1)S(1)}, u32[]{:S(2)}, u32[]{:S(2)}) %collective-permute-start.41) | collective-permute-done | bytes 153120 | tf_op jit(solution)/shard_map/ppermute | solution.py:55
  208.8 1.5 collective-permute-start.44
  210.3 1.5 collective-permute-start.43
  211.7 9.2 %collective-permute-done.45.refs_3_ = bf16[208,368]{1,0:T(8,128)(2,1)S(1)} collective-permute-done((bf16[208,368]{1,0:T(8,128)(2,1)S(1)}, bf16[208,368]{1,0:T(8,128)(2,1)S(1)}, u32[]{:S(2)}, u32[]{:S(2)}) %collective-permute-start.45) | collective-permute-done | bytes 153120 | tf_op jit(solution)/shard_map/ppermute | solution.py:60
  222.6 1.5 collective-permute-start.48
  224.7 1.7 finish_attention.1
  226.4 3.1 %finish_wide.2 = (f32[368,1792]{1,0:T(8,128)}, f32[368,1792]{1,0:T(8,128)}, f32[368,1792]{1,0:T(8,128)}) custom-call(s32[3]{0:T(128)S(1)} %copy-done.30, bf16[3872,128]{1,0:T(8,128)(2,1)S(1)} %bitcast.58, bf16[3872,128]{1,0:T(8,128)(2,1)S(1)} %collective-permute-done.38.refs_1_), custom_call_target="tpu_custom_call" | custom-call | flops 300000000 | tf_op jit(solution)/shard_map/finish_wide/pallas_call | solution.py:37
  230.1 4.1 %collective-permute-done.48.refs_2_ = bf16[1936,128]{1,0:T(8,128)(2,1)S(1)} collective-permute-done((bf16[1936,128]{1,0:T(8,128)(2,1)S(1)}, bf16[1936,128]{1,0:T(8,128)(2,1)S(1)}, u32[]{:S(2)}, u32[]{:S(2)}) %collective-permute-start.48) | collective-permute-done | bytes 495648 | tf_op jit(solution)/shard_map/ppermute | solution.py:60
  235.4 3.1 %finish_wide.3 = (f32[368,1792]{1,0:T(8,128)}, f32[368,1792]{1,0:T(8,128)}, f32[368,1792]{1,0:T(8,128)}) custom-call(s32[3]{0:T(128)S(1)} %copy-done.30, bf16[3872,128]{1,0:T(8,128)(2,1)S(1)} %collective-permute-done.39.refs_0_, bf16[1936,128]{1,0:T(8,128)(2,1)S(1)} %collective-permute-done.47.refs_1_, ...), custom_call_target="tpu_custom_call", output_to_operand_aliasing={{0}: (4, {}), {1}: (5, {}), {2}: (6, {})} | custom-call | flops 300000000 | tf_op jit(solution)/shard_map/finish_wide/pallas_call | solution.py:37
  (195 shorter events, 31.3 us)
Async XLA Ops:
  7.2 91.5 %all-gather.3.cloned.1.call-start = ((), (), s32[]{:S(2)}) async-start(), calls=%async_computation.2 | async-start | bytes 4956160 | tf_op jit(solution)/shard_map/all_gather | solution.py:577
  11.2 179.8 %reduce-scatter.2.cloned.1.call-start = ((), (), s32[]{:S(2)}) async-start(), calls=%async_computation.1 | async-start | bytes 4956160 | tf_op jit(solution)/shard_map/reduce_scatter | solution.py:673
  14.3 9.1 %collective-permute-start.2 = (bf16[208,384]{1,0:T(8,128)(2,1)}, bf16[208,384]{1,0:T(8,128)(2,1)S(1)}, u32[]{:S(2)}, u32[]{:S(2)}) collective-permute-start(bf16[208,384]{1,0:T(8,128)(2,1)} %pack_attention.1.refs_4_), channel_id=1, source_target_pairs={{0,24},{8,0},{16,8},{24,16},{1,25},{9,1},{17,9},{25,17},{2,26},{10... | collective-permute-start | bytes 479240 | tf_op jit(solution)/shard_map/ppermute | solution.py:55
  19.4 26.3 %collective-permute-start.5 = (bf16[80,1472]{1,0:T(8,128)(2,1)S(1)}, bf16[80,1472]{1,0:T(8,128)(2,1)S(1)}, u32[]{:S(2)}, u32[]{:S(2)}) collective-permute-start(bf16[80,1472]{1,0:T(8,128)(2,1)S(1)} %dynamic-slice_bitcast_fusion.1), channel_id=1, source_target_pairs={{0,6},{2,4},{4,2},{6,0},{1,7},{3,5},{5,3},{7,1},{8,14},{10,12},{12... | collective-permute-start | bytes 706568 | tf_op jit(solution)/shard_map/ppermute | solution.py:60
  22.4 23.3 %collective-permute-start.4 = (bf16[80,1472]{1,0:T(8,128)(2,1)S(1)}, bf16[80,1472]{1,0:T(8,128)(2,1)S(1)}, u32[]{:S(2)}, u32[]{:S(2)}) collective-permute-start(bf16[80,1472]{1,0:T(8,128)(2,1)S(1)} %dynamic-slice_bitcast_fusion.1), channel_id=1, source_target_pairs={{0,4},{2,6},{4,0},{6,2},{1,5},{3,7},{5,1},{7,3},{8,12},{10,14},{12... | collective-permute-start | bytes 706568 | tf_op jit(solution)/shard_map/ppermute | solution.py:60
  22.9 22.9 %collective-permute-start.3 = (bf16[80,1472]{1,0:T(8,128)(2,1)S(1)}, bf16[80,1472]{1,0:T(8,128)(2,1)S(1)}, u32[]{:S(2)}, u32[]{:S(2)}) collective-permute-start(bf16[80,1472]{1,0:T(8,128)(2,1)S(1)} %dynamic-slice_bitcast_fusion.1), channel_id=1, source_target_pairs={{0,2},{2,0},{4,6},{6,4},{1,3},{3,1},{5,7},{7,5},{8,10},{10,8},{12,... | collective-permute-start | bytes 706568 | tf_op jit(solution)/shard_map/ppermute | solution.py:60
  23.0 22.7 %collective-permute-start.1 = (bf16[208,384]{1,0:T(8,128)(2,1)}, bf16[208,384]{1,0:T(8,128)(2,1)S(1)}, u32[]{:S(2)}, u32[]{:S(2)}) collective-permute-start(bf16[208,384]{1,0:T(8,128)(2,1)} %pack_attention.1.refs_4_), channel_id=1, source_target_pairs={{0,16},{8,24},{16,0},{24,8},{1,17},{9,25},{17,1},{25,9},{2,18},{10... | collective-permute-start | bytes 479240 | tf_op jit(solution)/shard_map/ppermute | solution.py:55
  23.4 22.3 %collective-permute-start = (bf16[208,384]{1,0:T(8,128)(2,1)}, bf16[208,384]{1,0:T(8,128)(2,1)S(1)}, u32[]{:S(2)}, u32[]{:S(2)}) collective-permute-start(bf16[208,384]{1,0:T(8,128)(2,1)} %pack_attention.1.refs_4_), channel_id=1, source_target_pairs={{0,8},{8,16},{16,24},{24,0},{1,9},{9,17},{17,25},{25,1},{2,10},{10... | collective-permute-start | bytes 479240 | tf_op jit(solution)/shard_map/ppermute | solution.py:55
  45.9 3.8 %collective-permute-start.9 = (bf16[3,80,1472]{2,1,0:T(8,128)(2,1)S(1)}, bf16[3,80,1472]{2,1,0:T(8,128)(2,1)S(1)}, u32[]{:S(2)}, u32[]{:S(2)}) collective-permute-start(bf16[3,80,1472]{2,1,0:T(8,128)(2,1)S(1)} %pad_maximum_fusion), channel_id=1, source_target_pairs={{0,1},{1,0},{2,3},{3,2},{4,5},{5,4},{6,7},{7,6},{8,9},{9,8},{10,11... | collective-permute-start | bytes 2119688 | tf_op jit(solution)/shard_map/ppermute | solution.py:60
  46.1 14.8 %collective-permute-start.8 = (bf16[624,384]{1,0:T(8,128)(2,1)S(1)}, bf16[624,384]{1,0:T(8,128)(2,1)S(1)}, u32[]{:S(2)}, u32[]{:S(2)}) collective-permute-start(bf16[624,384]{1,0:T(8,128)(2,1)S(1)} %constant_dynamic-update-slice_fusion.refs_0_), channel_id=1, source_target_pairs={{0,6},{2,4},{4,2},{6,0},{1,7},{3,5},{5,3},{7,1},{8,14},{10,12},{12... | collective-permute-start | bytes 1437704 | tf_op jit(solution)/shard_map/ppermute | solution.py:60
  49.0 21.9 %collective-permute-start.7 = (bf16[624,384]{1,0:T(8,128)(2,1)S(1)}, bf16[624,384]{1,0:T(8,128)(2,1)S(1)}, u32[]{:S(2)}, u32[]{:S(2)}) collective-permute-start(bf16[624,384]{1,0:T(8,128)(2,1)S(1)} %constant_dynamic-update-slice_fusion.refs_0_), channel_id=1, source_target_pairs={{0,4},{2,6},{4,0},{6,2},{1,5},{3,7},{5,1},{7,3},{8,12},{10,14},{12... | collective-permute-start | bytes 1437704 | tf_op jit(solution)/shard_map/ppermute | solution.py:60
  49.5 21.4 %collective-permute-start.6 = (bf16[624,384]{1,0:T(8,128)(2,1)S(1)}, bf16[624,384]{1,0:T(8,128)(2,1)S(1)}, u32[]{:S(2)}, u32[]{:S(2)}) collective-permute-start(bf16[624,384]{1,0:T(8,128)(2,1)S(1)} %constant_dynamic-update-slice_fusion.refs_0_), channel_id=1, source_target_pairs={{0,2},{2,0},{4,6},{6,4},{1,3},{3,1},{5,7},{7,5},{8,10},{10,8},{12,... | collective-permute-start | bytes 1437704 | tf_op jit(solution)/shard_map/ppermute | solution.py:60
  70.9 15.3 %collective-permute-start.12 = (bf16[80,1472]{1,0:T(8,128)(2,1)S(1)}, bf16[80,1472]{1,0:T(8,128)(2,1)S(1)}, u32[]{:S(2)}, u32[]{:S(2)}) collective-permute-start(bf16[80,1472]{1,0:T(8,128)(2,1)S(1)} %dynamic-slice_bitcast_fusion), channel_id=1, source_target_pairs={{0,6},{2,4},{4,2},{6,0},{1,7},{3,5},{5,3},{7,1},{8,14},{10,12},{12... | collective-permute-start | bytes 706568 | tf_op jit(solution)/shard_map/ppermute | solution.py:60
  72.8 13.4 %collective-permute-start.11 = (bf16[80,1472]{1,0:T(8,128)(2,1)S(1)}, bf16[80,1472]{1,0:T(8,128)(2,1)S(1)}, u32[]{:S(2)}, u32[]{:S(2)}) collective-permute-start(bf16[80,1472]{1,0:T(8,128)(2,1)S(1)} %dynamic-slice_bitcast_fusion), channel_id=1, source_target_pairs={{0,4},{2,6},{4,0},{6,2},{1,5},{3,7},{5,1},{7,3},{8,12},{10,14},{12... | collective-permute-start | bytes 706568 | tf_op jit(solution)/shard_map/ppermute | solution.py:60
  74.1 12.1 %collective-permute-start.10 = (bf16[80,1472]{1,0:T(8,128)(2,1)S(1)}, bf16[80,1472]{1,0:T(8,128)(2,1)S(1)}, u32[]{:S(2)}, u32[]{:S(2)}) collective-permute-start(bf16[80,1472]{1,0:T(8,128)(2,1)S(1)} %dynamic-slice_bitcast_fusion), channel_id=1, source_target_pairs={{0,2},{2,0},{4,6},{6,4},{1,3},{3,1},{5,7},{7,5},{8,10},{10,8},{12,... | collective-permute-start | bytes 706568 | tf_op jit(solution)/shard_map/ppermute | solution.py:60
  92.0 4.5 %collective-permute-start.14 = (bf16[320,1472]{1,0:T(8,128)(2,1)S(1)}, bf16[320,1472]{1,0:T(8,128)(2,1)}, u32[]{:S(2)}, u32[]{:S(2)}) collective-permute-start(bf16[320,1472]{1,0:T(8,128)(2,1)S(1)} %get-tuple-element.110.nt_mine), channel_id=1, source_target_pairs={{0,1},{1,0},{2,3},{3,2},{4,5},{5,4},{6,7},{7,6},{8,9},{9,8},{10,11... | collective-permute-start | bytes 2826248 | tf_op jit(solution)/shard_map/ppermute | solution.py:60
  92.2 3.4 %collective-permute-start.15 = (bf16[3,80,1472]{2,1,0:T(8,128)(2,1)S(1)}, bf16[3,80,1472]{2,1,0:T(8,128)(2,1)S(1)}, u32[]{:S(2)}, u32[]{:S(2)}) collective-permute-start(bf16[3,80,1472]{2,1,0:T(8,128)(2,1)S(1)} %pad_maximum_fusion.1), channel_id=1, source_target_pairs={{0,1},{1,0},{2,3},{3,2},{4,5},{5,4},{6,7},{7,6},{8,9},{9,8},{10,11... | collective-permute-start | bytes 2119688 | tf_op jit(solution)/shard_map/ppermute | solution.py:60
  114.5 2.8 %collective-permute-start.16 = (bf16[4,80,1472]{2,1,0:T(8,128)(2,1)}, bf16[4,80,1472]{2,1,0:T(8,128)(2,1)S(1)}, u32[]{:S(2)}, u32[]{:S(2)}) collective-permute-start(bf16[4,80,1472]{2,1,0:T(8,128)(2,1)} %get-tuple-element.116), channel_id=1, source_target_pairs={{0,1},{1,0},{2,3},{3,2},{4,5},{5,4},{6,7},{7,6},{8,9},{9,8},{10,11... | collective-permute-start | bytes 2826248 | tf_op jit(solution)/shard_map/ppermute | solution.py:60
  118.9 9.8 %collective-permute-start.19 = (bf16[80,1472]{1,0:T(8,128)(2,1)S(1)}, bf16[80,1472]{1,0:T(8,128)(2,1)S(1)}, u32[]{:S(2)}, u32[]{:S(2)}) collective-permute-start(bf16[80,1472]{1,0:T(8,128)(2,1)S(1)} %get-tuple-element.189), channel_id=1, source_target_pairs={{0,6},{2,4},{4,2},{6,0},{1,7},{3,5},{5,3},{7,1},{8,14},{10,12},{12... | collective-permute-start | bytes 706568 | tf_op jit(solution)/shard_map/ppermute | solution.py:60
  121.8 11.5 %collective-permute-start.18 = (bf16[80,1472]{1,0:T(8,128)(2,1)S(1)}, bf16[80,1472]{1,0:T(8,128)(2,1)S(1)}, u32[]{:S(2)}, u32[]{:S(2)}) collective-permute-start(bf16[80,1472]{1,0:T(8,128)(2,1)S(1)} %get-tuple-element.190), channel_id=1, source_target_pairs={{0,4},{2,6},{4,0},{6,2},{1,5},{3,7},{5,1},{7,3},{8,12},{10,14},{12... | collective-permute-start | bytes 706568 | tf_op jit(solution)/shard_map/ppermute | solution.py:60
  122.3 11.1 %collective-permute-start.17 = (bf16[80,1472]{1,0:T(8,128)(2,1)S(1)}, bf16[80,1472]{1,0:T(8,128)(2,1)S(1)}, u32[]{:S(2)}, u32[]{:S(2)}) collective-permute-start(bf16[80,1472]{1,0:T(8,128)(2,1)S(1)} %get-tuple-element.191), channel_id=1, source_target_pairs={{0,2},{2,0},{4,6},{6,4},{1,3},{3,1},{5,7},{7,5},{8,10},{10,8},{12,... | collective-permute-start | bytes 706568 | tf_op jit(solution)/shard_map/ppermute | solution.py:60
  136.5 3.5 %collective-permute-start.21 = (bf16[4,80,1472]{2,1,0:T(8,128)(2,1)S(1)}, bf16[4,80,1472]{2,1,0:T(8,128)(2,1)S(1)}, u32[]{:S(2)}, u32[]{:S(2)}) collective-permute-start(bf16[4,80,1472]{2,1,0:T(8,128)(2,1)S(1)} %copy-done.49), channel_id=1, source_target_pairs={{0,1},{1,0},{2,3},{3,2},{4,5},{5,4},{6,7},{7,6},{8,9},{9,8},{10,11... | collective-permute-start | bytes 2826248 | tf_op jit(solution)/shard_map/ppermute | solution.py:60
  140.0 10.1 %collective-permute-start.31 = (bf16[80,1472]{1,0:T(8,128)(2,1)S(1)}, bf16[80,1472]{1,0:T(8,128)(2,1)S(1)}, u32[]{:S(2)}, u32[]{:S(2)}) collective-permute-start(bf16[80,1472]{1,0:T(8,128)(2,1)S(1)} %get-tuple-element.147.o_mine.refs_4_), channel_id=1, source_target_pairs={{0,6},{1,7},{8,14},{9,15},{16,22},{17,23},{24,30},{25,31}} | collective-permute-start | bytes 706568 | tf_op jit(solution)/shard_map/ppermute | solution.py:704
  143.7 9.7 %collective-permute-start.30 = (bf16[80,1472]{1,0:T(8,128)(2,1)S(1)}, bf16[80,1472]{1,0:T(8,128)(2,1)S(1)}, u32[]{:S(2)}, u32[]{:S(2)}) collective-permute-start(bf16[80,1472]{1,0:T(8,128)(2,1)S(1)} %get-tuple-element.147.o_mine.refs_4_), channel_id=1, source_target_pairs={{2,6},{3,7},{10,14},{11,15},{18,22},{19,23},{26,30},{27,31}} | collective-permute-start | bytes 706568 | tf_op jit(solution)/shard_map/ppermute | solution.py:704
  144.4 9.0 %collective-permute-start.29 = (bf16[80,1472]{1,0:T(8,128)(2,1)S(1)}, bf16[80,1472]{1,0:T(8,128)(2,1)S(1)}, u32[]{:S(2)}, u32[]{:S(2)}) collective-permute-start(bf16[80,1472]{1,0:T(8,128)(2,1)S(1)} %get-tuple-element.147.o_mine.refs_4_), channel_id=1, source_target_pairs={{4,6},{5,7},{12,14},{13,15},{20,22},{21,23},{28,30},{29,31}} | collective-permute-start | bytes 706568 | tf_op jit(solution)/shard_map/ppermute | solution.py:704
  145.1 10.1 %collective-permute-start.22 = (bf16[160,384]{1,0:T(8,128)(2,1)S(1)}, bf16[160,384]{1,0:T(8,128)(2,1)S(1)}, u32[]{:S(2)}, u32[]{:S(2)}) collective-permute-start(bf16[160,384]{1,0:T(8,128)(2,1)S(1)} %get-tuple-element.129), channel_id=1, source_target_pairs={{0,2},{2,0},{4,6},{6,4},{1,3},{3,1},{5,7},{7,5},{8,10},{10,8},{12,... | collective-permute-start | bytes 368648 | tf_op jit(solution)/shard_map/ppermute | solution.py:60
  146.4 8.8 %collective-permute-start.23 = (bf16[160,384]{1,0:T(8,128)(2,1)S(1)}, bf16[160,384]{1,0:T(8,128)(2,1)S(1)}, u32[]{:S(2)}, u32[]{:S(2)}) collective-permute-start(bf16[160,384]{1,0:T(8,128)(2,1)S(1)} %get-tuple-element.131), channel_id=1, source_target_pairs={{0,4},{2,6},{4,0},{6,2},{1,5},{3,7},{5,1},{7,3},{8,12},{10,14},{12... | collective-permute-start | bytes 368648 | tf_op jit(solution)/shard_map/ppermute | solution.py:60
  150.0 6.2 %collective-permute-start.24 = (bf16[160,384]{1,0:T(8,128)(2,1)S(1)}, bf16[160,384]{1,0:T(8,128)(2,1)S(1)}, u32[]{:S(2)}, u32[]{:S(2)}) collective-permute-start(bf16[160,384]{1,0:T(8,128)(2,1)S(1)} %get-tuple-element.133), channel_id=1, source_target_pairs={{0,6},{2,4},{4,2},{6,0},{1,7},{3,5},{5,3},{7,1},{8,14},{10,12},{12... | collective-permute-start | bytes 368648 | tf_op jit(solution)/shard_map/ppermute | solution.py:60
  153.6 17.3 %collective-permute-start.32 = (bf16[3,80,1472]{2,1,0:T(8,128)(2,1)S(1)}, bf16[3,80,1472]{2,1,0:T(8,128)(2,1)S(1)}, u32[]{:S(2)}, u32[]{:S(2)}) collective-permute-start(bf16[3,80,1472]{2,1,0:T(8,128)(2,1)S(1)} %pad_maximum_fusion.2), channel_id=1, source_target_pairs={{0,1},{1,0},{2,3},{3,2},{4,5},{5,4},{6,7},{7,6},{8,9},{9,8},{10,11... | collective-permute-start | bytes 2119688 | tf_op jit(solution)/shard_map/ppermute | solution.py:60
  157.6 7.9 %collective-permute-start.28 = (bf16[80,1472]{1,0:T(8,128)(2,1)S(1)}, bf16[80,1472]{1,0:T(8,128)(2,1)S(1)}, u32[]{:S(2)}, u32[]{:S(2)}) collective-permute-start(bf16[80,1472]{1,0:T(8,128)(2,1)S(1)} %get-tuple-element.144), channel_id=1, source_target_pairs={{0,1},{1,0},{2,3},{3,2},{4,5},{5,4},{6,7},{7,6},{8,9},{9,8},{10,11... | collective-permute-start | bytes 706568 | tf_op jit(solution)/shard_map/ppermute | solution.py:60
  157.7 8.8 %collective-permute-start.25 = (bf16[160,192]{1,0:T(8,128)(2,1)S(1)}, bf16[160,192]{1,0:T(8,128)(2,1)S(1)}, u32[]{:S(2)}, u32[]{:S(2)}) collective-permute-start(bf16[160,192]{1,0:T(8,128)(2,1)S(1)} %get-tuple-element.138), channel_id=1, source_target_pairs={{0,2},{2,0},{4,6},{6,4},{1,3},{3,1},{5,7},{7,5},{8,10},{10,8},{12,... | collective-permute-start | bytes 184328 | tf_op jit(solution)/shard_map/ppermute | solution.py:60
  163.0 6.3 %collective-permute-start.26 = (bf16[160,192]{1,0:T(8,128)(2,1)S(1)}, bf16[160,192]{1,0:T(8,128)(2,1)S(1)}, u32[]{:S(2)}, u32[]{:S(2)}) collective-permute-start(bf16[160,192]{1,0:T(8,128)(2,1)S(1)} %get-tuple-element.140), channel_id=1, source_target_pairs={{0,4},{2,6},{4,0},{6,2},{1,5},{3,7},{5,1},{7,3},{8,12},{10,14},{12... | collective-permute-start | bytes 184328 | tf_op jit(solution)/shard_map/ppermute | solution.py:60
  165.5 5.3 %collective-permute-start.27 = (bf16[160,192]{1,0:T(8,128)(2,1)S(1)}, bf16[160,192]{1,0:T(8,128)(2,1)S(1)}, u32[]{:S(2)}, u32[]{:S(2)}) collective-permute-start(bf16[160,192]{1,0:T(8,128)(2,1)S(1)} %get-tuple-element.142), channel_id=1, source_target_pairs={{0,6},{2,4},{4,2},{6,0},{1,7},{3,5},{5,3},{7,1},{8,14},{10,12},{12... | collective-permute-start | bytes 184328 | tf_op jit(solution)/shard_map/ppermute | solution.py:60
  170.9 9.2 %collective-permute-start.33 = (bf16[80,1472]{1,0:T(8,128)(2,1)}, bf16[80,1472]{1,0:T(8,128)(2,1)S(1)}, u32[]{:S(2)}, u32[]{:S(2)}) collective-permute-start(bf16[80,1472]{1,0:T(8,128)(2,1)} %get-tuple-element.149), channel_id=1, source_target_pairs={{0,2},{2,0},{4,6},{6,4},{1,3},{3,1},{5,7},{7,5},{8,10},{10,8},{12,... | collective-permute-start | bytes 706568 | tf_op jit(solution)/shard_map/ppermute | solution.py:60
  171.5 12.6 %collective-permute-start.34 = (bf16[80,1472]{1,0:T(8,128)(2,1)}, bf16[80,1472]{1,0:T(8,128)(2,1)S(1)}, u32[]{:S(2)}, u32[]{:S(2)}) collective-permute-start(bf16[80,1472]{1,0:T(8,128)(2,1)} %get-tuple-element.150), channel_id=1, source_target_pairs={{0,4},{2,6},{4,0},{6,2},{1,5},{3,7},{5,1},{7,3},{8,12},{10,14},{12... | collective-permute-start | bytes 706568 | tf_op jit(solution)/shard_map/ppermute | solution.py:60
  172.1 12.0 %collective-permute-start.35 = (bf16[80,1472]{1,0:T(8,128)(2,1)}, bf16[80,1472]{1,0:T(8,128)(2,1)S(1)}, u32[]{:S(2)}, u32[]{:S(2)}) collective-permute-start(bf16[80,1472]{1,0:T(8,128)(2,1)} %get-tuple-element.151), channel_id=1, source_target_pairs={{0,6},{2,4},{4,2},{6,0},{1,7},{3,5},{5,3},{7,1},{8,14},{10,12},{12... | collective-permute-start | bytes 706568 | tf_op jit(solution)/shard_map/ppermute | solution.py:60
  174.4 9.8 %collective-permute-start.36 = (bf16[80,1472]{1,0:T(8,128)(2,1)S(1)}, bf16[80,1472]{1,0:T(8,128)(2,1)S(1)}, u32[]{:S(2)}, u32[]{:S(2)}) collective-permute-start(bf16[80,1472]{1,0:T(8,128)(2,1)S(1)} %get-tuple-element.156.b_mine), channel_id=1, source_target_pairs={{0,1},{1,0},{2,3},{3,2},{4,5},{5,4},{6,7},{7,6},{8,9},{9,8},{10,11... | collective-permute-start | bytes 706568 | tf_op jit(solution)/shard_map/ppermute | solution.py:60
  191.0 31.5 %collective-permute-start.39 = (bf16[3872,128]{1,0:T(8,128)(2,1)}, bf16[3872,128]{1,0:T(8,128)(2,1)S(1)}, u32[]{:S(2)}, u32[]{:S(2)}) collective-permute-start(bf16[3872,128]{1,0:T(8,128)(2,1)} %bitcast.56), channel_id=1, source_target_pairs={{0,4},{2,6},{4,0},{6,2},{1,5},{3,7},{5,1},{7,3},{8,12},{10,14},{12... | collective-permute-start | bytes 2973704 | tf_op jit(solution)/shard_map/ppermute | solution.py:60
  192.4 30.1 %collective-permute-start.38 = (bf16[3872,128]{1,0:T(8,128)(2,1)}, bf16[3872,128]{1,0:T(8,128)(2,1)S(1)}, u32[]{:S(2)}, u32[]{:S(2)}) collective-permute-start(bf16[3872,128]{1,0:T(8,128)(2,1)} %bitcast.57), channel_id=1, source_target_pairs={{0,2},{2,0},{4,6},{6,4},{1,3},{3,1},{5,7},{7,5},{8,10},{10,8},{12,... | collective-permute-start | bytes 2973704 | tf_op jit(solution)/shard_map/ppermute | solution.py:60
  194.0 14.1 %collective-permute-start.41 = (bf16[208,368]{1,0:T(8,128)(2,1)S(1)}, bf16[208,368]{1,0:T(8,128)(2,1)S(1)}, u32[]{:S(2)}, u32[]{:S(2)}) collective-permute-start(bf16[208,368]{1,0:T(8,128)(2,1)S(1)} %get-tuple-element.165), channel_id=1, source_target_pairs={{0,16},{8,24},{16,0},{24,8},{1,17},{9,25},{17,1},{25,9},{2,18},{10... | collective-permute-start | bytes 459272 | tf_op jit(solution)/shard_map/ppermute | solution.py:55
  196.8 11.2 %collective-permute-start.42 = (bf16[208,368]{1,0:T(8,128)(2,1)S(1)}, bf16[208,368]{1,0:T(8,128)(2,1)S(1)}, u32[]{:S(2)}, u32[]{:S(2)}) collective-permute-start(bf16[208,368]{1,0:T(8,128)(2,1)S(1)} %get-tuple-element.166), channel_id=1, source_target_pairs={{0,24},{8,0},{16,8},{24,16},{1,25},{9,1},{17,9},{25,17},{2,26},{10... | collective-permute-start | bytes 459272 | tf_op jit(solution)/shard_map/ppermute | solution.py:55
  197.8 10.3 %collective-permute-start.40 = (bf16[208,368]{1,0:T(8,128)(2,1)S(1)}, bf16[208,368]{1,0:T(8,128)(2,1)S(1)}, u32[]{:S(2)}, u32[]{:S(2)}) collective-permute-start(bf16[208,368]{1,0:T(8,128)(2,1)S(1)} %get-tuple-element.164), channel_id=1, source_target_pairs={{0,8},{8,16},{16,24},{24,0},{1,9},{9,17},{17,25},{25,1},{2,10},{10... | collective-permute-start | bytes 459272 | tf_op jit(solution)/shard_map/ppermute | solution.py:55
  208.2 12.8 %collective-permute-start.45 = (bf16[208,368]{1,0:T(8,128)(2,1)S(1)}, bf16[208,368]{1,0:T(8,128)(2,1)S(1)}, u32[]{:S(2)}, u32[]{:S(2)}) collective-permute-start(bf16[208,368]{1,0:T(8,128)(2,1)S(1)} %fusion.2.refs_0_), channel_id=1, source_target_pairs={{0,6},{2,4},{4,2},{6,0},{1,7},{3,5},{5,3},{7,1},{8,14},{10,12},{12... | collective-permute-start | bytes 459272 | tf_op jit(solution)/shard_map/ppermute | solution.py:60
  208.8 12.5 %collective-permute-start.44 = (bf16[208,368]{1,0:T(8,128)(2,1)S(1)}, bf16[208,368]{1,0:T(8,128)(2,1)S(1)}, u32[]{:S(2)}, u32[]{:S(2)}) collective-permute-start(bf16[208,368]{1,0:T(8,128)(2,1)S(1)} %fusion.2.refs_0_), channel_id=1, source_target_pairs={{0,4},{2,6},{4,0},{6,2},{1,5},{3,7},{5,1},{7,3},{8,12},{10,14},{12... | collective-permute-start | bytes 459272 | tf_op jit(solution)/shard_map/ppermute | solution.py:60
  210.3 12.3 %collective-permute-start.43 = (bf16[208,368]{1,0:T(8,128)(2,1)S(1)}, bf16[208,368]{1,0:T(8,128)(2,1)S(1)}, u32[]{:S(2)}, u32[]{:S(2)}) collective-permute-start(bf16[208,368]{1,0:T(8,128)(2,1)S(1)} %fusion.2.refs_0_), channel_id=1, source_target_pairs={{0,2},{2,0},{4,6},{6,4},{1,3},{3,1},{5,7},{7,5},{8,10},{10,8},{12,... | collective-permute-start | bytes 459272 | tf_op jit(solution)/shard_map/ppermute | solution.py:60
  222.6 11.6 %collective-permute-start.48 = (bf16[1936,128]{1,0:T(8,128)(2,1)S(1)}, bf16[1936,128]{1,0:T(8,128)(2,1)S(1)}, u32[]{:S(2)}, u32[]{:S(2)}) collective-permute-start(bf16[1936,128]{1,0:T(8,128)(2,1)S(1)} %slice.95), channel_id=1, source_target_pairs={{0,2},{2,0},{4,6},{6,4},{1,3},{3,1},{5,7},{7,5},{8,10},{10,8},{12,... | collective-permute-start | bytes 1486856 | tf_op jit(solution)/shard_map/ppermute | solution.py:60
  224.2 11.2 %collective-permute-start.47 = (bf16[1936,128]{1,0:T(8,128)(2,1)S(1)}, bf16[1936,128]{1,0:T(8,128)(2,1)S(1)}, u32[]{:S(2)}, u32[]{:S(2)}) collective-permute-start(bf16[1936,128]{1,0:T(8,128)(2,1)S(1)} %slice.94), channel_id=1, source_target_pairs={{0,4},{2,6},{4,0},{6,2},{1,5},{3,7},{5,1},{7,3},{8,12},{10,14},{12... | collective-permute-start | bytes 1486856 | tf_op jit(solution)/shard_map/ppermute | solution.py:60
  226.4 3.1 %collective-permute-start.46 = (f32[2,368]{1,0:T(2,128)S(1)}, f32[2,368]{1,0:T(2,128)S(1)}, u32[]{:S(2)}, u32[]{:S(2)}) collective-permute-start(f32[2,368]{1,0:T(2,128)S(1)} %get-tuple-element.169), channel_id=1, source_target_pairs={{0,1},{1,0},{2,3},{3,2},{4,5},{5,4},{6,7},{7,6},{8,9},{9,8},{10,11... | collective-permute-start | bytes 8840 | tf_op jit(solution)/shard_map/ppermute | solution.py:60
  (53 other events, 695.7 us)
Sparse Core Ops, SparseCore 0:
  11.4 87.3 all-gather.2
  114.6 76.3 reduce-scatter.1

commit v5 on v4

--- a/solution.py
+++ b/solution.py
@@ -352,11 +352,12 @@
         gain_grad[j] = total[:, r * j : r * (j + 1)]
 
 
-def attend_back(n_ctx, heads, o_mine, o_other, soft, qkv, every, *refs):
-    kv, (q_grad, kv_all, mixed_grad) = refs[:n_ctx], refs[n_ctx:]
+def attend_back(n_ctx, heads, idx, o_mine, o_other, soft, qkv, every, mixed, *refs):
+    kv, for_out, (q_grad, kv_all, mixed_grad) = refs[:n_ctx], refs[n_ctx : 2 * n_ctx], refs[2 * n_ctx :]
     rows = o_mine.shape[0]
     length = n_ctx * rows
     inner = heads * DK
+    share_rows = for_out[0].shape[0]
     for m, o_in in ((0, o_mine), (1, o_other)):
         top, own = m * length, m * rows
         mixed_grad[own : own + rows, :] = dot_nt(o_in[...], every[3 * inner :, :]).astype(low)
@@ -377,6 +378,15 @@
             ).astype(low)
         for k in range(n_ctx):
             kv[k][own : own + rows, :] = kv_all[top + k * rows : top + (k + 1) * rows, :]
+    got = dot_tn(mixed[0:rows, :], o_mine[...])
+    got += dot_tn(mixed[length : length + rows, :], o_other[...])
+    got = got.astype(low)
+    for v in range(n_ctx):
+
+        @pl.when(idx[1] == v)
+        def _(v=v):
+            for k in range(n_ctx):
+                for_out[k][...] = got[(v ^ k) * share_rows : ((v ^ k) + 1) * share_rows, :]
 
 
 def first_grad(n_ctx, idx, *refs):
@@ -388,6 +398,7 @@
     )
     rows2, inner = q_grad.shape
     rows = rows2 // 2
+    size = inner // n_ctx
     three[:, 0:inner] = q_grad[...]
     three[:, inner:] = sum((p[...].astype(wide) for p in parts)).astype(low)
     for v in range(n_ctx):
@@ -395,58 +406,37 @@
         @pl.when(idx[1] == v)
         def _(v=v):
             for k in range(n_ctx):
-                which = min(v ^ k, 2)
-                pieces[k][...] = three[:, which * inner : (which + 1) * inner]
+                for i in range(3):
+                    at = i * inner + (v ^ k) * size
+                    pieces[k][:, i * size : (i + 1) * size] = three[:, at : at + size]
 
     got = dot_nn(three[...], every[0 : 3 * inner, :]).astype(low)
     out_mine[...] = got[0:rows]
     out_other[...] = got[rows:]
 
 
-def weight_grads(n_ctx, n_shard, idx, normed, mixed, *refs):
-    pieces, outs_mine, refs = refs[:n_ctx], refs[n_ctx : 2 * n_ctx], refs[2 * n_ctx :]
-    outs_rest, gain_one, gain_two = refs[:2], refs[2], refs[3]
-    stack, grads, held, pieces_held, sems = refs[4:]
-    s, c = idx[0], idx[1]
-    rows = outs_mine[0].shape[0]
-    length = n_ctx * rows
-    r = stack.shape[2]
-    inner = grads.shape[1]
+def weight_grads(n_ctx, n_shard, idx, normed, *refs):
+    pieces, for_out, refs = refs[:n_ctx], refs[n_ctx : 2 * n_ctx], refs[2 * n_ctx :]
+    gain_one, gain_two, stack, grads, held, sem = refs
+    s = idx[0]
+    copy = pltpu.make_async_copy(normed, held, sem)
+    copy.start()
+    size, r = for_out[0].shape[0], stack.shape[2]
+    rows = pieces[0].shape[0] // 2
+    out_rows = sum((p[...].astype(wide) for p in for_out))
     for j in range(n_shard):
-        stack[wrap(j - s, n_shard), inner : inner + 1, :] = gain_one[j].astype(low)
-        stack[wrap(j - s, n_shard), inner + 1 : inner + 2, :] = gain_two[j].astype(low)
-
-    def fetch(moves):
-        copies = [pltpu.make_async_copy(x, y, sems.at[i]) for i, (x, y) in enumerate(moves)]
-        for copy in copies:
-            copy.start()
-        for copy in copies:
-            copy.wait()
-
-    def emit(got):
-        for j in range(n_shard):
-            stack[wrap(j - s, n_shard), 0:inner, :] = got[:, r * j : r * (j + 1)].astype(low)
-
-    @pl.when(c != 3)
-    def _():
-        fetch([(normed, held)] + [(pieces[k], pieces_held.at[k]) for k in range(n_ctx)])
-        for m in range(2):
-            for k in range(n_ctx):
-                at = (m * n_ctx + k) * rows
-                grads[at : at + rows, :] = pieces_held[k, m * rows : (m + 1) * rows, :]
-        emit(dot_tn(grads[...], held[...]))
-
-    @pl.when(c == 3)
-    def _():
-        moves = [(mixed, grads)]
+        d = wrap(j - s, n_shard)
+        stack[d, 3 * size : 4 * size, :] = out_rows[:, r * j : r * (j + 1)].astype(low)
+        stack[d, 4 * size : 4 * size + 1, :] = gain_one[j].astype(low)
+        stack[d, 4 * size + 1 : 4 * size + 2, :] = gain_two[j].astype(low)
+    for m in range(2):
         for k in range(n_ctx):
-            moves.append((outs_mine[k], held.at[k * rows : (k + 1) * rows, :]))
-        moves.append((outs_rest[0], held.at[length : length + rows, :]))
-        for k in range(1, n_ctx):
-            at = length + k * rows
-            moves.append((outs_rest[1].at[k - 1], held.at[at : at + rows, :]))
-        fetch(moves)
-        emit(dot_tn(grads[...], held[...]))
+            at = (m * n_ctx + k) * rows
+            grads[at : at + rows, :] = pieces[k][m * rows : (m + 1) * rows, :]
+    copy.wait()
+    got = dot_tn(grads[...], held[...])
+    for j in range(n_shard):
+        stack[wrap(j - s, n_shard), 0 : 3 * size, :] = got[:, r * j : r * (j + 1)].astype(low)
 
 
 def place_outputs(idx, a_mine, a_other, b_mine, b_other, a, b):
@@ -519,15 +509,18 @@
 
 def finish_attention(n_ctx, idx, *refs):
     pieces, (outs, gains) = refs[:n_ctx], (refs[n_ctx:-1], refs[-1])
-    inner, r = outs[0].shape
+    inner, _ = outs[0].shape
+    size = inner // n_ctx
     for v in range(n_ctx):
 
         @pl.when(idx[1] == v)
         def _(v=v):
             for k in range(n_ctx):
-                outs[v ^ k][...] = pieces[k][0:inner, 0:r].astype(wide)
-
-    gains[...] = sum((p[inner : inner + 2, 0:r].astype(wide) for p in pieces))
+                at = (v ^ k) * size
+                for i in range(4):
+                    outs[i][at : at + size, :] = pieces[k][i * size : (i + 1) * size, :].astype(wide)
+
+    gains[...] = sum((p[inner : inner + 2, :].astype(wide) for p in pieces))
 
 
 def on_device(
@@ -585,7 +578,13 @@
         far=4,
         vmem=60,
     )
-    from_shard = [step(own_buf, "shard", k) for k in range(1, shards)]
+    if shards == 4:
+        low_one, high_one = step(own_buf, "shard", 1), step(own_buf, "shard", -1)
+        middle = own_buf.shape[0] // 2
+        far = [step(low_one[:middle], "shard", 1), step(high_one[middle:], "shard", -1)]
+        from_shard = [low_one, jnp.concatenate(far), high_one]
+    else:
+        from_shard = [step(own_buf, "shard", k) for k in range(1, shards)]
     mine_x = [swap(own_x, "ctx", k) for k in range(1, ctx)]
     table = lax.dynamic_slice_in_dim(bias_table, half * heads, heads, 1)
     (bias,) = run(
@@ -689,30 +688,28 @@
     got = run(
         functools.partial(attend_back, ctx, heads),
         "attend_back",
-        [((2 * rows, 2 * inner), low)] * ctx + [((2 * rows, inner), low)],
-        [out_in, out_in_other, soft, qkv, every],
-        scalars=0,
+        [((2 * rows, 2 * inner), low)] * ctx
+        + [((inner // ctx, width), low)] * ctx
+        + [((2 * rows, inner), low)],
+        [now, out_in, out_in_other, soft, qkv, every, mixed],
         scratch=[pltpu.VMEM((2 * length, 2 * inner), low), pltpu.VMEM((2 * rows, inner), low)],
         cost=4,
         vmem=24,
     )
-    kv_parts, q_grad = got[:ctx], got[ctx]
+    kv_parts, for_out, q_grad = got[:ctx], got[ctx : 2 * ctx], got[2 * ctx]
     now = after(now, feed_got, q_grad)
 
     kv_parts = [kv_parts[0]] + [swap(after(kv_parts[k], now), "ctx", k) for k in range(1, ctx)]
-    outs_mine = [out_in] + [
-        lax.ppermute(after(out_in, now), "ctx", [((ctx - 1) ^ k, ctx - 1)]) for k in range(1, ctx)
-    ]
-    feed_both = [add(feed_mine[k], feed_got[k]) for k in range(ctx)]
+    for_out = [for_out[0]] + [swap(after(for_out[k], now), "ctx", k) for k in range(1, ctx)]
     got = run(
         functools.partial(first_grad, ctx),
         "first_grad",
-        [((rows, width), low)] * 2 + [((2 * rows, inner), low)] * ctx,
+        [((rows, width), low)] * 2 + [((2 * rows, 3 * inner // ctx), low)] * ctx,
         [now, *kv_parts, q_grad, every],
         scratch=[pltpu.VMEM((2 * rows, 3 * inner), low)],
     )
     first_mine, first_other, pieces = got[0], got[1], got[2:]
-    now = after(now, first_other, *feed_both)
+    now = after(now, first_other)
 
     pieces = [pieces[0]] + [swap(after(pieces[k], now), "ctx", k) for k in range(1, ctx)]
     first_got = swap(after(first_other, now), "tensor")
@@ -722,26 +719,24 @@
         [((rows, width), low), ((shards, 1, r), wide)],
         [now, inputs, first_mine, first_got, middle_grad, gains],
     )
-    outs_rest = [out_in_other, swap(jnp.stack(outs_mine[1:]), "tensor")]
-    now = after(now, *pieces[1:], input_mine, outs_rest[1])
-
-    feed_parts = [feed_both[0]] + [swap(after(feed_both[k], now), "ctx", k) for k in range(1, ctx)]
-    input_other = swap(after(input_mine, now), "tensor")
     (four,) = run(
         functools.partial(weight_grads, ctx, shards),
         "weight_grads",
         [((shards, inner + 16, r), low)],
-        [now, normed_one, mixed, *pieces, *outs_mine, *outs_rest, gain_one, gain_two],
+        [now, normed_one, *pieces, *for_out, gain_one, gain_two],
         scratch=[
-            pltpu.VMEM((2 * length, inner), low),
+            pltpu.VMEM((2 * length, 3 * inner // ctx), low),
             pltpu.VMEM((2 * length, width), low),
-            pltpu.VMEM((ctx, 2 * rows, inner), low),
-            pltpu.SemaphoreType.DMA((2 * ctx + 1,)),
+            pltpu.SemaphoreType.DMA,
         ],
-        far=4 + 2 * ctx,
+        far=1,
         cost=2,
-        vmem=60,
-    )
+        vmem=24,
+    )
+    now = after(now, four, input_mine)
+
+    feed_both = [add(after(feed_mine, now)[k], feed_got[k]) for k in range(ctx)]
+    feed_parts = [feed_both[0]] + [swap(feed_both[k], "ctx", k) for k in range(1, ctx)]
     (produced_mine,) = run(
         functools.partial(produce, ctx),
         "produce",
@@ -749,10 +744,8 @@
         [*feed_parts, middle_own],
         scalars=0,
     )
-    now = after(now, produced_mine, four, input_other)
-
-    four_shard = [four[0]] + [step(after(four[d], now), "shard", d) for d in range(1, shards)]
-    produced_other = swap(after(produced_mine, now), "tensor")
+    input_other = swap(after(input_mine, now), "tensor")
+    produced_other = swap(produced_mine, "tensor")
     out_y, out_x = run(
         place_outputs,
         "place_outputs",
@@ -765,6 +758,7 @@
     half_rows = wide_rows // 2
     pair = ctx == 4
     wide_all = [swap(wide_own, "ctx", k) for k in ((1, 2) if pair else range(1, ctx))]
+    four_shard = [four[0]] + [step(after(four[d], now), "shard", d) for d in range(1, shards)]
     four_own = sum((part.astype(wide) for part in four_shard)).astype(low)
     four_all = [four_own] + [swap(after(four_own, now), "ctx", k) for k in range(1, ctx)]
     now = after(now, *wide_all, *four_all[1:])

time: 246 us -> 238 us (0.967)
  starting transfers between devices: 56.6 us -> 51.8 us
    ppermute x40 -> x42, waiting for transfers between devices: 69 us -> 80.6 us  [swap(): return lax.ppermute(x, axis, [(i, i ^ k) for i in range(n)])]
    ppermute x6 -> x7, waiting for transfers between devices: 25.8 us -> 16.3 us  [step(): return lax.ppermute(x, axis, [(i, (i + k) % n) for i in range(n)])]
    ppermute x3 -> x0, starting transfers between devices: 5.11 us -> none  [on_device(): lax.ppermute(after(out_in, now), 'ctx', [(ctx - 1 ^ k, ctx - 1)])]
    ppermute x6 -> x7, starting transfers between devices: 10.6 us -> 14.6 us  [step(): return lax.ppermute(x, axis, [(i, (i + k) % n) for i in range(n)])]
    ppermute x40 -> x42, starting transfers between devices: 40.9 us -> 37.1 us  [swap(): return lax.ppermute(x, axis, [(i, i ^ k) for i in range(n)])]
    ppermute x3 -> x0, waiting for transfers between devices: 3 us -> none  [on_device(): lax.ppermute(after(out_in, now), 'ctx', [(ctx - 1 ^ k, ctx - 1)])]
  transfers between devices with their start and end apart: 51 -> 51, of which waited for: 25 -> 28; matrix products, arithmetic and copies ran while one was open for 2% -> 1% of each run, Pallas kernels for 16% -> 16%
where the time goes in v5:
time: 238 us
  waiting for transfers between devices  105 us (44%)
  Pallas kernels  59.6 us (25%)
  starting transfers between devices  51.8 us (22%)
  between operations  14.7 us (6%)
  local copies, waits for them, and re-layouts  3.76 us (2%)
  other arithmetic  3.28 us (1%)
    ppermute x42, waiting for transfers between devices, swap(): return lax.ppermute(x, axis, [(i, i ^ k) for i in range(n)])  80.6 us
    pallas_call x17, Pallas kernels, run(): pl.pallas_call(body, name=name, out_shape=[jax.ShapeDtypeStruct(s, d) for...  59.6 us
    ppermute x42, starting transfers between devices, swap(): return lax.ppermute(x, axis, [(i, i ^ k) for i in range(n)])  37.1 us
    ppermute x7, waiting for transfers between devices, step(): return lax.ppermute(x, axis, [(i, (i + k) % n) for i in range(n)])  16.3 us
    ppermute x7, starting transfers between devices, step(): return lax.ppermute(x, axis, [(i, (i + k) % n) for i in range(n)])  14.6 us
  transfers between devices with their start and end apart: 51, of which 28 were waited for; matrix products, arithmetic and copies ran while one was open for 1% of the time, Pallas kernels for 16%

profile of v5, /device:TPU:0, one launch (start us, length us, event | category | flops | bytes accessed | tf_op | source)
XLA Modules:
  0.0 238.2 jit_solution(9540482066285652110)
XLA Ops:
  7.9 3.3 %pack_wide.1 = bf16[3872,128]{1,0:T(8,128)(2,1)} custom-call(s32[3]{0:T(128)} %pad_add_fusion.idx, bf16[368,1792]{1,0:T(8,128)(2,1)} %w_g.1, bf16[368,1792]{1,0:T(8,128)(2,1)} %w_u.1, bf16[368,1792]{1,0:T(8,128)(2,1)} %bitcast.64), custom_call_target="tpu_custom_call" | custom-call | flops 200000000 | tf_op jit(solution)/shard_map/pack_wide/pallas_call | solution.py:37
  11.9 2.3 pack_attention.1.refs_4_
  14.2 5.1 %collective-permute-start.2 = (bf16[208,384]{1,0:T(8,128)(2,1)}, bf16[208,384]{1,0:T(8,128)(2,1)S(1)}, u32[]{:S(2)}, u32[]{:S(2)}) collective-permute-start(bf16[208,384]{1,0:T(8,128)(2,1)} %pack_attention.1.refs_4_), channel_id=1, source_target_pairs={{0,24},{8,0},{16,8},{24,16},{1,25},{9,1},{17,9},{25,17},{2,26},{10... | collective-permute-start | bytes 479240 | tf_op jit(solution)/shard_map/ppermute | solution.py:55
  19.3 2.9 %collective-permute-start.6 = (bf16[80,1472]{1,0:T(8,128)(2,1)S(1)}, bf16[80,1472]{1,0:T(8,128)(2,1)S(1)}, u32[]{:S(2)}, u32[]{:S(2)}) collective-permute-start(bf16[80,1472]{1,0:T(8,128)(2,1)S(1)} %dynamic-slice_bitcast_fusion.1), channel_id=1, source_target_pairs={{0,6},{2,4},{4,2},{6,0},{1,7},{3,5},{5,3},{7,1},{8,14},{10,12},{12... | collective-permute-start | bytes 706568 | tf_op jit(solution)/shard_map/ppermute | solution.py:60
  23.0 5.3 %bias.1 = f32[3,320,320]{2,1,0:T(8,128)S(1)} custom-call(s32[3]{0:T(128)S(1)} %copy-done.28, f32[32,3]{1,0:T(8,128)S(1)} %copy.27.table), custom_call_target="tpu_custom_call" | custom-call | flops 500000000 | tf_op jit(solution)/shard_map/bias/pallas_call | solution.py:37
  28.3 3.9 %collective-permute-start.3 = (bf16[104,384]{1,0:T(8,128)(2,1)S(1)}, bf16[104,384]{1,0:T(8,128)(2,1)S(1)}, u32[]{:S(2)}, u32[]{:S(2)}) collective-permute-start(bf16[104,384]{1,0:T(8,128)(2,1)S(1)} %slice.105), channel_id=1, source_target_pairs={{0,24},{8,0},{16,8},{24,16},{1,25},{9,1},{17,9},{25,17},{2,26},{10... | collective-permute-start | bytes 239624 | tf_op jit(solution)/shard_map/ppermute | solution.py:55
  33.4 7.0 %collective-permute-done.1 = bf16[104,384]{1,0:T(8,128)(2,1)S(1)} collective-permute-done((bf16[104,384]{1,0:T(8,128)(2,1)S(1)}, bf16[104,384]{1,0:T(8,128)(2,1)S(1)}, u32[]{:S(2)}, u32[]{:S(2)}) %collective-permute-start.1) | collective-permute-done | bytes 79904 | tf_op jit(solution)/shard_map/ppermute | solution.py:55
  40.6 2.8 %collective-permute-start.9 = (bf16[624,384]{1,0:T(8,128)(2,1)S(1)}, bf16[624,384]{1,0:T(8,128)(2,1)S(1)}, u32[]{:S(2)}, u32[]{:S(2)}) collective-permute-start(bf16[624,384]{1,0:T(8,128)(2,1)S(1)} %constant_dynamic-update-slice_fusion.2.refs_0_), channel_id=1, source_target_pairs={{0,6},{2,4},{4,2},{6,0},{1,7},{3,5},{5,3},{7,1},{8,14},{10,12},{12... | collective-permute-start | bytes 1437704 | tf_op jit(solution)/shard_map/ppermute | solution.py:60
  45.5 9.9 %collective-permute-done.9.refs_3_ = bf16[624,384]{1,0:T(8,128)(2,1)S(1)} collective-permute-done((bf16[624,384]{1,0:T(8,128)(2,1)S(1)}, bf16[624,384]{1,0:T(8,128)(2,1)S(1)}, u32[]{:S(2)}, u32[]{:S(2)}) %collective-permute-start.9) | collective-permute-done | bytes 479264 | tf_op jit(solution)/shard_map/ppermute | solution.py:60
  55.4 9.9 %collective-permute-done.8.refs_2_ = bf16[624,384]{1,0:T(8,128)(2,1)S(1)} collective-permute-done((bf16[624,384]{1,0:T(8,128)(2,1)S(1)}, bf16[624,384]{1,0:T(8,128)(2,1)S(1)}, u32[]{:S(2)}, u32[]{:S(2)}) %collective-permute-start.8) | collective-permute-done | bytes 479264 | tf_op jit(solution)/shard_map/ppermute | solution.py:60
  65.3 1.9 collective-permute-start.13
  68.9 11.7 %attend.1 = (bf16[320,1472]{1,0:T(8,128)(2,1)S(1)}, bf16[320,1472]{1,0:T(8,128)(2,1)S(1)}, f32[2,3,80,320]{3,2,1,0:T(8,128)S(1)}, bf16[640,576]{1,0:T(8,128)(2,1...) custom-call(s32[3]{0:T(128)S(1)} %copy-done.28, bf16[640,1472]{1,0:T(8,128)(2,1)S(1)} %get-tuple-element.104.normed, ...), custom_call_target="tpu_custom_call" | custom-call | flops 1400000000 | tf_op jit(solution)/shard_map/attend/pallas_call | solution.py:37
  80.7 2.6 %collective-permute-done.14.refs_4_ = bf16[320,1472]{1,0:T(8,128)(2,1)S(1)} collective-permute-done((bf16[320,1472]{1,0:T(8,128)(2,1)S(1)}, bf16[320,1472]{1,0:T(8,128)(2,1)S(1)}, u32[]{:S(2)}, u32[]{:S(2)}) %collective-permute-start.14) | collective-permute-done | bytes 942112 | tf_op jit(solution)/shard_map/ppermute | solution.py:60
  87.0 2.9 %collective-permute-done.16.refs_3_ = bf16[3,80,1472]{2,1,0:T(8,128)(2,1)S(1)} collective-permute-done((bf16[3,80,1472]{2,1,0:T(8,128)(2,1)S(1)}, bf16[3,80,1472]{2,1,0:T(8,128)(2,1)S(1)}, u32[]{:S(2)}, u32[]{:S(2)}) %collective-permute-start.16) | collective-permute-done | bytes 706592 | tf_op jit(solution)/shard_map/ppermute | solution.py:60
  90.9 4.3 %all-gather.3.cloned.1.call-done = bf16[15488,128]{1,0:T(8,128)(2,1)} async-done(((bf16[3872,128]{1,0:T(8,128)(2,1)}), bf16[15488,128]{1,0:T(8,128)(2,1)}) %all-gather.3.cloned.1.call-update) | async-done | bytes 3964944 | tf_op jit(solution)/shard_map/all_gather | solution.py:570
  95.2 15.7 %feed_forward.1 = (bf16[4,3872,128]{2,1,0:T(8,128)(2,1)}, bf16[4,80,1472]{2,1,0:T(8,128)(2,1)}, bf16[4,80,1472]{2,1,0:T(8,128)(2,1)}, bf16[4,80,1472]{2,1,0:T(8,128)(2,1)}, bf16[4,80,1472]{2,1,0:T(8,128)(2,1)}) custom-call(s32[3]{0:T(128)} %pad_add_fusion.idx, bf16[4,3872,128]{2,1,0:T(8,128)(2,1)} %bitcast.62, bf16[320,1472]{1,0:T(8,128)(2,1)} %copy-done.16, ...), custom_call_target="tpu_custom_call" | custom-call | flops 2000000000 | tf_op jit(solution)/shard_map/feed_forward/pallas_call | solution.py:37
  111.1 2.7 %collective-permute-done.17 = bf16[4,80,1472]{2,1,0:T(8,128)(2,1)S(1)} collective-permute-done((bf16[4,80,1472]{2,1,0:T(8,128)(2,1)}, bf16[4,80,1472]{2,1,0:T(8,128)(2,1)S(1)}, u32[]{:S(2)}, u32[]{:S(2)}) %collective-permute-start.17) | collective-permute-done | bytes 942112 | tf_op jit(solution)/shard_map/ppermute | solution.py:60
  113.8 1.5 fusion.6
  115.3 3.0 %collective-permute-start.20 = (bf16[80,1472]{1,0:T(8,128)(2,1)S(1)}, bf16[80,1472]{1,0:T(8,128)(2,1)S(1)}, u32[]{:S(2)}, u32[]{:S(2)}) collective-permute-start(bf16[80,1472]{1,0:T(8,128)(2,1)S(1)} %get-tuple-element.193), channel_id=1, source_target_pairs={{0,6},{2,4},{4,2},{6,0},{1,7},{3,5},{5,3},{7,1},{8,14},{10,12},{12... | collective-permute-start | bytes 706568 | tf_op jit(solution)/shard_map/ppermute | solution.py:60
  118.9 6.2 %collective-permute-done.20.refs_3_ = bf16[80,1472]{1,0:T(8,128)(2,1)S(1)} collective-permute-done((bf16[80,1472]{1,0:T(8,128)(2,1)S(1)}, bf16[80,1472]{1,0:T(8,128)(2,1)S(1)}, u32[]{:S(2)}, u32[]{:S(2)}) %collective-permute-start.20) | collective-permute-done | bytes 235552 | tf_op jit(solution)/shard_map/ppermute | solution.py:60
  125.1 4.7 %collective-permute-done.19.refs_2_ = bf16[80,1472]{1,0:T(8,128)(2,1)S(1)} collective-permute-done((bf16[80,1472]{1,0:T(8,128)(2,1)S(1)}, bf16[80,1472]{1,0:T(8,128)(2,1)S(1)}, u32[]{:S(2)}, u32[]{:S(2)}) %collective-permute-start.19) | collective-permute-done | bytes 235552 | tf_op jit(solution)/shard_map/ppermute | solution.py:60
  132.6 4.1 %attend_back.1 = (bf16[160,384]{1,0:T(8,128)(2,1)S(1)}, bf16[160,384]{1,0:T(8,128)(2,1)S(1)}, bf16[160,384]{1,0:T(8,128)(2,1)S(1)}, bf16[160,384]{1,0:T(8,128)(2...) custom-call(s32[3]{0:T(128)S(1)} %copy-done.29, ...), custom_call_target="tpu_custom_call" | custom-call | flops 400000000 | tf_op jit(solution)/shard_map/attend_back/pallas_call | solution.py:37
  136.7 1.9 collective-permute-start.23
  140.3 2.1 collective-permute-done.23.refs_1_
  142.4 4.1 %collective-permute-done.24.refs_2_ = bf16[160,384]{1,0:T(8,128)(2,1)S(1)} collective-permute-done((bf16[160,384]{1,0:T(8,128)(2,1)S(1)}, bf16[160,384]{1,0:T(8,128)(2,1)S(1)}, u32[]{:S(2)}, u32[]{:S(2)}) %collective-permute-start.24) | collective-permute-done | bytes 122912 | tf_op jit(solution)/shard_map/ppermute | solution.py:60
  146.5 1.5 first_grad.1
  150.0 1.7 collective-permute-start.31
  152.1 2.8 %collective-permute-done.29.refs_5_ = bf16[48,1472]{1,0:T(8,128)(2,1)S(1)} collective-permute-done((bf16[48,1472]{1,0:T(8,128)(2,1)S(1)}, bf16[48,1472]{1,0:T(8,128)(2,1)S(1)}, u32[]{:S(2)}, u32[]{:S(2)}) %collective-permute-start.29) | collective-permute-done | bytes 141344 | tf_op jit(solution)/shard_map/ppermute | solution.py:60
  158.1 1.7 collective-permute-done.26.refs_1_
  161.2 1.7 weight_grads.1
  163.1 1.8 collective-permute-start.35
  164.9 1.4 collective-permute-start.34
  166.7 6.3 %collective-permute-done.35.refs_3_ = bf16[80,1472]{1,0:T(8,128)(2,1)S(1)} collective-permute-done((bf16[80,1472]{1,0:T(8,128)(2,1)S(1)}, bf16[80,1472]{1,0:T(8,128)(2,1)S(1)}, u32[]{:S(2)}, u32[]{:S(2)}) %collective-permute-start.35) | collective-permute-done | bytes 235552 | tf_op jit(solution)/shard_map/ppermute | solution.py:60
  173.0 3.8 %collective-permute-done.34.refs_2_ = bf16[80,1472]{1,0:T(8,128)(2,1)S(1)} collective-permute-done((bf16[80,1472]{1,0:T(8,128)(2,1)S(1)}, bf16[80,1472]{1,0:T(8,128)(2,1)S(1)}, u32[]{:S(2)}, u32[]{:S(2)}) %collective-permute-start.34) | collective-permute-done | bytes 235552 | tf_op jit(solution)/shard_map/ppermute | solution.py:60
  178.5 1.5 place_outputs.1
  180.0 3.9 %reduce-scatter.2.cloned.1.call-done = bf16[1,3872,128]{2,1,0:T(8,128)(2,1)} async-done(((bf16[4,3872,128]{2,1,0:T(8,128)(2,1)}), bf16[1,3872,128]{2,1,0:T(8,128)(2,1)}) %reduce-scatter.2.cloned.1.call-update) | async-done | bytes 991248 | tf_op jit(solution)/shard_map/reduce_scatter | solution.py:672
  183.9 1.5 collective-permute-start.39
  185.4 1.5 collective-permute-start.38
  187.0 2.8 %collective-permute-start.41 = (bf16[208,368]{1,0:T(8,128)(2,1)S(1)}, bf16[208,368]{1,0:T(8,128)(2,1)S(1)}, u32[]{:S(2)}, u32[]{:S(2)}) collective-permute-start(bf16[208,368]{1,0:T(8,128)(2,1)S(1)} %get-tuple-element.169), channel_id=1, source_target_pairs={{0,16},{8,24},{16,0},{24,8},{1,17},{9,25},{17,1},{25,9},{2,18},{10... | collective-permute-start | bytes 459272 | tf_op jit(solution)/shard_map/ppermute | solution.py:55
  191.8 9.2 %collective-permute-done.41 = bf16[208,368]{1,0:T(8,128)(2,1)S(1)} collective-permute-done((bf16[208,368]{1,0:T(8,128)(2,1)S(1)}, bf16[208,368]{1,0:T(8,128)(2,1)S(1)}, u32[]{:S(2)}, u32[]{:S(2)}) %collective-permute-start.41) | collective-permute-done | bytes 153120 | tf_op jit(solution)/shard_map/ppermute | solution.py:55
  201.7 1.5 collective-permute-start.44
  203.2 1.5 collective-permute-start.43
  204.7 9.2 %collective-permute-done.45.refs_3_ = bf16[208,368]{1,0:T(8,128)(2,1)S(1)} collective-permute-done((bf16[208,368]{1,0:T(8,128)(2,1)S(1)}, bf16[208,368]{1,0:T(8,128)(2,1)S(1)}, u32[]{:S(2)}, u32[]{:S(2)}) %collective-permute-start.45) | collective-permute-done | bytes 153120 | tf_op jit(solution)/shard_map/ppermute | solution.py:60
  215.6 1.5 collective-permute-start.48
  217.7 1.7 finish_attention.1
  219.3 3.1 %finish_wide.2 = (f32[368,1792]{1,0:T(8,128)}, f32[368,1792]{1,0:T(8,128)}, f32[368,1792]{1,0:T(8,128)}) custom-call(s32[3]{0:T(128)S(1)} %copy-done.29, bf16[3872,128]{1,0:T(8,128)(2,1)S(1)} %bitcast.55, bf16[3872,128]{1,0:T(8,128)(2,1)S(1)} %collective-permute-done.38.refs_1_), custom_call_target="tpu_custom_call" | custom-call | flops 300000000 | tf_op jit(solution)/shard_map/finish_wide/pallas_call | solution.py:37
  223.0 4.1 %collective-permute-done.48.refs_2_ = bf16[1936,128]{1,0:T(8,128)(2,1)S(1)} collective-permute-done((bf16[1936,128]{1,0:T(8,128)(2,1)S(1)}, bf16[1936,128]{1,0:T(8,128)(2,1)S(1)}, u32[]{:S(2)}, u32[]{:S(2)}) %collective-permute-start.48) | collective-permute-done | bytes 495648 | tf_op jit(solution)/shard_map/ppermute | solution.py:60
  228.3 3.1 %finish_wide.3 = (f32[368,1792]{1,0:T(8,128)}, f32[368,1792]{1,0:T(8,128)}, f32[368,1792]{1,0:T(8,128)}) custom-call(s32[3]{0:T(128)S(1)} %copy-done.29, bf16[3872,128]{1,0:T(8,128)(2,1)S(1)} %collective-permute-done.39.refs_0_, bf16[1936,128]{1,0:T(8,128)(2,1)S(1)} %collective-permute-done.47.refs_1_, ...), custom_call_target="tpu_custom_call", output_to_operand_aliasing={{0}: (4, {}), {1}: (5, {}), {2}: (6, {})} | custom-call | flops 300000000 | tf_op jit(solution)/shard_map/finish_wide/pallas_call | solution.py:37
  (173 shorter events, 33.0 us)
Async XLA Ops:
  7.2 88.0 %all-gather.3.cloned.1.call-start = ((), (), s32[]{:S(2)}) async-start(), calls=%async_computation.2 | async-start | bytes 4956160 | tf_op jit(solution)/shard_map/all_gather | solution.py:570
  11.2 172.7 %reduce-scatter.2.cloned.1.call-start = ((), (), s32[]{:S(2)}) async-start(), calls=%async_computation.1 | async-start | bytes 4956160 | tf_op jit(solution)/shard_map/reduce_scatter | solution.py:672
  14.2 14.1 %collective-permute-start.2 = (bf16[208,384]{1,0:T(8,128)(2,1)}, bf16[208,384]{1,0:T(8,128)(2,1)S(1)}, u32[]{:S(2)}, u32[]{:S(2)}) collective-permute-start(bf16[208,384]{1,0:T(8,128)(2,1)} %pack_attention.1.refs_4_), channel_id=1, source_target_pairs={{0,24},{8,0},{16,8},{24,16},{1,25},{9,1},{17,9},{25,17},{2,26},{10... | collective-permute-start | bytes 479240 | tf_op jit(solution)/shard_map/ppermute | solution.py:55
  19.3 12.9 %collective-permute-start = (bf16[208,384]{1,0:T(8,128)(2,1)}, bf16[208,384]{1,0:T(8,128)(2,1)S(1)}, u32[]{:S(2)}, u32[]{:S(2)}) collective-permute-start(bf16[208,384]{1,0:T(8,128)(2,1)} %pack_attention.1.refs_4_), channel_id=1, source_target_pairs={{0,8},{8,16},{16,24},{24,0},{1,9},{9,17},{17,25},{25,1},{2,10},{10... | collective-permute-start | bytes 479240 | tf_op jit(solution)/shard_map/ppermute | solution.py:55
  19.3 13.7 %collective-permute-start.6 = (bf16[80,1472]{1,0:T(8,128)(2,1)S(1)}, bf16[80,1472]{1,0:T(8,128)(2,1)S(1)}, u32[]{:S(2)}, u32[]{:S(2)}) collective-permute-start(bf16[80,1472]{1,0:T(8,128)(2,1)S(1)} %dynamic-slice_bitcast_fusion.1), channel_id=1, source_target_pairs={{0,6},{2,4},{4,2},{6,0},{1,7},{3,5},{5,3},{7,1},{8,14},{10,12},{12... | collective-permute-start | bytes 706568 | tf_op jit(solution)/shard_map/ppermute | solution.py:60
  22.3 10.9 %collective-permute-start.5 = (bf16[80,1472]{1,0:T(8,128)(2,1)S(1)}, bf16[80,1472]{1,0:T(8,128)(2,1)S(1)}, u32[]{:S(2)}, u32[]{:S(2)}) collective-permute-start(bf16[80,1472]{1,0:T(8,128)(2,1)S(1)} %dynamic-slice_bitcast_fusion.1), channel_id=1, source_target_pairs={{0,4},{2,6},{4,0},{6,2},{1,5},{3,7},{5,1},{7,3},{8,12},{10,14},{12... | collective-permute-start | bytes 706568 | tf_op jit(solution)/shard_map/ppermute | solution.py:60
  22.8 10.5 %collective-permute-start.4 = (bf16[80,1472]{1,0:T(8,128)(2,1)S(1)}, bf16[80,1472]{1,0:T(8,128)(2,1)S(1)}, u32[]{:S(2)}, u32[]{:S(2)}) collective-permute-start(bf16[80,1472]{1,0:T(8,128)(2,1)S(1)} %dynamic-slice_bitcast_fusion.1), channel_id=1, source_target_pairs={{0,2},{2,0},{4,6},{6,4},{1,3},{3,1},{5,7},{7,5},{8,10},{10,8},{12,... | collective-permute-start | bytes 706568 | tf_op jit(solution)/shard_map/ppermute | solution.py:60
  28.3 12.1 %collective-permute-start.3 = (bf16[104,384]{1,0:T(8,128)(2,1)S(1)}, bf16[104,384]{1,0:T(8,128)(2,1)S(1)}, u32[]{:S(2)}, u32[]{:S(2)}) collective-permute-start(bf16[104,384]{1,0:T(8,128)(2,1)S(1)} %slice.105), channel_id=1, source_target_pairs={{0,24},{8,0},{16,8},{24,16},{1,25},{9,1},{17,9},{25,17},{2,26},{10... | collective-permute-start | bytes 239624 | tf_op jit(solution)/shard_map/ppermute | solution.py:55
  32.2 8.2 %collective-permute-start.1 = (bf16[104,384]{1,0:T(8,128)(2,1)S(1)}, bf16[104,384]{1,0:T(8,128)(2,1)S(1)}, u32[]{:S(2)}, u32[]{:S(2)}) collective-permute-start(bf16[104,384]{1,0:T(8,128)(2,1)S(1)} %slice.104), channel_id=1, source_target_pairs={{0,8},{8,16},{16,24},{24,0},{1,9},{9,17},{17,25},{25,1},{2,10},{10... | collective-permute-start | bytes 239624 | tf_op jit(solution)/shard_map/ppermute | solution.py:55
  40.5 3.7 %collective-permute-start.10 = (bf16[3,80,1472]{2,1,0:T(8,128)(2,1)S(1)}, bf16[3,80,1472]{2,1,0:T(8,128)(2,1)S(1)}, u32[]{:S(2)}, u32[]{:S(2)}) collective-permute-start(bf16[3,80,1472]{2,1,0:T(8,128)(2,1)S(1)} %pad_maximum_fusion), channel_id=1, source_target_pairs={{0,1},{1,0},{2,3},{3,2},{4,5},{5,4},{6,7},{7,6},{8,9},{9,8},{10,11... | collective-permute-start | bytes 2119688 | tf_op jit(solution)/shard_map/ppermute | solution.py:60
  40.6 14.8 %collective-permute-start.9 = (bf16[624,384]{1,0:T(8,128)(2,1)S(1)}, bf16[624,384]{1,0:T(8,128)(2,1)S(1)}, u32[]{:S(2)}, u32[]{:S(2)}) collective-permute-start(bf16[624,384]{1,0:T(8,128)(2,1)S(1)} %constant_dynamic-update-slice_fusion.2.refs_0_), channel_id=1, source_target_pairs={{0,6},{2,4},{4,2},{6,0},{1,7},{3,5},{5,3},{7,1},{8,14},{10,12},{12... | collective-permute-start | bytes 1437704 | tf_op jit(solution)/shard_map/ppermute | solution.py:60
  43.4 21.9 %collective-permute-start.8 = (bf16[624,384]{1,0:T(8,128)(2,1)S(1)}, bf16[624,384]{1,0:T(8,128)(2,1)S(1)}, u32[]{:S(2)}, u32[]{:S(2)}) collective-permute-start(bf16[624,384]{1,0:T(8,128)(2,1)S(1)} %constant_dynamic-update-slice_fusion.2.refs_0_), channel_id=1, source_target_pairs={{0,4},{2,6},{4,0},{6,2},{1,5},{3,7},{5,1},{7,3},{8,12},{10,14},{12... | collective-permute-start | bytes 1437704 | tf_op jit(solution)/shard_map/ppermute | solution.py:60
  43.9 21.4 %collective-permute-start.7 = (bf16[624,384]{1,0:T(8,128)(2,1)S(1)}, bf16[624,384]{1,0:T(8,128)(2,1)S(1)}, u32[]{:S(2)}, u32[]{:S(2)}) collective-permute-start(bf16[624,384]{1,0:T(8,128)(2,1)S(1)} %constant_dynamic-update-slice_fusion.2.refs_0_), channel_id=1, source_target_pairs={{0,2},{2,0},{4,6},{6,4},{1,3},{3,1},{5,7},{7,5},{8,10},{10,8},{12,... | collective-permute-start | bytes 1437704 | tf_op jit(solution)/shard_map/ppermute | solution.py:60
  65.3 15.3 %collective-permute-start.13 = (bf16[80,1472]{1,0:T(8,128)(2,1)S(1)}, bf16[80,1472]{1,0:T(8,128)(2,1)S(1)}, u32[]{:S(2)}, u32[]{:S(2)}) collective-permute-start(bf16[80,1472]{1,0:T(8,128)(2,1)S(1)} %dynamic-slice_bitcast_fusion), channel_id=1, source_target_pairs={{0,6},{2,4},{4,2},{6,0},{1,7},{3,5},{5,3},{7,1},{8,14},{10,12},{12... | collective-permute-start | bytes 706568 | tf_op jit(solution)/shard_map/ppermute | solution.py:60
  67.2 13.4 %collective-permute-start.12 = (bf16[80,1472]{1,0:T(8,128)(2,1)S(1)}, bf16[80,1472]{1,0:T(8,128)(2,1)S(1)}, u32[]{:S(2)}, u32[]{:S(2)}) collective-permute-start(bf16[80,1472]{1,0:T(8,128)(2,1)S(1)} %dynamic-slice_bitcast_fusion), channel_id=1, source_target_pairs={{0,4},{2,6},{4,0},{6,2},{1,5},{3,7},{5,1},{7,3},{8,12},{10,14},{12... | collective-permute-start | bytes 706568 | tf_op jit(solution)/shard_map/ppermute | solution.py:60
  68.5 12.1 %collective-permute-start.11 = (bf16[80,1472]{1,0:T(8,128)(2,1)S(1)}, bf16[80,1472]{1,0:T(8,128)(2,1)S(1)}, u32[]{:S(2)}, u32[]{:S(2)}) collective-permute-start(bf16[80,1472]{1,0:T(8,128)(2,1)S(1)} %dynamic-slice_bitcast_fusion), channel_id=1, source_target_pairs={{0,2},{2,0},{4,6},{6,4},{1,3},{3,1},{5,7},{7,5},{8,10},{10,8},{12,... | collective-permute-start | bytes 706568 | tf_op jit(solution)/shard_map/ppermute | solution.py:60
  86.4 4.5 %collective-permute-start.15 = (bf16[320,1472]{1,0:T(8,128)(2,1)S(1)}, bf16[320,1472]{1,0:T(8,128)(2,1)}, u32[]{:S(2)}, u32[]{:S(2)}) collective-permute-start(bf16[320,1472]{1,0:T(8,128)(2,1)S(1)} %get-tuple-element.112.nt_mine), channel_id=1, source_target_pairs={{0,1},{1,0},{2,3},{3,2},{4,5},{5,4},{6,7},{7,6},{8,9},{9,8},{10,11... | collective-permute-start | bytes 2826248 | tf_op jit(solution)/shard_map/ppermute | solution.py:60
  86.6 3.4 %collective-permute-start.16 = (bf16[3,80,1472]{2,1,0:T(8,128)(2,1)S(1)}, bf16[3,80,1472]{2,1,0:T(8,128)(2,1)S(1)}, u32[]{:S(2)}, u32[]{:S(2)}) collective-permute-start(bf16[3,80,1472]{2,1,0:T(8,128)(2,1)S(1)} %pad_maximum_fusion.1), channel_id=1, source_target_pairs={{0,1},{1,0},{2,3},{3,2},{4,5},{5,4},{6,7},{7,6},{8,9},{9,8},{10,11... | collective-permute-start | bytes 2119688 | tf_op jit(solution)/shard_map/ppermute | solution.py:60
  110.9 2.8 %collective-permute-start.17 = (bf16[4,80,1472]{2,1,0:T(8,128)(2,1)}, bf16[4,80,1472]{2,1,0:T(8,128)(2,1)S(1)}, u32[]{:S(2)}, u32[]{:S(2)}) collective-permute-start(bf16[4,80,1472]{2,1,0:T(8,128)(2,1)} %get-tuple-element.118), channel_id=1, source_target_pairs={{0,1},{1,0},{2,3},{3,2},{4,5},{5,4},{6,7},{7,6},{8,9},{9,8},{10,11... | collective-permute-start | bytes 2826248 | tf_op jit(solution)/shard_map/ppermute | solution.py:60
  115.3 9.8 %collective-permute-start.20 = (bf16[80,1472]{1,0:T(8,128)(2,1)S(1)}, bf16[80,1472]{1,0:T(8,128)(2,1)S(1)}, u32[]{:S(2)}, u32[]{:S(2)}) collective-permute-start(bf16[80,1472]{1,0:T(8,128)(2,1)S(1)} %get-tuple-element.193), channel_id=1, source_target_pairs={{0,6},{2,4},{4,2},{6,0},{1,7},{3,5},{5,3},{7,1},{8,14},{10,12},{12... | collective-permute-start | bytes 706568 | tf_op jit(solution)/shard_map/ppermute | solution.py:60
  118.3 11.5 %collective-permute-start.19 = (bf16[80,1472]{1,0:T(8,128)(2,1)S(1)}, bf16[80,1472]{1,0:T(8,128)(2,1)S(1)}, u32[]{:S(2)}, u32[]{:S(2)}) collective-permute-start(bf16[80,1472]{1,0:T(8,128)(2,1)S(1)} %get-tuple-element.194), channel_id=1, source_target_pairs={{0,4},{2,6},{4,0},{6,2},{1,5},{3,7},{5,1},{7,3},{8,12},{10,14},{12... | collective-permute-start | bytes 706568 | tf_op jit(solution)/shard_map/ppermute | solution.py:60
  118.8 11.1 %collective-permute-start.18 = (bf16[80,1472]{1,0:T(8,128)(2,1)S(1)}, bf16[80,1472]{1,0:T(8,128)(2,1)S(1)}, u32[]{:S(2)}, u32[]{:S(2)}) collective-permute-start(bf16[80,1472]{1,0:T(8,128)(2,1)S(1)} %get-tuple-element.195), channel_id=1, source_target_pairs={{0,2},{2,0},{4,6},{6,4},{1,3},{3,1},{5,7},{7,5},{8,10},{10,8},{12,... | collective-permute-start | bytes 706568 | tf_op jit(solution)/shard_map/ppermute | solution.py:60
  132.4 4.3 %collective-permute-start.22 = (bf16[4,80,1472]{2,1,0:T(8,128)(2,1)S(1)}, bf16[4,80,1472]{2,1,0:T(8,128)(2,1)S(1)}, u32[]{:S(2)}, u32[]{:S(2)}) collective-permute-start(bf16[4,80,1472]{2,1,0:T(8,128)(2,1)S(1)} %copy-done.37), channel_id=1, source_target_pairs={{0,1},{1,0},{2,3},{3,2},{4,5},{5,4},{6,7},{7,6},{8,9},{9,8},{10,11... | collective-permute-start | bytes 2826248 | tf_op jit(solution)/shard_map/ppermute | solution.py:60
  136.7 5.7 %collective-permute-start.23 = (bf16[160,384]{1,0:T(8,128)(2,1)S(1)}, bf16[160,384]{1,0:T(8,128)(2,1)S(1)}, u32[]{:S(2)}, u32[]{:S(2)}) collective-permute-start(bf16[160,384]{1,0:T(8,128)(2,1)S(1)} %get-tuple-element.132), channel_id=1, source_target_pairs={{0,2},{2,0},{4,6},{6,4},{1,3},{3,1},{5,7},{7,5},{8,10},{10,8},{12,... | collective-permute-start | bytes 368648 | tf_op jit(solution)/shard_map/ppermute | solution.py:60
  138.6 7.9 %collective-permute-start.24 = (bf16[160,384]{1,0:T(8,128)(2,1)S(1)}, bf16[160,384]{1,0:T(8,128)(2,1)S(1)}, u32[]{:S(2)}, u32[]{:S(2)}) collective-permute-start(bf16[160,384]{1,0:T(8,128)(2,1)S(1)} %get-tuple-element.134), channel_id=1, source_target_pairs={{0,4},{2,6},{4,0},{6,2},{1,5},{3,7},{5,1},{7,3},{8,12},{10,14},{12... | collective-permute-start | bytes 368648 | tf_op jit(solution)/shard_map/ppermute | solution.py:60
  139.2 7.3 %collective-permute-start.25 = (bf16[160,384]{1,0:T(8,128)(2,1)S(1)}, bf16[160,384]{1,0:T(8,128)(2,1)S(1)}, u32[]{:S(2)}, u32[]{:S(2)}) collective-permute-start(bf16[160,384]{1,0:T(8,128)(2,1)S(1)} %get-tuple-element.136), channel_id=1, source_target_pairs={{0,6},{2,4},{4,2},{6,0},{1,7},{3,5},{5,3},{7,1},{8,14},{10,12},{12... | collective-permute-start | bytes 368648 | tf_op jit(solution)/shard_map/ppermute | solution.py:60
  148.1 7.4 %collective-permute-start.32 = (bf16[80,1472]{1,0:T(8,128)(2,1)S(1)}, bf16[80,1472]{1,0:T(8,128)(2,1)S(1)}, u32[]{:S(2)}, u32[]{:S(2)}) collective-permute-start(bf16[80,1472]{1,0:T(8,128)(2,1)S(1)} %get-tuple-element.154), channel_id=1, source_target_pairs={{0,1},{1,0},{2,3},{3,2},{4,5},{5,4},{6,7},{7,6},{8,9},{9,8},{10,11... | collective-permute-start | bytes 706568 | tf_op jit(solution)/shard_map/ppermute | solution.py:60
  148.2 6.7 %collective-permute-start.29 = (bf16[48,1472]{1,0:T(8,128)(2,1)S(1)}, bf16[48,1472]{1,0:T(8,128)(2,1)S(1)}, u32[]{:S(2)}, u32[]{:S(2)}) collective-permute-start(bf16[48,1472]{1,0:T(8,128)(2,1)S(1)} %get-tuple-element.148), channel_id=1, source_target_pairs={{0,2},{2,0},{4,6},{6,4},{1,3},{3,1},{5,7},{7,5},{8,10},{10,8},{12,... | collective-permute-start | bytes 423944 | tf_op jit(solution)/shard_map/ppermute | solution.py:60
  148.6 9.0 %collective-permute-start.30 = (bf16[48,1472]{1,0:T(8,128)(2,1)S(1)}, bf16[48,1472]{1,0:T(8,128)(2,1)S(1)}, u32[]{:S(2)}, u32[]{:S(2)}) collective-permute-start(bf16[48,1472]{1,0:T(8,128)(2,1)S(1)} %get-tuple-element.150), channel_id=1, source_target_pairs={{0,4},{2,6},{4,0},{6,2},{1,5},{3,7},{5,1},{7,3},{8,12},{10,14},{12... | collective-permute-start | bytes 423944 | tf_op jit(solution)/shard_map/ppermute | solution.py:60
  150.0 8.1 %collective-permute-start.31 = (bf16[48,1472]{1,0:T(8,128)(2,1)S(1)}, bf16[48,1472]{1,0:T(8,128)(2,1)S(1)}, u32[]{:S(2)}, u32[]{:S(2)}) collective-permute-start(bf16[48,1472]{1,0:T(8,128)(2,1)S(1)} %get-tuple-element.152), channel_id=1, source_target_pairs={{0,6},{2,4},{4,2},{6,0},{1,7},{3,5},{5,3},{7,1},{8,14},{10,12},{12... | collective-permute-start | bytes 423944 | tf_op jit(solution)/shard_map/ppermute | solution.py:60
  151.7 8.1 %collective-permute-start.26 = (bf16[160,144]{1,0:T(8,128)(2,1)S(1)}, bf16[160,144]{1,0:T(8,128)(2,1)S(1)}, u32[]{:S(2)}, u32[]{:S(2)}) collective-permute-start(bf16[160,144]{1,0:T(8,128)(2,1)S(1)} %get-tuple-element.141), channel_id=1, source_target_pairs={{0,2},{2,0},{4,6},{6,4},{1,3},{3,1},{5,7},{7,5},{8,10},{10,8},{12,... | collective-permute-start | bytes 138248 | tf_op jit(solution)/shard_map/ppermute | solution.py:60
  154.9 5.0 %collective-permute-start.27 = (bf16[160,144]{1,0:T(8,128)(2,1)S(1)}, bf16[160,144]{1,0:T(8,128)(2,1)S(1)}, u32[]{:S(2)}, u32[]{:S(2)}) collective-permute-start(bf16[160,144]{1,0:T(8,128)(2,1)S(1)} %get-tuple-element.143), channel_id=1, source_target_pairs={{0,4},{2,6},{4,0},{6,2},{1,5},{3,7},{5,1},{7,3},{8,12},{10,14},{12... | collective-permute-start | bytes 138248 | tf_op jit(solution)/shard_map/ppermute | solution.py:60
  155.5 5.7 %collective-permute-start.28 = (bf16[160,144]{1,0:T(8,128)(2,1)S(1)}, bf16[160,144]{1,0:T(8,128)(2,1)S(1)}, u32[]{:S(2)}, u32[]{:S(2)}) collective-permute-start(bf16[160,144]{1,0:T(8,128)(2,1)S(1)} %get-tuple-element.145), channel_id=1, source_target_pairs={{0,6},{2,4},{4,2},{6,0},{1,7},{3,5},{5,3},{7,1},{8,14},{10,12},{12... | collective-permute-start | bytes 138248 | tf_op jit(solution)/shard_map/ppermute | solution.py:60
  163.1 9.9 %collective-permute-start.35 = (bf16[80,1472]{1,0:T(8,128)(2,1)S(1)}, bf16[80,1472]{1,0:T(8,128)(2,1)S(1)}, u32[]{:S(2)}, u32[]{:S(2)}) collective-permute-start(bf16[80,1472]{1,0:T(8,128)(2,1)S(1)} %get-tuple-element.189), channel_id=1, source_target_pairs={{0,6},{2,4},{4,2},{6,0},{1,7},{3,5},{5,3},{7,1},{8,14},{10,12},{12... | collective-permute-start | bytes 706568 | tf_op jit(solution)/shard_map/ppermute | solution.py:60
  164.9 11.9 %collective-permute-start.34 = (bf16[80,1472]{1,0:T(8,128)(2,1)S(1)}, bf16[80,1472]{1,0:T(8,128)(2,1)S(1)}, u32[]{:S(2)}, u32[]{:S(2)}) collective-permute-start(bf16[80,1472]{1,0:T(8,128)(2,1)S(1)} %get-tuple-element.190), channel_id=1, source_target_pairs={{0,4},{2,6},{4,0},{6,2},{1,5},{3,7},{5,1},{7,3},{8,12},{10,14},{12... | collective-permute-start | bytes 706568 | tf_op jit(solution)/shard_map/ppermute | solution.py:60
  166.3 10.4 %collective-permute-start.33 = (bf16[80,1472]{1,0:T(8,128)(2,1)S(1)}, bf16[80,1472]{1,0:T(8,128)(2,1)S(1)}, u32[]{:S(2)}, u32[]{:S(2)}) collective-permute-start(bf16[80,1472]{1,0:T(8,128)(2,1)S(1)} %get-tuple-element.191), channel_id=1, source_target_pairs={{0,2},{2,0},{4,6},{6,4},{1,3},{3,1},{5,7},{7,5},{8,10},{10,8},{12,... | collective-permute-start | bytes 706568 | tf_op jit(solution)/shard_map/ppermute | solution.py:60
  166.7 10.5 %collective-permute-start.37 = (bf16[80,1472]{1,0:T(8,128)(2,1)S(1)}, bf16[80,1472]{1,0:T(8,128)(2,1)S(1)}, u32[]{:S(2)}, u32[]{:S(2)}) collective-permute-start(bf16[80,1472]{1,0:T(8,128)(2,1)S(1)} %get-tuple-element.162.b_mine), channel_id=1, source_target_pairs={{0,1},{1,0},{2,3},{3,2},{4,5},{5,4},{6,7},{7,6},{8,9},{9,8},{10,11... | collective-permute-start | bytes 706568 | tf_op jit(solution)/shard_map/ppermute | solution.py:60
  183.9 31.6 %collective-permute-start.39 = (bf16[3872,128]{1,0:T(8,128)(2,1)}, bf16[3872,128]{1,0:T(8,128)(2,1)S(1)}, u32[]{:S(2)}, u32[]{:S(2)}) collective-permute-start(bf16[3872,128]{1,0:T(8,128)(2,1)} %bitcast.53), channel_id=1, source_target_pairs={{0,4},{2,6},{4,0},{6,2},{1,5},{3,7},{5,1},{7,3},{8,12},{10,14},{12... | collective-permute-start | bytes 2973704 | tf_op jit(solution)/shard_map/ppermute | solution.py:60
  185.4 30.1 %collective-permute-start.38 = (bf16[3872,128]{1,0:T(8,128)(2,1)}, bf16[3872,128]{1,0:T(8,128)(2,1)S(1)}, u32[]{:S(2)}, u32[]{:S(2)}) collective-permute-start(bf16[3872,128]{1,0:T(8,128)(2,1)} %bitcast.54), channel_id=1, source_target_pairs={{0,2},{2,0},{4,6},{6,4},{1,3},{3,1},{5,7},{7,5},{8,10},{10,8},{12,... | collective-permute-start | bytes 2973704 | tf_op jit(solution)/shard_map/ppermute | solution.py:60
  187.0 14.1 %collective-permute-start.41 = (bf16[208,368]{1,0:T(8,128)(2,1)S(1)}, bf16[208,368]{1,0:T(8,128)(2,1)S(1)}, u32[]{:S(2)}, u32[]{:S(2)}) collective-permute-start(bf16[208,368]{1,0:T(8,128)(2,1)S(1)} %get-tuple-element.169), channel_id=1, source_target_pairs={{0,16},{8,24},{16,0},{24,8},{1,17},{9,25},{17,1},{25,9},{2,18},{10... | collective-permute-start | bytes 459272 | tf_op jit(solution)/shard_map/ppermute | solution.py:55
  189.8 11.3 %collective-permute-start.42 = (bf16[208,368]{1,0:T(8,128)(2,1)S(1)}, bf16[208,368]{1,0:T(8,128)(2,1)S(1)}, u32[]{:S(2)}, u32[]{:S(2)}) collective-permute-start(bf16[208,368]{1,0:T(8,128)(2,1)S(1)} %get-tuple-element.170), channel_id=1, source_target_pairs={{0,24},{8,0},{16,8},{24,16},{1,25},{9,1},{17,9},{25,17},{2,26},{10... | collective-permute-start | bytes 459272 | tf_op jit(solution)/shard_map/ppermute | solution.py:55
  190.7 10.3 %collective-permute-start.40 = (bf16[208,368]{1,0:T(8,128)(2,1)S(1)}, bf16[208,368]{1,0:T(8,128)(2,1)S(1)}, u32[]{:S(2)}, u32[]{:S(2)}) collective-permute-start(bf16[208,368]{1,0:T(8,128)(2,1)S(1)} %get-tuple-element.168), channel_id=1, source_target_pairs={{0,8},{8,16},{16,24},{24,0},{1,9},{9,17},{17,25},{25,1},{2,10},{10... | collective-permute-start | bytes 459272 | tf_op jit(solution)/shard_map/ppermute | solution.py:55
  201.1 12.7 %collective-permute-start.45 = (bf16[208,368]{1,0:T(8,128)(2,1)S(1)}, bf16[208,368]{1,0:T(8,128)(2,1)S(1)}, u32[]{:S(2)}, u32[]{:S(2)}) collective-permute-start(bf16[208,368]{1,0:T(8,128)(2,1)S(1)} %fusion.2.refs_0_), channel_id=1, source_target_pairs={{0,6},{2,4},{4,2},{6,0},{1,7},{3,5},{5,3},{7,1},{8,14},{10,12},{12... | collective-permute-start | bytes 459272 | tf_op jit(solution)/shard_map/ppermute | solution.py:60
  201.7 12.6 %collective-permute-start.44 = (bf16[208,368]{1,0:T(8,128)(2,1)S(1)}, bf16[208,368]{1,0:T(8,128)(2,1)S(1)}, u32[]{:S(2)}, u32[]{:S(2)}) collective-permute-start(bf16[208,368]{1,0:T(8,128)(2,1)S(1)} %fusion.2.refs_0_), channel_id=1, source_target_pairs={{0,4},{2,6},{4,0},{6,2},{1,5},{3,7},{5,1},{7,3},{8,12},{10,14},{12... | collective-permute-start | bytes 459272 | tf_op jit(solution)/shard_map/ppermute | solution.py:60
  203.2 12.3 %collective-permute-start.43 = (bf16[208,368]{1,0:T(8,128)(2,1)S(1)}, bf16[208,368]{1,0:T(8,128)(2,1)S(1)}, u32[]{:S(2)}, u32[]{:S(2)}) collective-permute-start(bf16[208,368]{1,0:T(8,128)(2,1)S(1)} %fusion.2.refs_0_), channel_id=1, source_target_pairs={{0,2},{2,0},{4,6},{6,4},{1,3},{3,1},{5,7},{7,5},{8,10},{10,8},{12,... | collective-permute-start | bytes 459272 | tf_op jit(solution)/shard_map/ppermute | solution.py:60
  215.6 11.5 %collective-permute-start.48 = (bf16[1936,128]{1,0:T(8,128)(2,1)S(1)}, bf16[1936,128]{1,0:T(8,128)(2,1)S(1)}, u32[]{:S(2)}, u32[]{:S(2)}) collective-permute-start(bf16[1936,128]{1,0:T(8,128)(2,1)S(1)} %slice.103), channel_id=1, source_target_pairs={{0,2},{2,0},{4,6},{6,4},{1,3},{3,1},{5,7},{7,5},{8,10},{10,8},{12,... | collective-permute-start | bytes 1486856 | tf_op jit(solution)/shard_map/ppermute | solution.py:60
  217.1 11.2 %collective-permute-start.47 = (bf16[1936,128]{1,0:T(8,128)(2,1)S(1)}, bf16[1936,128]{1,0:T(8,128)(2,1)S(1)}, u32[]{:S(2)}, u32[]{:S(2)}) collective-permute-start(bf16[1936,128]{1,0:T(8,128)(2,1)S(1)} %slice.102), channel_id=1, source_target_pairs={{0,4},{2,6},{4,0},{6,2},{1,5},{3,7},{5,1},{7,3},{8,12},{10,14},{12... | collective-permute-start | bytes 1486856 | tf_op jit(solution)/shard_map/ppermute | solution.py:60
  219.3 3.1 %collective-permute-start.46 = (f32[2,368]{1,0:T(2,128)S(1)}, f32[2,368]{1,0:T(2,128)S(1)}, u32[]{:S(2)}, u32[]{:S(2)}) collective-permute-start(f32[2,368]{1,0:T(2,128)S(1)} %get-tuple-element.173), channel_id=1, source_target_pairs={{0,1},{1,0},{2,3},{3,2},{4,5},{5,4},{6,7},{7,6},{8,9},{9,8},{10,11... | collective-permute-start | bytes 8840 | tf_op jit(solution)/shard_map/ppermute | solution.py:60
  (41 other events, 645.9 us)
Sparse Core Ops, SparseCore 0:
  11.3 83.7 all-gather.2
  111.0 72.8 reduce-scatter.1

commit v6 on v5

--- a/solution.py
+++ b/solution.py
@@ -95,13 +95,14 @@
     return parts, pl.cdiv(row, 32) * 32
 
 
-def pack_wide(n_ctx, widths, window, idx, w_g, w_u, w_d, buf, stage, held, sems):
+def pack_wide(n_ctx, widths, window, w_g, w_u, w_d, buf, held, sems):
+    c = lax.axis_index("ctx")
     r = w_g.shape[0]
     columns = sum(widths)
     parts, _ = wide_tiles(r, widths)
     for v in range(n_ctx):
 
-        @pl.when(idx[1] == v)
+        @pl.when(c == v)
         def _(v=v):
             start = min(v * columns // LANES * LANES, w_g.shape[1] - window)
             copies = [
@@ -114,12 +115,14 @@
                 copy.wait()
             at = v * columns - start
             for n, pieces in zip(widths, parts, strict=True):
-                for i in range(3):
-                    stage[:, i * n : (i + 1) * n] = held[i, :, at : at + n]
                 for row, size, top, lane, lanes, to in pieces:
-                    buf[row : row + size, to : to + lanes] = stage[
-                        top : top + size, lane : lane + lanes
-                    ]
+                    while lanes:
+                        which, inside = divmod(lane, n)
+                        take = min(lanes, n - inside)
+                        buf[row : row + size, to : to + take] = held[
+                            which, top : top + size, at + inside : at + inside + take
+                        ]
+                        lane, to, lanes = lane + take, to + take, lanes - take
                 at += n
 
 
@@ -242,44 +245,48 @@
             middle_own[...] = mid
 
 
+def unpack_wide(parts, r, buf, weights, j):
+    for e, pieces in enumerate(parts):
+        for row, size, top, lane, lanes, at in pieces:
+            weights[e][r * j + top : r * j + top + size, lane : lane + lanes] = buf[
+                j, row : row + size, at : at + lanes
+            ]
+
+
 def feed_forward(n_ctx, n_shard, widths, idx, buf_far, nt_mine, nt_other, cot_in, *refs):
     half = idx[2]
+    n_parts = len(widths)
     mine, rest, refs = refs[: n_ctx - 1], refs[n_ctx - 1], refs[n_ctx:]
-    sent, feed, two = refs[0], refs[1:3], refs[3:5]
-    n_parts = len(widths)
-    buf, nt, cot, feed_held, two_held, sems, sems_out = refs[5:12]
-    weights, hidden, pair = (refs[12 + i * n_parts : 12 + (i + 1) * n_parts] for i in range(3))
+    sent, given, refs = refs[0], refs[1 : 1 + 2 * n_parts], refs[1 + 2 * n_parts :]
+    buf, nt, cot, sems, sems_out = refs[:5]
+    weights, hidden, pair = (refs[5 + i * n_parts : 5 + (i + 1) * n_parts] for i in range(3))
     length, _ = nt_mine.shape
     rows = length // n_ctx
     r = weights[0].shape[0] // n_shard
 
-    def blocks(m, first, count=1):
-        at = (m * n_ctx + first) * rows
-        return slice(at, at + count * rows)
+    def block(m, k):
+        at = (m * n_ctx + k) * rows
+        return slice(at, at + rows)
 
     begun = [pltpu.make_async_copy(buf_far.at[0], buf.at[0], sems.at[0])]
     moves = [
         (nt_mine, nt.at[0:length, :]),
         (nt_other, nt.at[length : 2 * length, :]),
-        (cot_in.at[half], cot.at[blocks(0, 0), :]),
-        (cot_in.at[1 - half], cot.at[blocks(1, 0), :]),
+        (cot_in.at[half], cot.at[block(0, 0), :]),
+        (cot_in.at[1 - half], cot.at[block(1, 0), :]),
     ]
     moves += [(buf_far.at[j], buf.at[j]) for j in range(1, n_shard)]
     for k in range(1, n_ctx):
-        moves.append((mine[k - 1], cot.at[blocks(0, k), :]))
-        moves.append((rest.at[k - 1], cot.at[blocks(1, k), :]))
-    begun += [pltpu.make_async_copy(a, b, sems.at[i + 1]) for i, (a, b) in enumerate(moves)]
+        moves.append((mine[k - 1], cot.at[block(0, k), :]))
+        moves.append((rest.at[k - 1], cot.at[block(1, k), :]))
+    begun += [pltpu.make_async_copy(x, y, sems.at[i + 1]) for i, (x, y) in enumerate(moves)]
     for copy in begun:
         copy.start()
     loads = [begun[0]] + begun[5 : 4 + n_shard]
     parts, _ = wide_tiles(r, widths)
     for j in range(n_shard):
         loads[j].wait()
-        for e, pieces in enumerate(parts):
-            for row, size, top, lane, lanes, at in pieces:
-                weights[e][r * j + top : r * j + top + size, lane : lane + lanes] = buf[
-                    j, row : row + size, at : at + lanes
-                ]
+        unpack_wide(parts, r, buf, weights, j)
     for copy in begun[1:5] + begun[4 + n_shard :]:
         copy.wait()
     c0, c1 = 0.7978845608028654, 0.044715
@@ -304,14 +311,8 @@
             hidden[e][at, :] = (active * up).astype(low)
             pair[e][at, 0:n] = (back * up * slope).astype(low)
             pair[e][at, n : 2 * n] = (back * active).astype(low)
-        for held, given, make in (
-            (two_held, two, lambda e, n: dot_nt(pair[e][at, :], weights[e][:, 0 : 2 * n])),
-            (feed_held, feed, lambda e, n: dot_nt(hidden[e][at, :], weights[e][:, 2 * n : 3 * n])),
-        ):
-            total = sum((make(e, n) for e, n in enumerate(widths)))
-            for i in range(n_ctx):
-                held[m, i] = total[i * rows : (i + 1) * rows].astype(low)
-            write(held.at[m], given[m])
+    for source, target in zip((*hidden, *pair), given, strict=True):
+        write(source, target)
     for e, n in enumerate(widths):
         for_in = dot_tn(nt[...], pair[e][...]).astype(low)
         for_down = dot_tn(cot[...], hidden[e][...]).astype(low)
@@ -331,6 +332,48 @@
                     ]
             here = slice(first, last if e < n_parts - 1 else buf.shape[1])
             write(buf.at[j, here, :], sent.at[j, here, :])
+    for copy in out:
+        copy.wait()
+
+
+def feed_out(n_ctx, n_shard, widths, idx, buf_far, *refs):
+    n_parts = len(widths)
+    far, refs = refs[: 2 * n_parts], refs[2 * n_parts :]
+    feed, two, refs = refs[0:2], refs[2:4], refs[4:]
+    buf, feed_held, two_held, sems, sems_out = refs[:5]
+    weights, hidden, pair = (refs[5 + i * n_parts : 5 + (i + 1) * n_parts] for i in range(3))
+    _, _, rows, _ = two_held.shape
+    length = n_ctx * rows
+    r = weights[0].shape[0] // n_shard
+    parts, _ = wide_tiles(r, widths)
+    moves = [(buf_far.at[j], buf.at[j]) for j in range(n_shard)]
+    moves += list(zip(far, (*hidden, *pair), strict=True))
+    begun = [pltpu.make_async_copy(x, y, sems.at[i]) for i, (x, y) in enumerate(moves)]
+    for copy in begun:
+        copy.start()
+    for j in range(n_shard):
+        begun[j].wait()
+        unpack_wide(parts, r, buf, weights, j)
+    for copy in begun[n_shard:]:
+        copy.wait()
+    out = []
+    for held, given, lefts, first, last in (
+        (two_held, two, pair, 0, 2),
+        (feed_held, feed, hidden, 2, 3),
+    ):
+        for m in (1, 0):
+            at = slice(m * length, (m + 1) * length)
+            total = sum(
+                (
+                    dot_nt(lefts[e][at, :], weights[e][:, first * n : last * n])
+                    for e, n in enumerate(widths)
+                )
+            )
+            for i in range(n_ctx):
+                held[m, i] = total[i * rows : (i + 1) * rows].astype(low)
+            copy = pltpu.make_async_copy(held.at[m], given[m], sems_out.at[len(out)])
+            copy.start()
+            out.append(copy)
     for copy in out:
         copy.wait()
 
@@ -465,44 +508,70 @@
     out[...] = (middle[...] + sum((p[...].astype(wide) for p in parts))).astype(low)
 
 
-def finish_wide(n_ctx, widths, which, idx, *refs):
-    count = sum((n for _, n in which))
+def finish_wide(n_ctx, widths, groups, idx, *refs):
+    flat = [item for group in groups for item in group]
+    count = sum((pieces for _, pieces, _ in flat))
     sources, refs = refs[:count], refs[count:]
-    outs, (stage, held, sems) = refs[-6:-3], refs[-3:]
+    n_outs = 3
+    outs, (stage, held, sems) = refs[-3 - n_outs : -3], refs[-3:]
     r = outs[0].shape[0]
     columns = sum(widths)
     parts, rows = wide_tiles(r, widths)
-    span = held.shape[2]
     for v in range(n_ctx):
-        start = min(((v ^ k) * columns for k, _ in which))
 
         @pl.when(idx[1] == v)
-        def _(v=v, start=start):
+        def _(v=v):
             first = 0
-            for k, pieces in which:
-                size_each = rows // pieces
-                for i, n in enumerate(widths):
-                    for row, size, top, lane, lanes, at in parts[i]:
-                        done = 0
-                        while done < size:
-                            part, here = divmod(row + done, size_each)
-                            many = min(size - done, size_each - here)
-                            stage[top + done : top + done + many, lane : lane + lanes] = sources[
-                                first + part
-                            ][here : here + many, at : at + lanes].astype(wide)
-                            done += many
-                    at = (v ^ k) * columns + sum(widths[:i]) - start
-                    for j in range(3):
-                        held[j, :, at : at + n] = stage[:, j * n : (j + 1) * n]
-                first += pieces
-            copies = [
-                pltpu.make_async_copy(
-                    held.at[j], outs[j].at[:, start : start + span], sems.at[j]
-                )
-                for j in range(3)
-            ]
-            for copy in copies:
-                copy.start()
+            copies = []
+            for g, group in enumerate(groups):
+                taken = []
+                for k, pieces, lanes_kind in group:
+                    begin = (v ^ k) * columns
+                    tile_low = pl.cdiv(begin, LANES) * LANES - begin
+                    tile_high = (begin + columns) // LANES * LANES - begin
+                    if lanes_kind == "all":
+                        low_lane, high_lane = 0, columns
+                    elif lanes_kind == "full":
+                        low_lane, high_lane = tile_low, tile_high
+                    elif tile_low:
+                        low_lane, high_lane = 0, tile_low
+                    else:
+                        low_lane, high_lane = tile_high, columns
+                    taken.append((k, pieces, low_lane, high_lane, first))
+                    first += pieces
+                start = min(((v ^ k) * columns + lo for k, _, lo, _, _ in taken))
+                stop = max(((v ^ k) * columns + hi for k, _, _, hi, _ in taken))
+                for k, pieces, low_lane, high_lane, at_source in taken:
+                    size_each = rows // pieces
+                    for i, n in enumerate(widths):
+                        base = sum(widths[:i])
+                        lo, hi = max(low_lane, base), min(high_lane, base + n)
+                        if lo >= hi:
+                            continue
+                        for row, size, top, lane, lanes, at in parts[i]:
+                            done = 0
+                            while done < size:
+                                part, here = divmod(row + done, size_each)
+                                many = min(size - done, size_each - here)
+                                stage[top + done : top + done + many, lane : lane + lanes] = (
+                                    sources[at_source + part][
+                                        here : here + many, at : at + lanes
+                                    ].astype(wide)
+                                )
+                                done += many
+                        to = (v ^ k) * columns + lo - start
+                        for j in range(3):
+                            held[g, j, :, to : to + hi - lo] = stage[
+                                :, j * n + lo - base : j * n + hi - base
+                            ]
+                for j in range(3):
+                    copy = pltpu.make_async_copy(
+                        held.at[g, j, :, 0 : stop - start],
+                        outs[j].at[:, start:stop],
+                        sems.at[3 * g + j],
+                    )
+                    copy.start()
+                    copies.append(copy)
             for copy in copies:
                 copy.wait()
 
@@ -557,9 +626,9 @@
         functools.partial(pack_wide, ctx, widths, window),
         "pack_wide",
         [((wide_rows, LANES), low)],
-        [idx, w_gate, w_up, w_down.T],
+        [w_gate, w_up, w_down.T],
+        scalars=0,
         scratch=[
-            pltpu.VMEM((r, 3 * max(widths)), low),
             pltpu.VMEM((3, r, window), low),
             pltpu.SemaphoreType.DMA((3,)),
         ],
@@ -647,29 +716,48 @@
         return (a.astype(wide) + b.astype(wide)).astype(low)
 
     tokens_out = ((ctx, rows, width), low)
-    wide_grads, feed_mine, feed_other, two_mine, two_other = run(
+    units = [((2 * length, n), low) for n in (*widths, *(2 * n for n in widths))]
+    unit_scratch = [pltpu.VMEM(shape, kind) for shape, kind in units]
+    weight_scratch = [pltpu.VMEM((width, 3 * n), low) for n in widths]
+    wide_grads, *units = run(
         functools.partial(feed_forward, ctx, shards, widths),
         "feed_forward",
-        [((shards, wide_rows, LANES), low)] + [tokens_out] * 4,
+        [((shards, wide_rows, LANES), low), *units],
         [now, chunks, nt_mine, nt_other, cotangent, *mine_cot, rest_cot],
         scratch=[
             pltpu.VMEM((shards, wide_rows, LANES), low),
             pltpu.VMEM((2 * length, width), low),
             pltpu.VMEM((2 * length, width), low),
+            pltpu.SemaphoreType.DMA((3 + shards + 2 * ctx,)),
+            pltpu.SemaphoreType.DMA(((2 + shards) * len(widths),)),
+            *weight_scratch,
+            *unit_scratch,
+        ],
+        far=5 + ctx - 1,
+        far_out=True,
+        cost=14,
+        vmem=60,
+    )
+    wide_own = lax.psum_scatter(wide_grads, "shard", scatter_dimension=0, tiled=False)
+    feed_mine, feed_other, two_mine, two_other = run(
+        functools.partial(feed_out, ctx, shards, widths),
+        "feed_out",
+        [tokens_out] * 4,
+        [now, chunks, *units],
+        scratch=[
+            pltpu.VMEM((shards, wide_rows, LANES), low),
             pltpu.VMEM((2, ctx, rows, width), low),
             pltpu.VMEM((2, ctx, rows, width), low),
-            pltpu.SemaphoreType.DMA((3 + shards + 2 * ctx,)),
-            pltpu.SemaphoreType.DMA((4 + shards * len(widths),)),
-        ]
-        + [pltpu.VMEM((width, 3 * n), low) for n in widths]
-        + [pltpu.VMEM((2 * length, n), low) for n in widths]
-        + [pltpu.VMEM((2 * length, 2 * n), low) for n in widths],
-        far=5 + ctx - 1,
+            pltpu.SemaphoreType.DMA((shards + 2 * len(widths),)),
+            pltpu.SemaphoreType.DMA((4,)),
+            *weight_scratch,
+            *unit_scratch,
+        ],
+        far=1 + 2 * len(widths),
         far_out=True,
-        cost=20,
+        cost=5,
         vmem=60,
     )
-    wide_own = lax.psum_scatter(wide_grads, "shard", scatter_dimension=0, tiled=False)
     now = after(now, two_other)
 
     two_got = swap(after(two_other, now), "tensor")
@@ -719,6 +807,9 @@
         [((rows, width), low), ((shards, 1, r), wide)],
         [now, inputs, first_mine, first_got, middle_grad, gains],
     )
+    feed_both = [add(after(feed_mine, now)[k], feed_got[k]) for k in range(ctx)]
+    feed_parts = [feed_both[0]] + [swap(feed_both[k], "ctx", k) for k in range(1, ctx)]
+    now = after(now, *pieces[1:], *for_out[1:], *feed_parts[1:], input_mine)
     (four,) = run(
         functools.partial(weight_grads, ctx, shards),
         "weight_grads",
@@ -735,8 +826,6 @@
     )
     now = after(now, four, input_mine)
 
-    feed_both = [add(after(feed_mine, now)[k], feed_got[k]) for k in range(ctx)]
-    feed_parts = [feed_both[0]] + [swap(feed_both[k], "ctx", k) for k in range(1, ctx)]
     (produced_mine,) = run(
         functools.partial(produce, ctx),
         "produce",
@@ -746,19 +835,20 @@
     )
     input_other = swap(after(input_mine, now), "tensor")
     produced_other = swap(produced_mine, "tensor")
+    now = after(now, wide_own, produced_other, input_other)
+
+    wide_own = after(wide_own, now)
+    half_rows = wide_rows // 2
+    pair = ctx == 4
+    wide_all = [swap(wide_own, "ctx", k) for k in ((1, 2) if pair else range(1, ctx))]
+    four_shard = [four[0]] + [step(after(four[d], now), "shard", d) for d in range(1, shards)]
     out_y, out_x = run(
         place_outputs,
         "place_outputs",
         [(inputs.shape, low)] * 2,
         [now, produced_mine, produced_other, input_mine, input_other],
     )
-    now = after(now, wide_own, out_y)
-
-    wide_own = after(wide_own, now)
-    half_rows = wide_rows // 2
-    pair = ctx == 4
-    wide_all = [swap(wide_own, "ctx", k) for k in ((1, 2) if pair else range(1, ctx))]
-    four_shard = [four[0]] + [step(after(four[d], now), "shard", d) for d in range(1, shards)]
+    four_shard = [four[0]] + [after(part, out_y) for part in four_shard[1:]]
     four_own = sum((part.astype(wide) for part in four_shard)).astype(low)
     four_all = [four_own] + [swap(after(four_own, now), "ctx", k) for k in range(1, ctx)]
     now = after(now, *wide_all, *four_all[1:])
@@ -777,16 +867,16 @@
     )
     own_gain = own_gain + swap(own_gain, "tensor")
 
-    def finish(now, which, sources, span, before):
+    def finish(now, groups, sources, span, before):
         return run(
-            functools.partial(finish_wide, ctx, widths, which),
+            functools.partial(finish_wide, ctx, widths, groups),
             "finish_wide",
             [(w_gate.shape, wide)] * 3,
             [now, *sources, *before],
             scratch=[
                 pltpu.VMEM((r, 3 * max(widths)), wide),
-                pltpu.VMEM((3, r, span), wide),
-                pltpu.SemaphoreType.DMA((3,)),
+                pltpu.VMEM((len(groups), 3, r, span), wide),
+                pltpu.SemaphoreType.DMA((3 * len(groups),)),
             ],
             far_out=True,
             into=len(before),
@@ -795,12 +885,14 @@
         )
 
     if pair and 2 * columns % LANES == 0:
-        outs = finish(now, [(0, 1), (1, 1)], [wide_own, wide_all[0]], 2 * columns, [])
+        groups = [[(0, 1, "all"), (1, 1, "all")], [(2, 1, "full")]]
+        outs = finish(now, groups, [wide_own, *wide_all], 2 * columns, [])
         now = after(now, *far_halves, outs[0], own_gain)
-        outs = finish(now, [(2, 1), (3, 2)], [wide_all[1], *far_halves], 2 * columns, outs)
+        groups = [[(2, 1, "rest"), (3, 2, "all")]]
+        outs = finish(now, groups, [wide_all[1], *far_halves], 2 * columns, outs)
     else:
-        which = [(k, 1) for k in range(ctx)]
-        outs = finish(now, which, [wide_own, *wide_all], ctx * columns, [])
+        groups = [[(k, 1, "all") for k in range(ctx)]]
+        outs = finish(now, groups, [wide_own, *wide_all], ctx * columns, [])
     out_g, out_u, out_d = outs
 
     return (

time: 238 us -> 238 us (level); the launches traced: 238 us -> 234 us
  waiting for transfers between devices: 105 us -> 95.4 us
  Pallas kernels: 59.6 us -> 63.3 us
    ppermute x42, waiting for transfers between devices: 80.6 us -> 75.7 us  [swap(): return lax.ppermute(x, axis, [(i, i ^ k) for i in range(n)])]
    pallas_call x17 -> x18, Pallas kernels: 59.6 us -> 63.3 us  [run(): pl.pallas_call(body, name=name, out_shape=[jax.ShapeDtypeStruct(s, d) for...]
    reduce_scatter x1, waiting for transfers between devices: 3.9 us -> 0.3 us  [on_device(): lax.psum_scatter(wide_grads, 'shard', scatter_dimension=0, tiled=False)]
  transfers between devices with their start and end apart: 51 -> 51, of which waited for: 28 -> 27; matrix products, arithmetic and copies ran while one was open for 1% -> 2% of each run, Pallas kernels for 16% -> 20%
where the time goes in v6:
time: 238 us; the launch traced here: 234 us
  waiting for transfers between devices  95.4 us (40%)
  Pallas kernels  63.3 us (27%)
  starting transfers between devices  53 us (22%)
  between operations  15.2 us (6%)
  local copies, waits for them, and re-layouts  3.55 us (1%)
  other arithmetic  3.2 us (1%)
    ppermute x42, waiting for transfers between devices, swap(): return lax.ppermute(x, axis, [(i, i ^ k) for i in range(n)])  75.7 us
    pallas_call x18, Pallas kernels, run(): pl.pallas_call(body, name=name, out_shape=[jax.ShapeDtypeStruct(s, d) for...  63.3 us
    ppermute x42, starting transfers between devices, swap(): return lax.ppermute(x, axis, [(i, i ^ k) for i in range(n)])  38.2 us
    ppermute x7, starting transfers between devices, step(): return lax.ppermute(x, axis, [(i, (i + k) % n) for i in range(n)])  14.8 us
    ppermute x7, waiting for transfers between devices, step(): return lax.ppermute(x, axis, [(i, (i + k) % n) for i in range(n)])  14.6 us
  transfers between devices with their start and end apart: 51, of which 27 were waited for; matrix products, arithmetic and copies ran while one was open for 2% of the time, Pallas kernels for 20%

profile of v6, /device:TPU:0, one launch (start us, length us, event | category | flops | bytes accessed | tf_op | source)
XLA Modules:
  0.0 233.7 jit_solution(3939184732091844147)
XLA Ops:
  7.3 2.6 %pack_wide.1 = bf16[3872,128]{1,0:T(8,128)(2,1)} custom-call(bf16[368,1792]{1,0:T(8,128)(2,1)} %w_g.1, bf16[368,1792]{1,0:T(8,128)(2,1)} %w_u.1, bf16[368,1792]{1,0:T(8,128)(2,1)} %bitcast.65), custom_call_target="tpu_custom_call" | custom-call | flops 200000000 | tf_op jit(solution)/shard_map/pack_wide/pallas_call | solution.py:37
  11.1 2.3 pack_attention.1.refs_4_
  13.4 5.1 %collective-permute-start.2 = (bf16[208,384]{1,0:T(8,128)(2,1)}, bf16[208,384]{1,0:T(8,128)(2,1)S(1)}, u32[]{:S(2)}, u32[]{:S(2)}) collective-permute-start(bf16[208,384]{1,0:T(8,128)(2,1)} %pack_attention.1.refs_4_), channel_id=1, source_target_pairs={{0,24},{8,0},{16,8},{24,16},{1,25},{9,1},{17,9},{25,17},{2,26},{10... | collective-permute-start | bytes 479240 | tf_op jit(solution)/shard_map/ppermute | solution.py:55
  18.6 2.8 %collective-permute-start.6 = (bf16[80,1472]{1,0:T(8,128)(2,1)S(1)}, bf16[80,1472]{1,0:T(8,128)(2,1)S(1)}, u32[]{:S(2)}, u32[]{:S(2)}) collective-permute-start(bf16[80,1472]{1,0:T(8,128)(2,1)S(1)} %dynamic-slice_bitcast_fusion.1), channel_id=1, source_target_pairs={{0,6},{2,4},{4,2},{6,0},{1,7},{3,5},{5,3},{7,1},{8,14},{10,12},{12... | collective-permute-start | bytes 706568 | tf_op jit(solution)/shard_map/ppermute | solution.py:60
  22.8 5.3 %bias.1 = f32[3,320,320]{2,1,0:T(8,128)S(1)} custom-call(s32[3]{0:T(128)S(1)} %copy-done.26, f32[32,3]{1,0:T(8,128)S(1)} %copy.27.table), custom_call_target="tpu_custom_call" | custom-call | flops 500000000 | tf_op jit(solution)/shard_map/bias/pallas_call | solution.py:37
  28.2 3.9 %collective-permute-start.3 = (bf16[104,384]{1,0:T(8,128)(2,1)S(1)}, bf16[104,384]{1,0:T(8,128)(2,1)S(1)}, u32[]{:S(2)}, u32[]{:S(2)}) collective-permute-start(bf16[104,384]{1,0:T(8,128)(2,1)S(1)} %slice.105), channel_id=1, source_target_pairs={{0,24},{8,0},{16,8},{24,16},{1,25},{9,1},{17,9},{25,17},{2,26},{10... | collective-permute-start | bytes 239624 | tf_op jit(solution)/shard_map/ppermute | solution.py:55
  33.2 6.9 %collective-permute-done.1 = bf16[104,384]{1,0:T(8,128)(2,1)S(1)} collective-permute-done((bf16[104,384]{1,0:T(8,128)(2,1)S(1)}, bf16[104,384]{1,0:T(8,128)(2,1)S(1)}, u32[]{:S(2)}, u32[]{:S(2)}) %collective-permute-start.1) | collective-permute-done | bytes 79904 | tf_op jit(solution)/shard_map/ppermute | solution.py:55
  40.3 2.7 %collective-permute-start.9 = (bf16[624,384]{1,0:T(8,128)(2,1)S(1)}, bf16[624,384]{1,0:T(8,128)(2,1)S(1)}, u32[]{:S(2)}, u32[]{:S(2)}) collective-permute-start(bf16[624,384]{1,0:T(8,128)(2,1)S(1)} %constant_dynamic-update-slice_fusion.2.refs_0_), channel_id=1, source_target_pairs={{0,6},{2,4},{4,2},{6,0},{1,7},{3,5},{5,3},{7,1},{8,14},{10,12},{12... | collective-permute-start | bytes 1437704 | tf_op jit(solution)/shard_map/ppermute | solution.py:60
  45.3 9.8 %collective-permute-done.9.refs_3_ = bf16[624,384]{1,0:T(8,128)(2,1)S(1)} collective-permute-done((bf16[624,384]{1,0:T(8,128)(2,1)S(1)}, bf16[624,384]{1,0:T(8,128)(2,1)S(1)}, u32[]{:S(2)}, u32[]{:S(2)}) %collective-permute-start.9) | collective-permute-done | bytes 479264 | tf_op jit(solution)/shard_map/ppermute | solution.py:60
  55.1 9.8 %collective-permute-done.8.refs_2_ = bf16[624,384]{1,0:T(8,128)(2,1)S(1)} collective-permute-done((bf16[624,384]{1,0:T(8,128)(2,1)S(1)}, bf16[624,384]{1,0:T(8,128)(2,1)S(1)}, u32[]{:S(2)}, u32[]{:S(2)}) %collective-permute-start.8) | collective-permute-done | bytes 479264 | tf_op jit(solution)/shard_map/ppermute | solution.py:60
  65.0 1.8 collective-permute-start.13
  66.9 1.4 collective-permute-start.12
  68.6 11.7 %attend.1 = (bf16[320,1472]{1,0:T(8,128)(2,1)S(1)}, bf16[320,1472]{1,0:T(8,128)(2,1)S(1)}, f32[2,3,80,320]{3,2,1,0:T(8,128)S(1)}, bf16[640,576]{1,0:T(8,128)(2,1...) custom-call(s32[3]{0:T(128)S(1)} %copy-done.26, bf16[640,1472]{1,0:T(8,128)(2,1)S(1)} %get-tuple-element.112.normed, ...), custom_call_target="tpu_custom_call" | custom-call | flops 1400000000 | tf_op jit(solution)/shard_map/attend/pallas_call | solution.py:37
  80.4 2.6 %collective-permute-done.14.refs_4_ = bf16[320,1472]{1,0:T(8,128)(2,1)S(1)} collective-permute-done((bf16[320,1472]{1,0:T(8,128)(2,1)S(1)}, bf16[320,1472]{1,0:T(8,128)(2,1)S(1)}, u32[]{:S(2)}, u32[]{:S(2)}) %collective-permute-start.14) | collective-permute-done | bytes 942112 | tf_op jit(solution)/shard_map/ppermute | solution.py:60
  85.9 2.9 %collective-permute-done.16.refs_3_ = bf16[3,80,1472]{2,1,0:T(8,128)(2,1)S(1)} collective-permute-done((bf16[3,80,1472]{2,1,0:T(8,128)(2,1)S(1)}, bf16[3,80,1472]{2,1,0:T(8,128)(2,1)S(1)}, u32[]{:S(2)}, u32[]{:S(2)}) %collective-permute-start.16) | collective-permute-done | bytes 706592 | tf_op jit(solution)/shard_map/ppermute | solution.py:60
  89.7 4.7 %all-gather.3.cloned.1.call-done = bf16[15488,128]{1,0:T(8,128)(2,1)} async-done(((bf16[3872,128]{1,0:T(8,128)(2,1)}), bf16[15488,128]{1,0:T(8,128)(2,1)}) %all-gather.3.cloned.1.call-update) | async-done | bytes 3964944 | tf_op jit(solution)/shard_map/all_gather | solution.py:639
  94.4 12.3 %feed_forward.1 = (bf16[4,3872,128]{2,1,0:T(8,128)(2,1)}, bf16[640,256]{1,0:T(8,128)(2,1)}, bf16[640,192]{1,0:T(8,128)(2,1)}, bf16[640,512]{1,0:T(8,128)(2,1)}, bf16[640,384]{1,0:T(8,128)(2,1)}) custom-call(s32[3]{0:T(128)} %pad_add_fusion.idx, bf16[4,3872,128]{2,1,0:T(8,128)(2,1)} %bitcast.62, bf16[320,1472]{1,0:T(8,128)(2,1)} %copy-done.14, ...), custom_call_target="tpu_custom_call" | custom-call | flops 1400000000 | tf_op jit(solution)/shard_map/feed_forward/pallas_call | solution.py:37
  106.7 7.6 %feed_out.1 = (bf16[4,80,1472]{2,1,0:T(8,128)(2,1)}, bf16[4,80,1472]{2,1,0:T(8,128)(2,1)}, bf16[4,80,1472]{2,1,0:T(8,128)(2,1)}, bf16[4,80,1472]{2,1,0:T(8,128)(2,1)}) custom-call(s32[3]{0:T(128)} %pad_add_fusion.idx, bf16[4,3872,128]{2,1,0:T(8,128)(2,1)} %bitcast.63, bf16[640,256]{1,0:T(8,128)(2,1)} %get-tuple-element.123.refs_0_, ...), custom_call_target="tpu_custom_call" | custom-call | flops 500000000 | tf_op jit(solution)/shard_map/feed_out/pallas_call | solution.py:37
  114.5 2.7 %collective-permute-done.17 = bf16[4,80,1472]{2,1,0:T(8,128)(2,1)S(1)} collective-permute-done((bf16[4,80,1472]{2,1,0:T(8,128)(2,1)}, bf16[4,80,1472]{2,1,0:T(8,128)(2,1)S(1)}, u32[]{:S(2)}, u32[]{:S(2)}) %collective-permute-start.17) | collective-permute-done | bytes 942112 | tf_op jit(solution)/shard_map/ppermute | solution.py:60
  117.2 1.5 fusion.6
  118.8 2.8 %collective-permute-start.20 = (bf16[80,1472]{1,0:T(8,128)(2,1)S(1)}, bf16[80,1472]{1,0:T(8,128)(2,1)S(1)}, u32[]{:S(2)}, u32[]{:S(2)}) collective-permute-start(bf16[80,1472]{1,0:T(8,128)(2,1)S(1)} %get-tuple-element.209), channel_id=1, source_target_pairs={{0,6},{2,4},{4,2},{6,0},{1,7},{3,5},{5,3},{7,1},{8,14},{10,12},{12... | collective-permute-start | bytes 706568 | tf_op jit(solution)/shard_map/ppermute | solution.py:60
  122.3 6.2 %collective-permute-done.20.refs_3_ = bf16[80,1472]{1,0:T(8,128)(2,1)S(1)} collective-permute-done((bf16[80,1472]{1,0:T(8,128)(2,1)S(1)}, bf16[80,1472]{1,0:T(8,128)(2,1)S(1)}, u32[]{:S(2)}, u32[]{:S(2)}) %collective-permute-start.20) | collective-permute-done | bytes 235552 | tf_op jit(solution)/shard_map/ppermute | solution.py:60
  128.6 4.5 %collective-permute-done.19.refs_2_ = bf16[80,1472]{1,0:T(8,128)(2,1)S(1)} collective-permute-done((bf16[80,1472]{1,0:T(8,128)(2,1)S(1)}, bf16[80,1472]{1,0:T(8,128)(2,1)S(1)}, u32[]{:S(2)}, u32[]{:S(2)}) %collective-permute-start.19) | collective-permute-done | bytes 235552 | tf_op jit(solution)/shard_map/ppermute | solution.py:60
  134.3 1.4 collective-permute-done.21.o_other
  135.9 4.1 %attend_back.1 = (bf16[160,384]{1,0:T(8,128)(2,1)S(1)}, bf16[160,384]{1,0:T(8,128)(2,1)S(1)}, bf16[160,384]{1,0:T(8,128)(2,1)S(1)}, bf16[160,384]{1,0:T(8,128)(2...) custom-call(s32[3]{0:T(128)S(1)} %copy-done.27, ...), custom_call_target="tpu_custom_call" | custom-call | flops 400000000 | tf_op jit(solution)/shard_map/attend_back/pallas_call | solution.py:37
  140.0 1.8 collective-permute-start.23
  143.6 2.1 collective-permute-done.23.refs_1_
  145.7 4.1 %collective-permute-done.24.refs_2_ = bf16[160,384]{1,0:T(8,128)(2,1)S(1)} collective-permute-done((bf16[160,384]{1,0:T(8,128)(2,1)S(1)}, bf16[160,384]{1,0:T(8,128)(2,1)S(1)}, u32[]{:S(2)}, u32[]{:S(2)}) %collective-permute-start.24) | collective-permute-done | bytes 122912 | tf_op jit(solution)/shard_map/ppermute | solution.py:60
  149.8 1.8 first_grad.1
  154.0 1.4 collective-permute-start.33
  155.8 8.2 %collective-permute-done.29.refs_5_ = bf16[48,1472]{1,0:T(8,128)(2,1)S(1)} collective-permute-done((bf16[48,1472]{1,0:T(8,128)(2,1)S(1)}, bf16[48,1472]{1,0:T(8,128)(2,1)S(1)}, u32[]{:S(2)}, u32[]{:S(2)}) %collective-permute-start.29) | collective-permute-done | bytes 141344 | tf_op jit(solution)/shard_map/ppermute | solution.py:60
  164.0 1.5 collective-permute-start.30
  168.6 2.1 collective-permute-start.27
  174.3 1.8 collective-permute-done.28.refs_3_
  176.1 1.7 weight_grads.1
  177.8 1.5 collective-permute-done.37.b_other
  179.6 1.5 collective-permute-start.39
  181.1 1.5 collective-permute-start.38
  182.6 2.8 %collective-permute-start.41 = (bf16[208,368]{1,0:T(8,128)(2,1)S(1)}, bf16[208,368]{1,0:T(8,128)(2,1)S(1)}, u32[]{:S(2)}, u32[]{:S(2)}) collective-permute-start(bf16[208,368]{1,0:T(8,128)(2,1)S(1)} %get-tuple-element.183), channel_id=1, source_target_pairs={{0,16},{8,24},{16,0},{24,8},{1,17},{9,25},{17,1},{25,9},{2,18},{10... | collective-permute-start | bytes 459272 | tf_op jit(solution)/shard_map/ppermute | solution.py:55
  187.5 1.5 place_outputs.1
  189.0 7.7 %collective-permute-done.41 = bf16[208,368]{1,0:T(8,128)(2,1)S(1)} collective-permute-done((bf16[208,368]{1,0:T(8,128)(2,1)S(1)}, bf16[208,368]{1,0:T(8,128)(2,1)S(1)}, u32[]{:S(2)}, u32[]{:S(2)}) %collective-permute-start.41) | collective-permute-done | bytes 153120 | tf_op jit(solution)/shard_map/ppermute | solution.py:55
  198.9 1.5 collective-permute-start.43
  200.4 9.2 %collective-permute-done.45.refs_3_ = bf16[208,368]{1,0:T(8,128)(2,1)S(1)} collective-permute-done((bf16[208,368]{1,0:T(8,128)(2,1)S(1)}, bf16[208,368]{1,0:T(8,128)(2,1)S(1)}, u32[]{:S(2)}, u32[]{:S(2)}) %collective-permute-start.45) | collective-permute-done | bytes 153120 | tf_op jit(solution)/shard_map/ppermute | solution.py:60
  211.3 1.5 collective-permute-start.48
  213.3 1.7 finish_attention.1
  215.0 3.7 %finish_wide.2 = (f32[368,1792]{1,0:T(8,128)}, f32[368,1792]{1,0:T(8,128)}, f32[368,1792]{1,0:T(8,128)}) custom-call(s32[3]{0:T(128)S(1)} %copy-done.27, bf16[3872,128]{1,0:T(8,128)(2,1)S(1)} %bitcast.55, bf16[3872,128]{1,0:T(8,128)(2,1)S(1)} %collective-permute-done.38.refs_1_, bf16[3872,128]{1,0:T(8,128)(2,1)S(1)} %collective-permute-done.39.refs_2_.refs_0_), custom_call_target="tpu_custom_call" | custom-call | flops 300000000 | tf_op jit(solution)/shard_map/finish_wide/pallas_call | solution.py:37
  219.4 3.4 %collective-permute-done.48.refs_2_ = bf16[1936,128]{1,0:T(8,128)(2,1)S(1)} collective-permute-done((bf16[1936,128]{1,0:T(8,128)(2,1)S(1)}, bf16[1936,128]{1,0:T(8,128)(2,1)S(1)}, u32[]{:S(2)}, u32[]{:S(2)}) %collective-permute-start.48) | collective-permute-done | bytes 495648 | tf_op jit(solution)/shard_map/ppermute | solution.py:60
  224.0 2.4 %finish_wide.3 = (f32[368,1792]{1,0:T(8,128)}, f32[368,1792]{1,0:T(8,128)}, f32[368,1792]{1,0:T(8,128)}) custom-call(s32[3]{0:T(128)S(1)} %copy-done.27, bf16[3872,128]{1,0:T(8,128)(2,1)S(1)} %collective-permute-done.39.refs_2_.refs_0_, ...), custom_call_target="tpu_custom_call", output_to_operand_aliasing={{0}: (4, {}), {1}: (5, {}), {2}: (6, {})} | custom-call | flops 300000000 | tf_op jit(solution)/shard_map/finish_wide/pallas_call | solution.py:37
  (170 shorter events, 32.8 us)
Async XLA Ops:
  7.2 87.2 %all-gather.3.cloned.1.call-start = ((), (), s32[]{:S(2)}) async-start(), calls=%async_computation.2 | async-start | bytes 4956160 | tf_op jit(solution)/shard_map/all_gather | solution.py:639
  9.9 169.7 %reduce-scatter.2.cloned.1.call-start = ((), (), s32[]{:S(2)}) async-start(), calls=%async_computation.1 | async-start | bytes 4956160 | tf_op jit(solution)/shard_map/reduce_scatter | solution.py:741
  13.4 14.7 %collective-permute-start.2 = (bf16[208,384]{1,0:T(8,128)(2,1)}, bf16[208,384]{1,0:T(8,128)(2,1)S(1)}, u32[]{:S(2)}, u32[]{:S(2)}) collective-permute-start(bf16[208,384]{1,0:T(8,128)(2,1)} %pack_attention.1.refs_4_), channel_id=1, source_target_pairs={{0,24},{8,0},{16,8},{24,16},{1,25},{9,1},{17,9},{25,17},{2,26},{10... | collective-permute-start | bytes 479240 | tf_op jit(solution)/shard_map/ppermute | solution.py:55
  18.5 13.5 %collective-permute-start = (bf16[208,384]{1,0:T(8,128)(2,1)}, bf16[208,384]{1,0:T(8,128)(2,1)S(1)}, u32[]{:S(2)}, u32[]{:S(2)}) collective-permute-start(bf16[208,384]{1,0:T(8,128)(2,1)} %pack_attention.1.refs_4_), channel_id=1, source_target_pairs={{0,8},{8,16},{16,24},{24,0},{1,9},{9,17},{17,25},{25,1},{2,10},{10... | collective-permute-start | bytes 479240 | tf_op jit(solution)/shard_map/ppermute | solution.py:55
  18.6 14.4 %collective-permute-start.6 = (bf16[80,1472]{1,0:T(8,128)(2,1)S(1)}, bf16[80,1472]{1,0:T(8,128)(2,1)S(1)}, u32[]{:S(2)}, u32[]{:S(2)}) collective-permute-start(bf16[80,1472]{1,0:T(8,128)(2,1)S(1)} %dynamic-slice_bitcast_fusion.1), channel_id=1, source_target_pairs={{0,6},{2,4},{4,2},{6,0},{1,7},{3,5},{5,3},{7,1},{8,14},{10,12},{12... | collective-permute-start | bytes 706568 | tf_op jit(solution)/shard_map/ppermute | solution.py:60
  21.3 11.7 %collective-permute-start.5 = (bf16[80,1472]{1,0:T(8,128)(2,1)S(1)}, bf16[80,1472]{1,0:T(8,128)(2,1)S(1)}, u32[]{:S(2)}, u32[]{:S(2)}) collective-permute-start(bf16[80,1472]{1,0:T(8,128)(2,1)S(1)} %dynamic-slice_bitcast_fusion.1), channel_id=1, source_target_pairs={{0,4},{2,6},{4,0},{6,2},{1,5},{3,7},{5,1},{7,3},{8,12},{10,14},{12... | collective-permute-start | bytes 706568 | tf_op jit(solution)/shard_map/ppermute | solution.py:60
  21.8 11.2 %collective-permute-start.4 = (bf16[80,1472]{1,0:T(8,128)(2,1)S(1)}, bf16[80,1472]{1,0:T(8,128)(2,1)S(1)}, u32[]{:S(2)}, u32[]{:S(2)}) collective-permute-start(bf16[80,1472]{1,0:T(8,128)(2,1)S(1)} %dynamic-slice_bitcast_fusion.1), channel_id=1, source_target_pairs={{0,2},{2,0},{4,6},{6,4},{1,3},{3,1},{5,7},{7,5},{8,10},{10,8},{12,... | collective-permute-start | bytes 706568 | tf_op jit(solution)/shard_map/ppermute | solution.py:60
  28.2 12.0 %collective-permute-start.3 = (bf16[104,384]{1,0:T(8,128)(2,1)S(1)}, bf16[104,384]{1,0:T(8,128)(2,1)S(1)}, u32[]{:S(2)}, u32[]{:S(2)}) collective-permute-start(bf16[104,384]{1,0:T(8,128)(2,1)S(1)} %slice.105), channel_id=1, source_target_pairs={{0,24},{8,0},{16,8},{24,16},{1,25},{9,1},{17,9},{25,17},{2,26},{10... | collective-permute-start | bytes 239624 | tf_op jit(solution)/shard_map/ppermute | solution.py:55
  32.0 8.1 %collective-permute-start.1 = (bf16[104,384]{1,0:T(8,128)(2,1)S(1)}, bf16[104,384]{1,0:T(8,128)(2,1)S(1)}, u32[]{:S(2)}, u32[]{:S(2)}) collective-permute-start(bf16[104,384]{1,0:T(8,128)(2,1)S(1)} %slice.104), channel_id=1, source_target_pairs={{0,8},{8,16},{16,24},{24,0},{1,9},{9,17},{17,25},{25,1},{2,10},{10... | collective-permute-start | bytes 239624 | tf_op jit(solution)/shard_map/ppermute | solution.py:55
  40.2 3.7 %collective-permute-start.10 = (bf16[3,80,1472]{2,1,0:T(8,128)(2,1)S(1)}, bf16[3,80,1472]{2,1,0:T(8,128)(2,1)S(1)}, u32[]{:S(2)}, u32[]{:S(2)}) collective-permute-start(bf16[3,80,1472]{2,1,0:T(8,128)(2,1)S(1)} %pad_maximum_fusion), channel_id=1, source_target_pairs={{0,1},{1,0},{2,3},{3,2},{4,5},{5,4},{6,7},{7,6},{8,9},{9,8},{10,11... | collective-permute-start | bytes 2119688 | tf_op jit(solution)/shard_map/ppermute | solution.py:60
  40.3 14.8 %collective-permute-start.9 = (bf16[624,384]{1,0:T(8,128)(2,1)S(1)}, bf16[624,384]{1,0:T(8,128)(2,1)S(1)}, u32[]{:S(2)}, u32[]{:S(2)}) collective-permute-start(bf16[624,384]{1,0:T(8,128)(2,1)S(1)} %constant_dynamic-update-slice_fusion.2.refs_0_), channel_id=1, source_target_pairs={{0,6},{2,4},{4,2},{6,0},{1,7},{3,5},{5,3},{7,1},{8,14},{10,12},{12... | collective-permute-start | bytes 1437704 | tf_op jit(solution)/shard_map/ppermute | solution.py:60
  43.1 21.9 %collective-permute-start.8 = (bf16[624,384]{1,0:T(8,128)(2,1)S(1)}, bf16[624,384]{1,0:T(8,128)(2,1)S(1)}, u32[]{:S(2)}, u32[]{:S(2)}) collective-permute-start(bf16[624,384]{1,0:T(8,128)(2,1)S(1)} %constant_dynamic-update-slice_fusion.2.refs_0_), channel_id=1, source_target_pairs={{0,4},{2,6},{4,0},{6,2},{1,5},{3,7},{5,1},{7,3},{8,12},{10,14},{12... | collective-permute-start | bytes 1437704 | tf_op jit(solution)/shard_map/ppermute | solution.py:60
  43.6 21.4 %collective-permute-start.7 = (bf16[624,384]{1,0:T(8,128)(2,1)S(1)}, bf16[624,384]{1,0:T(8,128)(2,1)S(1)}, u32[]{:S(2)}, u32[]{:S(2)}) collective-permute-start(bf16[624,384]{1,0:T(8,128)(2,1)S(1)} %constant_dynamic-update-slice_fusion.2.refs_0_), channel_id=1, source_target_pairs={{0,2},{2,0},{4,6},{6,4},{1,3},{3,1},{5,7},{7,5},{8,10},{10,8},{12,... | collective-permute-start | bytes 1437704 | tf_op jit(solution)/shard_map/ppermute | solution.py:60
  65.0 15.3 %collective-permute-start.13 = (bf16[80,1472]{1,0:T(8,128)(2,1)S(1)}, bf16[80,1472]{1,0:T(8,128)(2,1)S(1)}, u32[]{:S(2)}, u32[]{:S(2)}) collective-permute-start(bf16[80,1472]{1,0:T(8,128)(2,1)S(1)} %dynamic-slice_bitcast_fusion), channel_id=1, source_target_pairs={{0,6},{2,4},{4,2},{6,0},{1,7},{3,5},{5,3},{7,1},{8,14},{10,12},{12... | collective-permute-start | bytes 706568 | tf_op jit(solution)/shard_map/ppermute | solution.py:60
  66.9 13.4 %collective-permute-start.12 = (bf16[80,1472]{1,0:T(8,128)(2,1)S(1)}, bf16[80,1472]{1,0:T(8,128)(2,1)S(1)}, u32[]{:S(2)}, u32[]{:S(2)}) collective-permute-start(bf16[80,1472]{1,0:T(8,128)(2,1)S(1)} %dynamic-slice_bitcast_fusion), channel_id=1, source_target_pairs={{0,4},{2,6},{4,0},{6,2},{1,5},{3,7},{5,1},{7,3},{8,12},{10,14},{12... | collective-permute-start | bytes 706568 | tf_op jit(solution)/shard_map/ppermute | solution.py:60
  68.2 12.1 %collective-permute-start.11 = (bf16[80,1472]{1,0:T(8,128)(2,1)S(1)}, bf16[80,1472]{1,0:T(8,128)(2,1)S(1)}, u32[]{:S(2)}, u32[]{:S(2)}) collective-permute-start(bf16[80,1472]{1,0:T(8,128)(2,1)S(1)} %dynamic-slice_bitcast_fusion), channel_id=1, source_target_pairs={{0,2},{2,0},{4,6},{6,4},{1,3},{3,1},{5,7},{7,5},{8,10},{10,8},{12,... | collective-permute-start | bytes 706568 | tf_op jit(solution)/shard_map/ppermute | solution.py:60
  85.2 4.5 %collective-permute-start.15 = (bf16[320,1472]{1,0:T(8,128)(2,1)S(1)}, bf16[320,1472]{1,0:T(8,128)(2,1)}, u32[]{:S(2)}, u32[]{:S(2)}) collective-permute-start(bf16[320,1472]{1,0:T(8,128)(2,1)S(1)} %get-tuple-element.120.nt_mine), channel_id=1, source_target_pairs={{0,1},{1,0},{2,3},{3,2},{4,5},{5,4},{6,7},{7,6},{8,9},{9,8},{10,11... | collective-permute-start | bytes 2826248 | tf_op jit(solution)/shard_map/ppermute | solution.py:60
  85.5 3.4 %collective-permute-start.16 = (bf16[3,80,1472]{2,1,0:T(8,128)(2,1)S(1)}, bf16[3,80,1472]{2,1,0:T(8,128)(2,1)S(1)}, u32[]{:S(2)}, u32[]{:S(2)}) collective-permute-start(bf16[3,80,1472]{2,1,0:T(8,128)(2,1)S(1)} %pad_maximum_fusion.1), channel_id=1, source_target_pairs={{0,1},{1,0},{2,3},{3,2},{4,5},{5,4},{6,7},{7,6},{8,9},{9,8},{10,11... | collective-permute-start | bytes 2119688 | tf_op jit(solution)/shard_map/ppermute | solution.py:60
  114.4 2.8 %collective-permute-start.17 = (bf16[4,80,1472]{2,1,0:T(8,128)(2,1)}, bf16[4,80,1472]{2,1,0:T(8,128)(2,1)S(1)}, u32[]{:S(2)}, u32[]{:S(2)}) collective-permute-start(bf16[4,80,1472]{2,1,0:T(8,128)(2,1)} %get-tuple-element.130), channel_id=1, source_target_pairs={{0,1},{1,0},{2,3},{3,2},{4,5},{5,4},{6,7},{7,6},{8,9},{9,8},{10,11... | collective-permute-start | bytes 2826248 | tf_op jit(solution)/shard_map/ppermute | solution.py:60
  118.8 9.8 %collective-permute-start.20 = (bf16[80,1472]{1,0:T(8,128)(2,1)S(1)}, bf16[80,1472]{1,0:T(8,128)(2,1)S(1)}, u32[]{:S(2)}, u32[]{:S(2)}) collective-permute-start(bf16[80,1472]{1,0:T(8,128)(2,1)S(1)} %get-tuple-element.209), channel_id=1, source_target_pairs={{0,6},{2,4},{4,2},{6,0},{1,7},{3,5},{5,3},{7,1},{8,14},{10,12},{12... | collective-permute-start | bytes 706568 | tf_op jit(solution)/shard_map/ppermute | solution.py:60
  121.5 11.5 %collective-permute-start.19 = (bf16[80,1472]{1,0:T(8,128)(2,1)S(1)}, bf16[80,1472]{1,0:T(8,128)(2,1)S(1)}, u32[]{:S(2)}, u32[]{:S(2)}) collective-permute-start(bf16[80,1472]{1,0:T(8,128)(2,1)S(1)} %get-tuple-element.210), channel_id=1, source_target_pairs={{0,4},{2,6},{4,0},{6,2},{1,5},{3,7},{5,1},{7,3},{8,12},{10,14},{12... | collective-permute-start | bytes 706568 | tf_op jit(solution)/shard_map/ppermute | solution.py:60
  122.0 11.1 %collective-permute-start.18 = (bf16[80,1472]{1,0:T(8,128)(2,1)S(1)}, bf16[80,1472]{1,0:T(8,128)(2,1)S(1)}, u32[]{:S(2)}, u32[]{:S(2)}) collective-permute-start(bf16[80,1472]{1,0:T(8,128)(2,1)S(1)} %get-tuple-element.211), channel_id=1, source_target_pairs={{0,2},{2,0},{4,6},{6,4},{1,3},{3,1},{5,7},{7,5},{8,10},{10,8},{12,... | collective-permute-start | bytes 706568 | tf_op jit(solution)/shard_map/ppermute | solution.py:60
  135.7 4.3 %collective-permute-start.22 = (bf16[4,80,1472]{2,1,0:T(8,128)(2,1)S(1)}, bf16[4,80,1472]{2,1,0:T(8,128)(2,1)S(1)}, u32[]{:S(2)}, u32[]{:S(2)}) collective-permute-start(bf16[4,80,1472]{2,1,0:T(8,128)(2,1)S(1)} %copy-done.35), channel_id=1, source_target_pairs={{0,1},{1,0},{2,3},{3,2},{4,5},{5,4},{6,7},{7,6},{8,9},{9,8},{10,11... | collective-permute-start | bytes 2826248 | tf_op jit(solution)/shard_map/ppermute | solution.py:60
  140.0 5.7 %collective-permute-start.23 = (bf16[160,384]{1,0:T(8,128)(2,1)S(1)}, bf16[160,384]{1,0:T(8,128)(2,1)S(1)}, u32[]{:S(2)}, u32[]{:S(2)}) collective-permute-start(bf16[160,384]{1,0:T(8,128)(2,1)S(1)} %get-tuple-element.144), channel_id=1, source_target_pairs={{0,2},{2,0},{4,6},{6,4},{1,3},{3,1},{5,7},{7,5},{8,10},{10,8},{12,... | collective-permute-start | bytes 368648 | tf_op jit(solution)/shard_map/ppermute | solution.py:60
  141.8 7.9 %collective-permute-start.24 = (bf16[160,384]{1,0:T(8,128)(2,1)S(1)}, bf16[160,384]{1,0:T(8,128)(2,1)S(1)}, u32[]{:S(2)}, u32[]{:S(2)}) collective-permute-start(bf16[160,384]{1,0:T(8,128)(2,1)S(1)} %get-tuple-element.146), channel_id=1, source_target_pairs={{0,4},{2,6},{4,0},{6,2},{1,5},{3,7},{5,1},{7,3},{8,12},{10,14},{12... | collective-permute-start | bytes 368648 | tf_op jit(solution)/shard_map/ppermute | solution.py:60
  142.4 7.3 %collective-permute-start.25 = (bf16[160,384]{1,0:T(8,128)(2,1)S(1)}, bf16[160,384]{1,0:T(8,128)(2,1)S(1)}, u32[]{:S(2)}, u32[]{:S(2)}) collective-permute-start(bf16[160,384]{1,0:T(8,128)(2,1)S(1)} %get-tuple-element.148), channel_id=1, source_target_pairs={{0,6},{2,4},{4,2},{6,0},{1,7},{3,5},{5,3},{7,1},{8,14},{10,12},{12... | collective-permute-start | bytes 368648 | tf_op jit(solution)/shard_map/ppermute | solution.py:60
  151.8 13.6 %collective-permute-start.34 = (bf16[80,1472]{1,0:T(8,128)(2,1)S(1)}, bf16[80,1472]{1,0:T(8,128)(2,1)S(1)}, u32[]{:S(2)}, u32[]{:S(2)}) collective-permute-start(bf16[80,1472]{1,0:T(8,128)(2,1)S(1)} %get-tuple-element.206), channel_id=1, source_target_pairs={{0,6},{2,4},{4,2},{6,0},{1,7},{3,5},{5,3},{7,1},{8,14},{10,12},{12... | collective-permute-start | bytes 706568 | tf_op jit(solution)/shard_map/ppermute | solution.py:60
  153.1 10.9 %collective-permute-start.29 = (bf16[48,1472]{1,0:T(8,128)(2,1)S(1)}, bf16[48,1472]{1,0:T(8,128)(2,1)S(1)}, u32[]{:S(2)}, u32[]{:S(2)}) collective-permute-start(bf16[48,1472]{1,0:T(8,128)(2,1)S(1)} %get-tuple-element.158), channel_id=1, source_target_pairs={{0,2},{2,0},{4,6},{6,4},{1,3},{3,1},{5,7},{7,5},{8,10},{10,8},{12,... | collective-permute-start | bytes 423944 | tf_op jit(solution)/shard_map/ppermute | solution.py:60
  154.0 12.6 %collective-permute-start.33 = (bf16[80,1472]{1,0:T(8,128)(2,1)S(1)}, bf16[80,1472]{1,0:T(8,128)(2,1)S(1)}, u32[]{:S(2)}, u32[]{:S(2)}) collective-permute-start(bf16[80,1472]{1,0:T(8,128)(2,1)S(1)} %get-tuple-element.207), channel_id=1, source_target_pairs={{0,4},{2,6},{4,0},{6,2},{1,5},{3,7},{5,1},{7,3},{8,12},{10,14},{12... | collective-permute-start | bytes 706568 | tf_op jit(solution)/shard_map/ppermute | solution.py:60
  155.4 13.3 %collective-permute-start.32 = (bf16[80,1472]{1,0:T(8,128)(2,1)S(1)}, bf16[80,1472]{1,0:T(8,128)(2,1)S(1)}, u32[]{:S(2)}, u32[]{:S(2)}) collective-permute-start(bf16[80,1472]{1,0:T(8,128)(2,1)S(1)} %get-tuple-element.208), channel_id=1, source_target_pairs={{0,2},{2,0},{4,6},{6,4},{1,3},{3,1},{5,7},{7,5},{8,10},{10,8},{12,... | collective-permute-start | bytes 706568 | tf_op jit(solution)/shard_map/ppermute | solution.py:60
  155.8 15.0 %collective-permute-start.35 = (bf16[80,1472]{1,0:T(8,128)(2,1)S(1)}, bf16[80,1472]{1,0:T(8,128)(2,1)S(1)}, u32[]{:S(2)}, u32[]{:S(2)}) collective-permute-start(bf16[80,1472]{1,0:T(8,128)(2,1)S(1)} %get-tuple-element.166), channel_id=1, source_target_pairs={{0,1},{1,0},{2,3},{3,2},{4,5},{5,4},{6,7},{7,6},{8,9},{9,8},{10,11... | collective-permute-start | bytes 706568 | tf_op jit(solution)/shard_map/ppermute | solution.py:60
  164.0 9.5 %collective-permute-start.30 = (bf16[48,1472]{1,0:T(8,128)(2,1)S(1)}, bf16[48,1472]{1,0:T(8,128)(2,1)S(1)}, u32[]{:S(2)}, u32[]{:S(2)}) collective-permute-start(bf16[48,1472]{1,0:T(8,128)(2,1)S(1)} %get-tuple-element.160), channel_id=1, source_target_pairs={{0,4},{2,6},{4,0},{6,2},{1,5},{3,7},{5,1},{7,3},{8,12},{10,14},{12... | collective-permute-start | bytes 423944 | tf_op jit(solution)/shard_map/ppermute | solution.py:60
  165.4 8.0 %collective-permute-start.31 = (bf16[48,1472]{1,0:T(8,128)(2,1)S(1)}, bf16[48,1472]{1,0:T(8,128)(2,1)S(1)}, u32[]{:S(2)}, u32[]{:S(2)}) collective-permute-start(bf16[48,1472]{1,0:T(8,128)(2,1)S(1)} %get-tuple-element.162), channel_id=1, source_target_pairs={{0,6},{2,4},{4,2},{6,0},{1,7},{3,5},{5,3},{7,1},{8,14},{10,12},{12... | collective-permute-start | bytes 423944 | tf_op jit(solution)/shard_map/ppermute | solution.py:60
  166.6 6.8 %collective-permute-start.26 = (bf16[160,144]{1,0:T(8,128)(2,1)S(1)}, bf16[160,144]{1,0:T(8,128)(2,1)S(1)}, u32[]{:S(2)}, u32[]{:S(2)}) collective-permute-start(bf16[160,144]{1,0:T(8,128)(2,1)S(1)} %get-tuple-element.152), channel_id=1, source_target_pairs={{0,2},{2,0},{4,6},{6,4},{1,3},{3,1},{5,7},{7,5},{8,10},{10,8},{12,... | collective-permute-start | bytes 138248 | tf_op jit(solution)/shard_map/ppermute | solution.py:60
  168.6 5.7 %collective-permute-start.27 = (bf16[160,144]{1,0:T(8,128)(2,1)S(1)}, bf16[160,144]{1,0:T(8,128)(2,1)S(1)}, u32[]{:S(2)}, u32[]{:S(2)}) collective-permute-start(bf16[160,144]{1,0:T(8,128)(2,1)S(1)} %get-tuple-element.154), channel_id=1, source_target_pairs={{0,4},{2,6},{4,0},{6,2},{1,5},{3,7},{5,1},{7,3},{8,12},{10,14},{12... | collective-permute-start | bytes 138248 | tf_op jit(solution)/shard_map/ppermute | solution.py:60
  170.7 5.3 %collective-permute-start.28 = (bf16[160,144]{1,0:T(8,128)(2,1)S(1)}, bf16[160,144]{1,0:T(8,128)(2,1)S(1)}, u32[]{:S(2)}, u32[]{:S(2)}) collective-permute-start(bf16[160,144]{1,0:T(8,128)(2,1)S(1)} %get-tuple-element.156), channel_id=1, source_target_pairs={{0,6},{2,4},{4,2},{6,0},{1,7},{3,5},{5,3},{7,1},{8,14},{10,12},{12... | collective-permute-start | bytes 138248 | tf_op jit(solution)/shard_map/ppermute | solution.py:60
  173.4 4.4 %collective-permute-start.36 = (bf16[80,1472]{1,0:T(8,128)(2,1)S(1)}, bf16[80,1472]{1,0:T(8,128)(2,1)S(1)}, u32[]{:S(2)}, u32[]{:S(2)}) collective-permute-start(bf16[80,1472]{1,0:T(8,128)(2,1)S(1)} %produce.1.a_mine), channel_id=1, source_target_pairs={{0,1},{1,0},{2,3},{3,2},{4,5},{5,4},{6,7},{7,6},{8,9},{9,8},{10,11... | collective-permute-start | bytes 706568 | tf_op jit(solution)/shard_map/ppermute | solution.py:60
  179.6 31.6 %collective-permute-start.39 = (bf16[3872,128]{1,0:T(8,128)(2,1)}, bf16[3872,128]{1,0:T(8,128)(2,1)S(1)}, u32[]{:S(2)}, u32[]{:S(2)}) collective-permute-start(bf16[3872,128]{1,0:T(8,128)(2,1)} %bitcast.53), channel_id=1, source_target_pairs={{0,4},{2,6},{4,0},{6,2},{1,5},{3,7},{5,1},{7,3},{8,12},{10,14},{12... | collective-permute-start | bytes 2973704 | tf_op jit(solution)/shard_map/ppermute | solution.py:60
  181.1 30.1 %collective-permute-start.38 = (bf16[3872,128]{1,0:T(8,128)(2,1)}, bf16[3872,128]{1,0:T(8,128)(2,1)S(1)}, u32[]{:S(2)}, u32[]{:S(2)}) collective-permute-start(bf16[3872,128]{1,0:T(8,128)(2,1)} %bitcast.54), channel_id=1, source_target_pairs={{0,2},{2,0},{4,6},{6,4},{1,3},{3,1},{5,7},{7,5},{8,10},{10,8},{12,... | collective-permute-start | bytes 2973704 | tf_op jit(solution)/shard_map/ppermute | solution.py:60
  182.6 14.1 %collective-permute-start.41 = (bf16[208,368]{1,0:T(8,128)(2,1)S(1)}, bf16[208,368]{1,0:T(8,128)(2,1)S(1)}, u32[]{:S(2)}, u32[]{:S(2)}) collective-permute-start(bf16[208,368]{1,0:T(8,128)(2,1)S(1)} %get-tuple-element.183), channel_id=1, source_target_pairs={{0,16},{8,24},{16,0},{24,8},{1,17},{9,25},{17,1},{25,9},{2,18},{10... | collective-permute-start | bytes 459272 | tf_op jit(solution)/shard_map/ppermute | solution.py:55
  185.5 11.3 %collective-permute-start.42 = (bf16[208,368]{1,0:T(8,128)(2,1)S(1)}, bf16[208,368]{1,0:T(8,128)(2,1)S(1)}, u32[]{:S(2)}, u32[]{:S(2)}) collective-permute-start(bf16[208,368]{1,0:T(8,128)(2,1)S(1)} %get-tuple-element.185), channel_id=1, source_target_pairs={{0,24},{8,0},{16,8},{24,16},{1,25},{9,1},{17,9},{25,17},{2,26},{10... | collective-permute-start | bytes 459272 | tf_op jit(solution)/shard_map/ppermute | solution.py:55
  186.4 10.3 %collective-permute-start.40 = (bf16[208,368]{1,0:T(8,128)(2,1)S(1)}, bf16[208,368]{1,0:T(8,128)(2,1)S(1)}, u32[]{:S(2)}, u32[]{:S(2)}) collective-permute-start(bf16[208,368]{1,0:T(8,128)(2,1)S(1)} %get-tuple-element.181), channel_id=1, source_target_pairs={{0,8},{8,16},{16,24},{24,0},{1,9},{9,17},{17,25},{25,1},{2,10},{10... | collective-permute-start | bytes 459272 | tf_op jit(solution)/shard_map/ppermute | solution.py:55
  196.8 12.8 %collective-permute-start.45 = (bf16[208,368]{1,0:T(8,128)(2,1)S(1)}, bf16[208,368]{1,0:T(8,128)(2,1)S(1)}, u32[]{:S(2)}, u32[]{:S(2)}) collective-permute-start(bf16[208,368]{1,0:T(8,128)(2,1)S(1)} %fusion.2.refs_0_), channel_id=1, source_target_pairs={{0,6},{2,4},{4,2},{6,0},{1,7},{3,5},{5,3},{7,1},{8,14},{10,12},{12... | collective-permute-start | bytes 459272 | tf_op jit(solution)/shard_map/ppermute | solution.py:60
  197.7 12.7 %collective-permute-start.44 = (bf16[208,368]{1,0:T(8,128)(2,1)S(1)}, bf16[208,368]{1,0:T(8,128)(2,1)S(1)}, u32[]{:S(2)}, u32[]{:S(2)}) collective-permute-start(bf16[208,368]{1,0:T(8,128)(2,1)S(1)} %fusion.2.refs_0_), channel_id=1, source_target_pairs={{0,4},{2,6},{4,0},{6,2},{1,5},{3,7},{5,1},{7,3},{8,12},{10,14},{12... | collective-permute-start | bytes 459272 | tf_op jit(solution)/shard_map/ppermute | solution.py:60
  198.9 12.3 %collective-permute-start.43 = (bf16[208,368]{1,0:T(8,128)(2,1)S(1)}, bf16[208,368]{1,0:T(8,128)(2,1)S(1)}, u32[]{:S(2)}, u32[]{:S(2)}) collective-permute-start(bf16[208,368]{1,0:T(8,128)(2,1)S(1)} %fusion.2.refs_0_), channel_id=1, source_target_pairs={{0,2},{2,0},{4,6},{6,4},{1,3},{3,1},{5,7},{7,5},{8,10},{10,8},{12,... | collective-permute-start | bytes 459272 | tf_op jit(solution)/shard_map/ppermute | solution.py:60
  211.3 11.5 %collective-permute-start.48 = (bf16[1936,128]{1,0:T(8,128)(2,1)S(1)}, bf16[1936,128]{1,0:T(8,128)(2,1)S(1)}, u32[]{:S(2)}, u32[]{:S(2)}) collective-permute-start(bf16[1936,128]{1,0:T(8,128)(2,1)S(1)} %slice.103), channel_id=1, source_target_pairs={{0,2},{2,0},{4,6},{6,4},{1,3},{3,1},{5,7},{7,5},{8,10},{10,8},{12,... | collective-permute-start | bytes 1486856 | tf_op jit(solution)/shard_map/ppermute | solution.py:60
  212.8 11.2 %collective-permute-start.47 = (bf16[1936,128]{1,0:T(8,128)(2,1)S(1)}, bf16[1936,128]{1,0:T(8,128)(2,1)S(1)}, u32[]{:S(2)}, u32[]{:S(2)}) collective-permute-start(bf16[1936,128]{1,0:T(8,128)(2,1)S(1)} %slice.102), channel_id=1, source_target_pairs={{0,4},{2,6},{4,0},{6,2},{1,5},{3,7},{5,1},{7,3},{8,12},{10,14},{12... | collective-permute-start | bytes 1486856 | tf_op jit(solution)/shard_map/ppermute | solution.py:60
  215.0 3.7 %collective-permute-start.46 = (f32[2,368]{1,0:T(2,128)S(1)}, f32[2,368]{1,0:T(2,128)S(1)}, u32[]{:S(2)}, u32[]{:S(2)}) collective-permute-start(f32[2,368]{1,0:T(2,128)S(1)} %get-tuple-element.189), channel_id=1, source_target_pairs={{0,1},{1,0},{2,3},{3,2},{4,5},{5,4},{6,7},{7,6},{8,9},{9,8},{10,11... | collective-permute-start | bytes 8840 | tf_op jit(solution)/shard_map/ppermute | solution.py:60
  (39 other events, 582.2 us)
Sparse Core Ops, SparseCore 0:
  10.2 84.1 all-gather.2
  106.9 72.7 reduce-scatter.1

commit v7 on v6

--- a/solution.py
+++ b/solution.py
@@ -95,18 +95,20 @@
     return parts, pl.cdiv(row, 32) * 32
 
 
-def pack_wide(n_ctx, widths, window, w_g, w_u, w_d, buf, held, sems):
+def pack_wide(period, widths, window, w_g, w_u, w_d, buf, held, sems):
     c = lax.axis_index("ctx")
     r = w_g.shape[0]
     columns = sum(widths)
     parts, _ = wide_tiles(r, widths)
-    for v in range(n_ctx):
-
-        @pl.when(c == v)
+    for v in range(period):
+
+        @pl.when(lax.rem(c, period) == v)
         def _(v=v):
-            start = min(v * columns // LANES * LANES, w_g.shape[1] - window)
+            start = v * columns // LANES * LANES
+            far = lax.div(c, period) * (period * columns) + start
+            here = pl.ds(pl.multiple_of(far, LANES), window)
             copies = [
-                pltpu.make_async_copy(ref.at[:, start : start + window], held.at[i], sems.at[i])
+                pltpu.make_async_copy(ref.at[:, here], held.at[i], sems.at[i])
                 for i, ref in enumerate((w_g, w_u, w_d))
             ]
             for copy in copies:
@@ -356,13 +358,13 @@
         unpack_wide(parts, r, buf, weights, j)
     for copy in begun[n_shard:]:
         copy.wait()
-    out = []
     for held, given, lefts, first, last in (
         (two_held, two, pair, 0, 2),
         (feed_held, feed, hidden, 2, 3),
     ):
-        for m in (1, 0):
-            at = slice(m * length, (m + 1) * length)
+
+        def half_rows(m, _, held=held, lefts=lefts, first=first, last=last):
+            at = pl.ds(pl.multiple_of(m * length, length), length)
             total = sum(
                 (
                     dot_nt(lefts[e][at, :], weights[e][:, first * n : last * n])
@@ -371,10 +373,17 @@
             )
             for i in range(n_ctx):
                 held[m, i] = total[i * rows : (i + 1) * rows].astype(low)
-            copy = pltpu.make_async_copy(held.at[m], given[m], sems_out.at[len(out)])
-            copy.start()
-            out.append(copy)
-    for copy in out:
+            return 0
+
+        lax.fori_loop(0, 2, half_rows, 0)
+    copies = [
+        pltpu.make_async_copy(held.at[m], given[m], sems_out.at[2 * i + m])
+        for i, (held, given) in enumerate(((two_held, two), (feed_held, feed)))
+        for m in range(2)
+    ]
+    for copy in copies:
+        copy.start()
+    for copy in copies:
         copy.wait()
 
 
@@ -508,7 +517,7 @@
     out[...] = (middle[...] + sum((p[...].astype(wide) for p in parts))).astype(low)
 
 
-def finish_wide(n_ctx, widths, groups, idx, *refs):
+def finish_wide(period, widths, groups, idx, *refs):
     flat = [item for group in groups for item in group]
     count = sum((pieces for _, pieces, _ in flat))
     sources, refs = refs[:count], refs[count:]
@@ -517,16 +526,17 @@
     r = outs[0].shape[0]
     columns = sum(widths)
     parts, rows = wide_tiles(r, widths)
-    for v in range(n_ctx):
-
-        @pl.when(idx[1] == v)
+    c = idx[1]
+    for v in range(period):
+
+        @pl.when(lax.rem(c, period) == v)
         def _(v=v):
             first = 0
             copies = []
             for g, group in enumerate(groups):
                 taken = []
                 for k, pieces, lanes_kind in group:
-                    begin = (v ^ k) * columns
+                    begin = ((v ^ k) % period) * columns
                     tile_low = pl.cdiv(begin, LANES) * LANES - begin
                     tile_high = (begin + columns) // LANES * LANES - begin
                     if lanes_kind == "all":
@@ -539,8 +549,9 @@
                         low_lane, high_lane = tile_high, columns
                     taken.append((k, pieces, low_lane, high_lane, first))
                     first += pieces
-                start = min(((v ^ k) * columns + lo for k, _, lo, _, _ in taken))
-                stop = max(((v ^ k) * columns + hi for k, _, _, hi, _ in taken))
+                start = min((((v ^ k) % period) * columns + lo for k, _, lo, _, _ in taken))
+                stop = max((((v ^ k) % period) * columns + hi for k, _, _, hi, _ in taken))
+                far = (lax.div(c, period) ^ (group[0][0] // period)) * (period * columns) + start
                 for k, pieces, low_lane, high_lane, at_source in taken:
                     size_each = rows // pieces
                     for i, n in enumerate(widths):
@@ -559,7 +570,7 @@
                                     ].astype(wide)
                                 )
                                 done += many
-                        to = (v ^ k) * columns + lo - start
+                        to = ((v ^ k) % period) * columns + lo - start
                         for j in range(3):
                             held[g, j, :, to : to + hi - lo] = stage[
                                 :, j * n + lo - base : j * n + hi - base
@@ -567,7 +578,7 @@
                 for j in range(3):
                     copy = pltpu.make_async_copy(
                         held.at[g, j, :, 0 : stop - start],
-                        outs[j].at[:, start:stop],
+                        outs[j].at[:, pl.ds(pl.multiple_of(far, LANES), stop - start)],
                         sems.at[3 * g + j],
                     )
                     copy.start()
@@ -621,9 +632,13 @@
 
 
     wide_rows = wide_tiles(r, widths)[1]
-    window = min(pl.cdiv(columns, LANES) * LANES, w_gate.shape[1])
+    period = next(p for p in range(1, ctx + 1) if p == ctx or p * columns % LANES == 0)
+    window = max(
+        pl.cdiv((v + 1) * columns, LANES) * LANES - v * columns // LANES * LANES
+        for v in range(period)
+    )
     (packed,) = run(
-        functools.partial(pack_wide, ctx, widths, window),
+        functools.partial(pack_wide, period, widths, window),
         "pack_wide",
         [((wide_rows, LANES), low)],
         [w_gate, w_up, w_down.T],
@@ -867,9 +882,12 @@
     )
     own_gain = own_gain + swap(own_gain, "tensor")
 
+    pairs = pair and period <= 2
+    period = 2 if pairs else ctx
+
     def finish(now, groups, sources, span, before):
         return run(
-            functools.partial(finish_wide, ctx, widths, groups),
+            functools.partial(finish_wide, period, widths, groups),
             "finish_wide",
             [(w_gate.shape, wide)] * 3,
             [now, *sources, *before],
@@ -884,7 +902,7 @@
             vmem=24,
         )
 
-    if pair and 2 * columns % LANES == 0:
+    if pairs:
         groups = [[(0, 1, "all"), (1, 1, "all")], [(2, 1, "full")]]
         outs = finish(now, groups, [wide_own, *wide_all], 2 * columns, [])
         now = after(now, *far_halves, outs[0], own_gain)

time: 238 us -> 233 us (0.979); the launches traced: 234 us -> 233 us
  transfers between devices with their start and end apart: 51 -> 51, of which waited for: 27 -> 26; matrix products, arithmetic and copies ran while one was open for 2% -> 2% of each run, Pallas kernels for 20% -> 20%
where the time goes in v7:
time: 233 us
  waiting for transfers between devices  95 us (41%)
  Pallas kernels  64 us (27%)
  starting transfers between devices  52.7 us (23%)
  between operations  14.8 us (6%)
  local copies, waits for them, and re-layouts  3.55 us (2%)
  other arithmetic  3.2 us (1%)
    ppermute x42, waiting for transfers between devices, swap(): return lax.ppermute(x, axis, [(i, i ^ k) for i in range(n)])  75.7 us
    pallas_call x18, Pallas kernels, run(): pl.pallas_call(body, name=name, out_shape=[jax.ShapeDtypeStruct(s, d) for...  64 us
    ppermute x42, starting transfers between devices, swap(): return lax.ppermute(x, axis, [(i, i ^ k) for i in range(n)])  37.8 us
    ppermute x7, starting transfers between devices, step(): return lax.ppermute(x, axis, [(i, (i + k) % n) for i in range(n)])  14.8 us
    ppermute x7, waiting for transfers between devices, step(): return lax.ppermute(x, axis, [(i, (i + k) % n) for i in range(n)])  14.6 us
    all_gather x1, waiting for transfers between devices, on_device(): chunks = lax.all_gather(packed, 'shard', axis=0, tiled=False)  4.67 us
  transfers between devices with their start and end apart: 51, of which 26 were waited for; matrix products, arithmetic and copies ran while one was open for 2% of the time, Pallas kernels for 20%

profile of v7, /device:TPU:0, one launch (start us, length us, event | category | flops | bytes accessed | tf_op | source)
XLA Modules:
  0.0 233.2 jit_solution(2899126907642710151)
XLA Ops:
  7.3 2.6 %pack_wide.1 = bf16[3872,128]{1,0:T(8,128)(2,1)} custom-call(bf16[368,1792]{1,0:T(8,128)(2,1)} %w_g.1, bf16[368,1792]{1,0:T(8,128)(2,1)} %w_u.1, bf16[368,1792]{1,0:T(8,128)(2,1)} %bitcast.65), custom_call_target="tpu_custom_call" | custom-call | flops 200000000 | tf_op jit(solution)/shard_map/pack_wide/pallas_call | solution.py:37
  11.1 2.3 pack_attention.1.refs_4_
  13.4 5.1 %collective-permute-start.2 = (bf16[208,384]{1,0:T(8,128)(2,1)}, bf16[208,384]{1,0:T(8,128)(2,1)S(1)}, u32[]{:S(2)}, u32[]{:S(2)}) collective-permute-start(bf16[208,384]{1,0:T(8,128)(2,1)} %pack_attention.1.refs_4_), channel_id=1, source_target_pairs={{0,24},{8,0},{16,8},{24,16},{1,25},{9,1},{17,9},{25,17},{2,26},{10... | collective-permute-start | bytes 479240 | tf_op jit(solution)/shard_map/ppermute | solution.py:55
  18.6 2.8 %collective-permute-start.6 = (bf16[80,1472]{1,0:T(8,128)(2,1)S(1)}, bf16[80,1472]{1,0:T(8,128)(2,1)S(1)}, u32[]{:S(2)}, u32[]{:S(2)}) collective-permute-start(bf16[80,1472]{1,0:T(8,128)(2,1)S(1)} %dynamic-slice_bitcast_fusion.1), channel_id=1, source_target_pairs={{0,6},{2,4},{4,2},{6,0},{1,7},{3,5},{5,3},{7,1},{8,14},{10,12},{12... | collective-permute-start | bytes 706568 | tf_op jit(solution)/shard_map/ppermute | solution.py:60
  22.8 5.3 %bias.1 = f32[3,320,320]{2,1,0:T(8,128)S(1)} custom-call(s32[3]{0:T(128)S(1)} %copy-done.26, f32[32,3]{1,0:T(8,128)S(1)} %copy.27.table), custom_call_target="tpu_custom_call" | custom-call | flops 500000000 | tf_op jit(solution)/shard_map/bias/pallas_call | solution.py:37
  28.2 3.9 %collective-permute-start.3 = (bf16[104,384]{1,0:T(8,128)(2,1)S(1)}, bf16[104,384]{1,0:T(8,128)(2,1)S(1)}, u32[]{:S(2)}, u32[]{:S(2)}) collective-permute-start(bf16[104,384]{1,0:T(8,128)(2,1)S(1)} %slice.105), channel_id=1, source_target_pairs={{0,24},{8,0},{16,8},{24,16},{1,25},{9,1},{17,9},{25,17},{2,26},{10... | collective-permute-start | bytes 239624 | tf_op jit(solution)/shard_map/ppermute | solution.py:55
  33.2 6.9 %collective-permute-done.1 = bf16[104,384]{1,0:T(8,128)(2,1)S(1)} collective-permute-done((bf16[104,384]{1,0:T(8,128)(2,1)S(1)}, bf16[104,384]{1,0:T(8,128)(2,1)S(1)}, u32[]{:S(2)}, u32[]{:S(2)}) %collective-permute-start.1) | collective-permute-done | bytes 79904 | tf_op jit(solution)/shard_map/ppermute | solution.py:55
  40.3 2.7 %collective-permute-start.9 = (bf16[624,384]{1,0:T(8,128)(2,1)S(1)}, bf16[624,384]{1,0:T(8,128)(2,1)S(1)}, u32[]{:S(2)}, u32[]{:S(2)}) collective-permute-start(bf16[624,384]{1,0:T(8,128)(2,1)S(1)} %constant_dynamic-update-slice_fusion.2.refs_0_), channel_id=1, source_target_pairs={{0,6},{2,4},{4,2},{6,0},{1,7},{3,5},{5,3},{7,1},{8,14},{10,12},{12... | collective-permute-start | bytes 1437704 | tf_op jit(solution)/shard_map/ppermute | solution.py:60
  45.3 9.8 %collective-permute-done.9.refs_3_ = bf16[624,384]{1,0:T(8,128)(2,1)S(1)} collective-permute-done((bf16[624,384]{1,0:T(8,128)(2,1)S(1)}, bf16[624,384]{1,0:T(8,128)(2,1)S(1)}, u32[]{:S(2)}, u32[]{:S(2)}) %collective-permute-start.9) | collective-permute-done | bytes 479264 | tf_op jit(solution)/shard_map/ppermute | solution.py:60
  55.1 9.9 %collective-permute-done.8.refs_2_ = bf16[624,384]{1,0:T(8,128)(2,1)S(1)} collective-permute-done((bf16[624,384]{1,0:T(8,128)(2,1)S(1)}, bf16[624,384]{1,0:T(8,128)(2,1)S(1)}, u32[]{:S(2)}, u32[]{:S(2)}) %collective-permute-start.8) | collective-permute-done | bytes 479264 | tf_op jit(solution)/shard_map/ppermute | solution.py:60
  65.0 1.8 collective-permute-start.13
  66.9 1.4 collective-permute-start.12
  68.6 11.7 %attend.1 = (bf16[320,1472]{1,0:T(8,128)(2,1)S(1)}, bf16[320,1472]{1,0:T(8,128)(2,1)S(1)}, f32[2,3,80,320]{3,2,1,0:T(8,128)S(1)}, bf16[640,576]{1,0:T(8,128)(2,1...) custom-call(s32[3]{0:T(128)S(1)} %copy-done.26, bf16[640,1472]{1,0:T(8,128)(2,1)S(1)} %get-tuple-element.112.normed, ...), custom_call_target="tpu_custom_call" | custom-call | flops 1400000000 | tf_op jit(solution)/shard_map/attend/pallas_call | solution.py:37
  80.4 2.6 %collective-permute-done.14.refs_4_ = bf16[320,1472]{1,0:T(8,128)(2,1)S(1)} collective-permute-done((bf16[320,1472]{1,0:T(8,128)(2,1)S(1)}, bf16[320,1472]{1,0:T(8,128)(2,1)S(1)}, u32[]{:S(2)}, u32[]{:S(2)}) %collective-permute-start.14) | collective-permute-done | bytes 942112 | tf_op jit(solution)/shard_map/ppermute | solution.py:60
  85.9 2.9 %collective-permute-done.16.refs_3_ = bf16[3,80,1472]{2,1,0:T(8,128)(2,1)S(1)} collective-permute-done((bf16[3,80,1472]{2,1,0:T(8,128)(2,1)S(1)}, bf16[3,80,1472]{2,1,0:T(8,128)(2,1)S(1)}, u32[]{:S(2)}, u32[]{:S(2)}) %collective-permute-start.16) | collective-permute-done | bytes 706592 | tf_op jit(solution)/shard_map/ppermute | solution.py:60
  89.7 4.7 %all-gather.3.cloned.1.call-done = bf16[15488,128]{1,0:T(8,128)(2,1)} async-done(((bf16[3872,128]{1,0:T(8,128)(2,1)}), bf16[15488,128]{1,0:T(8,128)(2,1)}) %all-gather.3.cloned.1.call-update) | async-done | bytes 3964944 | tf_op jit(solution)/shard_map/all_gather | solution.py:654
  94.4 12.3 %feed_forward.1 = (bf16[4,3872,128]{2,1,0:T(8,128)(2,1)}, bf16[640,256]{1,0:T(8,128)(2,1)}, bf16[640,192]{1,0:T(8,128)(2,1)}, bf16[640,512]{1,0:T(8,128)(2,1)}, bf16[640,384]{1,0:T(8,128)(2,1)}) custom-call(s32[3]{0:T(128)} %pad_add_fusion.idx, bf16[4,3872,128]{2,1,0:T(8,128)(2,1)} %bitcast.62, bf16[320,1472]{1,0:T(8,128)(2,1)} %copy-done.14, ...), custom_call_target="tpu_custom_call" | custom-call | flops 1400000000 | tf_op jit(solution)/shard_map/feed_forward/pallas_call | solution.py:37
  106.7 8.5 %feed_out.1 = (bf16[4,80,1472]{2,1,0:T(8,128)(2,1)}, bf16[4,80,1472]{2,1,0:T(8,128)(2,1)}, bf16[4,80,1472]{2,1,0:T(8,128)(2,1)}, bf16[4,80,1472]{2,1,0:T(8,128)(2,1)}) custom-call(s32[3]{0:T(128)} %pad_add_fusion.idx, bf16[4,3872,128]{2,1,0:T(8,128)(2,1)} %bitcast.63, bf16[640,256]{1,0:T(8,128)(2,1)} %get-tuple-element.123.refs_0_, ...), custom_call_target="tpu_custom_call" | custom-call | flops 500000000 | tf_op jit(solution)/shard_map/feed_out/pallas_call | solution.py:37
  115.4 2.7 %collective-permute-done.17 = bf16[4,80,1472]{2,1,0:T(8,128)(2,1)S(1)} collective-permute-done((bf16[4,80,1472]{2,1,0:T(8,128)(2,1)}, bf16[4,80,1472]{2,1,0:T(8,128)(2,1)S(1)}, u32[]{:S(2)}, u32[]{:S(2)}) %collective-permute-start.17) | collective-permute-done | bytes 942112 | tf_op jit(solution)/shard_map/ppermute | solution.py:60
  118.2 1.5 fusion.6
  119.7 2.8 %collective-permute-start.20 = (bf16[80,1472]{1,0:T(8,128)(2,1)S(1)}, bf16[80,1472]{1,0:T(8,128)(2,1)S(1)}, u32[]{:S(2)}, u32[]{:S(2)}) collective-permute-start(bf16[80,1472]{1,0:T(8,128)(2,1)S(1)} %get-tuple-element.209), channel_id=1, source_target_pairs={{0,6},{2,4},{4,2},{6,0},{1,7},{3,5},{5,3},{7,1},{8,14},{10,12},{12... | collective-permute-start | bytes 706568 | tf_op jit(solution)/shard_map/ppermute | solution.py:60
  123.3 6.2 %collective-permute-done.20.refs_3_ = bf16[80,1472]{1,0:T(8,128)(2,1)S(1)} collective-permute-done((bf16[80,1472]{1,0:T(8,128)(2,1)S(1)}, bf16[80,1472]{1,0:T(8,128)(2,1)S(1)}, u32[]{:S(2)}, u32[]{:S(2)}) %collective-permute-start.20) | collective-permute-done | bytes 235552 | tf_op jit(solution)/shard_map/ppermute | solution.py:60
  129.5 4.5 %collective-permute-done.19.refs_2_ = bf16[80,1472]{1,0:T(8,128)(2,1)S(1)} collective-permute-done((bf16[80,1472]{1,0:T(8,128)(2,1)S(1)}, bf16[80,1472]{1,0:T(8,128)(2,1)S(1)}, u32[]{:S(2)}, u32[]{:S(2)}) %collective-permute-start.19) | collective-permute-done | bytes 235552 | tf_op jit(solution)/shard_map/ppermute | solution.py:60
  135.2 1.4 collective-permute-done.21.o_other
  136.8 4.1 %attend_back.1 = (bf16[160,384]{1,0:T(8,128)(2,1)S(1)}, bf16[160,384]{1,0:T(8,128)(2,1)S(1)}, bf16[160,384]{1,0:T(8,128)(2,1)S(1)}, bf16[160,384]{1,0:T(8,128)(2...) custom-call(s32[3]{0:T(128)S(1)} %copy-done.27, ...), custom_call_target="tpu_custom_call" | custom-call | flops 400000000 | tf_op jit(solution)/shard_map/attend_back/pallas_call | solution.py:37
  141.0 1.8 collective-permute-start.23
  144.5 2.1 collective-permute-done.23.refs_1_
  146.6 4.1 %collective-permute-done.24.refs_2_ = bf16[160,384]{1,0:T(8,128)(2,1)S(1)} collective-permute-done((bf16[160,384]{1,0:T(8,128)(2,1)S(1)}, bf16[160,384]{1,0:T(8,128)(2,1)S(1)}, u32[]{:S(2)}, u32[]{:S(2)}) %collective-permute-start.24) | collective-permute-done | bytes 122912 | tf_op jit(solution)/shard_map/ppermute | solution.py:60
  150.7 1.5 first_grad.1
  154.6 1.4 collective-permute-start.33
  156.4 8.2 %collective-permute-done.29.refs_5_ = bf16[48,1472]{1,0:T(8,128)(2,1)S(1)} collective-permute-done((bf16[48,1472]{1,0:T(8,128)(2,1)S(1)}, bf16[48,1472]{1,0:T(8,128)(2,1)S(1)}, u32[]{:S(2)}, u32[]{:S(2)}) %collective-permute-start.29) | collective-permute-done | bytes 141344 | tf_op jit(solution)/shard_map/ppermute | solution.py:60
  164.7 1.5 collective-permute-start.30
  169.3 2.1 collective-permute-start.27
  175.0 1.8 collective-permute-done.28.refs_3_
  176.8 1.7 weight_grads.1
  178.5 1.5 collective-permute-done.37.b_other
  181.1 1.5 collective-permute-start.38
  182.6 2.8 %collective-permute-start.41 = (bf16[208,368]{1,0:T(8,128)(2,1)S(1)}, bf16[208,368]{1,0:T(8,128)(2,1)S(1)}, u32[]{:S(2)}, u32[]{:S(2)}) collective-permute-start(bf16[208,368]{1,0:T(8,128)(2,1)S(1)} %get-tuple-element.183), channel_id=1, source_target_pairs={{0,16},{8,24},{16,0},{24,8},{1,17},{9,25},{17,1},{25,9},{2,18},{10... | collective-permute-start | bytes 459272 | tf_op jit(solution)/shard_map/ppermute | solution.py:55
  187.5 1.5 place_outputs.1
  189.1 7.6 %collective-permute-done.41 = bf16[208,368]{1,0:T(8,128)(2,1)S(1)} collective-permute-done((bf16[208,368]{1,0:T(8,128)(2,1)S(1)}, bf16[208,368]{1,0:T(8,128)(2,1)S(1)}, u32[]{:S(2)}, u32[]{:S(2)}) %collective-permute-start.41) | collective-permute-done | bytes 153120 | tf_op jit(solution)/shard_map/ppermute | solution.py:55
  196.8 1.5 collective-permute-start.45
  198.9 1.5 collective-permute-start.43
  200.4 9.6 %collective-permute-done.45.refs_3_ = bf16[208,368]{1,0:T(8,128)(2,1)S(1)} collective-permute-done((bf16[208,368]{1,0:T(8,128)(2,1)S(1)}, bf16[208,368]{1,0:T(8,128)(2,1)S(1)}, u32[]{:S(2)}, u32[]{:S(2)}) %collective-permute-start.45) | collective-permute-done | bytes 153120 | tf_op jit(solution)/shard_map/ppermute | solution.py:60
  211.3 1.5 collective-permute-start.48
  213.4 1.7 finish_attention.1
  215.0 3.7 %finish_wide.2 = (f32[368,1792]{1,0:T(8,128)}, f32[368,1792]{1,0:T(8,128)}, f32[368,1792]{1,0:T(8,128)}) custom-call(s32[3]{0:T(128)S(1)} %copy-done.27, bf16[3872,128]{1,0:T(8,128)(2,1)S(1)} %bitcast.55, bf16[3872,128]{1,0:T(8,128)(2,1)S(1)} %collective-permute-done.38.refs_1_, bf16[3872,128]{1,0:T(8,128)(2,1)S(1)} %collective-permute-done.39.refs_2_.refs_0_), custom_call_target="tpu_custom_call" | custom-call | flops 300000000 | tf_op jit(solution)/shard_map/finish_wide/pallas_call | solution.py:37
  219.4 4.3 %collective-permute-done.48.refs_2_ = bf16[1936,128]{1,0:T(8,128)(2,1)S(1)} collective-permute-done((bf16[1936,128]{1,0:T(8,128)(2,1)S(1)}, bf16[1936,128]{1,0:T(8,128)(2,1)S(1)}, u32[]{:S(2)}, u32[]{:S(2)}) %collective-permute-start.48) | collective-permute-done | bytes 495648 | tf_op jit(solution)/shard_map/ppermute | solution.py:60
  224.0 2.4 %finish_wide.3 = (f32[368,1792]{1,0:T(8,128)}, f32[368,1792]{1,0:T(8,128)}, f32[368,1792]{1,0:T(8,128)}) custom-call(s32[3]{0:T(128)S(1)} %copy-done.27, bf16[3872,128]{1,0:T(8,128)(2,1)S(1)} %collective-permute-done.39.refs_2_.refs_0_, ...), custom_call_target="tpu_custom_call", output_to_operand_aliasing={{0}: (4, {}), {1}: (5, {}), {2}: (6, {})} | custom-call | flops 300000000 | tf_op jit(solution)/shard_map/finish_wide/pallas_call | solution.py:37
  (170 shorter events, 30.7 us)
Async XLA Ops:
  7.2 87.2 %all-gather.3.cloned.1.call-start = ((), (), s32[]{:S(2)}) async-start(), calls=%async_computation.2 | async-start | bytes 4956160 | tf_op jit(solution)/shard_map/all_gather | solution.py:654
  9.9 170.1 %reduce-scatter.2.cloned.1.call-start = ((), (), s32[]{:S(2)}) async-start(), calls=%async_computation.1 | async-start | bytes 4956160 | tf_op jit(solution)/shard_map/reduce_scatter | solution.py:756
  13.4 14.7 %collective-permute-start.2 = (bf16[208,384]{1,0:T(8,128)(2,1)}, bf16[208,384]{1,0:T(8,128)(2,1)S(1)}, u32[]{:S(2)}, u32[]{:S(2)}) collective-permute-start(bf16[208,384]{1,0:T(8,128)(2,1)} %pack_attention.1.refs_4_), channel_id=1, source_target_pairs={{0,24},{8,0},{16,8},{24,16},{1,25},{9,1},{17,9},{25,17},{2,26},{10... | collective-permute-start | bytes 479240 | tf_op jit(solution)/shard_map/ppermute | solution.py:55
  18.5 13.5 %collective-permute-start = (bf16[208,384]{1,0:T(8,128)(2,1)}, bf16[208,384]{1,0:T(8,128)(2,1)S(1)}, u32[]{:S(2)}, u32[]{:S(2)}) collective-permute-start(bf16[208,384]{1,0:T(8,128)(2,1)} %pack_attention.1.refs_4_), channel_id=1, source_target_pairs={{0,8},{8,16},{16,24},{24,0},{1,9},{9,17},{17,25},{25,1},{2,10},{10... | collective-permute-start | bytes 479240 | tf_op jit(solution)/shard_map/ppermute | solution.py:55
  18.6 14.4 %collective-permute-start.6 = (bf16[80,1472]{1,0:T(8,128)(2,1)S(1)}, bf16[80,1472]{1,0:T(8,128)(2,1)S(1)}, u32[]{:S(2)}, u32[]{:S(2)}) collective-permute-start(bf16[80,1472]{1,0:T(8,128)(2,1)S(1)} %dynamic-slice_bitcast_fusion.1), channel_id=1, source_target_pairs={{0,6},{2,4},{4,2},{6,0},{1,7},{3,5},{5,3},{7,1},{8,14},{10,12},{12... | collective-permute-start | bytes 706568 | tf_op jit(solution)/shard_map/ppermute | solution.py:60
  21.3 11.7 %collective-permute-start.5 = (bf16[80,1472]{1,0:T(8,128)(2,1)S(1)}, bf16[80,1472]{1,0:T(8,128)(2,1)S(1)}, u32[]{:S(2)}, u32[]{:S(2)}) collective-permute-start(bf16[80,1472]{1,0:T(8,128)(2,1)S(1)} %dynamic-slice_bitcast_fusion.1), channel_id=1, source_target_pairs={{0,4},{2,6},{4,0},{6,2},{1,5},{3,7},{5,1},{7,3},{8,12},{10,14},{12... | collective-permute-start | bytes 706568 | tf_op jit(solution)/shard_map/ppermute | solution.py:60
  21.8 11.2 %collective-permute-start.4 = (bf16[80,1472]{1,0:T(8,128)(2,1)S(1)}, bf16[80,1472]{1,0:T(8,128)(2,1)S(1)}, u32[]{:S(2)}, u32[]{:S(2)}) collective-permute-start(bf16[80,1472]{1,0:T(8,128)(2,1)S(1)} %dynamic-slice_bitcast_fusion.1), channel_id=1, source_target_pairs={{0,2},{2,0},{4,6},{6,4},{1,3},{3,1},{5,7},{7,5},{8,10},{10,8},{12,... | collective-permute-start | bytes 706568 | tf_op jit(solution)/shard_map/ppermute | solution.py:60
  28.2 12.0 %collective-permute-start.3 = (bf16[104,384]{1,0:T(8,128)(2,1)S(1)}, bf16[104,384]{1,0:T(8,128)(2,1)S(1)}, u32[]{:S(2)}, u32[]{:S(2)}) collective-permute-start(bf16[104,384]{1,0:T(8,128)(2,1)S(1)} %slice.105), channel_id=1, source_target_pairs={{0,24},{8,0},{16,8},{24,16},{1,25},{9,1},{17,9},{25,17},{2,26},{10... | collective-permute-start | bytes 239624 | tf_op jit(solution)/shard_map/ppermute | solution.py:55
  32.0 8.1 %collective-permute-start.1 = (bf16[104,384]{1,0:T(8,128)(2,1)S(1)}, bf16[104,384]{1,0:T(8,128)(2,1)S(1)}, u32[]{:S(2)}, u32[]{:S(2)}) collective-permute-start(bf16[104,384]{1,0:T(8,128)(2,1)S(1)} %slice.104), channel_id=1, source_target_pairs={{0,8},{8,16},{16,24},{24,0},{1,9},{9,17},{17,25},{25,1},{2,10},{10... | collective-permute-start | bytes 239624 | tf_op jit(solution)/shard_map/ppermute | solution.py:55
  40.2 3.7 %collective-permute-start.10 = (bf16[3,80,1472]{2,1,0:T(8,128)(2,1)S(1)}, bf16[3,80,1472]{2,1,0:T(8,128)(2,1)S(1)}, u32[]{:S(2)}, u32[]{:S(2)}) collective-permute-start(bf16[3,80,1472]{2,1,0:T(8,128)(2,1)S(1)} %pad_maximum_fusion), channel_id=1, source_target_pairs={{0,1},{1,0},{2,3},{3,2},{4,5},{5,4},{6,7},{7,6},{8,9},{9,8},{10,11... | collective-permute-start | bytes 2119688 | tf_op jit(solution)/shard_map/ppermute | solution.py:60
  40.3 14.8 %collective-permute-start.9 = (bf16[624,384]{1,0:T(8,128)(2,1)S(1)}, bf16[624,384]{1,0:T(8,128)(2,1)S(1)}, u32[]{:S(2)}, u32[]{:S(2)}) collective-permute-start(bf16[624,384]{1,0:T(8,128)(2,1)S(1)} %constant_dynamic-update-slice_fusion.2.refs_0_), channel_id=1, source_target_pairs={{0,6},{2,4},{4,2},{6,0},{1,7},{3,5},{5,3},{7,1},{8,14},{10,12},{12... | collective-permute-start | bytes 1437704 | tf_op jit(solution)/shard_map/ppermute | solution.py:60
  43.1 21.9 %collective-permute-start.8 = (bf16[624,384]{1,0:T(8,128)(2,1)S(1)}, bf16[624,384]{1,0:T(8,128)(2,1)S(1)}, u32[]{:S(2)}, u32[]{:S(2)}) collective-permute-start(bf16[624,384]{1,0:T(8,128)(2,1)S(1)} %constant_dynamic-update-slice_fusion.2.refs_0_), channel_id=1, source_target_pairs={{0,4},{2,6},{4,0},{6,2},{1,5},{3,7},{5,1},{7,3},{8,12},{10,14},{12... | collective-permute-start | bytes 1437704 | tf_op jit(solution)/shard_map/ppermute | solution.py:60
  43.6 21.4 %collective-permute-start.7 = (bf16[624,384]{1,0:T(8,128)(2,1)S(1)}, bf16[624,384]{1,0:T(8,128)(2,1)S(1)}, u32[]{:S(2)}, u32[]{:S(2)}) collective-permute-start(bf16[624,384]{1,0:T(8,128)(2,1)S(1)} %constant_dynamic-update-slice_fusion.2.refs_0_), channel_id=1, source_target_pairs={{0,2},{2,0},{4,6},{6,4},{1,3},{3,1},{5,7},{7,5},{8,10},{10,8},{12,... | collective-permute-start | bytes 1437704 | tf_op jit(solution)/shard_map/ppermute | solution.py:60
  65.0 15.3 %collective-permute-start.13 = (bf16[80,1472]{1,0:T(8,128)(2,1)S(1)}, bf16[80,1472]{1,0:T(8,128)(2,1)S(1)}, u32[]{:S(2)}, u32[]{:S(2)}) collective-permute-start(bf16[80,1472]{1,0:T(8,128)(2,1)S(1)} %dynamic-slice_bitcast_fusion), channel_id=1, source_target_pairs={{0,6},{2,4},{4,2},{6,0},{1,7},{3,5},{5,3},{7,1},{8,14},{10,12},{12... | collective-permute-start | bytes 706568 | tf_op jit(solution)/shard_map/ppermute | solution.py:60
  66.9 13.4 %collective-permute-start.12 = (bf16[80,1472]{1,0:T(8,128)(2,1)S(1)}, bf16[80,1472]{1,0:T(8,128)(2,1)S(1)}, u32[]{:S(2)}, u32[]{:S(2)}) collective-permute-start(bf16[80,1472]{1,0:T(8,128)(2,1)S(1)} %dynamic-slice_bitcast_fusion), channel_id=1, source_target_pairs={{0,4},{2,6},{4,0},{6,2},{1,5},{3,7},{5,1},{7,3},{8,12},{10,14},{12... | collective-permute-start | bytes 706568 | tf_op jit(solution)/shard_map/ppermute | solution.py:60
  68.2 12.1 %collective-permute-start.11 = (bf16[80,1472]{1,0:T(8,128)(2,1)S(1)}, bf16[80,1472]{1,0:T(8,128)(2,1)S(1)}, u32[]{:S(2)}, u32[]{:S(2)}) collective-permute-start(bf16[80,1472]{1,0:T(8,128)(2,1)S(1)} %dynamic-slice_bitcast_fusion), channel_id=1, source_target_pairs={{0,2},{2,0},{4,6},{6,4},{1,3},{3,1},{5,7},{7,5},{8,10},{10,8},{12,... | collective-permute-start | bytes 706568 | tf_op jit(solution)/shard_map/ppermute | solution.py:60
  85.3 4.5 %collective-permute-start.15 = (bf16[320,1472]{1,0:T(8,128)(2,1)S(1)}, bf16[320,1472]{1,0:T(8,128)(2,1)}, u32[]{:S(2)}, u32[]{:S(2)}) collective-permute-start(bf16[320,1472]{1,0:T(8,128)(2,1)S(1)} %get-tuple-element.120.nt_mine), channel_id=1, source_target_pairs={{0,1},{1,0},{2,3},{3,2},{4,5},{5,4},{6,7},{7,6},{8,9},{9,8},{10,11... | collective-permute-start | bytes 2826248 | tf_op jit(solution)/shard_map/ppermute | solution.py:60
  85.5 3.4 %collective-permute-start.16 = (bf16[3,80,1472]{2,1,0:T(8,128)(2,1)S(1)}, bf16[3,80,1472]{2,1,0:T(8,128)(2,1)S(1)}, u32[]{:S(2)}, u32[]{:S(2)}) collective-permute-start(bf16[3,80,1472]{2,1,0:T(8,128)(2,1)S(1)} %pad_maximum_fusion.1), channel_id=1, source_target_pairs={{0,1},{1,0},{2,3},{3,2},{4,5},{5,4},{6,7},{7,6},{8,9},{9,8},{10,11... | collective-permute-start | bytes 2119688 | tf_op jit(solution)/shard_map/ppermute | solution.py:60
  115.3 2.8 %collective-permute-start.17 = (bf16[4,80,1472]{2,1,0:T(8,128)(2,1)}, bf16[4,80,1472]{2,1,0:T(8,128)(2,1)S(1)}, u32[]{:S(2)}, u32[]{:S(2)}) collective-permute-start(bf16[4,80,1472]{2,1,0:T(8,128)(2,1)} %get-tuple-element.130), channel_id=1, source_target_pairs={{0,1},{1,0},{2,3},{3,2},{4,5},{5,4},{6,7},{7,6},{8,9},{9,8},{10,11... | collective-permute-start | bytes 2826248 | tf_op jit(solution)/shard_map/ppermute | solution.py:60
  119.7 9.8 %collective-permute-start.20 = (bf16[80,1472]{1,0:T(8,128)(2,1)S(1)}, bf16[80,1472]{1,0:T(8,128)(2,1)S(1)}, u32[]{:S(2)}, u32[]{:S(2)}) collective-permute-start(bf16[80,1472]{1,0:T(8,128)(2,1)S(1)} %get-tuple-element.209), channel_id=1, source_target_pairs={{0,6},{2,4},{4,2},{6,0},{1,7},{3,5},{5,3},{7,1},{8,14},{10,12},{12... | collective-permute-start | bytes 706568 | tf_op jit(solution)/shard_map/ppermute | solution.py:60
  122.5 11.5 %collective-permute-start.19 = (bf16[80,1472]{1,0:T(8,128)(2,1)S(1)}, bf16[80,1472]{1,0:T(8,128)(2,1)S(1)}, u32[]{:S(2)}, u32[]{:S(2)}) collective-permute-start(bf16[80,1472]{1,0:T(8,128)(2,1)S(1)} %get-tuple-element.210), channel_id=1, source_target_pairs={{0,4},{2,6},{4,0},{6,2},{1,5},{3,7},{5,1},{7,3},{8,12},{10,14},{12... | collective-permute-start | bytes 706568 | tf_op jit(solution)/shard_map/ppermute | solution.py:60
  123.0 11.1 %collective-permute-start.18 = (bf16[80,1472]{1,0:T(8,128)(2,1)S(1)}, bf16[80,1472]{1,0:T(8,128)(2,1)S(1)}, u32[]{:S(2)}, u32[]{:S(2)}) collective-permute-start(bf16[80,1472]{1,0:T(8,128)(2,1)S(1)} %get-tuple-element.211), channel_id=1, source_target_pairs={{0,2},{2,0},{4,6},{6,4},{1,3},{3,1},{5,7},{7,5},{8,10},{10,8},{12,... | collective-permute-start | bytes 706568 | tf_op jit(solution)/shard_map/ppermute | solution.py:60
  136.7 4.3 %collective-permute-start.22 = (bf16[4,80,1472]{2,1,0:T(8,128)(2,1)S(1)}, bf16[4,80,1472]{2,1,0:T(8,128)(2,1)S(1)}, u32[]{:S(2)}, u32[]{:S(2)}) collective-permute-start(bf16[4,80,1472]{2,1,0:T(8,128)(2,1)S(1)} %copy-done.35), channel_id=1, source_target_pairs={{0,1},{1,0},{2,3},{3,2},{4,5},{5,4},{6,7},{7,6},{8,9},{9,8},{10,11... | collective-permute-start | bytes 2826248 | tf_op jit(solution)/shard_map/ppermute | solution.py:60
  141.0 5.7 %collective-permute-start.23 = (bf16[160,384]{1,0:T(8,128)(2,1)S(1)}, bf16[160,384]{1,0:T(8,128)(2,1)S(1)}, u32[]{:S(2)}, u32[]{:S(2)}) collective-permute-start(bf16[160,384]{1,0:T(8,128)(2,1)S(1)} %get-tuple-element.144), channel_id=1, source_target_pairs={{0,2},{2,0},{4,6},{6,4},{1,3},{3,1},{5,7},{7,5},{8,10},{10,8},{12,... | collective-permute-start | bytes 368648 | tf_op jit(solution)/shard_map/ppermute | solution.py:60
  142.8 7.9 %collective-permute-start.24 = (bf16[160,384]{1,0:T(8,128)(2,1)S(1)}, bf16[160,384]{1,0:T(8,128)(2,1)S(1)}, u32[]{:S(2)}, u32[]{:S(2)}) collective-permute-start(bf16[160,384]{1,0:T(8,128)(2,1)S(1)} %get-tuple-element.146), channel_id=1, source_target_pairs={{0,4},{2,6},{4,0},{6,2},{1,5},{3,7},{5,1},{7,3},{8,12},{10,14},{12... | collective-permute-start | bytes 368648 | tf_op jit(solution)/shard_map/ppermute | solution.py:60
  143.4 7.3 %collective-permute-start.25 = (bf16[160,384]{1,0:T(8,128)(2,1)S(1)}, bf16[160,384]{1,0:T(8,128)(2,1)S(1)}, u32[]{:S(2)}, u32[]{:S(2)}) collective-permute-start(bf16[160,384]{1,0:T(8,128)(2,1)S(1)} %get-tuple-element.148), channel_id=1, source_target_pairs={{0,6},{2,4},{4,2},{6,0},{1,7},{3,5},{5,3},{7,1},{8,14},{10,12},{12... | collective-permute-start | bytes 368648 | tf_op jit(solution)/shard_map/ppermute | solution.py:60
  152.5 13.6 %collective-permute-start.34 = (bf16[80,1472]{1,0:T(8,128)(2,1)S(1)}, bf16[80,1472]{1,0:T(8,128)(2,1)S(1)}, u32[]{:S(2)}, u32[]{:S(2)}) collective-permute-start(bf16[80,1472]{1,0:T(8,128)(2,1)S(1)} %get-tuple-element.206), channel_id=1, source_target_pairs={{0,6},{2,4},{4,2},{6,0},{1,7},{3,5},{5,3},{7,1},{8,14},{10,12},{12... | collective-permute-start | bytes 706568 | tf_op jit(solution)/shard_map/ppermute | solution.py:60
  153.8 10.9 %collective-permute-start.29 = (bf16[48,1472]{1,0:T(8,128)(2,1)S(1)}, bf16[48,1472]{1,0:T(8,128)(2,1)S(1)}, u32[]{:S(2)}, u32[]{:S(2)}) collective-permute-start(bf16[48,1472]{1,0:T(8,128)(2,1)S(1)} %get-tuple-element.158), channel_id=1, source_target_pairs={{0,2},{2,0},{4,6},{6,4},{1,3},{3,1},{5,7},{7,5},{8,10},{10,8},{12,... | collective-permute-start | bytes 423944 | tf_op jit(solution)/shard_map/ppermute | solution.py:60
  154.6 12.7 %collective-permute-start.33 = (bf16[80,1472]{1,0:T(8,128)(2,1)S(1)}, bf16[80,1472]{1,0:T(8,128)(2,1)S(1)}, u32[]{:S(2)}, u32[]{:S(2)}) collective-permute-start(bf16[80,1472]{1,0:T(8,128)(2,1)S(1)} %get-tuple-element.207), channel_id=1, source_target_pairs={{0,4},{2,6},{4,0},{6,2},{1,5},{3,7},{5,1},{7,3},{8,12},{10,14},{12... | collective-permute-start | bytes 706568 | tf_op jit(solution)/shard_map/ppermute | solution.py:60
  156.1 13.2 %collective-permute-start.32 = (bf16[80,1472]{1,0:T(8,128)(2,1)S(1)}, bf16[80,1472]{1,0:T(8,128)(2,1)S(1)}, u32[]{:S(2)}, u32[]{:S(2)}) collective-permute-start(bf16[80,1472]{1,0:T(8,128)(2,1)S(1)} %get-tuple-element.208), channel_id=1, source_target_pairs={{0,2},{2,0},{4,6},{6,4},{1,3},{3,1},{5,7},{7,5},{8,10},{10,8},{12,... | collective-permute-start | bytes 706568 | tf_op jit(solution)/shard_map/ppermute | solution.py:60
  156.4 15.0 %collective-permute-start.35 = (bf16[80,1472]{1,0:T(8,128)(2,1)S(1)}, bf16[80,1472]{1,0:T(8,128)(2,1)S(1)}, u32[]{:S(2)}, u32[]{:S(2)}) collective-permute-start(bf16[80,1472]{1,0:T(8,128)(2,1)S(1)} %get-tuple-element.166), channel_id=1, source_target_pairs={{0,1},{1,0},{2,3},{3,2},{4,5},{5,4},{6,7},{7,6},{8,9},{9,8},{10,11... | collective-permute-start | bytes 706568 | tf_op jit(solution)/shard_map/ppermute | solution.py:60
  164.7 9.5 %collective-permute-start.30 = (bf16[48,1472]{1,0:T(8,128)(2,1)S(1)}, bf16[48,1472]{1,0:T(8,128)(2,1)S(1)}, u32[]{:S(2)}, u32[]{:S(2)}) collective-permute-start(bf16[48,1472]{1,0:T(8,128)(2,1)S(1)} %get-tuple-element.160), channel_id=1, source_target_pairs={{0,4},{2,6},{4,0},{6,2},{1,5},{3,7},{5,1},{7,3},{8,12},{10,14},{12... | collective-permute-start | bytes 423944 | tf_op jit(solution)/shard_map/ppermute | solution.py:60
  166.1 8.0 %collective-permute-start.31 = (bf16[48,1472]{1,0:T(8,128)(2,1)S(1)}, bf16[48,1472]{1,0:T(8,128)(2,1)S(1)}, u32[]{:S(2)}, u32[]{:S(2)}) collective-permute-start(bf16[48,1472]{1,0:T(8,128)(2,1)S(1)} %get-tuple-element.162), channel_id=1, source_target_pairs={{0,6},{2,4},{4,2},{6,0},{1,7},{3,5},{5,3},{7,1},{8,14},{10,12},{12... | collective-permute-start | bytes 423944 | tf_op jit(solution)/shard_map/ppermute | solution.py:60
  167.3 6.8 %collective-permute-start.26 = (bf16[160,144]{1,0:T(8,128)(2,1)S(1)}, bf16[160,144]{1,0:T(8,128)(2,1)S(1)}, u32[]{:S(2)}, u32[]{:S(2)}) collective-permute-start(bf16[160,144]{1,0:T(8,128)(2,1)S(1)} %get-tuple-element.152), channel_id=1, source_target_pairs={{0,2},{2,0},{4,6},{6,4},{1,3},{3,1},{5,7},{7,5},{8,10},{10,8},{12,... | collective-permute-start | bytes 138248 | tf_op jit(solution)/shard_map/ppermute | solution.py:60
  169.3 5.7 %collective-permute-start.27 = (bf16[160,144]{1,0:T(8,128)(2,1)S(1)}, bf16[160,144]{1,0:T(8,128)(2,1)S(1)}, u32[]{:S(2)}, u32[]{:S(2)}) collective-permute-start(bf16[160,144]{1,0:T(8,128)(2,1)S(1)} %get-tuple-element.154), channel_id=1, source_target_pairs={{0,4},{2,6},{4,0},{6,2},{1,5},{3,7},{5,1},{7,3},{8,12},{10,14},{12... | collective-permute-start | bytes 138248 | tf_op jit(solution)/shard_map/ppermute | solution.py:60
  171.4 5.3 %collective-permute-start.28 = (bf16[160,144]{1,0:T(8,128)(2,1)S(1)}, bf16[160,144]{1,0:T(8,128)(2,1)S(1)}, u32[]{:S(2)}, u32[]{:S(2)}) collective-permute-start(bf16[160,144]{1,0:T(8,128)(2,1)S(1)} %get-tuple-element.156), channel_id=1, source_target_pairs={{0,6},{2,4},{4,2},{6,0},{1,7},{3,5},{5,3},{7,1},{8,14},{10,12},{12... | collective-permute-start | bytes 138248 | tf_op jit(solution)/shard_map/ppermute | solution.py:60
  174.1 4.4 %collective-permute-start.36 = (bf16[80,1472]{1,0:T(8,128)(2,1)S(1)}, bf16[80,1472]{1,0:T(8,128)(2,1)S(1)}, u32[]{:S(2)}, u32[]{:S(2)}) collective-permute-start(bf16[80,1472]{1,0:T(8,128)(2,1)S(1)} %produce.1.a_mine), channel_id=1, source_target_pairs={{0,1},{1,0},{2,3},{3,2},{4,5},{5,4},{6,7},{7,6},{8,9},{9,8},{10,11... | collective-permute-start | bytes 706568 | tf_op jit(solution)/shard_map/ppermute | solution.py:60
  180.0 31.2 %collective-permute-start.39 = (bf16[3872,128]{1,0:T(8,128)(2,1)}, bf16[3872,128]{1,0:T(8,128)(2,1)S(1)}, u32[]{:S(2)}, u32[]{:S(2)}) collective-permute-start(bf16[3872,128]{1,0:T(8,128)(2,1)} %bitcast.53), channel_id=1, source_target_pairs={{0,4},{2,6},{4,0},{6,2},{1,5},{3,7},{5,1},{7,3},{8,12},{10,14},{12... | collective-permute-start | bytes 2973704 | tf_op jit(solution)/shard_map/ppermute | solution.py:60
  181.1 30.1 %collective-permute-start.38 = (bf16[3872,128]{1,0:T(8,128)(2,1)}, bf16[3872,128]{1,0:T(8,128)(2,1)S(1)}, u32[]{:S(2)}, u32[]{:S(2)}) collective-permute-start(bf16[3872,128]{1,0:T(8,128)(2,1)} %bitcast.54), channel_id=1, source_target_pairs={{0,2},{2,0},{4,6},{6,4},{1,3},{3,1},{5,7},{7,5},{8,10},{10,8},{12,... | collective-permute-start | bytes 2973704 | tf_op jit(solution)/shard_map/ppermute | solution.py:60
  182.6 14.1 %collective-permute-start.41 = (bf16[208,368]{1,0:T(8,128)(2,1)S(1)}, bf16[208,368]{1,0:T(8,128)(2,1)S(1)}, u32[]{:S(2)}, u32[]{:S(2)}) collective-permute-start(bf16[208,368]{1,0:T(8,128)(2,1)S(1)} %get-tuple-element.183), channel_id=1, source_target_pairs={{0,16},{8,24},{16,0},{24,8},{1,17},{9,25},{17,1},{25,9},{2,18},{10... | collective-permute-start | bytes 459272 | tf_op jit(solution)/shard_map/ppermute | solution.py:55
  185.5 11.2 %collective-permute-start.42 = (bf16[208,368]{1,0:T(8,128)(2,1)S(1)}, bf16[208,368]{1,0:T(8,128)(2,1)S(1)}, u32[]{:S(2)}, u32[]{:S(2)}) collective-permute-start(bf16[208,368]{1,0:T(8,128)(2,1)S(1)} %get-tuple-element.185), channel_id=1, source_target_pairs={{0,24},{8,0},{16,8},{24,16},{1,25},{9,1},{17,9},{25,17},{2,26},{10... | collective-permute-start | bytes 459272 | tf_op jit(solution)/shard_map/ppermute | solution.py:55
  186.4 10.3 %collective-permute-start.40 = (bf16[208,368]{1,0:T(8,128)(2,1)S(1)}, bf16[208,368]{1,0:T(8,128)(2,1)S(1)}, u32[]{:S(2)}, u32[]{:S(2)}) collective-permute-start(bf16[208,368]{1,0:T(8,128)(2,1)S(1)} %get-tuple-element.181), channel_id=1, source_target_pairs={{0,8},{8,16},{16,24},{24,0},{1,9},{9,17},{17,25},{25,1},{2,10},{10... | collective-permute-start | bytes 459272 | tf_op jit(solution)/shard_map/ppermute | solution.py:55
  196.8 13.2 %collective-permute-start.45 = (bf16[208,368]{1,0:T(8,128)(2,1)S(1)}, bf16[208,368]{1,0:T(8,128)(2,1)S(1)}, u32[]{:S(2)}, u32[]{:S(2)}) collective-permute-start(bf16[208,368]{1,0:T(8,128)(2,1)S(1)} %fusion.2.refs_0_), channel_id=1, source_target_pairs={{0,6},{2,4},{4,2},{6,0},{1,7},{3,5},{5,3},{7,1},{8,14},{10,12},{12... | collective-permute-start | bytes 459272 | tf_op jit(solution)/shard_map/ppermute | solution.py:60
  198.3 12.7 %collective-permute-start.44 = (bf16[208,368]{1,0:T(8,128)(2,1)S(1)}, bf16[208,368]{1,0:T(8,128)(2,1)S(1)}, u32[]{:S(2)}, u32[]{:S(2)}) collective-permute-start(bf16[208,368]{1,0:T(8,128)(2,1)S(1)} %fusion.2.refs_0_), channel_id=1, source_target_pairs={{0,4},{2,6},{4,0},{6,2},{1,5},{3,7},{5,1},{7,3},{8,12},{10,14},{12... | collective-permute-start | bytes 459272 | tf_op jit(solution)/shard_map/ppermute | solution.py:60
  198.9 12.3 %collective-permute-start.43 = (bf16[208,368]{1,0:T(8,128)(2,1)S(1)}, bf16[208,368]{1,0:T(8,128)(2,1)S(1)}, u32[]{:S(2)}, u32[]{:S(2)}) collective-permute-start(bf16[208,368]{1,0:T(8,128)(2,1)S(1)} %fusion.2.refs_0_), channel_id=1, source_target_pairs={{0,2},{2,0},{4,6},{6,4},{1,3},{3,1},{5,7},{7,5},{8,10},{10,8},{12,... | collective-permute-start | bytes 459272 | tf_op jit(solution)/shard_map/ppermute | solution.py:60
  211.3 12.5 %collective-permute-start.48 = (bf16[1936,128]{1,0:T(8,128)(2,1)S(1)}, bf16[1936,128]{1,0:T(8,128)(2,1)S(1)}, u32[]{:S(2)}, u32[]{:S(2)}) collective-permute-start(bf16[1936,128]{1,0:T(8,128)(2,1)S(1)} %slice.103), channel_id=1, source_target_pairs={{0,2},{2,0},{4,6},{6,4},{1,3},{3,1},{5,7},{7,5},{8,10},{10,8},{12,... | collective-permute-start | bytes 1486856 | tf_op jit(solution)/shard_map/ppermute | solution.py:60
  212.8 11.2 %collective-permute-start.47 = (bf16[1936,128]{1,0:T(8,128)(2,1)S(1)}, bf16[1936,128]{1,0:T(8,128)(2,1)S(1)}, u32[]{:S(2)}, u32[]{:S(2)}) collective-permute-start(bf16[1936,128]{1,0:T(8,128)(2,1)S(1)} %slice.102), channel_id=1, source_target_pairs={{0,4},{2,6},{4,0},{6,2},{1,5},{3,7},{5,1},{7,3},{8,12},{10,14},{12... | collective-permute-start | bytes 1486856 | tf_op jit(solution)/shard_map/ppermute | solution.py:60
  215.0 3.8 %collective-permute-start.46 = (f32[2,368]{1,0:T(2,128)S(1)}, f32[2,368]{1,0:T(2,128)S(1)}, u32[]{:S(2)}, u32[]{:S(2)}) collective-permute-start(f32[2,368]{1,0:T(2,128)S(1)} %get-tuple-element.189), channel_id=1, source_target_pairs={{0,1},{1,0},{2,3},{3,2},{4,5},{5,4},{6,7},{7,6},{8,9},{9,8},{10,11... | collective-permute-start | bytes 8840 | tf_op jit(solution)/shard_map/ppermute | solution.py:60
  (39 other events, 581.6 us)
Sparse Core Ops, SparseCore 0:
  10.2 84.1 all-gather.2
  106.9 72.7 reduce-scatter.1

commit v8 on v7

--- a/solution.py
+++ b/solution.py
@@ -358,13 +358,13 @@
         unpack_wide(parts, r, buf, weights, j)
     for copy in begun[n_shard:]:
         copy.wait()
+    out = []
     for held, given, lefts, first, last in (
         (two_held, two, pair, 0, 2),
         (feed_held, feed, hidden, 2, 3),
     ):
-
-        def half_rows(m, _, held=held, lefts=lefts, first=first, last=last):
-            at = pl.ds(pl.multiple_of(m * length, length), length)
+        for m in (1, 0):
+            at = slice(m * length, (m + 1) * length)
             total = sum(
                 (
                     dot_nt(lefts[e][at, :], weights[e][:, first * n : last * n])
@@ -373,17 +373,10 @@
             )
             for i in range(n_ctx):
                 held[m, i] = total[i * rows : (i + 1) * rows].astype(low)
-            return 0
-
-        lax.fori_loop(0, 2, half_rows, 0)
-    copies = [
-        pltpu.make_async_copy(held.at[m], given[m], sems_out.at[2 * i + m])
-        for i, (held, given) in enumerate(((two_held, two), (feed_held, feed)))
-        for m in range(2)
-    ]
-    for copy in copies:
-        copy.start()
-    for copy in copies:
+            copy = pltpu.make_async_copy(held.at[m], given[m], sems_out.at[len(out)])
+            copy.start()
+            out.append(copy)
+    for copy in out:
         copy.wait()
 
 
@@ -669,7 +662,6 @@
         from_shard = [low_one, jnp.concatenate(far), high_one]
     else:
         from_shard = [step(own_buf, "shard", k) for k in range(1, shards)]
-    mine_x = [swap(own_x, "ctx", k) for k in range(1, ctx)]
     table = lax.dynamic_slice_in_dim(bias_table, half * heads, heads, 1)
     (bias,) = run(
         functools.partial(bias_body, rows, rows // 5, distance_marks),
@@ -679,6 +671,7 @@
         scalars=2,
         cost=5,
     )
+    mine_x = [swap(after(own_x, bias), "ctx", k) for k in range(1, ctx)]
     now = after(idx, *from_shard, *mine_x, bias)
 
     group = jnp.concatenate(from_shard)
@@ -848,15 +841,15 @@
         [*feed_parts, middle_own],
         scalars=0,
     )
-    input_other = swap(after(input_mine, now), "tensor")
-    produced_other = swap(produced_mine, "tensor")
-    now = after(now, wide_own, produced_other, input_other)
+    now = after(now, wide_own, produced_mine, input_mine)
 
     wide_own = after(wide_own, now)
     half_rows = wide_rows // 2
     pair = ctx == 4
     wide_all = [swap(wide_own, "ctx", k) for k in ((1, 2) if pair else range(1, ctx))]
     four_shard = [four[0]] + [step(after(four[d], now), "shard", d) for d in range(1, shards)]
+    input_other = swap(after(input_mine, now), "tensor")
+    produced_other = swap(after(produced_mine, now), "tensor")
     out_y, out_x = run(
         place_outputs,
         "place_outputs",

time: 233 us -> 233 us (level)
  waiting for transfers between devices: 95 us -> 97.6 us
    ppermute x42, waiting for transfers between devices: 75.7 us -> 81.8 us  [swap(): return lax.ppermute(x, axis, [(i, i ^ k) for i in range(n)])]
    ppermute x7, waiting for transfers between devices: 14.6 us -> 11.2 us  [step(): return lax.ppermute(x, axis, [(i, (i + k) % n) for i in range(n)])]
  transfers between devices with their start and end apart: 51 -> 51, of which waited for: 26 -> 27; matrix products, arithmetic and copies ran while one was open for 2% -> 2% of each run, Pallas kernels for 20% -> 20%
where the time goes in v8:
time: 233 us
  waiting for transfers between devices  97.6 us (42%)
  Pallas kernels  63.4 us (27%)
  starting transfers between devices  50.5 us (22%)
  between operations  14.7 us (6%)
  local copies, waits for them, and re-layouts  3.65 us (2%)
  other arithmetic  3.2 us (1%)
    ppermute x42, waiting for transfers between devices, swap(): return lax.ppermute(x, axis, [(i, i ^ k) for i in range(n)])  81.8 us
    pallas_call x18, Pallas kernels, run(): pl.pallas_call(body, name=name, out_shape=[jax.ShapeDtypeStruct(s, d) for...  63.4 us
    ppermute x42, starting transfers between devices, swap(): return lax.ppermute(x, axis, [(i, i ^ k) for i in range(n)])  36.6 us
    ppermute x7, starting transfers between devices, step(): return lax.ppermute(x, axis, [(i, (i + k) % n) for i in range(n)])  13.8 us
    ppermute x7, waiting for transfers between devices, step(): return lax.ppermute(x, axis, [(i, (i + k) % n) for i in range(n)])  11.2 us
  transfers between devices with their start and end apart: 51, of which 27 were waited for; matrix products, arithmetic and copies ran while one was open for 2% of the time, Pallas kernels for 20%

profile of v8, /device:TPU:0, one launch (start us, length us, event | category | flops | bytes accessed | tf_op | source)
XLA Modules:
  0.0 233.1 jit_solution(2522498143989997102)
XLA Ops:
  7.3 2.6 %pack_wide.1 = bf16[3872,128]{1,0:T(8,128)(2,1)} custom-call(bf16[368,1792]{1,0:T(8,128)(2,1)} %w_g.1, bf16[368,1792]{1,0:T(8,128)(2,1)} %w_u.1, bf16[368,1792]{1,0:T(8,128)(2,1)} %bitcast.65), custom_call_target="tpu_custom_call" | custom-call | flops 200000000 | tf_op jit(solution)/shard_map/pack_wide/pallas_call | solution.py:37
  11.2 2.3 pack_attention.1.refs_4_
  13.5 5.1 %collective-permute-start.2 = (bf16[208,384]{1,0:T(8,128)(2,1)}, bf16[208,384]{1,0:T(8,128)(2,1)S(1)}, u32[]{:S(2)}, u32[]{:S(2)}) collective-permute-start(bf16[208,384]{1,0:T(8,128)(2,1)} %pack_attention.1.refs_4_), channel_id=1, source_target_pairs={{0,24},{8,0},{16,8},{24,16},{1,25},{9,1},{17,9},{25,17},{2,26},{10... | collective-permute-start | bytes 479240 | tf_op jit(solution)/shard_map/ppermute | solution.py:55
  19.5 5.3 %bias.1 = f32[3,320,320]{2,1,0:T(8,128)S(1)} custom-call(s32[3]{0:T(128)S(1)} %copy-done.20, f32[32,3]{1,0:T(8,128)S(1)} %copy.27.table), custom_call_target="tpu_custom_call" | custom-call | flops 500000000 | tf_op jit(solution)/shard_map/bias/pallas_call | solution.py:37
  24.8 2.8 %collective-permute-start.6 = (bf16[80,1472]{1,0:T(8,128)(2,1)S(1)}, bf16[80,1472]{1,0:T(8,128)(2,1)S(1)}, u32[]{:S(2)}, u32[]{:S(2)}) collective-permute-start(bf16[80,1472]{1,0:T(8,128)(2,1)S(1)} %get-tuple-element.111), channel_id=1, source_target_pairs={{0,6},{2,4},{4,2},{6,0},{1,7},{3,5},{5,3},{7,1},{8,14},{10,12},{12... | collective-permute-start | bytes 706568 | tf_op jit(solution)/shard_map/ppermute | solution.py:60
  28.3 3.9 %collective-permute-start.3 = (bf16[104,384]{1,0:T(8,128)(2,1)S(1)}, bf16[104,384]{1,0:T(8,128)(2,1)S(1)}, u32[]{:S(2)}, u32[]{:S(2)}) collective-permute-start(bf16[104,384]{1,0:T(8,128)(2,1)S(1)} %slice.105), channel_id=1, source_target_pairs={{0,24},{8,0},{16,8},{24,16},{1,25},{9,1},{17,9},{25,17},{2,26},{10... | collective-permute-start | bytes 239624 | tf_op jit(solution)/shard_map/ppermute | solution.py:55
  33.1 1.5 collective-permute-done.6.refs_2_
  34.6 3.8 %collective-permute-done.5.refs_1_ = bf16[80,1472]{1,0:T(8,128)(2,1)S(1)} collective-permute-done((bf16[80,1472]{1,0:T(8,128)(2,1)S(1)}, bf16[80,1472]{1,0:T(8,128)(2,1)S(1)}, u32[]{:S(2)}, u32[]{:S(2)}) %collective-permute-start.5) | collective-permute-done | bytes 235552 | tf_op jit(solution)/shard_map/ppermute | solution.py:60
  38.6 1.8 collective-permute-done.1
  40.6 2.7 %collective-permute-start.9 = (bf16[624,384]{1,0:T(8,128)(2,1)S(1)}, bf16[624,384]{1,0:T(8,128)(2,1)S(1)}, u32[]{:S(2)}, u32[]{:S(2)}) collective-permute-start(bf16[624,384]{1,0:T(8,128)(2,1)S(1)} %constant_dynamic-update-slice_fusion.2.refs_0_), channel_id=1, source_target_pairs={{0,6},{2,4},{4,2},{6,0},{1,7},{3,5},{5,3},{7,1},{8,14},{10,12},{12... | collective-permute-start | bytes 1437704 | tf_op jit(solution)/shard_map/ppermute | solution.py:60
  45.4 9.9 %collective-permute-done.9.refs_3_ = bf16[624,384]{1,0:T(8,128)(2,1)S(1)} collective-permute-done((bf16[624,384]{1,0:T(8,128)(2,1)S(1)}, bf16[624,384]{1,0:T(8,128)(2,1)S(1)}, u32[]{:S(2)}, u32[]{:S(2)}) %collective-permute-start.9) | collective-permute-done | bytes 479264 | tf_op jit(solution)/shard_map/ppermute | solution.py:60
  55.3 9.8 %collective-permute-done.8.refs_2_ = bf16[624,384]{1,0:T(8,128)(2,1)S(1)} collective-permute-done((bf16[624,384]{1,0:T(8,128)(2,1)S(1)}, bf16[624,384]{1,0:T(8,128)(2,1)S(1)}, u32[]{:S(2)}, u32[]{:S(2)}) %collective-permute-start.8) | collective-permute-done | bytes 479264 | tf_op jit(solution)/shard_map/ppermute | solution.py:60
  65.2 1.8 collective-permute-start.13
  67.0 1.4 collective-permute-start.12
  68.7 11.7 %attend.1 = (bf16[320,1472]{1,0:T(8,128)(2,1)S(1)}, bf16[320,1472]{1,0:T(8,128)(2,1)S(1)}, f32[2,3,80,320]{3,2,1,0:T(8,128)S(1)}, bf16[640,576]{1,0:T(8,128)(2,1...) custom-call(s32[3]{0:T(128)S(1)} %copy-done.20, bf16[640,1472]{1,0:T(8,128)(2,1)S(1)} %get-tuple-element.115.normed, ...), custom_call_target="tpu_custom_call" | custom-call | flops 1400000000 | tf_op jit(solution)/shard_map/attend/pallas_call | solution.py:37
  80.6 2.6 %collective-permute-done.14.refs_4_ = bf16[320,1472]{1,0:T(8,128)(2,1)S(1)} collective-permute-done((bf16[320,1472]{1,0:T(8,128)(2,1)S(1)}, bf16[320,1472]{1,0:T(8,128)(2,1)S(1)}, u32[]{:S(2)}, u32[]{:S(2)}) %collective-permute-start.14) | collective-permute-done | bytes 942112 | tf_op jit(solution)/shard_map/ppermute | solution.py:60
  86.1 2.9 %collective-permute-done.16.refs_3_ = bf16[3,80,1472]{2,1,0:T(8,128)(2,1)S(1)} collective-permute-done((bf16[3,80,1472]{2,1,0:T(8,128)(2,1)S(1)}, bf16[3,80,1472]{2,1,0:T(8,128)(2,1)S(1)}, u32[]{:S(2)}, u32[]{:S(2)}) %collective-permute-start.16) | collective-permute-done | bytes 706592 | tf_op jit(solution)/shard_map/ppermute | solution.py:60
  89.9 4.6 %all-gather.3.cloned.1.call-done = bf16[15488,128]{1,0:T(8,128)(2,1)} async-done(((bf16[3872,128]{1,0:T(8,128)(2,1)}), bf16[15488,128]{1,0:T(8,128)(2,1)}) %all-gather.3.cloned.1.call-update) | async-done | bytes 3964944 | tf_op jit(solution)/shard_map/all_gather | solution.py:647
  94.5 12.3 %feed_forward.1 = (bf16[4,3872,128]{2,1,0:T(8,128)(2,1)}, bf16[640,256]{1,0:T(8,128)(2,1)}, bf16[640,192]{1,0:T(8,128)(2,1)}, bf16[640,512]{1,0:T(8,128)(2,1)}, bf16[640,384]{1,0:T(8,128)(2,1)}) custom-call(s32[3]{0:T(128)} %pad_add_fusion.idx, bf16[4,3872,128]{2,1,0:T(8,128)(2,1)} %bitcast.62, bf16[320,1472]{1,0:T(8,128)(2,1)} %copy-done.8, ...), custom_call_target="tpu_custom_call" | custom-call | flops 1400000000 | tf_op jit(solution)/shard_map/feed_forward/pallas_call | solution.py:37
  106.8 7.6 %feed_out.1 = (bf16[4,80,1472]{2,1,0:T(8,128)(2,1)}, bf16[4,80,1472]{2,1,0:T(8,128)(2,1)}, bf16[4,80,1472]{2,1,0:T(8,128)(2,1)}, bf16[4,80,1472]{2,1,0:T(8,128)(2,1)}) custom-call(s32[3]{0:T(128)} %pad_add_fusion.idx, bf16[4,3872,128]{2,1,0:T(8,128)(2,1)} %bitcast.63, bf16[640,256]{1,0:T(8,128)(2,1)} %get-tuple-element.126.refs_0_, ...), custom_call_target="tpu_custom_call" | custom-call | flops 500000000 | tf_op jit(solution)/shard_map/feed_out/pallas_call | solution.py:37
  114.6 2.7 %collective-permute-done.17 = bf16[4,80,1472]{2,1,0:T(8,128)(2,1)S(1)} collective-permute-done((bf16[4,80,1472]{2,1,0:T(8,128)(2,1)}, bf16[4,80,1472]{2,1,0:T(8,128)(2,1)S(1)}, u32[]{:S(2)}, u32[]{:S(2)}) %collective-permute-start.17) | collective-permute-done | bytes 942112 | tf_op jit(solution)/shard_map/ppermute | solution.py:60
  117.3 1.5 fusion.6
  118.9 2.8 %collective-permute-start.20 = (bf16[80,1472]{1,0:T(8,128)(2,1)S(1)}, bf16[80,1472]{1,0:T(8,128)(2,1)S(1)}, u32[]{:S(2)}, u32[]{:S(2)}) collective-permute-start(bf16[80,1472]{1,0:T(8,128)(2,1)S(1)} %get-tuple-element.213), channel_id=1, source_target_pairs={{0,6},{2,4},{4,2},{6,0},{1,7},{3,5},{5,3},{7,1},{8,14},{10,12},{12... | collective-permute-start | bytes 706568 | tf_op jit(solution)/shard_map/ppermute | solution.py:60
  122.4 6.2 %collective-permute-done.20.refs_3_ = bf16[80,1472]{1,0:T(8,128)(2,1)S(1)} collective-permute-done((bf16[80,1472]{1,0:T(8,128)(2,1)S(1)}, bf16[80,1472]{1,0:T(8,128)(2,1)S(1)}, u32[]{:S(2)}, u32[]{:S(2)}) %collective-permute-start.20) | collective-permute-done | bytes 235552 | tf_op jit(solution)/shard_map/ppermute | solution.py:60
  128.7 4.5 %collective-permute-done.19.refs_2_ = bf16[80,1472]{1,0:T(8,128)(2,1)S(1)} collective-permute-done((bf16[80,1472]{1,0:T(8,128)(2,1)S(1)}, bf16[80,1472]{1,0:T(8,128)(2,1)S(1)}, u32[]{:S(2)}, u32[]{:S(2)}) %collective-permute-start.19) | collective-permute-done | bytes 235552 | tf_op jit(solution)/shard_map/ppermute | solution.py:60
  134.4 1.4 collective-permute-done.21.o_other
  136.0 4.1 %attend_back.1 = (bf16[160,384]{1,0:T(8,128)(2,1)S(1)}, bf16[160,384]{1,0:T(8,128)(2,1)S(1)}, bf16[160,384]{1,0:T(8,128)(2,1)S(1)}, bf16[160,384]{1,0:T(8,128)(2...) custom-call(s32[3]{0:T(128)S(1)} %copy-done.21, ...), custom_call_target="tpu_custom_call" | custom-call | flops 400000000 | tf_op jit(solution)/shard_map/attend_back/pallas_call | solution.py:37
  140.1 1.8 collective-permute-start.23
  143.7 1.7 collective-permute-start.29
  146.0 4.3 %collective-permute-done.24.refs_2_ = bf16[160,384]{1,0:T(8,128)(2,1)S(1)} collective-permute-done((bf16[160,384]{1,0:T(8,128)(2,1)S(1)}, bf16[160,384]{1,0:T(8,128)(2,1)S(1)}, u32[]{:S(2)}, u32[]{:S(2)}) %collective-permute-start.24) | collective-permute-done | bytes 122912 | tf_op jit(solution)/shard_map/ppermute | solution.py:60
  150.3 1.8 first_grad.1
  154.5 1.5 collective-permute-start.32
  157.3 12.9 %collective-permute-done.31.refs_7_ = bf16[48,1472]{1,0:T(8,128)(2,1)S(1)} collective-permute-done((bf16[48,1472]{1,0:T(8,128)(2,1)S(1)}, bf16[48,1472]{1,0:T(8,128)(2,1)S(1)}, u32[]{:S(2)}, u32[]{:S(2)}) %collective-permute-start.31) | collective-permute-done | bytes 141344 | tf_op jit(solution)/shard_map/ppermute | solution.py:60
  170.8 3.9 %collective-permute-done.26.refs_1_ = bf16[160,144]{1,0:T(8,128)(2,1)S(1)} collective-permute-done((bf16[160,144]{1,0:T(8,128)(2,1)S(1)}, bf16[160,144]{1,0:T(8,128)(2,1)S(1)}, u32[]{:S(2)}, u32[]{:S(2)}) %collective-permute-start.26) | collective-permute-done | bytes 46112 | tf_op jit(solution)/shard_map/ppermute | solution.py:60
  177.6 1.8 collective-permute-done.27.refs_2_
  179.4 1.4 collective-permute-done.28.refs_3_
  180.8 1.7 weight_grads.1
  182.7 1.4 collective-permute-start.39
  186.1 3.1 %collective-permute-start.42 = (bf16[208,368]{1,0:T(8,128)(2,1)S(1)}, bf16[208,368]{1,0:T(8,128)(2,1)S(1)}, u32[]{:S(2)}, u32[]{:S(2)}) collective-permute-start(bf16[208,368]{1,0:T(8,128)(2,1)S(1)} %get-tuple-element.189), channel_id=1, source_target_pairs={{0,24},{8,0},{16,8},{24,16},{1,25},{9,1},{17,9},{25,17},{2,26},{10... | collective-permute-start | bytes 459272 | tf_op jit(solution)/shard_map/ppermute | solution.py:55
  189.2 1.5 place_outputs.1
  190.7 6.6 %collective-permute-done.41 = bf16[208,368]{1,0:T(8,128)(2,1)S(1)} collective-permute-done((bf16[208,368]{1,0:T(8,128)(2,1)S(1)}, bf16[208,368]{1,0:T(8,128)(2,1)S(1)}, u32[]{:S(2)}, u32[]{:S(2)}) %collective-permute-start.41) | collective-permute-done | bytes 153120 | tf_op jit(solution)/shard_map/ppermute | solution.py:55
  197.3 2.9 %collective-permute-done.40 = bf16[208,368]{1,0:T(8,128)(2,1)S(1)} collective-permute-done((bf16[208,368]{1,0:T(8,128)(2,1)S(1)}, bf16[208,368]{1,0:T(8,128)(2,1)S(1)}, u32[]{:S(2)}, u32[]{:S(2)}) %collective-permute-start.40) | collective-permute-done | bytes 153120 | tf_op jit(solution)/shard_map/ppermute | solution.py:55
  200.3 1.7 collective-permute-start.45
  203.8 7.0 %collective-permute-done.45.refs_3_ = bf16[208,368]{1,0:T(8,128)(2,1)S(1)} collective-permute-done((bf16[208,368]{1,0:T(8,128)(2,1)S(1)}, bf16[208,368]{1,0:T(8,128)(2,1)S(1)}, u32[]{:S(2)}, u32[]{:S(2)}) %collective-permute-start.45) | collective-permute-done | bytes 153120 | tf_op jit(solution)/shard_map/ppermute | solution.py:60
  214.6 1.7 finish_attention.1
  216.3 3.7 %finish_wide.2 = (f32[368,1792]{1,0:T(8,128)}, f32[368,1792]{1,0:T(8,128)}, f32[368,1792]{1,0:T(8,128)}) custom-call(s32[3]{0:T(128)S(1)} %copy-done.21, bf16[3872,128]{1,0:T(8,128)(2,1)S(1)} %bitcast.55, bf16[3872,128]{1,0:T(8,128)(2,1)S(1)} %collective-permute-done.38.refs_1_, bf16[3872,128]{1,0:T(8,128)(2,1)S(1)} %collective-permute-done.39.refs_2_.refs_0_), custom_call_target="tpu_custom_call" | custom-call | flops 300000000 | tf_op jit(solution)/shard_map/finish_wide/pallas_call | solution.py:37
  220.6 2.6 %collective-permute-done.48.refs_2_ = bf16[1936,128]{1,0:T(8,128)(2,1)S(1)} collective-permute-done((bf16[1936,128]{1,0:T(8,128)(2,1)S(1)}, bf16[1936,128]{1,0:T(8,128)(2,1)S(1)}, u32[]{:S(2)}, u32[]{:S(2)}) %collective-permute-start.48) | collective-permute-done | bytes 495648 | tf_op jit(solution)/shard_map/ppermute | solution.py:60
  223.8 2.4 %finish_wide.3 = (f32[368,1792]{1,0:T(8,128)}, f32[368,1792]{1,0:T(8,128)}, f32[368,1792]{1,0:T(8,128)}) custom-call(s32[3]{0:T(128)S(1)} %copy-done.21, bf16[3872,128]{1,0:T(8,128)(2,1)S(1)} %collective-permute-done.39.refs_2_.refs_0_, ...), custom_call_target="tpu_custom_call", output_to_operand_aliasing={{0}: (4, {}), {1}: (5, {}), {2}: (6, {})} | custom-call | flops 300000000 | tf_op jit(solution)/shard_map/finish_wide/pallas_call | solution.py:37
  (157 shorter events, 31.4 us)
Async XLA Ops:
  7.2 87.3 %all-gather.3.cloned.1.call-start = ((), (), s32[]{:S(2)}) async-start(), calls=%async_computation.2 | async-start | bytes 4956160 | tf_op jit(solution)/shard_map/all_gather | solution.py:647
  9.9 172.7 %reduce-scatter.2.cloned.1.call-start = ((), (), s32[]{:S(2)}) async-start(), calls=%async_computation.1 | async-start | bytes 4956160 | tf_op jit(solution)/shard_map/reduce_scatter | solution.py:749
  13.5 14.8 %collective-permute-start.2 = (bf16[208,384]{1,0:T(8,128)(2,1)}, bf16[208,384]{1,0:T(8,128)(2,1)S(1)}, u32[]{:S(2)}, u32[]{:S(2)}) collective-permute-start(bf16[208,384]{1,0:T(8,128)(2,1)} %pack_attention.1.refs_4_), channel_id=1, source_target_pairs={{0,24},{8,0},{16,8},{24,16},{1,25},{9,1},{17,9},{25,17},{2,26},{10... | collective-permute-start | bytes 479240 | tf_op jit(solution)/shard_map/ppermute | solution.py:55
  18.6 13.6 %collective-permute-start = (bf16[208,384]{1,0:T(8,128)(2,1)}, bf16[208,384]{1,0:T(8,128)(2,1)S(1)}, u32[]{:S(2)}, u32[]{:S(2)}) collective-permute-start(bf16[208,384]{1,0:T(8,128)(2,1)} %pack_attention.1.refs_4_), channel_id=1, source_target_pairs={{0,8},{8,16},{16,24},{24,0},{1,9},{9,17},{17,25},{25,1},{2,10},{10... | collective-permute-start | bytes 479240 | tf_op jit(solution)/shard_map/ppermute | solution.py:55
  24.8 9.9 %collective-permute-start.6 = (bf16[80,1472]{1,0:T(8,128)(2,1)S(1)}, bf16[80,1472]{1,0:T(8,128)(2,1)S(1)}, u32[]{:S(2)}, u32[]{:S(2)}) collective-permute-start(bf16[80,1472]{1,0:T(8,128)(2,1)S(1)} %get-tuple-element.111), channel_id=1, source_target_pairs={{0,6},{2,4},{4,2},{6,0},{1,7},{3,5},{5,3},{7,1},{8,14},{10,12},{12... | collective-permute-start | bytes 706568 | tf_op jit(solution)/shard_map/ppermute | solution.py:60
  27.5 10.9 %collective-permute-start.5 = (bf16[80,1472]{1,0:T(8,128)(2,1)S(1)}, bf16[80,1472]{1,0:T(8,128)(2,1)S(1)}, u32[]{:S(2)}, u32[]{:S(2)}) collective-permute-start(bf16[80,1472]{1,0:T(8,128)(2,1)S(1)} %get-tuple-element.111), channel_id=1, source_target_pairs={{0,4},{2,6},{4,0},{6,2},{1,5},{3,7},{5,1},{7,3},{8,12},{10,14},{12... | collective-permute-start | bytes 706568 | tf_op jit(solution)/shard_map/ppermute | solution.py:60
  28.0 10.5 %collective-permute-start.4 = (bf16[80,1472]{1,0:T(8,128)(2,1)S(1)}, bf16[80,1472]{1,0:T(8,128)(2,1)S(1)}, u32[]{:S(2)}, u32[]{:S(2)}) collective-permute-start(bf16[80,1472]{1,0:T(8,128)(2,1)S(1)} %get-tuple-element.111), channel_id=1, source_target_pairs={{0,2},{2,0},{4,6},{6,4},{1,3},{3,1},{5,7},{7,5},{8,10},{10,8},{12,... | collective-permute-start | bytes 706568 | tf_op jit(solution)/shard_map/ppermute | solution.py:60
  28.3 12.1 %collective-permute-start.3 = (bf16[104,384]{1,0:T(8,128)(2,1)S(1)}, bf16[104,384]{1,0:T(8,128)(2,1)S(1)}, u32[]{:S(2)}, u32[]{:S(2)}) collective-permute-start(bf16[104,384]{1,0:T(8,128)(2,1)S(1)} %slice.105), channel_id=1, source_target_pairs={{0,24},{8,0},{16,8},{24,16},{1,25},{9,1},{17,9},{25,17},{2,26},{10... | collective-permute-start | bytes 239624 | tf_op jit(solution)/shard_map/ppermute | solution.py:55
  32.3 8.1 %collective-permute-start.1 = (bf16[104,384]{1,0:T(8,128)(2,1)S(1)}, bf16[104,384]{1,0:T(8,128)(2,1)S(1)}, u32[]{:S(2)}, u32[]{:S(2)}) collective-permute-start(bf16[104,384]{1,0:T(8,128)(2,1)S(1)} %slice.104), channel_id=1, source_target_pairs={{0,8},{8,16},{16,24},{24,0},{1,9},{9,17},{17,25},{25,1},{2,10},{10... | collective-permute-start | bytes 239624 | tf_op jit(solution)/shard_map/ppermute | solution.py:55
  40.4 3.7 %collective-permute-start.10 = (bf16[3,80,1472]{2,1,0:T(8,128)(2,1)S(1)}, bf16[3,80,1472]{2,1,0:T(8,128)(2,1)S(1)}, u32[]{:S(2)}, u32[]{:S(2)}) collective-permute-start(bf16[3,80,1472]{2,1,0:T(8,128)(2,1)S(1)} %pad_maximum_fusion), channel_id=1, source_target_pairs={{0,1},{1,0},{2,3},{3,2},{4,5},{5,4},{6,7},{7,6},{8,9},{9,8},{10,11... | collective-permute-start | bytes 2119688 | tf_op jit(solution)/shard_map/ppermute | solution.py:60
  40.6 14.8 %collective-permute-start.9 = (bf16[624,384]{1,0:T(8,128)(2,1)S(1)}, bf16[624,384]{1,0:T(8,128)(2,1)S(1)}, u32[]{:S(2)}, u32[]{:S(2)}) collective-permute-start(bf16[624,384]{1,0:T(8,128)(2,1)S(1)} %constant_dynamic-update-slice_fusion.2.refs_0_), channel_id=1, source_target_pairs={{0,6},{2,4},{4,2},{6,0},{1,7},{3,5},{5,3},{7,1},{8,14},{10,12},{12... | collective-permute-start | bytes 1437704 | tf_op jit(solution)/shard_map/ppermute | solution.py:60
  43.3 21.9 %collective-permute-start.8 = (bf16[624,384]{1,0:T(8,128)(2,1)S(1)}, bf16[624,384]{1,0:T(8,128)(2,1)S(1)}, u32[]{:S(2)}, u32[]{:S(2)}) collective-permute-start(bf16[624,384]{1,0:T(8,128)(2,1)S(1)} %constant_dynamic-update-slice_fusion.2.refs_0_), channel_id=1, source_target_pairs={{0,4},{2,6},{4,0},{6,2},{1,5},{3,7},{5,1},{7,3},{8,12},{10,14},{12... | collective-permute-start | bytes 1437704 | tf_op jit(solution)/shard_map/ppermute | solution.py:60
  43.8 21.4 %collective-permute-start.7 = (bf16[624,384]{1,0:T(8,128)(2,1)S(1)}, bf16[624,384]{1,0:T(8,128)(2,1)S(1)}, u32[]{:S(2)}, u32[]{:S(2)}) collective-permute-start(bf16[624,384]{1,0:T(8,128)(2,1)S(1)} %constant_dynamic-update-slice_fusion.2.refs_0_), channel_id=1, source_target_pairs={{0,2},{2,0},{4,6},{6,4},{1,3},{3,1},{5,7},{7,5},{8,10},{10,8},{12,... | collective-permute-start | bytes 1437704 | tf_op jit(solution)/shard_map/ppermute | solution.py:60
  65.2 15.2 %collective-permute-start.13 = (bf16[80,1472]{1,0:T(8,128)(2,1)S(1)}, bf16[80,1472]{1,0:T(8,128)(2,1)S(1)}, u32[]{:S(2)}, u32[]{:S(2)}) collective-permute-start(bf16[80,1472]{1,0:T(8,128)(2,1)S(1)} %get-tuple-element.117), channel_id=1, source_target_pairs={{0,6},{2,4},{4,2},{6,0},{1,7},{3,5},{5,3},{7,1},{8,14},{10,12},{12... | collective-permute-start | bytes 706568 | tf_op jit(solution)/shard_map/ppermute | solution.py:60
  67.0 13.5 %collective-permute-start.12 = (bf16[80,1472]{1,0:T(8,128)(2,1)S(1)}, bf16[80,1472]{1,0:T(8,128)(2,1)S(1)}, u32[]{:S(2)}, u32[]{:S(2)}) collective-permute-start(bf16[80,1472]{1,0:T(8,128)(2,1)S(1)} %get-tuple-element.117), channel_id=1, source_target_pairs={{0,4},{2,6},{4,0},{6,2},{1,5},{3,7},{5,1},{7,3},{8,12},{10,14},{12... | collective-permute-start | bytes 706568 | tf_op jit(solution)/shard_map/ppermute | solution.py:60
  68.4 12.1 %collective-permute-start.11 = (bf16[80,1472]{1,0:T(8,128)(2,1)S(1)}, bf16[80,1472]{1,0:T(8,128)(2,1)S(1)}, u32[]{:S(2)}, u32[]{:S(2)}) collective-permute-start(bf16[80,1472]{1,0:T(8,128)(2,1)S(1)} %get-tuple-element.117), channel_id=1, source_target_pairs={{0,2},{2,0},{4,6},{6,4},{1,3},{3,1},{5,7},{7,5},{8,10},{10,8},{12,... | collective-permute-start | bytes 706568 | tf_op jit(solution)/shard_map/ppermute | solution.py:60
  85.4 4.5 %collective-permute-start.15 = (bf16[320,1472]{1,0:T(8,128)(2,1)S(1)}, bf16[320,1472]{1,0:T(8,128)(2,1)}, u32[]{:S(2)}, u32[]{:S(2)}) collective-permute-start(bf16[320,1472]{1,0:T(8,128)(2,1)S(1)} %get-tuple-element.123.nt_mine), channel_id=1, source_target_pairs={{0,1},{1,0},{2,3},{3,2},{4,5},{5,4},{6,7},{7,6},{8,9},{9,8},{10,11... | collective-permute-start | bytes 2826248 | tf_op jit(solution)/shard_map/ppermute | solution.py:60
  85.7 3.4 %collective-permute-start.16 = (bf16[3,80,1472]{2,1,0:T(8,128)(2,1)S(1)}, bf16[3,80,1472]{2,1,0:T(8,128)(2,1)S(1)}, u32[]{:S(2)}, u32[]{:S(2)}) collective-permute-start(bf16[3,80,1472]{2,1,0:T(8,128)(2,1)S(1)} %pad_maximum_fusion.1), channel_id=1, source_target_pairs={{0,1},{1,0},{2,3},{3,2},{4,5},{5,4},{6,7},{7,6},{8,9},{9,8},{10,11... | collective-permute-start | bytes 2119688 | tf_op jit(solution)/shard_map/ppermute | solution.py:60
  114.5 2.8 %collective-permute-start.17 = (bf16[4,80,1472]{2,1,0:T(8,128)(2,1)}, bf16[4,80,1472]{2,1,0:T(8,128)(2,1)S(1)}, u32[]{:S(2)}, u32[]{:S(2)}) collective-permute-start(bf16[4,80,1472]{2,1,0:T(8,128)(2,1)} %get-tuple-element.133), channel_id=1, source_target_pairs={{0,1},{1,0},{2,3},{3,2},{4,5},{5,4},{6,7},{7,6},{8,9},{9,8},{10,11... | collective-permute-start | bytes 2826248 | tf_op jit(solution)/shard_map/ppermute | solution.py:60
  118.9 9.8 %collective-permute-start.20 = (bf16[80,1472]{1,0:T(8,128)(2,1)S(1)}, bf16[80,1472]{1,0:T(8,128)(2,1)S(1)}, u32[]{:S(2)}, u32[]{:S(2)}) collective-permute-start(bf16[80,1472]{1,0:T(8,128)(2,1)S(1)} %get-tuple-element.213), channel_id=1, source_target_pairs={{0,6},{2,4},{4,2},{6,0},{1,7},{3,5},{5,3},{7,1},{8,14},{10,12},{12... | collective-permute-start | bytes 706568 | tf_op jit(solution)/shard_map/ppermute | solution.py:60
  121.6 11.5 %collective-permute-start.19 = (bf16[80,1472]{1,0:T(8,128)(2,1)S(1)}, bf16[80,1472]{1,0:T(8,128)(2,1)S(1)}, u32[]{:S(2)}, u32[]{:S(2)}) collective-permute-start(bf16[80,1472]{1,0:T(8,128)(2,1)S(1)} %get-tuple-element.214), channel_id=1, source_target_pairs={{0,4},{2,6},{4,0},{6,2},{1,5},{3,7},{5,1},{7,3},{8,12},{10,14},{12... | collective-permute-start | bytes 706568 | tf_op jit(solution)/shard_map/ppermute | solution.py:60
  122.1 11.1 %collective-permute-start.18 = (bf16[80,1472]{1,0:T(8,128)(2,1)S(1)}, bf16[80,1472]{1,0:T(8,128)(2,1)S(1)}, u32[]{:S(2)}, u32[]{:S(2)}) collective-permute-start(bf16[80,1472]{1,0:T(8,128)(2,1)S(1)} %get-tuple-element.215), channel_id=1, source_target_pairs={{0,2},{2,0},{4,6},{6,4},{1,3},{3,1},{5,7},{7,5},{8,10},{10,8},{12,... | collective-permute-start | bytes 706568 | tf_op jit(solution)/shard_map/ppermute | solution.py:60
  135.8 4.3 %collective-permute-start.22 = (bf16[4,80,1472]{2,1,0:T(8,128)(2,1)S(1)}, bf16[4,80,1472]{2,1,0:T(8,128)(2,1)S(1)}, u32[]{:S(2)}, u32[]{:S(2)}) collective-permute-start(bf16[4,80,1472]{2,1,0:T(8,128)(2,1)S(1)} %copy-done.29), channel_id=1, source_target_pairs={{0,1},{1,0},{2,3},{3,2},{4,5},{5,4},{6,7},{7,6},{8,9},{9,8},{10,11... | collective-permute-start | bytes 2826248 | tf_op jit(solution)/shard_map/ppermute | solution.py:60
  140.1 5.9 %collective-permute-start.23 = (bf16[160,384]{1,0:T(8,128)(2,1)S(1)}, bf16[160,384]{1,0:T(8,128)(2,1)S(1)}, u32[]{:S(2)}, u32[]{:S(2)}) collective-permute-start(bf16[160,384]{1,0:T(8,128)(2,1)S(1)} %get-tuple-element.147), channel_id=1, source_target_pairs={{0,2},{2,0},{4,6},{6,4},{1,3},{3,1},{5,7},{7,5},{8,10},{10,8},{12,... | collective-permute-start | bytes 368648 | tf_op jit(solution)/shard_map/ppermute | solution.py:60
  141.9 8.4 %collective-permute-start.24 = (bf16[160,384]{1,0:T(8,128)(2,1)S(1)}, bf16[160,384]{1,0:T(8,128)(2,1)S(1)}, u32[]{:S(2)}, u32[]{:S(2)}) collective-permute-start(bf16[160,384]{1,0:T(8,128)(2,1)S(1)} %get-tuple-element.149), channel_id=1, source_target_pairs={{0,4},{2,6},{4,0},{6,2},{1,5},{3,7},{5,1},{7,3},{8,12},{10,14},{12... | collective-permute-start | bytes 368648 | tf_op jit(solution)/shard_map/ppermute | solution.py:60
  142.5 7.8 %collective-permute-start.25 = (bf16[160,384]{1,0:T(8,128)(2,1)S(1)}, bf16[160,384]{1,0:T(8,128)(2,1)S(1)}, u32[]{:S(2)}, u32[]{:S(2)}) collective-permute-start(bf16[160,384]{1,0:T(8,128)(2,1)S(1)} %get-tuple-element.151), channel_id=1, source_target_pairs={{0,6},{2,4},{4,2},{6,0},{1,7},{3,5},{5,3},{7,1},{8,14},{10,12},{12... | collective-permute-start | bytes 368648 | tf_op jit(solution)/shard_map/ppermute | solution.py:60
  143.7 10.8 %collective-permute-start.29 = (bf16[48,1472]{1,0:T(8,128)(2,1)S(1)}, bf16[48,1472]{1,0:T(8,128)(2,1)S(1)}, u32[]{:S(2)}, u32[]{:S(2)}) collective-permute-start(bf16[48,1472]{1,0:T(8,128)(2,1)S(1)} %get-tuple-element.161), channel_id=1, source_target_pairs={{0,2},{2,0},{4,6},{6,4},{1,3},{3,1},{5,7},{7,5},{8,10},{10,8},{12,... | collective-permute-start | bytes 423944 | tf_op jit(solution)/shard_map/ppermute | solution.py:60
  145.4 10.6 %collective-permute-start.30 = (bf16[48,1472]{1,0:T(8,128)(2,1)S(1)}, bf16[48,1472]{1,0:T(8,128)(2,1)S(1)}, u32[]{:S(2)}, u32[]{:S(2)}) collective-permute-start(bf16[48,1472]{1,0:T(8,128)(2,1)S(1)} %get-tuple-element.163), channel_id=1, source_target_pairs={{0,4},{2,6},{4,0},{6,2},{1,5},{3,7},{5,1},{7,3},{8,12},{10,14},{12... | collective-permute-start | bytes 423944 | tf_op jit(solution)/shard_map/ppermute | solution.py:60
  152.2 23.3 %collective-permute-start.35 = (bf16[80,1472]{1,0:T(8,128)(2,1)S(1)}, bf16[80,1472]{1,0:T(8,128)(2,1)S(1)}, u32[]{:S(2)}, u32[]{:S(2)}) collective-permute-start(bf16[80,1472]{1,0:T(8,128)(2,1)S(1)} %get-tuple-element.169), channel_id=1, source_target_pairs={{0,1},{1,0},{2,3},{3,2},{4,5},{5,4},{6,7},{7,6},{8,9},{9,8},{10,11... | collective-permute-start | bytes 706568 | tf_op jit(solution)/shard_map/ppermute | solution.py:60
  152.5 28.3 %collective-permute-start.34 = (bf16[80,1472]{1,0:T(8,128)(2,1)S(1)}, bf16[80,1472]{1,0:T(8,128)(2,1)S(1)}, u32[]{:S(2)}, u32[]{:S(2)}) collective-permute-start(bf16[80,1472]{1,0:T(8,128)(2,1)S(1)} %get-tuple-element.210), channel_id=1, source_target_pairs={{0,6},{2,4},{4,2},{6,0},{1,7},{3,5},{5,3},{7,1},{8,14},{10,12},{12... | collective-permute-start | bytes 706568 | tf_op jit(solution)/shard_map/ppermute | solution.py:60
  153.8 26.9 %collective-permute-start.33 = (bf16[80,1472]{1,0:T(8,128)(2,1)S(1)}, bf16[80,1472]{1,0:T(8,128)(2,1)S(1)}, u32[]{:S(2)}, u32[]{:S(2)}) collective-permute-start(bf16[80,1472]{1,0:T(8,128)(2,1)S(1)} %get-tuple-element.211), channel_id=1, source_target_pairs={{0,4},{2,6},{4,0},{6,2},{1,5},{3,7},{5,1},{7,3},{8,12},{10,14},{12... | collective-permute-start | bytes 706568 | tf_op jit(solution)/shard_map/ppermute | solution.py:60
  154.5 26.3 %collective-permute-start.32 = (bf16[80,1472]{1,0:T(8,128)(2,1)S(1)}, bf16[80,1472]{1,0:T(8,128)(2,1)S(1)}, u32[]{:S(2)}, u32[]{:S(2)}) collective-permute-start(bf16[80,1472]{1,0:T(8,128)(2,1)S(1)} %get-tuple-element.212), channel_id=1, source_target_pairs={{0,2},{2,0},{4,6},{6,4},{1,3},{3,1},{5,7},{7,5},{8,10},{10,8},{12,... | collective-permute-start | bytes 706568 | tf_op jit(solution)/shard_map/ppermute | solution.py:60
  156.0 14.2 %collective-permute-start.31 = (bf16[48,1472]{1,0:T(8,128)(2,1)S(1)}, bf16[48,1472]{1,0:T(8,128)(2,1)S(1)}, u32[]{:S(2)}, u32[]{:S(2)}) collective-permute-start(bf16[48,1472]{1,0:T(8,128)(2,1)S(1)} %get-tuple-element.165), channel_id=1, source_target_pairs={{0,6},{2,4},{4,2},{6,0},{1,7},{3,5},{5,3},{7,1},{8,14},{10,12},{12... | collective-permute-start | bytes 423944 | tf_op jit(solution)/shard_map/ppermute | solution.py:60
  170.3 4.4 %collective-permute-start.26 = (bf16[160,144]{1,0:T(8,128)(2,1)S(1)}, bf16[160,144]{1,0:T(8,128)(2,1)S(1)}, u32[]{:S(2)}, u32[]{:S(2)}) collective-permute-start(bf16[160,144]{1,0:T(8,128)(2,1)S(1)} %get-tuple-element.155), channel_id=1, source_target_pairs={{0,2},{2,0},{4,6},{6,4},{1,3},{3,1},{5,7},{7,5},{8,10},{10,8},{12,... | collective-permute-start | bytes 138248 | tf_op jit(solution)/shard_map/ppermute | solution.py:60
  174.7 4.6 %collective-permute-start.27 = (bf16[160,144]{1,0:T(8,128)(2,1)S(1)}, bf16[160,144]{1,0:T(8,128)(2,1)S(1)}, u32[]{:S(2)}, u32[]{:S(2)}) collective-permute-start(bf16[160,144]{1,0:T(8,128)(2,1)S(1)} %get-tuple-element.157), channel_id=1, source_target_pairs={{0,4},{2,6},{4,0},{6,2},{1,5},{3,7},{5,1},{7,3},{8,12},{10,14},{12... | collective-permute-start | bytes 138248 | tf_op jit(solution)/shard_map/ppermute | solution.py:60
  175.4 5.3 %collective-permute-start.28 = (bf16[160,144]{1,0:T(8,128)(2,1)S(1)}, bf16[160,144]{1,0:T(8,128)(2,1)S(1)}, u32[]{:S(2)}, u32[]{:S(2)}) collective-permute-start(bf16[160,144]{1,0:T(8,128)(2,1)S(1)} %get-tuple-element.159), channel_id=1, source_target_pairs={{0,6},{2,4},{4,2},{6,0},{1,7},{3,5},{5,3},{7,1},{8,14},{10,12},{12... | collective-permute-start | bytes 138248 | tf_op jit(solution)/shard_map/ppermute | solution.py:60
  182.7 29.8 %collective-permute-start.39 = (bf16[3872,128]{1,0:T(8,128)(2,1)}, bf16[3872,128]{1,0:T(8,128)(2,1)S(1)}, u32[]{:S(2)}, u32[]{:S(2)}) collective-permute-start(bf16[3872,128]{1,0:T(8,128)(2,1)} %bitcast.53), channel_id=1, source_target_pairs={{0,4},{2,6},{4,0},{6,2},{1,5},{3,7},{5,1},{7,3},{8,12},{10,14},{12... | collective-permute-start | bytes 2973704 | tf_op jit(solution)/shard_map/ppermute | solution.py:60
  184.1 28.4 %collective-permute-start.38 = (bf16[3872,128]{1,0:T(8,128)(2,1)}, bf16[3872,128]{1,0:T(8,128)(2,1)S(1)}, u32[]{:S(2)}, u32[]{:S(2)}) collective-permute-start(bf16[3872,128]{1,0:T(8,128)(2,1)} %bitcast.54), channel_id=1, source_target_pairs={{0,2},{2,0},{4,6},{6,4},{1,3},{3,1},{5,7},{7,5},{8,10},{10,8},{12,... | collective-permute-start | bytes 2973704 | tf_op jit(solution)/shard_map/ppermute | solution.py:60
  184.6 4.6 %collective-permute-start.37 = (bf16[80,1472]{1,0:T(8,128)(2,1)S(1)}, bf16[80,1472]{1,0:T(8,128)(2,1)S(1)}, u32[]{:S(2)}, u32[]{:S(2)}) collective-permute-start(bf16[80,1472]{1,0:T(8,128)(2,1)S(1)} %get-tuple-element.181.b_mine), channel_id=1, source_target_pairs={{0,1},{1,0},{2,3},{3,2},{4,5},{5,4},{6,7},{7,6},{8,9},{9,8},{10,11... | collective-permute-start | bytes 706568 | tf_op jit(solution)/shard_map/ppermute | solution.py:60
  185.1 12.2 %collective-permute-start.41 = (bf16[208,368]{1,0:T(8,128)(2,1)S(1)}, bf16[208,368]{1,0:T(8,128)(2,1)S(1)}, u32[]{:S(2)}, u32[]{:S(2)}) collective-permute-start(bf16[208,368]{1,0:T(8,128)(2,1)S(1)} %get-tuple-element.187), channel_id=1, source_target_pairs={{0,16},{8,24},{16,0},{24,8},{1,17},{9,25},{17,1},{25,9},{2,18},{10... | collective-permute-start | bytes 459272 | tf_op jit(solution)/shard_map/ppermute | solution.py:55
  186.1 11.2 %collective-permute-start.42 = (bf16[208,368]{1,0:T(8,128)(2,1)S(1)}, bf16[208,368]{1,0:T(8,128)(2,1)S(1)}, u32[]{:S(2)}, u32[]{:S(2)}) collective-permute-start(bf16[208,368]{1,0:T(8,128)(2,1)S(1)} %get-tuple-element.189), channel_id=1, source_target_pairs={{0,24},{8,0},{16,8},{24,16},{1,25},{9,1},{17,9},{25,17},{2,26},{10... | collective-permute-start | bytes 459272 | tf_op jit(solution)/shard_map/ppermute | solution.py:55
  189.2 11.0 %collective-permute-start.40 = (bf16[208,368]{1,0:T(8,128)(2,1)S(1)}, bf16[208,368]{1,0:T(8,128)(2,1)S(1)}, u32[]{:S(2)}, u32[]{:S(2)}) collective-permute-start(bf16[208,368]{1,0:T(8,128)(2,1)S(1)} %get-tuple-element.185), channel_id=1, source_target_pairs={{0,8},{8,16},{16,24},{24,0},{1,9},{9,17},{17,25},{25,1},{2,10},{10... | collective-permute-start | bytes 459272 | tf_op jit(solution)/shard_map/ppermute | solution.py:55
  200.3 10.5 %collective-permute-start.45 = (bf16[208,368]{1,0:T(8,128)(2,1)S(1)}, bf16[208,368]{1,0:T(8,128)(2,1)S(1)}, u32[]{:S(2)}, u32[]{:S(2)}) collective-permute-start(bf16[208,368]{1,0:T(8,128)(2,1)S(1)} %fusion.2.refs_0_), channel_id=1, source_target_pairs={{0,6},{2,4},{4,2},{6,0},{1,7},{3,5},{5,3},{7,1},{8,14},{10,12},{12... | collective-permute-start | bytes 459272 | tf_op jit(solution)/shard_map/ppermute | solution.py:60
  202.0 9.2 %collective-permute-start.44 = (bf16[208,368]{1,0:T(8,128)(2,1)S(1)}, bf16[208,368]{1,0:T(8,128)(2,1)S(1)}, u32[]{:S(2)}, u32[]{:S(2)}) collective-permute-start(bf16[208,368]{1,0:T(8,128)(2,1)S(1)} %fusion.2.refs_0_), channel_id=1, source_target_pairs={{0,4},{2,6},{4,0},{6,2},{1,5},{3,7},{5,1},{7,3},{8,12},{10,14},{12... | collective-permute-start | bytes 459272 | tf_op jit(solution)/shard_map/ppermute | solution.py:60
  203.3 9.2 %collective-permute-start.43 = (bf16[208,368]{1,0:T(8,128)(2,1)S(1)}, bf16[208,368]{1,0:T(8,128)(2,1)S(1)}, u32[]{:S(2)}, u32[]{:S(2)}) collective-permute-start(bf16[208,368]{1,0:T(8,128)(2,1)S(1)} %fusion.2.refs_0_), channel_id=1, source_target_pairs={{0,2},{2,0},{4,6},{6,4},{1,3},{3,1},{5,7},{7,5},{8,10},{10,8},{12,... | collective-permute-start | bytes 459272 | tf_op jit(solution)/shard_map/ppermute | solution.py:60
  212.6 10.6 %collective-permute-start.48 = (bf16[1936,128]{1,0:T(8,128)(2,1)S(1)}, bf16[1936,128]{1,0:T(8,128)(2,1)S(1)}, u32[]{:S(2)}, u32[]{:S(2)}) collective-permute-start(bf16[1936,128]{1,0:T(8,128)(2,1)S(1)} %slice.103), channel_id=1, source_target_pairs={{0,2},{2,0},{4,6},{6,4},{1,3},{3,1},{5,7},{7,5},{8,10},{10,8},{12,... | collective-permute-start | bytes 1486856 | tf_op jit(solution)/shard_map/ppermute | solution.py:60
  213.3 10.5 %collective-permute-start.47 = (bf16[1936,128]{1,0:T(8,128)(2,1)S(1)}, bf16[1936,128]{1,0:T(8,128)(2,1)S(1)}, u32[]{:S(2)}, u32[]{:S(2)}) collective-permute-start(bf16[1936,128]{1,0:T(8,128)(2,1)S(1)} %slice.102), channel_id=1, source_target_pairs={{0,4},{2,6},{4,0},{6,2},{1,5},{3,7},{5,1},{7,3},{8,12},{10,14},{12... | collective-permute-start | bytes 1486856 | tf_op jit(solution)/shard_map/ppermute | solution.py:60
  216.3 3.8 %collective-permute-start.46 = (f32[2,368]{1,0:T(2,128)S(1)}, f32[2,368]{1,0:T(2,128)S(1)}, u32[]{:S(2)}, u32[]{:S(2)}) collective-permute-start(f32[2,368]{1,0:T(2,128)S(1)} %get-tuple-element.193), channel_id=1, source_target_pairs={{0,1},{1,0},{2,3},{3,2},{4,5},{5,4},{6,7},{7,6},{8,9},{9,8},{10,11... | collective-permute-start | bytes 8840 | tf_op jit(solution)/shard_map/ppermute | solution.py:60
  (33 other events, 485.8 us)
Sparse Core Ops, SparseCore 0:
  10.2 84.2 all-gather.2
  106.9 72.7 reduce-scatter.1

commit v9 on v8

--- a/solution.py
+++ b/solution.py
@@ -515,7 +515,7 @@
     count = sum((pieces for _, pieces, _ in flat))
     sources, refs = refs[:count], refs[count:]
     n_outs = 3
-    outs, (stage, held, sems) = refs[-3 - n_outs : -3], refs[-3:]
+    outs, (held, sems) = refs[-2 - n_outs : -2], refs[-2:]
     r = outs[0].shape[0]
     columns = sum(widths)
     parts, rows = wide_tiles(r, widths)
@@ -547,27 +547,27 @@
                 far = (lax.div(c, period) ^ (group[0][0] // period)) * (period * columns) + start
                 for k, pieces, low_lane, high_lane, at_source in taken:
                     size_each = rows // pieces
+                    begin = ((v ^ k) % period) * columns - start
                     for i, n in enumerate(widths):
                         base = sum(widths[:i])
-                        lo, hi = max(low_lane, base), min(high_lane, base + n)
-                        if lo >= hi:
-                            continue
                         for row, size, top, lane, lanes, at in parts[i]:
-                            done = 0
-                            while done < size:
-                                part, here = divmod(row + done, size_each)
-                                many = min(size - done, size_each - here)
-                                stage[top + done : top + done + many, lane : lane + lanes] = (
-                                    sources[at_source + part][
-                                        here : here + many, at : at + lanes
-                                    ].astype(wide)
-                                )
-                                done += many
-                        to = ((v ^ k) % period) * columns + lo - start
-                        for j in range(3):
-                            held[g, j, :, to : to + hi - lo] = stage[
-                                :, j * n + lo - base : j * n + hi - base
-                            ]
+                            while lanes:
+                                j, inside = divmod(lane, n)
+                                take = min(lanes, n - inside)
+                                lo = max(low_lane, base + inside)
+                                hi = min(high_lane, base + inside + take)
+                                skip = lo - base - inside
+                                done = 0 if lo < hi else size
+                                while done < size:
+                                    part, here = divmod(row + done, size_each)
+                                    many = min(size - done, size_each - here)
+                                    held[g, j, top + done : top + done + many, begin + lo : begin + hi] = (
+                                        sources[at_source + part][
+                                            here : here + many, at + skip : at + skip + hi - lo
+                                        ].astype(wide)
+                                    )
+                                    done += many
+                                lane, at, lanes = lane + take, at + take, lanes - take
                 for j in range(3):
                     copy = pltpu.make_async_copy(
                         held.at[g, j, :, 0 : stop - start],
@@ -885,7 +885,6 @@
             [(w_gate.shape, wide)] * 3,
             [now, *sources, *before],
             scratch=[
-                pltpu.VMEM((r, 3 * max(widths)), wide),
                 pltpu.VMEM((len(groups), 3, r, span), wide),
                 pltpu.SemaphoreType.DMA((3 * len(groups),)),
             ],

time: 233 us -> 233 us (level)
  no operation moved by 1% of the time
where the time goes in v9:
time: 233 us
  waiting for transfers between devices  97.8 us (42%)
  Pallas kernels  63.1 us (27%)
  starting transfers between devices  50.5 us (22%)
  between operations  14.7 us (6%)
  local copies, waits for them, and re-layouts  3.65 us (2%)
  other arithmetic  3.2 us (1%)
    ppermute x42, waiting for transfers between devices, swap(): return lax.ppermute(x, axis, [(i, i ^ k) for i in range(n)])  82 us
    pallas_call x18, Pallas kernels, run(): pl.pallas_call(body, name=name, out_shape=[jax.ShapeDtypeStruct(s, d) for...  63.1 us
    ppermute x42, starting transfers between devices, swap(): return lax.ppermute(x, axis, [(i, i ^ k) for i in range(n)])  36.6 us
    ppermute x7, starting transfers between devices, step(): return lax.ppermute(x, axis, [(i, (i + k) % n) for i in range(n)])  13.8 us
    ppermute x7, waiting for transfers between devices, step(): return lax.ppermute(x, axis, [(i, (i + k) % n) for i in range(n)])  11.2 us
  transfers between devices with their start and end apart: 51, of which 27 were waited for; matrix products, arithmetic and copies ran while one was open for 2% of the time, Pallas kernels for 20%

profile of v9, /device:TPU:0, one launch (start us, length us, event | category | flops | bytes accessed | tf_op | source)
XLA Modules:
  0.0 233.0 jit_solution(1222516301053068447)
XLA Ops:
  7.3 2.6 %pack_wide.1 = bf16[3872,128]{1,0:T(8,128)(2,1)} custom-call(bf16[368,1792]{1,0:T(8,128)(2,1)} %w_g.1, bf16[368,1792]{1,0:T(8,128)(2,1)} %w_u.1, bf16[368,1792]{1,0:T(8,128)(2,1)} %bitcast.65), custom_call_target="tpu_custom_call" | custom-call | flops 200000000 | tf_op jit(solution)/shard_map/pack_wide/pallas_call | solution.py:37
  11.2 2.3 pack_attention.1.refs_4_
  13.5 5.1 %collective-permute-start.2 = (bf16[208,384]{1,0:T(8,128)(2,1)}, bf16[208,384]{1,0:T(8,128)(2,1)S(1)}, u32[]{:S(2)}, u32[]{:S(2)}) collective-permute-start(bf16[208,384]{1,0:T(8,128)(2,1)} %pack_attention.1.refs_4_), channel_id=1, source_target_pairs={{0,24},{8,0},{16,8},{24,16},{1,25},{9,1},{17,9},{25,17},{2,26},{10... | collective-permute-start | bytes 479240 | tf_op jit(solution)/shard_map/ppermute | solution.py:55
  19.5 5.3 %bias.1 = f32[3,320,320]{2,1,0:T(8,128)S(1)} custom-call(s32[3]{0:T(128)S(1)} %copy-done.20, f32[32,3]{1,0:T(8,128)S(1)} %copy.27.table), custom_call_target="tpu_custom_call" | custom-call | flops 500000000 | tf_op jit(solution)/shard_map/bias/pallas_call | solution.py:37
  24.8 2.8 %collective-permute-start.6 = (bf16[80,1472]{1,0:T(8,128)(2,1)S(1)}, bf16[80,1472]{1,0:T(8,128)(2,1)S(1)}, u32[]{:S(2)}, u32[]{:S(2)}) collective-permute-start(bf16[80,1472]{1,0:T(8,128)(2,1)S(1)} %get-tuple-element.111), channel_id=1, source_target_pairs={{0,6},{2,4},{4,2},{6,0},{1,7},{3,5},{5,3},{7,1},{8,14},{10,12},{12... | collective-permute-start | bytes 706568 | tf_op jit(solution)/shard_map/ppermute | solution.py:60
  28.3 3.9 %collective-permute-start.3 = (bf16[104,384]{1,0:T(8,128)(2,1)S(1)}, bf16[104,384]{1,0:T(8,128)(2,1)S(1)}, u32[]{:S(2)}, u32[]{:S(2)}) collective-permute-start(bf16[104,384]{1,0:T(8,128)(2,1)S(1)} %slice.105), channel_id=1, source_target_pairs={{0,24},{8,0},{16,8},{24,16},{1,25},{9,1},{17,9},{25,17},{2,26},{10... | collective-permute-start | bytes 239624 | tf_op jit(solution)/shard_map/ppermute | solution.py:55
  33.1 1.5 collective-permute-done.6.refs_2_
  34.6 3.8 %collective-permute-done.5.refs_1_ = bf16[80,1472]{1,0:T(8,128)(2,1)S(1)} collective-permute-done((bf16[80,1472]{1,0:T(8,128)(2,1)S(1)}, bf16[80,1472]{1,0:T(8,128)(2,1)S(1)}, u32[]{:S(2)}, u32[]{:S(2)}) %collective-permute-start.5) | collective-permute-done | bytes 235552 | tf_op jit(solution)/shard_map/ppermute | solution.py:60
  38.6 1.8 collective-permute-done.1
  40.6 2.7 %collective-permute-start.9 = (bf16[624,384]{1,0:T(8,128)(2,1)S(1)}, bf16[624,384]{1,0:T(8,128)(2,1)S(1)}, u32[]{:S(2)}, u32[]{:S(2)}) collective-permute-start(bf16[624,384]{1,0:T(8,128)(2,1)S(1)} %constant_dynamic-update-slice_fusion.2.refs_0_), channel_id=1, source_target_pairs={{0,6},{2,4},{4,2},{6,0},{1,7},{3,5},{5,3},{7,1},{8,14},{10,12},{12... | collective-permute-start | bytes 1437704 | tf_op jit(solution)/shard_map/ppermute | solution.py:60
  45.4 9.9 %collective-permute-done.9.refs_3_ = bf16[624,384]{1,0:T(8,128)(2,1)S(1)} collective-permute-done((bf16[624,384]{1,0:T(8,128)(2,1)S(1)}, bf16[624,384]{1,0:T(8,128)(2,1)S(1)}, u32[]{:S(2)}, u32[]{:S(2)}) %collective-permute-start.9) | collective-permute-done | bytes 479264 | tf_op jit(solution)/shard_map/ppermute | solution.py:60
  55.3 9.8 %collective-permute-done.8.refs_2_ = bf16[624,384]{1,0:T(8,128)(2,1)S(1)} collective-permute-done((bf16[624,384]{1,0:T(8,128)(2,1)S(1)}, bf16[624,384]{1,0:T(8,128)(2,1)S(1)}, u32[]{:S(2)}, u32[]{:S(2)}) %collective-permute-start.8) | collective-permute-done | bytes 479264 | tf_op jit(solution)/shard_map/ppermute | solution.py:60
  65.2 1.8 collective-permute-start.13
  67.0 1.4 collective-permute-start.12
  68.7 11.7 %attend.1 = (bf16[320,1472]{1,0:T(8,128)(2,1)S(1)}, bf16[320,1472]{1,0:T(8,128)(2,1)S(1)}, f32[2,3,80,320]{3,2,1,0:T(8,128)S(1)}, bf16[640,576]{1,0:T(8,128)(2,1...) custom-call(s32[3]{0:T(128)S(1)} %copy-done.20, bf16[640,1472]{1,0:T(8,128)(2,1)S(1)} %get-tuple-element.115.normed, ...), custom_call_target="tpu_custom_call" | custom-call | flops 1400000000 | tf_op jit(solution)/shard_map/attend/pallas_call | solution.py:37
  80.6 2.6 %collective-permute-done.14.refs_4_ = bf16[320,1472]{1,0:T(8,128)(2,1)S(1)} collective-permute-done((bf16[320,1472]{1,0:T(8,128)(2,1)S(1)}, bf16[320,1472]{1,0:T(8,128)(2,1)S(1)}, u32[]{:S(2)}, u32[]{:S(2)}) %collective-permute-start.14) | collective-permute-done | bytes 942112 | tf_op jit(solution)/shard_map/ppermute | solution.py:60
  86.1 2.9 %collective-permute-done.16.refs_3_ = bf16[3,80,1472]{2,1,0:T(8,128)(2,1)S(1)} collective-permute-done((bf16[3,80,1472]{2,1,0:T(8,128)(2,1)S(1)}, bf16[3,80,1472]{2,1,0:T(8,128)(2,1)S(1)}, u32[]{:S(2)}, u32[]{:S(2)}) %collective-permute-start.16) | collective-permute-done | bytes 706592 | tf_op jit(solution)/shard_map/ppermute | solution.py:60
  89.9 4.6 %all-gather.3.cloned.1.call-done = bf16[15488,128]{1,0:T(8,128)(2,1)} async-done(((bf16[3872,128]{1,0:T(8,128)(2,1)}), bf16[15488,128]{1,0:T(8,128)(2,1)}) %all-gather.3.cloned.1.call-update) | async-done | bytes 3964944 | tf_op jit(solution)/shard_map/all_gather | solution.py:647
  94.5 12.3 %feed_forward.1 = (bf16[4,3872,128]{2,1,0:T(8,128)(2,1)}, bf16[640,256]{1,0:T(8,128)(2,1)}, bf16[640,192]{1,0:T(8,128)(2,1)}, bf16[640,512]{1,0:T(8,128)(2,1)}, bf16[640,384]{1,0:T(8,128)(2,1)}) custom-call(s32[3]{0:T(128)} %pad_add_fusion.idx, bf16[4,3872,128]{2,1,0:T(8,128)(2,1)} %bitcast.62, bf16[320,1472]{1,0:T(8,128)(2,1)} %copy-done.8, ...), custom_call_target="tpu_custom_call" | custom-call | flops 1400000000 | tf_op jit(solution)/shard_map/feed_forward/pallas_call | solution.py:37
  106.8 7.6 %feed_out.1 = (bf16[4,80,1472]{2,1,0:T(8,128)(2,1)}, bf16[4,80,1472]{2,1,0:T(8,128)(2,1)}, bf16[4,80,1472]{2,1,0:T(8,128)(2,1)}, bf16[4,80,1472]{2,1,0:T(8,128)(2,1)}) custom-call(s32[3]{0:T(128)} %pad_add_fusion.idx, bf16[4,3872,128]{2,1,0:T(8,128)(2,1)} %bitcast.63, bf16[640,256]{1,0:T(8,128)(2,1)} %get-tuple-element.126.refs_0_, ...), custom_call_target="tpu_custom_call" | custom-call | flops 500000000 | tf_op jit(solution)/shard_map/feed_out/pallas_call | solution.py:37
  114.6 2.7 %collective-permute-done.17 = bf16[4,80,1472]{2,1,0:T(8,128)(2,1)S(1)} collective-permute-done((bf16[4,80,1472]{2,1,0:T(8,128)(2,1)}, bf16[4,80,1472]{2,1,0:T(8,128)(2,1)S(1)}, u32[]{:S(2)}, u32[]{:S(2)}) %collective-permute-start.17) | collective-permute-done | bytes 942112 | tf_op jit(solution)/shard_map/ppermute | solution.py:60
  117.3 1.5 fusion.6
  118.9 2.8 %collective-permute-start.20 = (bf16[80,1472]{1,0:T(8,128)(2,1)S(1)}, bf16[80,1472]{1,0:T(8,128)(2,1)S(1)}, u32[]{:S(2)}, u32[]{:S(2)}) collective-permute-start(bf16[80,1472]{1,0:T(8,128)(2,1)S(1)} %get-tuple-element.213), channel_id=1, source_target_pairs={{0,6},{2,4},{4,2},{6,0},{1,7},{3,5},{5,3},{7,1},{8,14},{10,12},{12... | collective-permute-start | bytes 706568 | tf_op jit(solution)/shard_map/ppermute | solution.py:60
  122.4 6.2 %collective-permute-done.20.refs_3_ = bf16[80,1472]{1,0:T(8,128)(2,1)S(1)} collective-permute-done((bf16[80,1472]{1,0:T(8,128)(2,1)S(1)}, bf16[80,1472]{1,0:T(8,128)(2,1)S(1)}, u32[]{:S(2)}, u32[]{:S(2)}) %collective-permute-start.20) | collective-permute-done | bytes 235552 | tf_op jit(solution)/shard_map/ppermute | solution.py:60
  128.7 4.5 %collective-permute-done.19.refs_2_ = bf16[80,1472]{1,0:T(8,128)(2,1)S(1)} collective-permute-done((bf16[80,1472]{1,0:T(8,128)(2,1)S(1)}, bf16[80,1472]{1,0:T(8,128)(2,1)S(1)}, u32[]{:S(2)}, u32[]{:S(2)}) %collective-permute-start.19) | collective-permute-done | bytes 235552 | tf_op jit(solution)/shard_map/ppermute | solution.py:60
  134.4 1.4 collective-permute-done.21.o_other
  136.0 4.1 %attend_back.1 = (bf16[160,384]{1,0:T(8,128)(2,1)S(1)}, bf16[160,384]{1,0:T(8,128)(2,1)S(1)}, bf16[160,384]{1,0:T(8,128)(2,1)S(1)}, bf16[160,384]{1,0:T(8,128)(2...) custom-call(s32[3]{0:T(128)S(1)} %copy-done.21, ...), custom_call_target="tpu_custom_call" | custom-call | flops 400000000 | tf_op jit(solution)/shard_map/attend_back/pallas_call | solution.py:37
  140.1 1.8 collective-permute-start.23
  143.7 1.7 collective-permute-start.29
  146.0 4.3 %collective-permute-done.24.refs_2_ = bf16[160,384]{1,0:T(8,128)(2,1)S(1)} collective-permute-done((bf16[160,384]{1,0:T(8,128)(2,1)S(1)}, bf16[160,384]{1,0:T(8,128)(2,1)S(1)}, u32[]{:S(2)}, u32[]{:S(2)}) %collective-permute-start.24) | collective-permute-done | bytes 122912 | tf_op jit(solution)/shard_map/ppermute | solution.py:60
  150.3 1.8 first_grad.1
  154.5 1.5 collective-permute-start.32
  157.3 12.9 %collective-permute-done.31.refs_7_ = bf16[48,1472]{1,0:T(8,128)(2,1)S(1)} collective-permute-done((bf16[48,1472]{1,0:T(8,128)(2,1)S(1)}, bf16[48,1472]{1,0:T(8,128)(2,1)S(1)}, u32[]{:S(2)}, u32[]{:S(2)}) %collective-permute-start.31) | collective-permute-done | bytes 141344 | tf_op jit(solution)/shard_map/ppermute | solution.py:60
  170.8 3.9 %collective-permute-done.26.refs_1_ = bf16[160,144]{1,0:T(8,128)(2,1)S(1)} collective-permute-done((bf16[160,144]{1,0:T(8,128)(2,1)S(1)}, bf16[160,144]{1,0:T(8,128)(2,1)S(1)}, u32[]{:S(2)}, u32[]{:S(2)}) %collective-permute-start.26) | collective-permute-done | bytes 46112 | tf_op jit(solution)/shard_map/ppermute | solution.py:60
  177.6 1.8 collective-permute-done.27.refs_2_
  179.4 1.4 collective-permute-done.28.refs_3_
  180.8 1.7 weight_grads.1
  182.7 1.4 collective-permute-start.39
  186.1 3.1 %collective-permute-start.42 = (bf16[208,368]{1,0:T(8,128)(2,1)S(1)}, bf16[208,368]{1,0:T(8,128)(2,1)S(1)}, u32[]{:S(2)}, u32[]{:S(2)}) collective-permute-start(bf16[208,368]{1,0:T(8,128)(2,1)S(1)} %get-tuple-element.189), channel_id=1, source_target_pairs={{0,24},{8,0},{16,8},{24,16},{1,25},{9,1},{17,9},{25,17},{2,26},{10... | collective-permute-start | bytes 459272 | tf_op jit(solution)/shard_map/ppermute | solution.py:55
  189.2 1.5 place_outputs.1
  190.7 6.6 %collective-permute-done.41 = bf16[208,368]{1,0:T(8,128)(2,1)S(1)} collective-permute-done((bf16[208,368]{1,0:T(8,128)(2,1)S(1)}, bf16[208,368]{1,0:T(8,128)(2,1)S(1)}, u32[]{:S(2)}, u32[]{:S(2)}) %collective-permute-start.41) | collective-permute-done | bytes 153120 | tf_op jit(solution)/shard_map/ppermute | solution.py:55
  197.3 2.9 %collective-permute-done.40 = bf16[208,368]{1,0:T(8,128)(2,1)S(1)} collective-permute-done((bf16[208,368]{1,0:T(8,128)(2,1)S(1)}, bf16[208,368]{1,0:T(8,128)(2,1)S(1)}, u32[]{:S(2)}, u32[]{:S(2)}) %collective-permute-start.40) | collective-permute-done | bytes 153120 | tf_op jit(solution)/shard_map/ppermute | solution.py:55
  200.3 1.7 collective-permute-start.45
  203.8 7.0 %collective-permute-done.45.refs_3_ = bf16[208,368]{1,0:T(8,128)(2,1)S(1)} collective-permute-done((bf16[208,368]{1,0:T(8,128)(2,1)S(1)}, bf16[208,368]{1,0:T(8,128)(2,1)S(1)}, u32[]{:S(2)}, u32[]{:S(2)}) %collective-permute-start.45) | collective-permute-done | bytes 153120 | tf_op jit(solution)/shard_map/ppermute | solution.py:60
  214.6 1.7 finish_attention.1
  216.3 3.5 %finish_wide.2 = (f32[368,1792]{1,0:T(8,128)}, f32[368,1792]{1,0:T(8,128)}, f32[368,1792]{1,0:T(8,128)}) custom-call(s32[3]{0:T(128)S(1)} %copy-done.21, bf16[3872,128]{1,0:T(8,128)(2,1)S(1)} %bitcast.55, bf16[3872,128]{1,0:T(8,128)(2,1)S(1)} %collective-permute-done.38.refs_1_, bf16[3872,128]{1,0:T(8,128)(2,1)S(1)} %collective-permute-done.39.refs_2_.refs_0_), custom_call_target="tpu_custom_call" | custom-call | flops 300000000 | tf_op jit(solution)/shard_map/finish_wide/pallas_call | solution.py:37
  220.4 2.7 %collective-permute-done.48.refs_2_ = bf16[1936,128]{1,0:T(8,128)(2,1)S(1)} collective-permute-done((bf16[1936,128]{1,0:T(8,128)(2,1)S(1)}, bf16[1936,128]{1,0:T(8,128)(2,1)S(1)}, u32[]{:S(2)}, u32[]{:S(2)}) %collective-permute-start.48) | collective-permute-done | bytes 495648 | tf_op jit(solution)/shard_map/ppermute | solution.py:60
  223.8 2.3 finish_wide.3
  (157 shorter events, 31.4 us)
Async XLA Ops:
  7.2 87.3 %all-gather.3.cloned.1.call-start = ((), (), s32[]{:S(2)}) async-start(), calls=%async_computation.2 | async-start | bytes 4956160 | tf_op jit(solution)/shard_map/all_gather | solution.py:647
  9.9 172.7 %reduce-scatter.2.cloned.1.call-start = ((), (), s32[]{:S(2)}) async-start(), calls=%async_computation.1 | async-start | bytes 4956160 | tf_op jit(solution)/shard_map/reduce_scatter | solution.py:749
  13.5 14.8 %collective-permute-start.2 = (bf16[208,384]{1,0:T(8,128)(2,1)}, bf16[208,384]{1,0:T(8,128)(2,1)S(1)}, u32[]{:S(2)}, u32[]{:S(2)}) collective-permute-start(bf16[208,384]{1,0:T(8,128)(2,1)} %pack_attention.1.refs_4_), channel_id=1, source_target_pairs={{0,24},{8,0},{16,8},{24,16},{1,25},{9,1},{17,9},{25,17},{2,26},{10... | collective-permute-start | bytes 479240 | tf_op jit(solution)/shard_map/ppermute | solution.py:55
  18.6 13.6 %collective-permute-start = (bf16[208,384]{1,0:T(8,128)(2,1)}, bf16[208,384]{1,0:T(8,128)(2,1)S(1)}, u32[]{:S(2)}, u32[]{:S(2)}) collective-permute-start(bf16[208,384]{1,0:T(8,128)(2,1)} %pack_attention.1.refs_4_), channel_id=1, source_target_pairs={{0,8},{8,16},{16,24},{24,0},{1,9},{9,17},{17,25},{25,1},{2,10},{10... | collective-permute-start | bytes 479240 | tf_op jit(solution)/shard_map/ppermute | solution.py:55
  24.8 9.9 %collective-permute-start.6 = (bf16[80,1472]{1,0:T(8,128)(2,1)S(1)}, bf16[80,1472]{1,0:T(8,128)(2,1)S(1)}, u32[]{:S(2)}, u32[]{:S(2)}) collective-permute-start(bf16[80,1472]{1,0:T(8,128)(2,1)S(1)} %get-tuple-element.111), channel_id=1, source_target_pairs={{0,6},{2,4},{4,2},{6,0},{1,7},{3,5},{5,3},{7,1},{8,14},{10,12},{12... | collective-permute-start | bytes 706568 | tf_op jit(solution)/shard_map/ppermute | solution.py:60
  27.5 10.9 %collective-permute-start.5 = (bf16[80,1472]{1,0:T(8,128)(2,1)S(1)}, bf16[80,1472]{1,0:T(8,128)(2,1)S(1)}, u32[]{:S(2)}, u32[]{:S(2)}) collective-permute-start(bf16[80,1472]{1,0:T(8,128)(2,1)S(1)} %get-tuple-element.111), channel_id=1, source_target_pairs={{0,4},{2,6},{4,0},{6,2},{1,5},{3,7},{5,1},{7,3},{8,12},{10,14},{12... | collective-permute-start | bytes 706568 | tf_op jit(solution)/shard_map/ppermute | solution.py:60
  28.0 10.5 %collective-permute-start.4 = (bf16[80,1472]{1,0:T(8,128)(2,1)S(1)}, bf16[80,1472]{1,0:T(8,128)(2,1)S(1)}, u32[]{:S(2)}, u32[]{:S(2)}) collective-permute-start(bf16[80,1472]{1,0:T(8,128)(2,1)S(1)} %get-tuple-element.111), channel_id=1, source_target_pairs={{0,2},{2,0},{4,6},{6,4},{1,3},{3,1},{5,7},{7,5},{8,10},{10,8},{12,... | collective-permute-start | bytes 706568 | tf_op jit(solution)/shard_map/ppermute | solution.py:60
  28.3 12.1 %collective-permute-start.3 = (bf16[104,384]{1,0:T(8,128)(2,1)S(1)}, bf16[104,384]{1,0:T(8,128)(2,1)S(1)}, u32[]{:S(2)}, u32[]{:S(2)}) collective-permute-start(bf16[104,384]{1,0:T(8,128)(2,1)S(1)} %slice.105), channel_id=1, source_target_pairs={{0,24},{8,0},{16,8},{24,16},{1,25},{9,1},{17,9},{25,17},{2,26},{10... | collective-permute-start | bytes 239624 | tf_op jit(solution)/shard_map/ppermute | solution.py:55
  32.3 8.1 %collective-permute-start.1 = (bf16[104,384]{1,0:T(8,128)(2,1)S(1)}, bf16[104,384]{1,0:T(8,128)(2,1)S(1)}, u32[]{:S(2)}, u32[]{:S(2)}) collective-permute-start(bf16[104,384]{1,0:T(8,128)(2,1)S(1)} %slice.104), channel_id=1, source_target_pairs={{0,8},{8,16},{16,24},{24,0},{1,9},{9,17},{17,25},{25,1},{2,10},{10... | collective-permute-start | bytes 239624 | tf_op jit(solution)/shard_map/ppermute | solution.py:55
  40.4 3.7 %collective-permute-start.10 = (bf16[3,80,1472]{2,1,0:T(8,128)(2,1)S(1)}, bf16[3,80,1472]{2,1,0:T(8,128)(2,1)S(1)}, u32[]{:S(2)}, u32[]{:S(2)}) collective-permute-start(bf16[3,80,1472]{2,1,0:T(8,128)(2,1)S(1)} %pad_maximum_fusion), channel_id=1, source_target_pairs={{0,1},{1,0},{2,3},{3,2},{4,5},{5,4},{6,7},{7,6},{8,9},{9,8},{10,11... | collective-permute-start | bytes 2119688 | tf_op jit(solution)/shard_map/ppermute | solution.py:60
  40.6 14.8 %collective-permute-start.9 = (bf16[624,384]{1,0:T(8,128)(2,1)S(1)}, bf16[624,384]{1,0:T(8,128)(2,1)S(1)}, u32[]{:S(2)}, u32[]{:S(2)}) collective-permute-start(bf16[624,384]{1,0:T(8,128)(2,1)S(1)} %constant_dynamic-update-slice_fusion.2.refs_0_), channel_id=1, source_target_pairs={{0,6},{2,4},{4,2},{6,0},{1,7},{3,5},{5,3},{7,1},{8,14},{10,12},{12... | collective-permute-start | bytes 1437704 | tf_op jit(solution)/shard_map/ppermute | solution.py:60
  43.3 21.9 %collective-permute-start.8 = (bf16[624,384]{1,0:T(8,128)(2,1)S(1)}, bf16[624,384]{1,0:T(8,128)(2,1)S(1)}, u32[]{:S(2)}, u32[]{:S(2)}) collective-permute-start(bf16[624,384]{1,0:T(8,128)(2,1)S(1)} %constant_dynamic-update-slice_fusion.2.refs_0_), channel_id=1, source_target_pairs={{0,4},{2,6},{4,0},{6,2},{1,5},{3,7},{5,1},{7,3},{8,12},{10,14},{12... | collective-permute-start | bytes 1437704 | tf_op jit(solution)/shard_map/ppermute | solution.py:60
  43.8 21.4 %collective-permute-start.7 = (bf16[624,384]{1,0:T(8,128)(2,1)S(1)}, bf16[624,384]{1,0:T(8,128)(2,1)S(1)}, u32[]{:S(2)}, u32[]{:S(2)}) collective-permute-start(bf16[624,384]{1,0:T(8,128)(2,1)S(1)} %constant_dynamic-update-slice_fusion.2.refs_0_), channel_id=1, source_target_pairs={{0,2},{2,0},{4,6},{6,4},{1,3},{3,1},{5,7},{7,5},{8,10},{10,8},{12,... | collective-permute-start | bytes 1437704 | tf_op jit(solution)/shard_map/ppermute | solution.py:60
  65.2 15.2 %collective-permute-start.13 = (bf16[80,1472]{1,0:T(8,128)(2,1)S(1)}, bf16[80,1472]{1,0:T(8,128)(2,1)S(1)}, u32[]{:S(2)}, u32[]{:S(2)}) collective-permute-start(bf16[80,1472]{1,0:T(8,128)(2,1)S(1)} %get-tuple-element.117), channel_id=1, source_target_pairs={{0,6},{2,4},{4,2},{6,0},{1,7},{3,5},{5,3},{7,1},{8,14},{10,12},{12... | collective-permute-start | bytes 706568 | tf_op jit(solution)/shard_map/ppermute | solution.py:60
  67.0 13.5 %collective-permute-start.12 = (bf16[80,1472]{1,0:T(8,128)(2,1)S(1)}, bf16[80,1472]{1,0:T(8,128)(2,1)S(1)}, u32[]{:S(2)}, u32[]{:S(2)}) collective-permute-start(bf16[80,1472]{1,0:T(8,128)(2,1)S(1)} %get-tuple-element.117), channel_id=1, source_target_pairs={{0,4},{2,6},{4,0},{6,2},{1,5},{3,7},{5,1},{7,3},{8,12},{10,14},{12... | collective-permute-start | bytes 706568 | tf_op jit(solution)/shard_map/ppermute | solution.py:60
  68.4 12.1 %collective-permute-start.11 = (bf16[80,1472]{1,0:T(8,128)(2,1)S(1)}, bf16[80,1472]{1,0:T(8,128)(2,1)S(1)}, u32[]{:S(2)}, u32[]{:S(2)}) collective-permute-start(bf16[80,1472]{1,0:T(8,128)(2,1)S(1)} %get-tuple-element.117), channel_id=1, source_target_pairs={{0,2},{2,0},{4,6},{6,4},{1,3},{3,1},{5,7},{7,5},{8,10},{10,8},{12,... | collective-permute-start | bytes 706568 | tf_op jit(solution)/shard_map/ppermute | solution.py:60
  85.4 4.5 %collective-permute-start.15 = (bf16[320,1472]{1,0:T(8,128)(2,1)S(1)}, bf16[320,1472]{1,0:T(8,128)(2,1)}, u32[]{:S(2)}, u32[]{:S(2)}) collective-permute-start(bf16[320,1472]{1,0:T(8,128)(2,1)S(1)} %get-tuple-element.123.nt_mine), channel_id=1, source_target_pairs={{0,1},{1,0},{2,3},{3,2},{4,5},{5,4},{6,7},{7,6},{8,9},{9,8},{10,11... | collective-permute-start | bytes 2826248 | tf_op jit(solution)/shard_map/ppermute | solution.py:60
  85.7 3.4 %collective-permute-start.16 = (bf16[3,80,1472]{2,1,0:T(8,128)(2,1)S(1)}, bf16[3,80,1472]{2,1,0:T(8,128)(2,1)S(1)}, u32[]{:S(2)}, u32[]{:S(2)}) collective-permute-start(bf16[3,80,1472]{2,1,0:T(8,128)(2,1)S(1)} %pad_maximum_fusion.1), channel_id=1, source_target_pairs={{0,1},{1,0},{2,3},{3,2},{4,5},{5,4},{6,7},{7,6},{8,9},{9,8},{10,11... | collective-permute-start | bytes 2119688 | tf_op jit(solution)/shard_map/ppermute | solution.py:60
  114.5 2.8 %collective-permute-start.17 = (bf16[4,80,1472]{2,1,0:T(8,128)(2,1)}, bf16[4,80,1472]{2,1,0:T(8,128)(2,1)S(1)}, u32[]{:S(2)}, u32[]{:S(2)}) collective-permute-start(bf16[4,80,1472]{2,1,0:T(8,128)(2,1)} %get-tuple-element.133), channel_id=1, source_target_pairs={{0,1},{1,0},{2,3},{3,2},{4,5},{5,4},{6,7},{7,6},{8,9},{9,8},{10,11... | collective-permute-start | bytes 2826248 | tf_op jit(solution)/shard_map/ppermute | solution.py:60
  118.9 9.8 %collective-permute-start.20 = (bf16[80,1472]{1,0:T(8,128)(2,1)S(1)}, bf16[80,1472]{1,0:T(8,128)(2,1)S(1)}, u32[]{:S(2)}, u32[]{:S(2)}) collective-permute-start(bf16[80,1472]{1,0:T(8,128)(2,1)S(1)} %get-tuple-element.213), channel_id=1, source_target_pairs={{0,6},{2,4},{4,2},{6,0},{1,7},{3,5},{5,3},{7,1},{8,14},{10,12},{12... | collective-permute-start | bytes 706568 | tf_op jit(solution)/shard_map/ppermute | solution.py:60
  121.6 11.5 %collective-permute-start.19 = (bf16[80,1472]{1,0:T(8,128)(2,1)S(1)}, bf16[80,1472]{1,0:T(8,128)(2,1)S(1)}, u32[]{:S(2)}, u32[]{:S(2)}) collective-permute-start(bf16[80,1472]{1,0:T(8,128)(2,1)S(1)} %get-tuple-element.214), channel_id=1, source_target_pairs={{0,4},{2,6},{4,0},{6,2},{1,5},{3,7},{5,1},{7,3},{8,12},{10,14},{12... | collective-permute-start | bytes 706568 | tf_op jit(solution)/shard_map/ppermute | solution.py:60
  122.1 11.1 %collective-permute-start.18 = (bf16[80,1472]{1,0:T(8,128)(2,1)S(1)}, bf16[80,1472]{1,0:T(8,128)(2,1)S(1)}, u32[]{:S(2)}, u32[]{:S(2)}) collective-permute-start(bf16[80,1472]{1,0:T(8,128)(2,1)S(1)} %get-tuple-element.215), channel_id=1, source_target_pairs={{0,2},{2,0},{4,6},{6,4},{1,3},{3,1},{5,7},{7,5},{8,10},{10,8},{12,... | collective-permute-start | bytes 706568 | tf_op jit(solution)/shard_map/ppermute | solution.py:60
  135.8 4.3 %collective-permute-start.22 = (bf16[4,80,1472]{2,1,0:T(8,128)(2,1)S(1)}, bf16[4,80,1472]{2,1,0:T(8,128)(2,1)S(1)}, u32[]{:S(2)}, u32[]{:S(2)}) collective-permute-start(bf16[4,80,1472]{2,1,0:T(8,128)(2,1)S(1)} %copy-done.29), channel_id=1, source_target_pairs={{0,1},{1,0},{2,3},{3,2},{4,5},{5,4},{6,7},{7,6},{8,9},{9,8},{10,11... | collective-permute-start | bytes 2826248 | tf_op jit(solution)/shard_map/ppermute | solution.py:60
  140.1 5.9 %collective-permute-start.23 = (bf16[160,384]{1,0:T(8,128)(2,1)S(1)}, bf16[160,384]{1,0:T(8,128)(2,1)S(1)}, u32[]{:S(2)}, u32[]{:S(2)}) collective-permute-start(bf16[160,384]{1,0:T(8,128)(2,1)S(1)} %get-tuple-element.147), channel_id=1, source_target_pairs={{0,2},{2,0},{4,6},{6,4},{1,3},{3,1},{5,7},{7,5},{8,10},{10,8},{12,... | collective-permute-start | bytes 368648 | tf_op jit(solution)/shard_map/ppermute | solution.py:60
  141.9 8.4 %collective-permute-start.24 = (bf16[160,384]{1,0:T(8,128)(2,1)S(1)}, bf16[160,384]{1,0:T(8,128)(2,1)S(1)}, u32[]{:S(2)}, u32[]{:S(2)}) collective-permute-start(bf16[160,384]{1,0:T(8,128)(2,1)S(1)} %get-tuple-element.149), channel_id=1, source_target_pairs={{0,4},{2,6},{4,0},{6,2},{1,5},{3,7},{5,1},{7,3},{8,12},{10,14},{12... | collective-permute-start | bytes 368648 | tf_op jit(solution)/shard_map/ppermute | solution.py:60
  142.5 7.8 %collective-permute-start.25 = (bf16[160,384]{1,0:T(8,128)(2,1)S(1)}, bf16[160,384]{1,0:T(8,128)(2,1)S(1)}, u32[]{:S(2)}, u32[]{:S(2)}) collective-permute-start(bf16[160,384]{1,0:T(8,128)(2,1)S(1)} %get-tuple-element.151), channel_id=1, source_target_pairs={{0,6},{2,4},{4,2},{6,0},{1,7},{3,5},{5,3},{7,1},{8,14},{10,12},{12... | collective-permute-start | bytes 368648 | tf_op jit(solution)/shard_map/ppermute | solution.py:60
  143.7 10.8 %collective-permute-start.29 = (bf16[48,1472]{1,0:T(8,128)(2,1)S(1)}, bf16[48,1472]{1,0:T(8,128)(2,1)S(1)}, u32[]{:S(2)}, u32[]{:S(2)}) collective-permute-start(bf16[48,1472]{1,0:T(8,128)(2,1)S(1)} %get-tuple-element.161), channel_id=1, source_target_pairs={{0,2},{2,0},{4,6},{6,4},{1,3},{3,1},{5,7},{7,5},{8,10},{10,8},{12,... | collective-permute-start | bytes 423944 | tf_op jit(solution)/shard_map/ppermute | solution.py:60
  145.4 10.6 %collective-permute-start.30 = (bf16[48,1472]{1,0:T(8,128)(2,1)S(1)}, bf16[48,1472]{1,0:T(8,128)(2,1)S(1)}, u32[]{:S(2)}, u32[]{:S(2)}) collective-permute-start(bf16[48,1472]{1,0:T(8,128)(2,1)S(1)} %get-tuple-element.163), channel_id=1, source_target_pairs={{0,4},{2,6},{4,0},{6,2},{1,5},{3,7},{5,1},{7,3},{8,12},{10,14},{12... | collective-permute-start | bytes 423944 | tf_op jit(solution)/shard_map/ppermute | solution.py:60
  152.2 23.3 %collective-permute-start.35 = (bf16[80,1472]{1,0:T(8,128)(2,1)S(1)}, bf16[80,1472]{1,0:T(8,128)(2,1)S(1)}, u32[]{:S(2)}, u32[]{:S(2)}) collective-permute-start(bf16[80,1472]{1,0:T(8,128)(2,1)S(1)} %get-tuple-element.169), channel_id=1, source_target_pairs={{0,1},{1,0},{2,3},{3,2},{4,5},{5,4},{6,7},{7,6},{8,9},{9,8},{10,11... | collective-permute-start | bytes 706568 | tf_op jit(solution)/shard_map/ppermute | solution.py:60
  152.5 28.3 %collective-permute-start.34 = (bf16[80,1472]{1,0:T(8,128)(2,1)S(1)}, bf16[80,1472]{1,0:T(8,128)(2,1)S(1)}, u32[]{:S(2)}, u32[]{:S(2)}) collective-permute-start(bf16[80,1472]{1,0:T(8,128)(2,1)S(1)} %get-tuple-element.210), channel_id=1, source_target_pairs={{0,6},{2,4},{4,2},{6,0},{1,7},{3,5},{5,3},{7,1},{8,14},{10,12},{12... | collective-permute-start | bytes 706568 | tf_op jit(solution)/shard_map/ppermute | solution.py:60
  153.8 26.9 %collective-permute-start.33 = (bf16[80,1472]{1,0:T(8,128)(2,1)S(1)}, bf16[80,1472]{1,0:T(8,128)(2,1)S(1)}, u32[]{:S(2)}, u32[]{:S(2)}) collective-permute-start(bf16[80,1472]{1,0:T(8,128)(2,1)S(1)} %get-tuple-element.211), channel_id=1, source_target_pairs={{0,4},{2,6},{4,0},{6,2},{1,5},{3,7},{5,1},{7,3},{8,12},{10,14},{12... | collective-permute-start | bytes 706568 | tf_op jit(solution)/shard_map/ppermute | solution.py:60
  154.5 26.3 %collective-permute-start.32 = (bf16[80,1472]{1,0:T(8,128)(2,1)S(1)}, bf16[80,1472]{1,0:T(8,128)(2,1)S(1)}, u32[]{:S(2)}, u32[]{:S(2)}) collective-permute-start(bf16[80,1472]{1,0:T(8,128)(2,1)S(1)} %get-tuple-element.212), channel_id=1, source_target_pairs={{0,2},{2,0},{4,6},{6,4},{1,3},{3,1},{5,7},{7,5},{8,10},{10,8},{12,... | collective-permute-start | bytes 706568 | tf_op jit(solution)/shard_map/ppermute | solution.py:60
  156.0 14.2 %collective-permute-start.31 = (bf16[48,1472]{1,0:T(8,128)(2,1)S(1)}, bf16[48,1472]{1,0:T(8,128)(2,1)S(1)}, u32[]{:S(2)}, u32[]{:S(2)}) collective-permute-start(bf16[48,1472]{1,0:T(8,128)(2,1)S(1)} %get-tuple-element.165), channel_id=1, source_target_pairs={{0,6},{2,4},{4,2},{6,0},{1,7},{3,5},{5,3},{7,1},{8,14},{10,12},{12... | collective-permute-start | bytes 423944 | tf_op jit(solution)/shard_map/ppermute | solution.py:60
  170.3 4.4 %collective-permute-start.26 = (bf16[160,144]{1,0:T(8,128)(2,1)S(1)}, bf16[160,144]{1,0:T(8,128)(2,1)S(1)}, u32[]{:S(2)}, u32[]{:S(2)}) collective-permute-start(bf16[160,144]{1,0:T(8,128)(2,1)S(1)} %get-tuple-element.155), channel_id=1, source_target_pairs={{0,2},{2,0},{4,6},{6,4},{1,3},{3,1},{5,7},{7,5},{8,10},{10,8},{12,... | collective-permute-start | bytes 138248 | tf_op jit(solution)/shard_map/ppermute | solution.py:60
  174.7 4.6 %collective-permute-start.27 = (bf16[160,144]{1,0:T(8,128)(2,1)S(1)}, bf16[160,144]{1,0:T(8,128)(2,1)S(1)}, u32[]{:S(2)}, u32[]{:S(2)}) collective-permute-start(bf16[160,144]{1,0:T(8,128)(2,1)S(1)} %get-tuple-element.157), channel_id=1, source_target_pairs={{0,4},{2,6},{4,0},{6,2},{1,5},{3,7},{5,1},{7,3},{8,12},{10,14},{12... | collective-permute-start | bytes 138248 | tf_op jit(solution)/shard_map/ppermute | solution.py:60
  175.4 5.3 %collective-permute-start.28 = (bf16[160,144]{1,0:T(8,128)(2,1)S(1)}, bf16[160,144]{1,0:T(8,128)(2,1)S(1)}, u32[]{:S(2)}, u32[]{:S(2)}) collective-permute-start(bf16[160,144]{1,0:T(8,128)(2,1)S(1)} %get-tuple-element.159), channel_id=1, source_target_pairs={{0,6},{2,4},{4,2},{6,0},{1,7},{3,5},{5,3},{7,1},{8,14},{10,12},{12... | collective-permute-start | bytes 138248 | tf_op jit(solution)/shard_map/ppermute | solution.py:60
  182.7 29.8 %collective-permute-start.39 = (bf16[3872,128]{1,0:T(8,128)(2,1)}, bf16[3872,128]{1,0:T(8,128)(2,1)S(1)}, u32[]{:S(2)}, u32[]{:S(2)}) collective-permute-start(bf16[3872,128]{1,0:T(8,128)(2,1)} %bitcast.53), channel_id=1, source_target_pairs={{0,4},{2,6},{4,0},{6,2},{1,5},{3,7},{5,1},{7,3},{8,12},{10,14},{12... | collective-permute-start | bytes 2973704 | tf_op jit(solution)/shard_map/ppermute | solution.py:60
  184.1 28.4 %collective-permute-start.38 = (bf16[3872,128]{1,0:T(8,128)(2,1)}, bf16[3872,128]{1,0:T(8,128)(2,1)S(1)}, u32[]{:S(2)}, u32[]{:S(2)}) collective-permute-start(bf16[3872,128]{1,0:T(8,128)(2,1)} %bitcast.54), channel_id=1, source_target_pairs={{0,2},{2,0},{4,6},{6,4},{1,3},{3,1},{5,7},{7,5},{8,10},{10,8},{12,... | collective-permute-start | bytes 2973704 | tf_op jit(solution)/shard_map/ppermute | solution.py:60
  184.6 4.6 %collective-permute-start.37 = (bf16[80,1472]{1,0:T(8,128)(2,1)S(1)}, bf16[80,1472]{1,0:T(8,128)(2,1)S(1)}, u32[]{:S(2)}, u32[]{:S(2)}) collective-permute-start(bf16[80,1472]{1,0:T(8,128)(2,1)S(1)} %get-tuple-element.181.b_mine), channel_id=1, source_target_pairs={{0,1},{1,0},{2,3},{3,2},{4,5},{5,4},{6,7},{7,6},{8,9},{9,8},{10,11... | collective-permute-start | bytes 706568 | tf_op jit(solution)/shard_map/ppermute | solution.py:60
  185.1 12.2 %collective-permute-start.41 = (bf16[208,368]{1,0:T(8,128)(2,1)S(1)}, bf16[208,368]{1,0:T(8,128)(2,1)S(1)}, u32[]{:S(2)}, u32[]{:S(2)}) collective-permute-start(bf16[208,368]{1,0:T(8,128)(2,1)S(1)} %get-tuple-element.187), channel_id=1, source_target_pairs={{0,16},{8,24},{16,0},{24,8},{1,17},{9,25},{17,1},{25,9},{2,18},{10... | collective-permute-start | bytes 459272 | tf_op jit(solution)/shard_map/ppermute | solution.py:55
  186.1 11.2 %collective-permute-start.42 = (bf16[208,368]{1,0:T(8,128)(2,1)S(1)}, bf16[208,368]{1,0:T(8,128)(2,1)S(1)}, u32[]{:S(2)}, u32[]{:S(2)}) collective-permute-start(bf16[208,368]{1,0:T(8,128)(2,1)S(1)} %get-tuple-element.189), channel_id=1, source_target_pairs={{0,24},{8,0},{16,8},{24,16},{1,25},{9,1},{17,9},{25,17},{2,26},{10... | collective-permute-start | bytes 459272 | tf_op jit(solution)/shard_map/ppermute | solution.py:55
  189.2 11.0 %collective-permute-start.40 = (bf16[208,368]{1,0:T(8,128)(2,1)S(1)}, bf16[208,368]{1,0:T(8,128)(2,1)S(1)}, u32[]{:S(2)}, u32[]{:S(2)}) collective-permute-start(bf16[208,368]{1,0:T(8,128)(2,1)S(1)} %get-tuple-element.185), channel_id=1, source_target_pairs={{0,8},{8,16},{16,24},{24,0},{1,9},{9,17},{17,25},{25,1},{2,10},{10... | collective-permute-start | bytes 459272 | tf_op jit(solution)/shard_map/ppermute | solution.py:55
  200.3 10.5 %collective-permute-start.45 = (bf16[208,368]{1,0:T(8,128)(2,1)S(1)}, bf16[208,368]{1,0:T(8,128)(2,1)S(1)}, u32[]{:S(2)}, u32[]{:S(2)}) collective-permute-start(bf16[208,368]{1,0:T(8,128)(2,1)S(1)} %fusion.2.refs_0_), channel_id=1, source_target_pairs={{0,6},{2,4},{4,2},{6,0},{1,7},{3,5},{5,3},{7,1},{8,14},{10,12},{12... | collective-permute-start | bytes 459272 | tf_op jit(solution)/shard_map/ppermute | solution.py:60
  202.0 9.2 %collective-permute-start.44 = (bf16[208,368]{1,0:T(8,128)(2,1)S(1)}, bf16[208,368]{1,0:T(8,128)(2,1)S(1)}, u32[]{:S(2)}, u32[]{:S(2)}) collective-permute-start(bf16[208,368]{1,0:T(8,128)(2,1)S(1)} %fusion.2.refs_0_), channel_id=1, source_target_pairs={{0,4},{2,6},{4,0},{6,2},{1,5},{3,7},{5,1},{7,3},{8,12},{10,14},{12... | collective-permute-start | bytes 459272 | tf_op jit(solution)/shard_map/ppermute | solution.py:60
  203.3 9.2 %collective-permute-start.43 = (bf16[208,368]{1,0:T(8,128)(2,1)S(1)}, bf16[208,368]{1,0:T(8,128)(2,1)S(1)}, u32[]{:S(2)}, u32[]{:S(2)}) collective-permute-start(bf16[208,368]{1,0:T(8,128)(2,1)S(1)} %fusion.2.refs_0_), channel_id=1, source_target_pairs={{0,2},{2,0},{4,6},{6,4},{1,3},{3,1},{5,7},{7,5},{8,10},{10,8},{12,... | collective-permute-start | bytes 459272 | tf_op jit(solution)/shard_map/ppermute | solution.py:60
  212.6 10.6 %collective-permute-start.48 = (bf16[1936,128]{1,0:T(8,128)(2,1)S(1)}, bf16[1936,128]{1,0:T(8,128)(2,1)S(1)}, u32[]{:S(2)}, u32[]{:S(2)}) collective-permute-start(bf16[1936,128]{1,0:T(8,128)(2,1)S(1)} %slice.103), channel_id=1, source_target_pairs={{0,2},{2,0},{4,6},{6,4},{1,3},{3,1},{5,7},{7,5},{8,10},{10,8},{12,... | collective-permute-start | bytes 1486856 | tf_op jit(solution)/shard_map/ppermute | solution.py:60
  213.3 10.5 %collective-permute-start.47 = (bf16[1936,128]{1,0:T(8,128)(2,1)S(1)}, bf16[1936,128]{1,0:T(8,128)(2,1)S(1)}, u32[]{:S(2)}, u32[]{:S(2)}) collective-permute-start(bf16[1936,128]{1,0:T(8,128)(2,1)S(1)} %slice.102), channel_id=1, source_target_pairs={{0,4},{2,6},{4,0},{6,2},{1,5},{3,7},{5,1},{7,3},{8,12},{10,14},{12... | collective-permute-start | bytes 1486856 | tf_op jit(solution)/shard_map/ppermute | solution.py:60
  216.3 3.6 %collective-permute-start.46 = (f32[2,368]{1,0:T(2,128)S(1)}, f32[2,368]{1,0:T(2,128)S(1)}, u32[]{:S(2)}, u32[]{:S(2)}) collective-permute-start(f32[2,368]{1,0:T(2,128)S(1)} %get-tuple-element.193), channel_id=1, source_target_pairs={{0,1},{1,0},{2,3},{3,2},{4,5},{5,4},{6,7},{7,6},{8,9},{9,8},{10,11... | collective-permute-start | bytes 8840 | tf_op jit(solution)/shard_map/ppermute | solution.py:60
  (33 other events, 485.7 us)
Sparse Core Ops, SparseCore 0:
  10.2 84.2 all-gather.2
  106.9 72.7 reduce-scatter.1
